TPU v7x, 32 devices: a whole 2x2x4 slice. The times are simulated.
32 devices in a mesh: dp: 8 (over z, y), tensor: 4 (over x, core).
Axes of the slice: x: 2, y: 2, z: 4, core: 2. Of those that a mesh axis runs over, the one named last changes fastest.
Arguments:
- x_embed: bfloat16 [8, 1024, 768], P('dp', 'tensor'), may hold values from -6 to 6
- thoughts: bfloat16 [8, 6, 768], P('dp'), may hold values from -6 to 6
- thought_pos: int32 [8, 6], P('dp'), may hold values from 0 to 1023, as said below
- img_start: int32 [8, 2], P('dp'), may hold values from 0 to 768, as said below
- pre_attn_gain: bfloat16 [768], P('dp'), may hold values from 0.5 to 1.5
- pre_attn_bias: bfloat16 [768], P('dp'), may hold values from -4 to 4
- w_qkv: bfloat16 [3, 768, 768], P(None, 'dp', 'tensor'), may hold values from -0.21875 to 0.21875
- b_qv: bfloat16 [2, 768], P(None, ('tensor', 'dp')), may hold values from -4 to 4
- w_proj: bfloat16 [768, 768], P('tensor', 'dp'), may hold values from -0.875 to 0.875
- b_proj: bfloat16 [768], P('dp'), may hold values from -4 to 4
- pre_mlp_gain: bfloat16 [768], P('dp'), may hold values from 0.5 to 1.5
- pre_mlp_bias: bfloat16 [768], P('dp'), may hold values from -4 to 4
- w_up: bfloat16 [768, 3072], P('dp', 'tensor'), may hold values from -0.21875 to 0.21875
- b_up: bfloat16 [3072], P(('tensor', 'dp')), may hold values from -4 to 4
- w_down: bfloat16 [3072, 768], P('tensor', 'dp'), may hold values from -0.109375 to 0.109375
- b_down: bfloat16 [768], P('dp'), may hold values from -4 to 4
- grad_out: bfloat16 [8, 1024, 768], P('dp', 'tensor'), may hold values from -6 to 6
Outputs:
- block_out: bfloat16 [8, 1024, 768], P('dp', 'tensor')
- grad_embed: float32 [8, 1024, 768], P('dp', 'tensor')
- grad_thoughts: float32 [8, 6, 768], P('dp', None, 'tensor')
- grad_pre_attn_gain: float32 [768], P('dp')
- grad_pre_attn_bias: float32 [768], P('dp')
- grad_w_qkv: float32 [3, 768, 768], P(None, 'dp', 'tensor')
- grad_b_qv: float32 [2, 768], P(None, ('tensor', 'dp'))
- grad_w_proj: float32 [768, 768], P('tensor', 'dp')
- grad_b_proj: float32 [768], P('dp')
- grad_pre_mlp_gain: float32 [768], P('dp')
- grad_pre_mlp_bias: float32 [768], P('dp')
- grad_w_up: float32 [768, 3072], P('dp', 'tensor')
- grad_b_up: float32 [3072], P(('tensor', 'dp'))
- grad_w_down: float32 [3072, 768], P('tensor', 'dp')
- grad_b_down: float32 [768], P('dp')
Inputs may be any that keep to these rules, and one draw needn't show every extreme that they name: `thought_pos`: in each sequence the 6 thought positions are consecutive and ascending. `img_start`: span i of a sequence starts between i * 512 and (i + 1) * 512 - 256, so the spans of a sequence never intersect.
All inputs are finite; a program needn't handle non-finite values.
Results may differ from a plain program's by a relative error of at most 0.017.
Values may be sent and summed in bfloat16 or wider, within the bound.
No kernel may reach another device: no remote copies, remote signals or barrier semaphores. Data moves between devices by JAX's collectives and lax.ppermute only.
A program may use at most 128 MiB of HBM per device.

v0:
```python
import functools

import jax
import jax.numpy as jnp
from jax import lax
from jax.experimental import pallas as pl
from jax.experimental.pallas import tpu as pltpu
from jax.sharding import PartitionSpec as P

HD = 64
IMG = 256
EPSILON = 1e-05
F32 = jnp.float32
LOW = jnp.bfloat16
COST = 1000


def swapped(array, axis, mask):
    return lax.ppermute(array, axis, [(i, i ^ mask) for i in range(lax.axis_size(axis))])


def dp_steps():
    size = lax.axis_size("dp")
    if size == 8:
        return ((6, 4), (2, 6), (1, 1))
    return tuple((1 << b, 1 << b) for b in reversed(range(size.bit_length() - 1)))


def parity(index, mask):
    bit = jnp.int32(0)
    for b in range(mask.bit_length()):
        if mask >> b & 1:
            bit = bit ^ ((index >> b) & 1)
    return bit


def slot_owners(steps):
    owners = [0]
    for mask, _ in steps:
        owners = owners + [o ^ mask for o in owners]
    return owners


def dp_gather(shard):
    steps, me = dp_steps(), lax.axis_index("dp")
    slots = shard[None]
    for mask, kinds in steps:
        other = swapped(slots, "dp", mask)
        first = parity(me, kinds) == 0
        slots = jnp.where(
            first, jnp.concatenate([slots, other]), jnp.concatenate([other, slots])
        )
    owners = slot_owners(steps)
    return jnp.stack([slots[owners.index(s)] for s in range(len(owners))])


MASKS = ((0,), (1,), (6,), (2, 4), (7,), (3, 5))


def rows_pick(own, other):
    first = (lax.axis_index("tensor") >> 1) == 0
    return jnp.stack([jnp.where(first, own, other), jnp.where(first, other, own)])


def dp_scatter_sum(blocks, place):
    steps, me = dp_steps(), lax.axis_index("dp")
    slots = jnp.stack([blocks[s] for s in slot_owners(steps)])
    for mask, kinds in reversed(steps):
        half = slots.shape[0] // 2
        first = parity(me, kinds) == 0
        keep = jnp.where(first, slots[:half], slots[half:])
        send = jnp.where(first, slots[half:], slots[:half])
        slots = keep.astype(F32) + swapped(send, "dp", mask).astype(F32)
    return slots[0]


def rows_gather(own):
    both = rows_pick(own, swapped(own, "tensor", 2))
    return both, swapped(both, "tensor", 1)


def after(value, *others):
    return lax.optimization_barrier((value, *others))[0]


def together(*values):
    return lax.optimization_barrier(values)


def dot(a, b, ca, cb, precision=None):
    return lax.dot_general(
        a, b, (((ca,), (cb,)), ((), ())), precision=precision, preferred_element_type=F32
    )


def normalised(values):
    centred = values - jnp.mean(values, axis=-1, keepdims=True)
    inverse = lax.rsqrt(jnp.mean(centred * centred, axis=-1, keepdims=True) + EPSILON)
    return centred * inverse, inverse


def norm_back(upstream, xhat, inverse, gain):
    scaled = upstream * gain
    return inverse * (
        scaled
        - jnp.mean(scaled, axis=-1, keepdims=True)
        - xhat * jnp.mean(scaled * xhat, axis=-1, keepdims=True)
    )


def gelu_pair(u):
    k, a = 0.7978845608028654, 0.044715
    square = u * u
    t = jnp.tanh(u * (k + (k * a) * square))
    rise = 0.5 * (1.0 + t)
    return u * rise, rise + (0.5 * u) * (1.0 - t * t) * (k + (3.0 * k * a) * square)


def cots_rows(cots, chunk):
    return jnp.concatenate([c[chunk] for c in cots])


def iota(shape, dim):
    return lax.broadcasted_iota(jnp.int32, shape, dim)


def call(kernel, outs, *args, scratch=(), mib=8, piped=False):
    if piped:
        whole = lambda shape: pl.BlockSpec(shape, lambda i: (0,) * len(shape))
        return pl.pallas_call(
            kernel,
            out_shape=tuple(jax.ShapeDtypeStruct(s, t) for s, t in outs),
            grid=(1,),
            in_specs=[whole(a.shape) for a in args],
            out_specs=tuple(pl.BlockSpec(memory_space=pltpu.VMEM) for _ in outs),
            compiler_params=pltpu.CompilerParams(vmem_limit_bytes=mib << 20),
            cost_estimate=pl.CostEstimate(flops=COST, bytes_accessed=0, transcendentals=0),
        )(*args)
    spec = lambda a: pl.BlockSpec(
        memory_space=pltpu.SMEM if a.ndim == 1 and a.dtype == jnp.int32 else pltpu.VMEM
    )
    return pl.pallas_call(
        kernel,
        out_shape=tuple(jax.ShapeDtypeStruct(s, t) for s, t in outs),
        in_specs=[spec(a) for a in args],
        out_specs=tuple(pl.BlockSpec(memory_space=pltpu.VMEM) for _ in outs),
        scratch_shapes=scratch,
        compiler_params=pltpu.CompilerParams(vmem_limit_bytes=mib << 20),
        cost_estimate=pl.CostEstimate(flops=COST, bytes_accessed=0, transcendentals=0),
    )(*args)


def input_kernel(
    place, x_zero, x_one, thoughts, thought_pos, vecs, w_in, bias,
    spliced_ref, xhat_ref, normed_ref, q_ref, k_ref, v_ref,
):
    core = place[0]
    rows = x_zero.shape[1]
    cols = q_ref.shape[1]
    gain, shift = vecs[0:1, :], vecs[1:2, :]
    for upper in range(2):
        for rel, ref in enumerate((x_zero, x_one)):
            first = upper * 2 * rows + (core ^ rel) * rows
            part = slice((2 * upper + rel) * rows, (2 * upper + rel + 1) * rows)
            match = (first + iota((rows, 1), 0)) == thought_pos[...]
            covered = jnp.sum(match.astype(F32), axis=1, keepdims=True) > 0.0
            picked = dot(match.astype(LOW), thoughts[...], 1, 0)
            spliced = jnp.where(covered, picked, ref[upper].astype(F32))
            xhat, _ = normalised(spliced)
            spliced_ref[part, :] = spliced.astype(LOW)
            xhat_ref[part, :] = xhat.astype(LOW)
            normed = (xhat * gain + shift).astype(LOW)
            normed_ref[part, :] = normed
            mixed = (dot(normed, w_in[...], 1, 0) + bias[...]).astype(LOW)
            q_ref[part, :] = mixed[:, :cols]
            k_ref[part, :] = mixed[:, cols : 2 * cols]
            v_ref[part, :] = mixed[:, 2 * cols :]


def query_limits(place, starts, chunk, rows):
    core, start = place[0], starts[chunk]
    col = iota((1, 2 * rows), 1)
    query = 2 * rows * chunk + jnp.where(col < rows, col + core * rows, col - core * rows)
    inside = (query >= start) & (query < start + IMG)
    return jnp.where(inside, start + (IMG - 1), query)


def key_positions(place, block, rows):
    first = (block >> 1) * (2 * rows) + (place[0] ^ (block & 1)) * rows
    return first + iota((rows, 1), 0)


def attend_kernel(
    chunk, place, starts, q_ref, k_ref, v_ref, w_proj,
    att_ref, log_ref, keep_ref, send_ref, acc_ref, top_ref, sum_ref,
):
    half, cols = att_ref.shape
    rows = half // 2
    heads = cols // HD
    head_of = iota((1, cols), 1) // HD
    limits = query_limits(place, starts, chunk, rows)
    queries = q_ref[chunk * half : (chunk + 1) * half, :] * LOW(0.125)
    acc_ref[...] = jnp.zeros_like(acc_ref)
    top_ref[...] = jnp.full_like(top_ref, -1e30)
    sum_ref[...] = jnp.zeros_like(sum_ref)

    @pl.loop(0, 2 * chunk + 2)
    def _(block):
        span = pl.ds(pl.multiple_of(block * rows, rows), rows)
        keys = k_ref[span, :]
        values = v_ref[span, :].T
        allowed = key_positions(place, block, rows) <= limits
        for head in range(heads):
            scores = dot(jnp.where(head_of == head, keys, LOW(0)), queries, 1, 1)
            scores = jnp.where(allowed, scores, -1e30)
            top = top_ref[head : head + 1, :]
            new_top = jnp.maximum(top, jnp.max(scores, axis=0, keepdims=True))
            exps = jnp.exp(scores - new_top)
            fade = jnp.exp(top - new_top)
            top_ref[head : head + 1, :] = new_top
            sum_ref[head : head + 1, :] = sum_ref[head : head + 1, :] * fade + jnp.sum(
                exps, axis=0, keepdims=True
            )
            part = slice(head * HD, (head + 1) * HD)
            acc_ref[part, :] = acc_ref[part, :] * fade + dot(values[part, :], exps.astype(LOW), 1, 0)

    for head in range(heads):
        part = slice(head * HD, (head + 1) * HD)
        acc_ref[part, :] = acc_ref[part, :] / sum_ref[head : head + 1, :]
    log_ref[...] = top_ref[...] + jnp.log(jnp.maximum(sum_ref[...], 1e-30))
    attended = acc_ref[...].T.astype(LOW)
    att_ref[...] = attended
    branch = dot(attended, w_proj[...], 1, 1)
    keep_ref[...] = branch[:rows]
    send_ref[...] = branch[rows:].astype(LOW)


def attend(chunk, place, starts, queries, keys, values, w_proj):
    length, cols = queries.shape
    half, width = length // 2, w_proj.shape[0]
    return call(
        functools.partial(attend_kernel, chunk),
        (
            ((half, cols), LOW),
            ((8, half), F32),
            ((half // 2, width), F32),
            ((half // 2, width), LOW),
        ),
        place,
        starts,
        queries,
        keys,
        values,
        w_proj,
        scratch=(
            pltpu.VMEM((cols, half), F32),
            pltpu.VMEM((8, half), F32),
            pltpu.VMEM((8, half), F32),
        ),
    )


def feed_kernel(
    chunk, spliced, total, other, cot_zero, cot_one, vecs, up_bias, w_up, w_down,
    residual_ref, normed_ref, hidden_ref, grad_ref, sum_ref, keep_ref, send_ref,
):
    half, width = residual_ref.shape
    rows = half // 2
    for rel, ref in enumerate((total, other)):
        part = slice(rel * rows, (rel + 1) * rows)
        residual = (
            spliced[chunk * half + rel * rows : chunk * half + (rel + 1) * rows, :].astype(F32)
            + ref[...].astype(F32)
            + vecs[2:3, :]
        )
        residual_ref[part, :] = residual
        xhat, _ = normalised(residual)
        normed_ref[part, :] = (xhat * vecs[3:4, :] + vecs[4:5, :]).astype(LOW)
    hidden_cols = w_up.shape[1]
    step = 256 if hidden_cols % 256 == 0 else hidden_cols
    for first in range(0, hidden_cols, step):
        cols = slice(first, first + step)
        hidden, slope = gelu_pair(dot(normed_ref[...], w_up[:, cols], 1, 0) + up_bias[:, cols])
        hidden_ref[:, cols] = hidden.astype(LOW)
        back = jnp.concatenate(
            [dot(cot_zero[chunk], w_down[:, cols], 1, 0), dot(cot_one[chunk], w_down[:, cols], 1, 0)]
        )
        grad = (back * slope).astype(LOW)
        grad_ref[:, cols] = grad
        sum_ref[:, cols] = jnp.sum(grad.astype(F32), axis=0, keepdims=True)
    back = dot(grad_ref[...], w_up[...], 1, 1)
    keep_ref[...] = back[:rows]
    send_ref[...] = back[rows:].astype(LOW)


def feed(chunk, spliced, total, other, cots, vecs, up_bias, w_up, w_down):
    length, width = spliced.shape
    half, hidden = length // 2, w_up.shape[1]
    return call(
        functools.partial(feed_kernel, chunk),
        (
            ((half, width), F32),
            ((half, width), LOW),
            ((half, hidden), LOW),
            ((half, hidden), LOW),
            ((1, hidden), F32),
            ((half // 2, width), F32),
            ((half // 2, width), LOW),
        ),
        spliced,
        total,
        other,
        *cots,
        vecs,
        up_bias,
        w_up,
        w_down,
    )


def back_kernel(
    chunk, place, starts, total, other, residual, cot_zero, cot_one, vecs, w_proj, q_ref, k_ref, v_ref, att, log, *rest,
):
    keys_in, rest = (rest[:2], rest[2:]) if chunk else ((), rest)
    grad_res_ref, branch_ref, dq_ref, dk_ref, dv_ref, sums_ref, dqt_ref, delta_ref, gatt_ref = rest
    half, width = residual.shape
    rows = half // 2
    cols = q_ref.shape[1]
    heads = cols // HD
    gain = vecs[3:4, :]
    sums = [0.0, 0.0, 0.0, 0.0]
    for rel, (ref, cot) in enumerate(((total, cot_zero), (other, cot_one))):
        part = slice(rel * rows, (rel + 1) * rows)
        upstream = ref[...].astype(F32)
        xhat, inverse = normalised(residual[part, :])
        out_grad = cot[chunk].astype(F32)
        grad_res = out_grad + norm_back(upstream, xhat, inverse, gain)
        grad_res_ref[part, :] = grad_res
        branch_ref[part, :] = grad_res.astype(LOW)
        for k, term in enumerate((upstream * xhat, upstream, grad_res, out_grad)):
            sums[k] = sums[k] + jnp.sum(term, axis=0, keepdims=True)
    for k in range(4):
        sums_ref[k : k + 1, :] = sums[k]
    grad_att = dot(branch_ref[...], w_proj[...], 1, 0).astype(LOW)
    gatt_ref[...] = grad_att
    head_of = iota((1, cols), 1) // HD
    head_rows = (iota((8, cols), 0) == iota((8, cols), 1) // HD).astype(F32)
    delta_ref[...] = dot(
        head_rows, grad_att.astype(F32) * att[...].astype(F32), 1, 1, lax.Precision.HIGHEST
    )
    limits = query_limits(place, starts, chunk, rows)
    dqt_ref[...] = jnp.zeros_like(dqt_ref)

    @pl.loop(0, 2 * chunk + 2)
    def _(block):
        span = pl.ds(pl.multiple_of(block * rows, rows), rows)
        keys, values = k_ref[span, :], v_ref[span, :]
        keys_t = keys.T
        queries = q_ref[chunk * half : (chunk + 1) * half, :] * LOW(0.125)
        grad_att = gatt_ref[...]
        allowed = key_positions(place, block, rows) <= limits
        dk = jnp.zeros((rows, cols), F32)
        dv = jnp.zeros((rows, cols), F32)
        for head in range(heads):
            mine = head_of == head
            scores = dot(jnp.where(mine, keys, LOW(0)), queries, 1, 1)
            probs = jnp.exp(jnp.where(allowed, scores, -1e30) - log[head : head + 1, :])
            grad_probs = dot(jnp.where(mine, values, LOW(0)), grad_att, 1, 1)
            grad_scores = (probs * (grad_probs - delta_ref[head : head + 1, :])).astype(LOW)
            dv = dv + dot(probs.astype(LOW), jnp.where(mine, grad_att, LOW(0)), 1, 0)
            dk = dk + dot(grad_scores, jnp.where(mine, queries, LOW(0)), 1, 0)
            part = slice(head * HD, (head + 1) * HD)
            dqt_ref[part, :] = dqt_ref[part, :] + dot(keys_t[part, :], grad_scores, 1, 0)
        if chunk:
            seen = jnp.where(block < 2, 1.0, 0.0)
            early = pl.ds(pl.multiple_of((block & 1) * rows, rows), rows)
            dk = dk + keys_in[0][early, :] * seen
            dv = dv + keys_in[1][early, :] * seen
        dk_ref[span, :] = dk.astype(dk_ref.dtype)
        dv_ref[span, :] = dv.astype(dv_ref.dtype)

    dq_ref[...] = (dqt_ref[...] * 0.125).T.astype(LOW)


def back(chunk, place, starts, total, other, residual, cots, vecs, w_proj, queries, keys, values, att, log, early):
    length, cols = queries.shape
    half, width = residual.shape
    kind = (((half * (chunk + 1), cols), LOW if chunk else F32),) * 2
    return call(
        functools.partial(back_kernel, chunk),
        (((half, width), F32), ((half, width), LOW), ((half, cols), LOW), *kind, ((8, width), F32)),
        place,
        starts,
        total,
        other,
        residual,
        *cots,
        vecs,
        w_proj,
        queries,
        keys,
        values,
        att,
        log,
        *early,
        scratch=(
            pltpu.VMEM((cols, half), F32),
            pltpu.VMEM((8, half), F32),
            pltpu.VMEM((half, cols), LOW),
        ),
    )


def input_back_kernel(
    place, thought_pos, dq_zero, dq_one, dk, dv, w_in, xhat, res_zero, res_one,
    keep_ref, send_ref, mixed_ref, small_ref, colsum_ref, picked_ref, grad_ref,
):
    half, cols = dq_zero.shape
    rows = half // 2
    sums = [0.0, 0.0, 0.0]
    for upper, dq in enumerate((dq_zero, dq_one)):
        for rel in range(2):
            part = slice((2 * upper + rel) * rows, (2 * upper + rel + 1) * rows)
            mixed = jnp.concatenate(
                [dq[rel * rows : (rel + 1) * rows, :], dk[part, :], dv[part, :]], axis=1
            )
            mixed_ref[part, :] = mixed
            grad = dot(mixed, w_in[...], 1, 1)
            grad_ref[part, :] = grad
            if rel:
                send_ref[upper] = grad.astype(LOW)
            else:
                keep_ref[upper] = grad
            terms = (grad * xhat[part, :].astype(F32), grad, mixed.astype(F32))
            sums = [a + jnp.sum(b, axis=0, keepdims=True) for a, b in zip(sums, terms)]
    small_ref[...] = jnp.zeros_like(small_ref)
    picked_ref[...] = jnp.zeros_like(picked_ref)
    count = thought_pos.shape[0]
    for k in range(count):
        at = thought_pos[k]
        row = (at // half) * half + (((at // rows) & 1) ^ place[0]) * rows + at % rows
        small_ref[k : k + 1, :] = grad_ref[pl.ds(row, 1), :]
        low = res_zero[pl.ds(jnp.minimum(row, half - 1), 1), :]
        high = res_one[pl.ds(jnp.maximum(row - half, 0), 1), :]
        picked_ref[k : k + 1, :] = jnp.where(row < half, low, high)
    small_ref[count : count + 1, :] = sums[0]
    small_ref[count + 1 : count + 2, :] = sums[1]
    colsum_ref[...] = sums[2]


def output_kernel(place, keep, got, spliced, res_zero, res_one, vecs, thought_pos, thoughts, small, picked, embed_ref, rows_ref):
    rows = keep.shape[0]
    gain = vecs[0:1, :]
    own = pl.ds(pl.multiple_of(place[3] * (2 * rows), 2 * rows), rows)
    xhat, inverse = normalised(spliced[own, :].astype(F32))
    residual = jnp.where(place[3] == 0, res_zero[:rows, :], res_one[:rows, :])
    grad = norm_back(keep[...] + got[...].astype(F32), xhat, inverse, gain) + residual
    at = (2 * place[3] + place[0]) * rows + iota((rows, 1), 0)
    covered = jnp.sum((at == thought_pos[...]).astype(F32), axis=1, keepdims=True) > 0.0
    embed_ref[...] = jnp.where(covered, 0.0, grad)
    count = thoughts.shape[0]
    xhat, inverse = normalised(thoughts[...].astype(F32))
    grad = norm_back(small[:count, :], xhat, inverse, gain) + picked[:count, :]
    cols = rows_ref.shape[1]
    rank = 2 * place[3] + place[0]
    rows_ref[...] = sum(
        jnp.where(rank == k, 1.0, 0.0) * grad[:, k * cols : (k + 1) * cols] for k in range(4)
    )


def fold_kernel(bit, place, keep, got, keep_ref, send_ref):
    half = keep_ref.shape[0]
    mine = place[bit] * half
    rest = half - mine
    for k in range(half):
        keep_ref[k] = keep[mine + k] + got[mine + k].astype(F32)
        send_ref[k] = (keep[rest + k] + got[rest + k].astype(F32)).astype(LOW)


def fold(bit, place, keep, got):
    shape = (keep.shape[0] // 2, *keep.shape[1:])
    return call(functools.partial(fold_kernel, bit), ((shape, F32), (shape, LOW)), place, keep, got)


def add_kernel(a, b, out):
    out[...] = (a[...].astype(F32) + b[...].astype(F32)).astype(LOW)


def add_full_kernel(a, b, out):
    out[...] = a[...] + b[...]


def add_full(a, b):
    return call(add_full_kernel, ((a.shape, F32),), a, b)[0]


def add_low(a, b):
    return call(add_kernel, ((a.shape, LOW),), a, b)[0]


def to_slots(place, sum_ref, keep_ref, send_ref, rows):
    for slot, owner in enumerate((0, 6, 2, 4)):
        mine = pl.multiple_of((owner ^ place[7]) * rows, rows)
        rest = pl.multiple_of((owner ^ 1 ^ place[7]) * rows, rows)
        keep_ref[slot, :rows, :] = sum_ref[pl.ds(mine, rows), :]
        send_ref[slot, :rows, :] = sum_ref[pl.ds(rest, rows), :].astype(LOW)


def product(left, right):
    return sum(dot(a[...], b[...], 0, 0) for a, b in zip(left, right))


def grad_kernel(place, *refs):
    *sides, keep_ref, send_ref, sum_ref = refs
    half = len(sides) // 2
    sum_ref[...] = product(sides[:half], sides[half:])
    to_slots(place, sum_ref, keep_ref, send_ref, keep_ref.shape[1])


def cot_grad_kernel(place, cot_zero, cot_one, hidden_zero, hidden_one, keep_ref, send_ref, sum_ref):
    rows = cot_zero.shape[1]
    left = [c[upper] for upper in range(2) for c in (cot_zero, cot_one)]
    right = [h[k * rows : (k + 1) * rows, :] for h in (hidden_zero, hidden_one) for k in range(2)]
    sum_ref[...] = sum(dot(a, b, 0, 0) for a, b in zip(left, right))
    to_slots(place, sum_ref, keep_ref, send_ref, keep_ref.shape[1])


def last_kernel(normed, mixed, branch_zero, branch_one, att_zero, att_one, out_ref):
    cols = mixed.shape[1]
    out_ref[:, :cols] = dot(normed[...], mixed[...], 0, 0)
    out_ref[:, cols:] = product((branch_zero, branch_one), (att_zero, att_one))


def slot_kernel(place, sums, small, back_zero, back_one, up_zero, up_one, mixed_sums, keep_ref, send_ref, flat_ref):
    rows = keep_ref.shape[1] - 8
    to_slots(place, sums, keep_ref, send_ref, rows)
    cols = (mixed_sums.shape[1]) // 3
    count = small.shape[0] - 2
    back = back_zero[...] + back_one[...]
    wide = [small[count : count + 1, :], small[count + 1 :, :], back[2:3], back[0:1], back[1:2], back[3:4]]
    wide += [up_zero[...] + up_one[...], mixed_sums[:, :cols], mixed_sums[:, 2 * cols :]]
    for owner in range(8):
        parts = []
        for v in wide:
            n = v.shape[1] // 8
            parts.append(v[:, owner * n : (owner + 1) * n])
        parts.append(jnp.zeros((1, keep_ref.shape[2] - sum(p.shape[1] for p in parts)), F32))
        flat_ref[owner : owner + 1, :] = jnp.concatenate(parts, axis=1)
    for slot, owner in enumerate((0, 6, 2, 4)):
        space = (8, keep_ref.shape[2])
        keep_ref[slot, rows:, :] = jnp.broadcast_to(flat_ref[pl.ds(owner ^ place[7], 1), :], space)
        send_ref[slot, rows:, :] = jnp.broadcast_to(flat_ref[pl.ds(owner ^ 1 ^ place[7], 1), :], space).astype(LOW)


def finish_kernel(keep, got, in_ref, proj_ref, flat_ref):
    rows, cols = in_ref.shape[1:]
    total = keep[0] + got[0].astype(F32)
    for k in range(3):
        in_ref[k] = total[:rows, k * cols : (k + 1) * cols]
    proj_ref[...] = total[:rows, 3 * cols :].T
    flat_ref[...] = total[rows : rows + 1, :]


def pair_kernel(up_keep, up_got, down_keep, down_got, up_ref, down_ref):
    up_ref[...] = up_keep[0] + up_got[0].astype(F32)
    down_ref[...] = (down_keep[0] + down_got[0].astype(F32)).T


def result_kernel(place, keep, got, res_zero, res_one, vecs, out_ref):
    rows = out_ref.shape[0]
    residual = jnp.where(place[3] == 0, res_zero[:rows, :], res_one[:rows, :])
    out_ref[...] = (residual + (keep[...] + got[...].astype(F32)) + vecs[5:6, :]).astype(LOW)


def pick_kernel(place, own, other, out_ref):
    out_ref[place[3]] = own[...]
    out_ref[1 - place[3]] = other[...]


def pick(place, own, other):
    return call(pick_kernel, (((2, *own.shape), own.dtype),), place, own, other)[0]


def stack_kernel(a, b, out_ref):
    out_ref[0] = a[...]
    out_ref[1] = b[...]


def stacked(a, b):
    return call(stack_kernel, (((2, *a.shape), a.dtype),), a, b)[0]


def grad_blocks(kernel, place, shard_rows, *sides):
    width, cols = 8 * shard_rows, sides[-1].shape[1]
    shape = (4, shard_rows, cols)
    scratch = (pltpu.VMEM((width, cols), F32),)
    return call(kernel, ((shape, F32), (shape, LOW)), place, *sides, scratch=scratch, mib=12)


def plain_grad(shard_rows, *sides):
    half = len(sides) // 2
    total = sum(dot(a, b, 0, 0) for a, b in zip(sides[:half], sides[half:])).astype(LOW)
    return dp_scatter_sum(total.reshape(-1, shard_rows, total.shape[1]), None)


def fast(shard_rows):
    return lax.axis_size("dp") == 8 and shard_rows % 16 == 0


def place_pieces(masks, place, pieces, write):
    for piece, owners in zip(pieces, masks):
        for k, mask in enumerate(owners):
            write(place[4] ^ mask, piece, k)


def first_kernel(masks, spans, hidden_cols, place, *refs):
    pieces, (w_in_ref, w_proj_ref, vecs_ref, up_ref, bias_ref, flat_ref) = refs[: len(masks)], refs[len(masks) :]
    width, qkv_cols = w_in_ref.shape
    shard_rows = width // 8

    def write(owner, piece, k):
        at = pl.ds(pl.multiple_of(owner * shard_rows, shard_rows), shard_rows)
        w_in_ref[at, :] = piece[k, :shard_rows, :qkv_cols]
        w_proj_ref[at, :] = piece[k, :shard_rows, qkv_cols:]
        flat_ref[pl.ds(owner, 1), :] = piece[k, shard_rows : shard_rows + 1, :].astype(F32)

    place_pieces(masks, place, pieces, write)
    flat = flat_ref[...]
    joined = [
        jnp.concatenate([flat[s : s + 1, a:b] for s in range(8)], axis=1) for a, b in zip(spans, spans[1:])
    ]
    for k in range(6):
        vecs_ref[k : k + 1, :] = joined[k]
    up_ref[...] = joined[6]
    bias_ref[...] = jnp.concatenate([joined[7], jnp.zeros_like(joined[7]), joined[8]], axis=1)


def plain_kernel(masks, place, *refs):
    out_ref = refs[-1]
    rows = out_ref.shape[0] // 8

    def write(owner, piece, k):
        out_ref[pl.ds(pl.multiple_of(owner * rows, rows), rows), :] = piece[k]

    place_pieces(masks, place, refs[:-1], write)


def pack_kernel(w_qkv, w_proj, w_down, *refs):
    *vectors, first_ref, down_ref = refs
    rows = w_qkv.shape[1]
    parts = [w_qkv[0], w_qkv[1], w_qkv[2], w_proj[...].T]
    first_ref[:rows, :] = jnp.concatenate(parts, axis=1)
    rows_of = [v[...].astype(F32) for v in vectors]
    rows_of = rows_of[:-1] + [rows_of[-1][0:1], rows_of[-1][1:2]]
    flat = jnp.concatenate(rows_of, axis=1)
    flat = jnp.concatenate([flat, jnp.zeros((1, first_ref.shape[1] - flat.shape[1]), F32)], axis=1)
    first_ref[rows:, :] = jnp.broadcast_to(flat, (8, flat.shape[1])).astype(LOW)
    down_ref[...] = w_down[...].T


def spans_of(vectors):
    spans = [0]
    for n in (*(v.shape[1] for v in vectors), vectors[-1].shape[1]):
        spans.append(spans[-1] + n)
    return spans


def first_unpacked(place, pieces, vectors, qkv_cols, head_cols, width):
    shapes = (
        ((width, qkv_cols), LOW),
        ((width, head_cols), LOW),
        ((6, width), F32),
        ((1, 8 * vectors[6].shape[1]), F32),
        ((1, qkv_cols), F32),
    )
    return call(
        functools.partial(first_kernel, MASKS, spans_of(vectors), 0),
        shapes,
        place,
        *pieces,
        scratch=(pltpu.VMEM((8, qkv_cols + head_cols), F32),),
    )


def unpacked(place, pieces):
    rows, cols = pieces[0].shape[1:]
    return call(functools.partial(plain_kernel, MASKS), (((8 * rows, cols), LOW),), place, *pieces)[0]


def plain_first(shard, vectors, qkv_cols, width):
    flat = dp_gather(jnp.concatenate([*vectors[:-1], vectors[-1][0:1], vectors[-1][1:2]], axis=1))[:, 0].astype(F32)
    whole = dp_gather(shard).reshape(width, -1)
    spans = spans_of(vectors)
    joined = [flat[:, a:b].reshape(1, -1) for a, b in zip(spans, spans[1:])]
    return (
        whole[:, :qkv_cols],
        whole[:, qkv_cols:],
        jnp.concatenate(joined[:6]),
        joined[6],
        jnp.concatenate([joined[7], jnp.zeros_like(joined[7]), joined[8]], axis=1),
    )


def down_kernel(hidden_zero, hidden_one, w_down, keep_ref, send_ref):
    rows = keep_ref.shape[1]
    for upper, hidden in enumerate((hidden_zero, hidden_one)):
        part = dot(hidden[...], w_down[...], 1, 1)
        keep_ref[upper] = part[:rows]
        send_ref[upper] = part[rows:].astype(LOW)


def local(
    x_embed,
    thoughts,
    thought_pos,
    img_start,
    pre_attn_gain,
    pre_attn_bias,
    w_qkv,
    b_qv,
    w_proj,
    b_proj,
    pre_mlp_gain,
    pre_mlp_bias,
    w_up,
    b_up,
    w_down,
    b_down,
    grad_out,
):
    dp = lax.axis_size("dp")
    tensor_rank = lax.axis_index("tensor")
    dp_rank = lax.axis_index("dp")
    _, rows, width = x_embed.shape
    length, half = 4 * rows, 2 * rows
    shard_rows = w_qkv.shape[1]
    head_cols = w_qkv.shape[2]
    qkv_cols = 3 * head_cols
    hidden_cols = w_up.shape[1]
    table = []
    for d in range(dp):
        for t in range(4):
            table.append((t & 1, 0, 0, t >> 1, d, (d >> 1 ^ d >> 2) & 1, d >> 2 & 1, d & 1))
    place = jnp.asarray(table, jnp.int32)[dp_rank * 4 + tensor_rank]
    starts = img_start[0]

    flat = [v.reshape(1, -1) for v in (pre_attn_gain, pre_attn_bias, b_proj, pre_mlp_gain, pre_mlp_bias, b_down, b_up)]
    flat.append(b_qv)
    sizes = (qkv_cols, head_cols, width)
    quick = fast(shard_rows)

    if quick:
        pack_one, pack_three = call(
            pack_kernel,
            (((shard_rows + 8, qkv_cols + head_cols), LOW), ((shard_rows, hidden_cols), LOW)),
            w_qkv,
            w_proj,
            w_down,
            *flat,
            piped=True,
        )
        x_far = swapped(x_embed[0], "tensor", 2)
        far_one = swapped(pack_one, "dp", 6)
        across_one = swapped(pack_one, "dp", 1)
        across_two = swapped(w_up, "dp", 1)
        x_far, far_one, across_one, across_two = together(x_far, far_one, across_one, across_two)

        x_both = pick(place, x_embed[0], x_far)
        cot_far = swapped(after(grad_out[0], x_far), "tensor", 2)
        near_one = swapped(stacked(pack_one, far_one), "dp", 2)
        far_across_one = swapped(far_one, "dp", 1)
        across_three = swapped(after(pack_three, across_two), "dp", 1)
        x_other = swapped(x_both, "tensor", 1)
        near_one, far_across_one, across_three, x_other, cot_far = together(
            near_one, far_across_one, across_three, x_other, cot_far
        )

        near_across_one = swapped(near_one, "dp", 1)
        far_two = swapped(after(w_up, near_one), "dp", 6)
        cot_both = pick(place, grad_out[0], cot_far)
        cot_other = swapped(cot_both, "tensor", 1)
        near_across_one, far_two, cot_other = together(near_across_one, far_two, cot_other)

        pieces = (pack_one[None], across_one[None], far_one[None], near_one, far_across_one[None], near_across_one)
        w_in, w_proj_t, vecs, up_bias, all_bias = first_unpacked(place, pieces, flat, *sizes)
        near_two = swapped(stacked(w_up, far_two), "dp", 2)
        far_across_two = swapped(far_two, "dp", 1)
        x_rows, cots = (x_both, x_other), (cot_both, cot_other)
    else:
        x_rows, cots = rows_gather(x_embed[0]), rows_gather(grad_out[0])
        first_pack = jnp.concatenate([w_qkv[0], w_qkv[1], w_qkv[2], w_proj.T], axis=1)
        w_in, w_proj_t, vecs, up_bias, all_bias = plain_first(first_pack, flat, qkv_cols, width)
        w_up_all = dp_gather(w_up).reshape(width, hidden_cols)
        w_down_t = dp_gather(w_down.T).reshape(width, hidden_cols)

    spliced, xhat_one, normed, queries, keys, values = call(
        input_kernel,
        (((length, width), LOW),) * 3 + (((length, head_cols), LOW),) * 3,
        place,
        *x_rows,
        thoughts[0],
        thought_pos,
        vecs,
        w_in,
        all_bias,
    )

    def core_sum(keep, send):
        return add_low(keep, swapped(send, "tensor", 1))

    att_zero, log_zero, *part = attend(0, place, starts, queries, keys, values, w_proj_t)
    if quick:
        near_two, far_across_two, part[1] = together(near_two, far_across_two, part[1])
    branch_zero = core_sum(*part)
    far_zero = swapped(branch_zero, "tensor", 2)
    if quick:
        near_across_two = swapped(near_two, "dp", 1)
        far_three = swapped(after(pack_three, near_two), "dp", 6)
    att_one, log_one, *part = attend(1, after(place, branch_zero), starts, queries, keys, values, w_proj_t)
    if quick:
        near_across_two, far_three, part[1] = together(near_across_two, far_three, part[1])
        near_three = swapped(stacked(pack_three, far_three), "dp", 2)
        far_across_three = swapped(far_three, "dp", 1)
    branch_one = core_sum(*part)
    far_zero, branch_one = together(far_zero, branch_one)
    far_one = swapped(branch_one, "tensor", 2)
    total_zero = add_low(branch_zero, far_zero)
    other_zero = swapped(total_zero, "tensor", 1)
    if quick:
        pieces = (w_up[None], across_two[None], far_two[None], near_two, far_across_two[None], near_across_two)
        w_up_all = unpacked(after(place, other_zero), pieces)
        near_three, far_across_three, w_up_all = together(near_three, far_across_three, w_up_all)
        near_across_three = swapped(near_three, "dp", 1)
        pieces = (pack_three[None], across_three[None], far_three[None], near_three, far_across_three[None], near_across_three)
        w_down_t = unpacked(place, pieces)
    total_one = add_low(branch_one, far_one)
    other_one = swapped(total_one, "tensor", 1)
    attended, logs = (att_zero, att_one), (log_zero, log_one)

    weights = (vecs, up_bias, w_up_all, w_down_t)
    fed_zero = feed(0, spliced, total_zero, other_zero, cots, *weights)
    grad_zero = core_sum(*fed_zero[5:])
    far_zero = swapped(grad_zero, "tensor", 2)
    fed_one = feed(1, after(spliced, grad_zero), total_one, other_one, cots, *weights)
    grad_one = core_sum(*fed_one[5:])
    residual, normed_two, hidden, grad_hidden, up_sums = zip(fed_zero[:5], fed_one[:5])
    ups = (*normed_two, *grad_hidden)
    if quick:
        up_keep, up_send = grad_blocks(grad_kernel, after(place, grad_one), shard_rows, *ups)
        up_got = swapped(up_send, "dp", 1)
        down_keep, down_send = grad_blocks(cot_grad_kernel, after(place, up_keep), shard_rows, *cots, *hidden)
        far_zero, down_send = together(far_zero, down_send)
    else:
        downs = (cots_rows(cots, 0), cots_rows(cots, 1), *hidden)
        out_up, out_down = plain_grad(shard_rows, *ups), plain_grad(shard_rows, *downs)
    far_one = swapped(after(grad_one, far_zero), "tensor", 2)
    total_zero = add_low(grad_zero, far_zero)
    other_zero = swapped(total_zero, "tensor", 1)
    mlp_keep, mlp_send = call(
        down_kernel,
        (((2, rows, width), F32), ((2, rows, width), LOW)),
        after(hidden[0], total_zero),
        hidden[1],
        w_down_t,
    )
    mlp_got = swapped(mlp_send, "tensor", 1)

    back_zero = back(
        0, after(place, mlp_keep), starts, total_zero, other_zero, residual[0], cots, vecs, w_proj_t,
        queries, keys, values, attended[0], logs[0], (),
    )
    if quick:
        up_got, far_one, back_dk = together(up_got, far_one, back_zero[3])
        back_zero = (*back_zero[:3], back_dk, *back_zero[4:])
        up_keep, up_send = fold(5, place, up_keep, up_got)
        up_got = swapped(up_send, "dp", 2)
        down_got = swapped(after(down_send, up_got), "dp", 1)
    total_one = add_low(grad_one, far_one)
    other_one = swapped(total_one, "tensor", 1)
    mlp_keep, mlp_send = fold(3, place, mlp_keep, mlp_got)
    mlp_got = swapped(after(mlp_send, far_one), "tensor", 2)
    back_one = back(
        1, after(place, mlp_keep), starts, total_one, other_one, residual[1], cots, vecs, w_proj_t,
        queries, keys, values, attended[1], logs[1], back_zero[3:5],
    )
    grad_residual, grad_branch, grad_queries = zip(back_zero[:3], back_one[:3])
    grad_keys, grad_values = back_one[3:5]
    if quick:
        grad_keys, mlp_got, up_got = together(grad_keys, mlp_got, up_got)
        up_keep, up_send = fold(6, place, up_keep, up_got)
        up_got = swapped(up_send, "dp", 6)

    count = thoughts.shape[1]
    keep, send, grad_mixed, small, mixed_sums, picked = call(
        input_back_kernel,
        (
            ((2, rows, width), F32),
            ((2, rows, width), LOW),
            ((length, qkv_cols), LOW),
            ((-(-(count + 2) // 8) * 8, width), F32),
            ((1, qkv_cols), F32),
            ((-(-count // 8) * 8, width), F32),
        ),
        place,
        thought_pos[0],
        *grad_queries,
        grad_keys,
        grad_values,
        w_in,
        xhat_one,
        *grad_residual,
        scratch=(pltpu.VMEM((length, width), F32),),
    )
    got = swapped(send, "tensor", 1)
    small_got = swapped(small, "tensor", 1)
    lasts = (normed, grad_mixed, *grad_branch, *attended)
    if quick:
        got, small_got = together(got, small_got)
    keep, send = fold(3, place, keep, got)
    got = swapped(send, "tensor", 2)
    small = add_full(small, small_got)
    small_got = swapped(small, "tensor", 2)
    if quick:
        last = call(last_kernel, (((width, qkv_cols + head_cols), F32),), after(normed, send, small), *lasts[1:])[0]
        last, small_got = together(last, small_got)
    small = add_full(small, small_got)
    rest = (small, back_zero[5], back_one[5], *up_sums, mixed_sums)
    if quick:
        shape = (4, shard_rows + 8, qkv_cols + head_cols)
        scratch = (pltpu.VMEM((8, qkv_cols + head_cols), F32),)
        last_keep, last_send = call(slot_kernel, ((shape, F32), (shape, LOW)), place, last, *rest, scratch=scratch)
        last_got = swapped(last_send, "dp", 1)
        down_keep, down_send = fold(5, place, down_keep, after(down_got, last_send))
        down_got = swapped(down_send, "dp", 2)
        last_got, up_got = together(last_got, up_got)
        last_keep, last_send = fold(5, place, last_keep, last_got)
        last_got = swapped(last_send, "dp", 2)
        down_keep, down_send = fold(6, place, down_keep, down_got)
        down_got = swapped(down_send, "dp", 6)
    mlp = (mlp_keep[0], mlp_got[0], *residual, vecs)
    block_out = call(result_kernel, (((rows, width), LOW),), place, *mlp)[0]
    grad_embed, grad_thoughts = call(
        output_kernel,
        (((rows, width), F32), ((count, width // 4), F32)),
        place,
        keep[0],
        got[0],
        spliced,
        *grad_residual,
        vecs,
        thought_pos,
        thoughts[0],
        small,
        picked,
    )
    if quick:
        last_keep, last_send = fold(6, place, last_keep, last_got)
        last_got = swapped(last_send, "dp", 6)
        out_up, out_down = call(
            pair_kernel,
            (((shard_rows, hidden_cols), F32), ((hidden_cols, shard_rows), F32)),
            up_keep,
            up_got,
            down_keep,
            down_got,
        )
        out_in, out_proj, vec = call(
            finish_kernel,
            (((3, shard_rows, head_cols), F32), ((head_cols, shard_rows), F32), ((1, qkv_cols + head_cols), F32)),
            last_keep,
            last_got,
        )
        vec = vec[0]
    else:
        out_in = plain_grad(shard_rows, *lasts[:2])
        out_in = jnp.moveaxis(out_in.reshape(shard_rows, 3, head_cols), 1, 0)
        out_proj = plain_grad(shard_rows, *lasts[2:]).T
        out_down = out_down.T
        two = back_zero[5] + back_one[5]
        vec = (small[count], small[count + 1], two[2], two[0], two[1], two[3], up_sums[0] + up_sums[1])
        vec += (mixed_sums[0, :head_cols], mixed_sums[0, 2 * head_cols :])
        vec = jnp.concatenate([v.reshape(dp, -1) for v in vec], axis=1)
        vec = dp_scatter_sum(vec[:, None, :], None)[0]
    outs, first = [], 0
    for n in (*(v.shape[1] for v in flat[:7]), b_qv.size):
        outs.append(vec[first : first + n])
        first += n
    out_gain_one, out_bias_one, out_b_proj, out_gain_two, out_bias_two, out_b_down, out_b_up, out_qv = outs

    return (
        block_out[None],
        grad_embed[None],
        grad_thoughts[None],
        out_gain_one,
        out_bias_one,
        out_in,
        out_qv.reshape(2, -1),
        out_proj,
        out_b_proj,
        out_gain_two,
        out_bias_two,
        out_up,
        out_b_up,
        out_down,
        out_b_down,
    )


def solution(mesh):
    in_specs = (
        P("dp", "tensor", None),
        P("dp", None, None),
        P("dp", None),
        P("dp", None),
        P("dp"),
        P("dp"),
        P(None, "dp", "tensor"),
        P(None, ("tensor", "dp")),
        P("tensor", "dp"),
        P("dp"),
        P("dp"),
        P("dp"),
        P("dp", "tensor"),
        P(("tensor", "dp")),
        P("tensor", "dp"),
        P("dp"),
        P("dp", "tensor", None),
    )
    out_specs = (
        P("dp", "tensor", None),
        P("dp", "tensor", None),
        P("dp", None, "tensor"),
        P("dp"),
        P("dp"),
        P(None, "dp", "tensor"),
        P(None, ("tensor", "dp")),
        P("tensor", "dp"),
        P("dp"),
        P("dp"),
        P("dp"),
        P("dp", "tensor"),
        P(("tensor", "dp")),
        P("tensor", "dp"),
        P("dp"),
    )
    return jax.shard_map(local, mesh=mesh, in_specs=in_specs, out_specs=out_specs, check_vma=False)
```

profile of v0, /device:TPU:0, one launch (start us, length us, event | category | flops | bytes accessed | tf_op | source)
XLA Modules:
  0.0 206.1 jit_solution(14228285475893139655)
XLA Ops:
  0.7 3.0 %collective-permute-start = (bf16[256,768]{1,0:T(8,128)(2,1)}, bf16[256,768]{1,0:T(8,128)(2,1)S(1)}, u32[]{:S(2)}, u32[]{:S(2)}) collective-permute-start(bf16[256,768]{1,0:T(8,128)(2,1)} %bitcast.57), channel_id=1, source_target_pairs={{0,2},{1,3},{2,0},{3,1},{4,6},{5,7},{6,4},{7,5},{8,10},{9,11},{10,... | collective-permute-start | bytes 1179656 | tf_op jit(solution)/shard_map/ppermute | solution.py:19
  3.7 1.1 copy.33.w_down
  4.7 0.9 copy-done.3
  11.9 1.6 collective-permute-start.2
  13.5 3.6 %collective-permute-start.1 = (bf16[104,768]{1,0:T(8,128)(2,1)S(1)}, bf16[104,768]{1,0:T(8,128)(2,1)S(1)}, u32[]{:S(2)}, u32[]{:S(2)}) collective-permute-start(bf16[104,768]{1,0:T(8,128)(2,1)S(1)} %get-tuple-element.153.a), channel_id=1, source_target_pairs={{0,24},{4,28},{8,16},{12,20},{16,8},{20,12},{24,0},{28,4},{1,25},{... | collective-permute-start | bytes 479240 | tf_op jit(solution)/shard_map/ppermute | solution.py:19
  18.3 4.2 %collective-permute-done.3 = bf16[96,768]{1,0:T(8,128)(2,1)S(1)} collective-permute-done((bf16[96,768]{1,0:T(8,128)(2,1)}, bf16[96,768]{1,0:T(8,128)(2,1)S(1)}, u32[]{:S(2)}, u32[]{:S(2)}) %collective-permute-start.3) | collective-permute-done | bytes 147488 | tf_op jit(solution)/shard_map/ppermute | solution.py:19
  22.4 1.0 copy-done.1
  24.7 1.4 collective-permute-start.4
  26.7 1.5 collective-permute-start.6
  28.2 7.0 %collective-permute-done.6 = bf16[96,768]{1,0:T(8,128)(2,1)S(1)} collective-permute-done((bf16[96,768]{1,0:T(8,128)(2,1)S(1)}, bf16[96,768]{1,0:T(8,128)(2,1)S(1)}, u32[]{:S(2)}, u32[]{:S(2)}) %collective-permute-start.6) | collective-permute-done | bytes 147488 | tf_op jit(solution)/shard_map/ppermute | solution.py:19
  36.9 2.9 %collective-permute-start.10 = (bf16[96,768]{1,0:T(8,128)(2,1)S(1)}, bf16[96,768]{1,0:T(8,128)(2,1)S(1)}, u32[]{:S(2)}, u32[]{:S(2)}) collective-permute-start(bf16[96,768]{1,0:T(8,128)(2,1)S(1)} %copy-done), channel_id=1, source_target_pairs={{0,24},{4,28},{8,16},{12,20},{16,8},{20,12},{24,0},{28,4},{1,25},{... | collective-permute-start | bytes 442376 | tf_op jit(solution)/shard_map/ppermute | solution.py:19
  39.8 5.0 %collective-permute-done.10.b = bf16[96,768]{1,0:T(8,128)(2,1)S(1)} collective-permute-done((bf16[96,768]{1,0:T(8,128)(2,1)S(1)}, bf16[96,768]{1,0:T(8,128)(2,1)S(1)}, u32[]{:S(2)}, u32[]{:S(2)}) %collective-permute-start.10) | collective-permute-done | bytes 147488 | tf_op jit(solution)/shard_map/ppermute | solution.py:19
  44.7 1.5 collective-permute-done.9.refs_5_
  46.3 1.4 collective-permute-start.12
  47.7 1.2 collective-permute-start.13
  48.9 0.8 shard_map.293
  49.8 3.8 %shard_map.294 = (bf16[1024,768]{1,0:T(8,128)(2,1)S(1)}, bf16[1024,768]{1,0:T(8,128)(2,1)S(1)}, bf16[1024,768]{1,0:T(8,128)(2,1)S(1)}, bf16[1024,192]{1,0:T(8,12...) custom-call(s32[8]{0:T(128)S(1)} %dynamic-slice_bitcast_fusion.place, ...), custom_call_target="tpu_custom_call" | custom-call | flops 1000 | tf_op jit(solution)/shard_map/pallas_call | solution.py:142
  53.6 3.6 %shard_map.295 = (bf16[512,192]{1,0:T(8,128)(2,1)S(1)}, f32[8,512]{1,0:T(8,128)S(1)}, f32[256,768]{1,0:T(8,128)S(1)}, bf16[256,768]{1,0:T(8,128)(2,1)S(1)}) custom-call(s32[8]{0:T(128)S(1)} %dynamic-slice_bitcast_fusion.place, s32[2]{0:T(128)S(1)} %bitcast.69, bf16[1024,192]{1,0:T(8,128)(2,1)S(1)} %get-tuple-element.171.q_ref, ...), custom_call_target="tpu_custom_call" | custom-call | flops 1000 | tf_op jit(solution)/shard_map/pallas_call | solution.py:142
  57.3 0.8 collective-permute-start.16
  58.1 2.5 %collective-permute-start.17 = (bf16[96,768]{1,0:T(8,128)(2,1)S(1)}, bf16[96,768]{1,0:T(8,128)(2,1)S(1)}, u32[]{:S(2)}, u32[]{:S(2)}) collective-permute-start(bf16[96,768]{1,0:T(8,128)(2,1)S(1)} %get-tuple-element.182.a), channel_id=1, source_target_pairs={{0,24},{4,28},{8,16},{12,20},{16,8},{20,12},{24,0},{28,4},{1,25},{... | collective-permute-start | bytes 442376 | tf_op jit(solution)/shard_map/ppermute | solution.py:19
  60.7 6.4 %shard_map.298 = (bf16[512,192]{1,0:T(8,128)(2,1)S(1)}, f32[8,512]{1,0:T(8,128)S(1)}, f32[256,768]{1,0:T(8,128)S(1)}, bf16[256,768]{1,0:T(8,128)(2,1)S(1)}) custom-call(s32[8]{0:T(128)S(1)} %dynamic-slice_bitcast_fusion.place, s32[2]{0:T(128)S(1)} %bitcast.70, bf16[1024,192]{1,0:T(8,128)(2,1)S(1)} %get-tuple-element.171.q_ref, ...), custom_call_target="tpu_custom_call" | custom-call | flops 1000 | tf_op jit(solution)/shard_map/pallas_call | solution.py:142
  67.8 1.1 collective-permute-done.18.b
  69.0 9.7 %collective-permute-done.15.b = bf16[256,768]{1,0:T(8,128)(2,1)S(1)} collective-permute-done((bf16[256,768]{1,0:T(8,128)(2,1)S(1)}, bf16[256,768]{1,0:T(8,128)(2,1)S(1)}, u32[]{:S(2)}, u32[]{:S(2)}) %collective-permute-start.15) | collective-permute-done | bytes 393248 | tf_op jit(solution)/shard_map/ppermute | solution.py:19
  78.9 0.8 collective-permute-start.20
  80.5 0.8 collective-permute-start.25
  81.9 3.8 %collective-permute-done.21 = bf16[96,768]{1,0:T(8,128)(2,1)S(1)} collective-permute-done((bf16[96,768]{1,0:T(8,128)(2,1)S(1)}, bf16[96,768]{1,0:T(8,128)(2,1)S(1)}, u32[]{:S(2)}, u32[]{:S(2)}) %collective-permute-start.21) | collective-permute-done | bytes 147488 | tf_op jit(solution)/shard_map/ppermute | solution.py:19
  85.7 2.7 %collective-permute-done.20.refs_3_ = bf16[2,96,768]{2,1,0:T(8,128)(2,1)S(1)} collective-permute-done((bf16[2,96,768]{2,1,0:T(8,128)(2,1)S(1)}, bf16[2,96,768]{2,1,0:T(8,128)(2,1)S(1)}, u32[]{:S(2)}, u32[]{:S(2)}) %collective-permute-start.20) | collective-permute-done | bytes 294944 | tf_op jit(solution)/shard_map/ppermute | solution.py:19
  88.4 1.2 collective-permute-start.22
  89.6 7.4 %collective-permute-done.22.refs_5_ = bf16[2,96,768]{2,1,0:T(8,128)(2,1)S(1)} collective-permute-done((bf16[2,96,768]{2,1,0:T(8,128)(2,1)S(1)}, bf16[2,96,768]{2,1,0:T(8,128)(2,1)S(1)}, u32[]{:S(2)}, u32[]{:S(2)}) %collective-permute-start.22) | collective-permute-done | bytes 294944 | tf_op jit(solution)/shard_map/ppermute | solution.py:19
  97.6 2.8 %shard_map.304 = (f32[512,768]{1,0:T(8,128)S(1)}, bf16[512,768]{1,0:T(8,128)(2,1)S(1)}, bf16[512,768]{1,0:T(8,128)(2,1)S(1)}, bf16[512,768]{1,0:T(8,128)(2,1)S(1...) custom-call(bf16[1024,768]{1,0:T(8,128)(2,1)S(1)} %get-tuple-element.199.spliced, ...), custom_call_target="tpu_custom_call" | custom-call | flops 1000 | tf_op jit(solution)/shard_map/pallas_call | solution.py:142
  101.2 1.0 collective-permute-done.23.b
  102.8 2.8 %shard_map.307 = (f32[512,768]{1,0:T(8,128)S(1)}, bf16[512,768]{1,0:T(8,128)(2,1)S(1)}, bf16[512,768]{1,0:T(8,128)(2,1)S(1)}, bf16[512,768]{1,0:T(8,128)(2,1)S(1...) custom-call(bf16[1024,768]{1,0:T(8,128)(2,1)S(1)} %get-tuple-element.199.spliced, ...), custom_call_target="tpu_custom_call" | custom-call | flops 1000 | tf_op jit(solution)/shard_map/pallas_call | solution.py:142
  106.4 1.0 collective-permute-done.27.b
  107.5 2.1 %shard_map.309 = (f32[4,96,768]{2,1,0:T(8,128)S(1)}, bf16[4,96,768]{2,1,0:T(8,128)(2,1)S(1)}) custom-call(s32[8]{0:T(128)S(1)} %dynamic-slice_bitcast_fusion.place, bf16[512,768]{1,0:T(8,128)(2,1)S(1)} %get-tuple-element.204.refs_0_, bf16[512,768]{1,0:T(8,128)(2,1)S(1)} %get-tuple-element.205.refs_1_, bf16[512,768]{1,0:T(8,128)(2,1)S(1)} %get-tuple-element.206.refs_2_, ...), custom_call_target="tpu_custom_call" | custom-call | flops 1000 | tf_op jit(solution)/shard_map/pallas_call | solution.py:142
  109.6 2.1 %shard_map.310 = (f32[4,96,768]{2,1,0:T(8,128)S(1)}, bf16[4,96,768]{2,1,0:T(8,128)(2,1)S(1)}) custom-call(s32[8]{0:T(128)S(1)} %dynamic-slice_bitcast_fusion.place, bf16[2,256,768]{2,1,0:T(8,128)(2,1)S(1)} %shard_map.292.cot_zero, bf16[2,256,768]{2,1,0:T(8,128)(2,1)S(1)} %collective-permute-done.11.cot_one, ...), custom_call_target="tpu_custom_call" | custom-call | flops 1000 | tf_op jit(solution)/shard_map/pallas_call | solution.py:142
  111.8 5.5 %collective-permute-done.24.b = bf16[256,768]{1,0:T(8,128)(2,1)S(1)} collective-permute-done((bf16[256,768]{1,0:T(8,128)(2,1)S(1)}, bf16[256,768]{1,0:T(8,128)(2,1)S(1)}, u32[]{:S(2)}, u32[]{:S(2)}) %collective-permute-start.24) | collective-permute-done | bytes 393248 | tf_op jit(solution)/shard_map/ppermute | solution.py:19
  117.4 1.4 shard_map.312
  118.9 1.3 collective-permute-start.29
  120.9 1.0 collective-permute-done.31.other
  121.9 5.9 %shard_map.314 = (f32[512,768]{1,0:T(8,128)S(1)}, bf16[512,768]{1,0:T(8,128)(2,1)S(1)}, bf16[512,192]{1,0:T(8,128)(2,1)S(1)}, f32[512,192]{1,0:T(8,128)S(1)}, f3...) custom-call(s32[8]{0:T(128)S(1)} %dynamic-slice_bitcast_fusion.place, s32[2]{0:T(128)S(1)} %bitcast.71, ...), custom_call_target="tpu_custom_call" | custom-call | flops 1000 | tf_op jit(solution)/shard_map/pallas_call | solution.py:142
  127.8 3.9 %collective-permute-done.30.b = bf16[256,768]{1,0:T(8,128)(2,1)S(1)} collective-permute-done((bf16[256,768]{1,0:T(8,128)(2,1)S(1)}, bf16[256,768]{1,0:T(8,128)(2,1)S(1)}, u32[]{:S(2)}, u32[]{:S(2)}) %collective-permute-start.30) | collective-permute-done | bytes 393248 | tf_op jit(solution)/shard_map/ppermute | solution.py:19
  131.7 2.9 %collective-permute-done.29.got = bf16[4,96,768]{2,1,0:T(8,128)(2,1)S(1)} collective-permute-done((bf16[4,96,768]{2,1,0:T(8,128)(2,1)S(1)}, bf16[4,96,768]{2,1,0:T(8,128)(2,1)S(1)}, u32[]{:S(2)}, u32[]{:S(2)}) %collective-permute-start.29) | collective-permute-done | bytes 589856 | tf_op jit(solution)/shard_map/ppermute | solution.py:19
  136.8 1.3 collective-permute-start.34
  138.1 8.9 %shard_map.316 = (f32[512,768]{1,0:T(8,128)S(1)}, bf16[512,768]{1,0:T(8,128)(2,1)S(1)}, bf16[512,192]{1,0:T(8,128)(2,1)S(1)}, bf16[1024,192]{1,0:T(8,128)(2,1)S(...) custom-call(s32[8]{0:T(128)S(1)} %dynamic-slice_bitcast_fusion.place, s32[2]{0:T(128)S(1)} %bitcast.72, ...), custom_call_target="tpu_custom_call" | custom-call | flops 1000 | tf_op jit(solution)/shard_map/pallas_call | solution.py:142
  147.1 2.2 %shard_map.319 = (f32[2,256,768]{2,1,0:T(8,128)S(1)}, bf16[2,256,768]{2,1,0:T(8,128)(2,1)S(1)}, bf16[1024,576]{1,0:T(8,128)(2,1)S(1)}, f32[8,768]{1,0:T(8,128)S(...) custom-call(s32[8]{0:T(128)S(1)} %dynamic-slice_bitcast_fusion.place, s32[6]{0:T(128)S(1)} %bitcast.74, ...), custom_call_target="tpu_custom_call" | custom-call | flops 1000 | tf_op jit(solution)/shard_map/pallas_call | solution.py:142
  149.9 1.8 collective-permute-done.36.b
  151.7 1.0 collective-permute-start.38
  153.4 1.9 shard_map.322.sums
  156.4 1.3 collective-permute-start.39
  159.1 2.5 %collective-permute-start.40 = (bf16[1,96,768]{2,1,0:T(8,128)(2,1)S(1)}, bf16[1,96,768]{2,1,0:T(8,128)(2,1)S(1)}, u32[]{:S(2)}, u32[]{:S(2)}) collective-permute-start(bf16[1,96,768]{2,1,0:T(8,128)(2,1)S(1)} %get-tuple-element.270), channel_id=1, source_target_pairs={{0,24},{4,28},{8,16},{12,20},{16,8},{20,12},{24,0},{28,4},{1,25},{... | collective-permute-start | bytes 442376 | tf_op jit(solution)/shard_map/ppermute | solution.py:19
  161.6 4.6 %collective-permute-done.40.up_got = bf16[1,96,768]{2,1,0:T(8,128)(2,1)S(1)} collective-permute-done((bf16[1,96,768]{2,1,0:T(8,128)(2,1)S(1)}, bf16[1,96,768]{2,1,0:T(8,128)(2,1)S(1)}, u32[]{:S(2)}, u32[]{:S(2)}) %collective-permute-start.40) | collective-permute-done | bytes 147488 | tf_op jit(solution)/shard_map/ppermute | solution.py:19
  166.2 7.6 %collective-permute-done.39.got = bf16[4,104,768]{2,1,0:T(8,128)(2,1)S(1)} collective-permute-done((bf16[4,104,768]{2,1,0:T(8,128)(2,1)S(1)}, bf16[4,104,768]{2,1,0:T(8,128)(2,1)S(1)}, u32[]{:S(2)}, u32[]{:S(2)}) %collective-permute-start.39) | collective-permute-done | bytes 639008 | tf_op jit(solution)/shard_map/ppermute | solution.py:19
  174.5 1.0 collective-permute-start.41
  175.5 9.5 %collective-permute-done.43.got = bf16[4,96,768]{2,1,0:T(8,128)(2,1)S(1)} collective-permute-done((bf16[4,96,768]{2,1,0:T(8,128)(2,1)S(1)}, bf16[4,96,768]{2,1,0:T(8,128)(2,1)S(1)}, u32[]{:S(2)}, u32[]{:S(2)}) %collective-permute-start.43) | collective-permute-done | bytes 589856 | tf_op jit(solution)/shard_map/ppermute | solution.py:19
  185.7 1.3 collective-permute-start.44
  188.2 2.1 %collective-permute-start.42 = (bf16[1,104,768]{2,1,0:T(8,128)(2,1)S(1)}, bf16[1,104,768]{2,1,0:T(8,128)(2,1)S(1)}, u32[]{:S(2)}, u32[]{:S(2)}) collective-permute-start(bf16[1,104,768]{2,1,0:T(8,128)(2,1)S(1)} %get-tuple-element.275), channel_id=1, source_target_pairs={{0,24},{4,28},{8,16},{12,20},{16,8},{20,12},{24,0},{28,4},{1,25},{... | collective-permute-start | bytes 479240 | tf_op jit(solution)/shard_map/ppermute | solution.py:19
  190.3 4.1 %collective-permute-done.44.got = bf16[2,96,768]{2,1,0:T(8,128)(2,1)S(1)} collective-permute-done((bf16[2,96,768]{2,1,0:T(8,128)(2,1)S(1)}, bf16[2,96,768]{2,1,0:T(8,128)(2,1)S(1)}, u32[]{:S(2)}, u32[]{:S(2)}) %collective-permute-start.44) | collective-permute-done | bytes 294944 | tf_op jit(solution)/shard_map/ppermute | solution.py:19
  195.1 2.2 %collective-permute-start.45 = (bf16[1,96,768]{2,1,0:T(8,128)(2,1)S(1)}, bf16[1,96,768]{2,1,0:T(8,128)(2,1)S(1)}, u32[]{:S(2)}, u32[]{:S(2)}) collective-permute-start(bf16[1,96,768]{2,1,0:T(8,128)(2,1)S(1)} %get-tuple-element.288), channel_id=1, source_target_pairs={{0,24},{4,28},{8,16},{12,20},{16,8},{20,12},{24,0},{28,4},{1,25},{... | collective-permute-start | bytes 442376 | tf_op jit(solution)/shard_map/ppermute | solution.py:19
  197.3 1.4 shard_map.318
  198.7 2.1 shard_map.324
  201.4 0.8 collective-permute-done.45.down_got
  202.2 0.9 shard_map.332
  203.0 0.9 copy.35
  203.9 0.9 shard_map.329
  (111 shorter events, 28.1 us)
Async XLA Ops:
  0.6 23.5 %copy-start.2 = (bf16[1,256,768]{2,1,0:T(8,128)(2,1)S(1)}, bf16[1,256,768]{2,1,0:T(8,128)(2,1)}, u32[]{:S(2)}) copy-start(bf16[1,256,768]{2,1,0:T(8,128)(2,1)} %param.34) | copy-start | bytes 1179652
  0.7 21.8 %collective-permute-start = (bf16[256,768]{1,0:T(8,128)(2,1)}, bf16[256,768]{1,0:T(8,128)(2,1)S(1)}, u32[]{:S(2)}, u32[]{:S(2)}) collective-permute-start(bf16[256,768]{1,0:T(8,128)(2,1)} %bitcast.57), channel_id=1, source_target_pairs={{0,2},{1,3},{2,0},{3,1},{4,6},{5,7},{6,4},{7,5},{8,10},{9,11},{10,... | collective-permute-start | bytes 1179656 | tf_op jit(solution)/shard_map/ppermute | solution.py:19
  4.7 0.9 copy-start.3
  5.7 0.8 copy-start.4
  6.4 0.7 copy-start.8
  7.1 0.7 copy-start.9
  7.8 0.7 copy-start.10
  8.4 0.7 copy-start.11
  9.1 0.7 copy-start.12
  9.7 0.7 copy-start.13
  10.4 0.7 copy-start.14
  11.0 0.7 copy-start.15
  11.9 10.5 %collective-permute-start.2 = (bf16[104,768]{1,0:T(8,128)(2,1)S(1)}, bf16[104,768]{1,0:T(8,128)(2,1)S(1)}, u32[]{:S(2)}, u32[]{:S(2)}) collective-permute-start(bf16[104,768]{1,0:T(8,128)(2,1)S(1)} %get-tuple-element.153.a), channel_id=1, source_target_pairs={{0,4},{4,0},{8,12},{12,8},{16,20},{20,16},{24,28},{28,24},{1,5},{5... | collective-permute-start | bytes 479240 | tf_op jit(solution)/shard_map/ppermute | solution.py:19
  13.5 9.0 %collective-permute-start.1 = (bf16[104,768]{1,0:T(8,128)(2,1)S(1)}, bf16[104,768]{1,0:T(8,128)(2,1)S(1)}, u32[]{:S(2)}, u32[]{:S(2)}) collective-permute-start(bf16[104,768]{1,0:T(8,128)(2,1)S(1)} %get-tuple-element.153.a), channel_id=1, source_target_pairs={{0,24},{4,28},{8,16},{12,20},{16,8},{20,12},{24,0},{28,4},{1,25},{... | collective-permute-start | bytes 479240 | tf_op jit(solution)/shard_map/ppermute | solution.py:19
  17.1 5.4 %collective-permute-start.3 = (bf16[96,768]{1,0:T(8,128)(2,1)}, bf16[96,768]{1,0:T(8,128)(2,1)S(1)}, u32[]{:S(2)}, u32[]{:S(2)}) collective-permute-start(bf16[96,768]{1,0:T(8,128)(2,1)} %a.1), channel_id=1, source_target_pairs={{0,4},{4,0},{8,12},{12,8},{16,20},{20,16},{24,28},{28,24},{1,5},{5... | collective-permute-start | bytes 442376 | tf_op jit(solution)/shard_map/ppermute | solution.py:19
  18.3 18.6 %copy-start = (bf16[96,768]{1,0:T(8,128)(2,1)S(1)}, bf16[96,768]{1,0:T(8,128)(2,1)}, u32[]{:S(2)}) copy-start(bf16[96,768]{1,0:T(8,128)(2,1)} %a.1) | copy-start | bytes 442372
  22.4 1.0 copy-start.1
  24.0 11.6 %collective-permute-start.7 = (bf16[2,256,768]{2,1,0:T(8,128)(2,1)S(1)}, bf16[2,256,768]{2,1,0:T(8,128)(2,1)S(1)}, u32[]{:S(2)}, u32[]{:S(2)}) collective-permute-start(bf16[2,256,768]{2,1,0:T(8,128)(2,1)S(1)} %shard_map.290.x_zero), channel_id=1, source_target_pairs={{0,1},{1,0},{2,3},{3,2},{4,5},{5,4},{6,7},{7,6},{8,9},{9,8},{10,11... | collective-permute-start | bytes 2359304 | tf_op jit(solution)/shard_map/ppermute | solution.py:19
  24.1 11.5 %collective-permute-start.8 = (bf16[256,768]{1,0:T(8,128)(2,1)S(1)}, bf16[256,768]{1,0:T(8,128)(2,1)S(1)}, u32[]{:S(2)}, u32[]{:S(2)}) collective-permute-start(bf16[256,768]{1,0:T(8,128)(2,1)S(1)} %bitcast.59), channel_id=1, source_target_pairs={{0,2},{1,3},{2,0},{3,1},{4,6},{5,7},{6,4},{7,5},{8,10},{9,11},{10,... | collective-permute-start | bytes 1179656 | tf_op jit(solution)/shard_map/ppermute | solution.py:19
  24.7 10.5 %collective-permute-start.4 = (bf16[2,104,768]{2,1,0:T(8,128)(2,1)S(1)}, bf16[2,104,768]{2,1,0:T(8,128)(2,1)S(1)}, u32[]{:S(2)}, u32[]{:S(2)}) collective-permute-start(bf16[2,104,768]{2,1,0:T(8,128)(2,1)S(1)} %shard_map.291), channel_id=1, source_target_pairs={{0,8},{4,12},{8,0},{12,4},{16,24},{20,28},{24,16},{28,20},{1,9},{5... | collective-permute-start | bytes 958472 | tf_op jit(solution)/shard_map/ppermute | solution.py:19
  26.1 9.1 %collective-permute-start.5 = (bf16[104,768]{1,0:T(8,128)(2,1)S(1)}, bf16[104,768]{1,0:T(8,128)(2,1)S(1)}, u32[]{:S(2)}, u32[]{:S(2)}) collective-permute-start(bf16[104,768]{1,0:T(8,128)(2,1)S(1)} %collective-permute-done.1.b), channel_id=1, source_target_pairs={{0,4},{4,0},{8,12},{12,8},{16,20},{20,16},{24,28},{28,24},{1,5},{5... | collective-permute-start | bytes 479240 | tf_op jit(solution)/shard_map/ppermute | solution.py:19
  26.6 23.1 %copy-start.5 = (bf16[1,6,768]{2,1,0:T(8,128)(2,1)S(1)}, bf16[1,6,768]{2,1,0:T(8,128)(2,1)}, u32[]{:S(2)}) copy-start(bf16[1,6,768]{2,1,0:T(8,128)(2,1)} %param.19) | copy-start | bytes 27652
  26.6 23.1 %copy-start.7 = (s32[1,6]{1,0:T(1,128)S(1)}, s32[1,6]{1,0:T(1,128)}, u32[]{:S(2)}) copy-start(s32[1,6]{1,0:T(1,128)} %thought_pos.3) | copy-start | bytes 76
  26.7 8.5 %collective-permute-start.6 = (bf16[96,768]{1,0:T(8,128)(2,1)S(1)}, bf16[96,768]{1,0:T(8,128)(2,1)S(1)}, u32[]{:S(2)}, u32[]{:S(2)}) collective-permute-start(bf16[96,768]{1,0:T(8,128)(2,1)S(1)} %get-tuple-element.182.a), channel_id=1, source_target_pairs={{0,4},{4,0},{8,12},{12,8},{16,20},{20,16},{24,28},{28,24},{1,5},{5... | collective-permute-start | bytes 442376 | tf_op jit(solution)/shard_map/ppermute | solution.py:19
  36.3 10.0 %collective-permute-start.11 = (bf16[2,256,768]{2,1,0:T(8,128)(2,1)S(1)}, bf16[2,256,768]{2,1,0:T(8,128)(2,1)S(1)}, u32[]{:S(2)}, u32[]{:S(2)}) collective-permute-start(bf16[2,256,768]{2,1,0:T(8,128)(2,1)S(1)} %shard_map.292.cot_zero), channel_id=1, source_target_pairs={{0,1},{1,0},{2,3},{3,2},{4,5},{5,4},{6,7},{7,6},{8,9},{9,8},{10,11... | collective-permute-start | bytes 2359304 | tf_op jit(solution)/shard_map/ppermute | solution.py:19
  36.3 10.0 %collective-permute-start.9 = (bf16[2,104,768]{2,1,0:T(8,128)(2,1)S(1)}, bf16[2,104,768]{2,1,0:T(8,128)(2,1)S(1)}, u32[]{:S(2)}, u32[]{:S(2)}) collective-permute-start(bf16[2,104,768]{2,1,0:T(8,128)(2,1)S(1)} %collective-permute-done.4.refs_3_), channel_id=1, source_target_pairs={{0,4},{4,0},{8,12},{12,8},{16,20},{20,16},{24,28},{28,24},{1,5},{5... | collective-permute-start | bytes 958472 | tf_op jit(solution)/shard_map/ppermute | solution.py:19
  36.9 7.8 %collective-permute-start.10 = (bf16[96,768]{1,0:T(8,128)(2,1)S(1)}, bf16[96,768]{1,0:T(8,128)(2,1)S(1)}, u32[]{:S(2)}, u32[]{:S(2)}) collective-permute-start(bf16[96,768]{1,0:T(8,128)(2,1)S(1)} %copy-done), channel_id=1, source_target_pairs={{0,24},{4,28},{8,16},{12,20},{16,8},{20,12},{24,0},{28,4},{1,25},{... | collective-permute-start | bytes 442376 | tf_op jit(solution)/shard_map/ppermute | solution.py:19
  46.3 10.9 %collective-permute-start.12 = (bf16[2,96,768]{2,1,0:T(8,128)(2,1)S(1)}, bf16[2,96,768]{2,1,0:T(8,128)(2,1)S(1)}, u32[]{:S(2)}, u32[]{:S(2)}) collective-permute-start(bf16[2,96,768]{2,1,0:T(8,128)(2,1)S(1)} %shard_map.296), channel_id=1, source_target_pairs={{0,8},{4,12},{8,0},{12,4},{16,24},{20,28},{24,16},{28,20},{1,9},{5... | collective-permute-start | bytes 884744 | tf_op jit(solution)/shard_map/ppermute | solution.py:19
  47.7 9.5 %collective-permute-start.13 = (bf16[96,768]{1,0:T(8,128)(2,1)S(1)}, bf16[96,768]{1,0:T(8,128)(2,1)S(1)}, u32[]{:S(2)}, u32[]{:S(2)}) collective-permute-start(bf16[96,768]{1,0:T(8,128)(2,1)S(1)} %collective-permute-done.10.b), channel_id=1, source_target_pairs={{0,4},{4,0},{8,12},{12,8},{16,20},{20,16},{24,28},{28,24},{1,5},{5... | collective-permute-start | bytes 442376 | tf_op jit(solution)/shard_map/ppermute | solution.py:19
  49.8 3.8 %copy-start.6 = (s32[1,2]{1,0:T(1,128)S(1)}, s32[1,2]{1,0:T(1,128)}, u32[]{:S(2)}) copy-start(s32[1,2]{1,0:T(1,128)} %param.21) | copy-start | bytes 28
  57.2 3.4 %collective-permute-start.14 = (bf16[256,768]{1,0:T(8,128)(2,1)S(1)}, bf16[256,768]{1,0:T(8,128)(2,1)S(1)}, u32[]{:S(2)}, u32[]{:S(2)}) collective-permute-start(bf16[256,768]{1,0:T(8,128)(2,1)S(1)} %get-tuple-element.178), channel_id=1, source_target_pairs={{0,1},{1,0},{2,3},{3,2},{4,5},{5,4},{6,7},{7,6},{8,9},{9,8},{10,11... | collective-permute-start | bytes 1179656 | tf_op jit(solution)/shard_map/ppermute | solution.py:19
  57.3 9.8 %collective-permute-start.16 = (bf16[2,96,768]{2,1,0:T(8,128)(2,1)S(1)}, bf16[2,96,768]{2,1,0:T(8,128)(2,1)S(1)}, u32[]{:S(2)}, u32[]{:S(2)}) collective-permute-start(bf16[2,96,768]{2,1,0:T(8,128)(2,1)S(1)} %collective-permute-done.12.refs_3_), channel_id=1, source_target_pairs={{0,4},{4,0},{8,12},{12,8},{16,20},{20,16},{24,28},{28,24},{1,5},{5... | collective-permute-start | bytes 884744 | tf_op jit(solution)/shard_map/ppermute | solution.py:19
  58.1 8.9 %collective-permute-start.17 = (bf16[96,768]{1,0:T(8,128)(2,1)S(1)}, bf16[96,768]{1,0:T(8,128)(2,1)S(1)}, u32[]{:S(2)}, u32[]{:S(2)}) collective-permute-start(bf16[96,768]{1,0:T(8,128)(2,1)S(1)} %get-tuple-element.182.a), channel_id=1, source_target_pairs={{0,24},{4,28},{8,16},{12,20},{16,8},{20,12},{24,0},{28,4},{1,25},{... | collective-permute-start | bytes 442376 | tf_op jit(solution)/shard_map/ppermute | solution.py:19
  67.1 1.8 collective-permute-start.18
  67.2 11.5 %collective-permute-start.15 = (bf16[256,768]{1,0:T(8,128)(2,1)S(1)}, bf16[256,768]{1,0:T(8,128)(2,1)S(1)}, u32[]{:S(2)}, u32[]{:S(2)}) collective-permute-start(bf16[256,768]{1,0:T(8,128)(2,1)S(1)} %shard_map.297.a), channel_id=1, source_target_pairs={{0,2},{1,3},{2,0},{3,1},{4,6},{5,7},{6,4},{7,5},{8,10},{9,11},{10,... | collective-permute-start | bytes 1179656 | tf_op jit(solution)/shard_map/ppermute | solution.py:19
  78.8 2.5 %collective-permute-start.19 = (bf16[256,768]{1,0:T(8,128)(2,1)S(1)}, bf16[256,768]{1,0:T(8,128)(2,1)S(1)}, u32[]{:S(2)}, u32[]{:S(2)}) collective-permute-start(bf16[256,768]{1,0:T(8,128)(2,1)S(1)} %shard_map.300.total), channel_id=1, source_target_pairs={{0,1},{1,0},{2,3},{3,2},{4,5},{5,4},{6,7},{7,6},{8,9},{9,8},{10,11... | collective-permute-start | bytes 1179656 | tf_op jit(solution)/shard_map/ppermute | solution.py:19
  78.9 9.5 %collective-permute-start.20 = (bf16[2,96,768]{2,1,0:T(8,128)(2,1)S(1)}, bf16[2,96,768]{2,1,0:T(8,128)(2,1)S(1)}, u32[]{:S(2)}, u32[]{:S(2)}) collective-permute-start(bf16[2,96,768]{2,1,0:T(8,128)(2,1)S(1)} %shard_map.301), channel_id=1, source_target_pairs={{0,8},{4,12},{8,0},{12,4},{16,24},{20,28},{24,16},{28,20},{1,9},{5... | collective-permute-start | bytes 884744 | tf_op jit(solution)/shard_map/ppermute | solution.py:19
  79.7 6.0 %collective-permute-start.21 = (bf16[96,768]{1,0:T(8,128)(2,1)S(1)}, bf16[96,768]{1,0:T(8,128)(2,1)S(1)}, u32[]{:S(2)}, u32[]{:S(2)}) collective-permute-start(bf16[96,768]{1,0:T(8,128)(2,1)S(1)} %collective-permute-done.17.b), channel_id=1, source_target_pairs={{0,4},{4,0},{8,12},{12,8},{16,20},{20,16},{24,28},{28,24},{1,5},{5... | collective-permute-start | bytes 442376 | tf_op jit(solution)/shard_map/ppermute | solution.py:19
  80.5 20.1 %collective-permute-start.25 = (bf16[256,768]{1,0:T(8,128)(2,1)S(1)}, bf16[256,768]{1,0:T(8,128)(2,1)S(1)}, u32[]{:S(2)}, u32[]{:S(2)}) collective-permute-start(bf16[256,768]{1,0:T(8,128)(2,1)S(1)} %shard_map.299.a), channel_id=1, source_target_pairs={{0,2},{1,3},{2,0},{3,1},{4,6},{5,7},{6,4},{7,5},{8,10},{9,11},{10,... | collective-permute-start | bytes 1179656 | tf_op jit(solution)/shard_map/ppermute | solution.py:19
  88.4 8.6 %collective-permute-start.22 = (bf16[2,96,768]{2,1,0:T(8,128)(2,1)S(1)}, bf16[2,96,768]{2,1,0:T(8,128)(2,1)S(1)}, u32[]{:S(2)}, u32[]{:S(2)}) collective-permute-start(bf16[2,96,768]{2,1,0:T(8,128)(2,1)S(1)} %collective-permute-done.20.refs_3_), channel_id=1, source_target_pairs={{0,4},{4,0},{8,12},{12,8},{16,20},{20,16},{24,28},{28,24},{1,5},{5... | collective-permute-start | bytes 884744 | tf_op jit(solution)/shard_map/ppermute | solution.py:19
  100.5 1.8 collective-permute-start.23
  100.7 2.2 %collective-permute-start.26 = (bf16[256,768]{1,0:T(8,128)(2,1)S(1)}, bf16[256,768]{1,0:T(8,128)(2,1)S(1)}, u32[]{:S(2)}, u32[]{:S(2)}) collective-permute-start(bf16[256,768]{1,0:T(8,128)(2,1)S(1)} %shard_map.306.total), channel_id=1, source_target_pairs={{0,1},{1,0},{2,3},{3,2},{4,5},{5,4},{6,7},{7,6},{8,9},{9,8},{10,11... | collective-permute-start | bytes 1179656 | tf_op jit(solution)/shard_map/ppermute | solution.py:19
  105.7 1.8 collective-permute-start.27
  105.9 11.4 %collective-permute-start.24 = (bf16[256,768]{1,0:T(8,128)(2,1)S(1)}, bf16[256,768]{1,0:T(8,128)(2,1)S(1)}, u32[]{:S(2)}, u32[]{:S(2)}) collective-permute-start(bf16[256,768]{1,0:T(8,128)(2,1)S(1)} %shard_map.305.a), channel_id=1, source_target_pairs={{0,2},{1,3},{2,0},{3,1},{4,6},{5,7},{6,4},{7,5},{8,10},{9,11},{10,... | collective-permute-start | bytes 1179656 | tf_op jit(solution)/shard_map/ppermute | solution.py:19
  118.8 16.0 %collective-permute-start.28 = (bf16[2,256,768]{2,1,0:T(8,128)(2,1)S(1)}, bf16[2,256,768]{2,1,0:T(8,128)(2,1)S(1)}, u32[]{:S(2)}, u32[]{:S(2)}) collective-permute-start(bf16[2,256,768]{2,1,0:T(8,128)(2,1)S(1)} %get-tuple-element.215), channel_id=1, source_target_pairs={{0,1},{1,0},{2,3},{3,2},{4,5},{5,4},{6,7},{7,6},{8,9},{9,8},{10,11... | collective-permute-start | bytes 2359304 | tf_op jit(solution)/shard_map/ppermute | solution.py:19
  118.9 15.7 %collective-permute-start.29 = (bf16[4,96,768]{2,1,0:T(8,128)(2,1)S(1)}, bf16[4,96,768]{2,1,0:T(8,128)(2,1)S(1)}, u32[]{:S(2)}, u32[]{:S(2)}) collective-permute-start(bf16[4,96,768]{2,1,0:T(8,128)(2,1)S(1)} %get-tuple-element.218), channel_id=1, source_target_pairs={{0,4},{4,0},{8,12},{12,8},{16,20},{20,16},{24,28},{28,24},{1,5},{5... | collective-permute-start | bytes 1769480 | tf_op jit(solution)/shard_map/ppermute | solution.py:19
  120.2 1.7 collective-permute-start.31
  120.3 11.4 %collective-permute-start.30 = (bf16[256,768]{1,0:T(8,128)(2,1)S(1)}, bf16[256,768]{1,0:T(8,128)(2,1)S(1)}, u32[]{:S(2)}, u32[]{:S(2)}) collective-permute-start(bf16[256,768]{1,0:T(8,128)(2,1)S(1)} %shard_map.308.a), channel_id=1, source_target_pairs={{0,2},{1,3},{2,0},{3,1},{4,6},{5,7},{6,4},{7,5},{8,10},{9,11},{10,... | collective-permute-start | bytes 1179656 | tf_op jit(solution)/shard_map/ppermute | solution.py:19
  134.7 3.4 %collective-permute-start.32 = (bf16[256,768]{1,0:T(8,128)(2,1)S(1)}, bf16[256,768]{1,0:T(8,128)(2,1)S(1)}, u32[]{:S(2)}, u32[]{:S(2)}) collective-permute-start(bf16[256,768]{1,0:T(8,128)(2,1)S(1)} %shard_map.315.total), channel_id=1, source_target_pairs={{0,1},{1,0},{2,3},{3,2},{4,5},{5,4},{6,7},{7,6},{8,9},{9,8},{10,11... | collective-permute-start | bytes 1179656 | tf_op jit(solution)/shard_map/ppermute | solution.py:19
  135.5 11.6 %collective-permute-start.33 = (bf16[1,256,768]{2,1,0:T(8,128)(2,1)S(1)}, bf16[1,256,768]{2,1,0:T(8,128)(2,1)S(1)}, u32[]{:S(2)}, u32[]{:S(2)}) collective-permute-start(bf16[1,256,768]{2,1,0:T(8,128)(2,1)S(1)} %get-tuple-element.233), channel_id=1, source_target_pairs={{0,2},{1,3},{2,0},{3,1},{4,6},{5,7},{6,4},{7,5},{8,10},{9,11},{10,... | collective-permute-start | bytes 1179656 | tf_op jit(solution)/shard_map/ppermute | solution.py:19
  136.8 10.2 %collective-permute-start.34 = (bf16[2,96,768]{2,1,0:T(8,128)(2,1)S(1)}, bf16[2,96,768]{2,1,0:T(8,128)(2,1)S(1)}, u32[]{:S(2)}, u32[]{:S(2)}) collective-permute-start(bf16[2,96,768]{2,1,0:T(8,128)(2,1)S(1)} %get-tuple-element.235), channel_id=1, source_target_pairs={{0,8},{4,12},{8,0},{12,4},{16,24},{20,28},{24,16},{28,20},{1,9},{5... | collective-permute-start | bytes 884744 | tf_op jit(solution)/shard_map/ppermute | solution.py:19
  149.3 2.4 %collective-permute-start.35 = (bf16[2,256,768]{2,1,0:T(8,128)(2,1)S(1)}, bf16[2,256,768]{2,1,0:T(8,128)(2,1)S(1)}, u32[]{:S(2)}, u32[]{:S(2)}) collective-permute-start(bf16[2,256,768]{2,1,0:T(8,128)(2,1)S(1)} %get-tuple-element.245), channel_id=1, source_target_pairs={{0,1},{1,0},{2,3},{3,2},{4,5},{5,4},{6,7},{7,6},{8,9},{9,8},{10,11... | collective-permute-start | bytes 2359304 | tf_op jit(solution)/shard_map/ppermute | solution.py:19
  149.4 2.3 %collective-permute-start.36 = (f32[8,768]{1,0:T(8,128)S(1)}, f32[8,768]{1,0:T(8,128)S(1)}, u32[]{:S(2)}, u32[]{:S(2)}) collective-permute-start(f32[8,768]{1,0:T(8,128)S(1)} %get-tuple-element.246.a), channel_id=1, source_target_pairs={{0,1},{1,0},{2,3},{3,2},{4,5},{5,4},{6,7},{7,6},{8,9},{9,8},{10,11... | collective-permute-start | bytes 73736 | tf_op jit(solution)/shard_map/ppermute | solution.py:19
  151.7 3.9 %collective-permute-start.38 = (f32[8,768]{1,0:T(8,128)S(1)}, f32[8,768]{1,0:T(8,128)S(1)}, u32[]{:S(2)}, u32[]{:S(2)}) collective-permute-start(f32[8,768]{1,0:T(8,128)S(1)} %shard_map.321.a), channel_id=1, source_target_pairs={{0,2},{1,3},{2,0},{3,1},{4,6},{5,7},{6,4},{7,5},{8,10},{9,11},{10,... | collective-permute-start | bytes 73736 | tf_op jit(solution)/shard_map/ppermute | solution.py:19
  156.4 17.4 %collective-permute-start.39 = (bf16[4,104,768]{2,1,0:T(8,128)(2,1)S(1)}, bf16[4,104,768]{2,1,0:T(8,128)(2,1)S(1)}, u32[]{:S(2)}, u32[]{:S(2)}) collective-permute-start(bf16[4,104,768]{2,1,0:T(8,128)(2,1)S(1)} %get-tuple-element.267), channel_id=1, source_target_pairs={{0,4},{4,0},{8,12},{12,8},{16,20},{20,16},{24,28},{28,24},{1,5},{5... | collective-permute-start | bytes 1916936 | tf_op jit(solution)/shard_map/ppermute | solution.py:19
  157.7 27.3 %collective-permute-start.43 = (bf16[4,96,768]{2,1,0:T(8,128)(2,1)S(1)}, bf16[4,96,768]{2,1,0:T(8,128)(2,1)S(1)}, u32[]{:S(2)}, u32[]{:S(2)}) collective-permute-start(bf16[4,96,768]{2,1,0:T(8,128)(2,1)S(1)} %get-tuple-element.283), channel_id=1, source_target_pairs={{0,4},{4,0},{8,12},{12,8},{16,20},{20,16},{24,28},{28,24},{1,5},{5... | collective-permute-start | bytes 1769480 | tf_op jit(solution)/shard_map/ppermute | solution.py:19
  159.1 7.1 %collective-permute-start.40 = (bf16[1,96,768]{2,1,0:T(8,128)(2,1)S(1)}, bf16[1,96,768]{2,1,0:T(8,128)(2,1)S(1)}, u32[]{:S(2)}, u32[]{:S(2)}) collective-permute-start(bf16[1,96,768]{2,1,0:T(8,128)(2,1)S(1)} %get-tuple-element.270), channel_id=1, source_target_pairs={{0,24},{4,28},{8,16},{12,20},{16,8},{20,12},{24,0},{28,4},{1,25},{... | collective-permute-start | bytes 442376 | tf_op jit(solution)/shard_map/ppermute | solution.py:19
  174.5 13.1 %collective-permute-start.41 = (bf16[2,104,768]{2,1,0:T(8,128)(2,1)S(1)}, bf16[2,104,768]{2,1,0:T(8,128)(2,1)S(1)}, u32[]{:S(2)}, u32[]{:S(2)}) collective-permute-start(bf16[2,104,768]{2,1,0:T(8,128)(2,1)S(1)} %get-tuple-element.273), channel_id=1, source_target_pairs={{0,8},{4,12},{8,0},{12,4},{16,24},{20,28},{24,16},{28,20},{1,9},{5... | collective-permute-start | bytes 958472 | tf_op jit(solution)/shard_map/ppermute | solution.py:19
  185.7 8.8 %collective-permute-start.44 = (bf16[2,96,768]{2,1,0:T(8,128)(2,1)S(1)}, bf16[2,96,768]{2,1,0:T(8,128)(2,1)S(1)}, u32[]{:S(2)}, u32[]{:S(2)}) collective-permute-start(bf16[2,96,768]{2,1,0:T(8,128)(2,1)S(1)} %get-tuple-element.286), channel_id=1, source_target_pairs={{0,8},{4,12},{8,0},{12,4},{16,24},{20,28},{24,16},{28,20},{1,9},{5... | collective-permute-start | bytes 884744 | tf_op jit(solution)/shard_map/ppermute | solution.py:19
  187.0 11.7 %collective-permute-start.37 = (bf16[1,256,768]{2,1,0:T(8,128)(2,1)S(1)}, bf16[1,256,768]{2,1,0:T(8,128)(2,1)S(1)}, u32[]{:S(2)}, u32[]{:S(2)}) collective-permute-start(bf16[1,256,768]{2,1,0:T(8,128)(2,1)S(1)} %get-tuple-element.249), channel_id=1, source_target_pairs={{0,2},{1,3},{2,0},{3,1},{4,6},{5,7},{6,4},{7,5},{8,10},{9,11},{10,... | collective-permute-start | bytes 1179656 | tf_op jit(solution)/shard_map/ppermute | solution.py:19
  188.2 15.7 %collective-permute-start.42 = (bf16[1,104,768]{2,1,0:T(8,128)(2,1)S(1)}, bf16[1,104,768]{2,1,0:T(8,128)(2,1)S(1)}, u32[]{:S(2)}, u32[]{:S(2)}) collective-permute-start(bf16[1,104,768]{2,1,0:T(8,128)(2,1)S(1)} %get-tuple-element.275), channel_id=1, source_target_pairs={{0,24},{4,28},{8,16},{12,20},{16,8},{20,12},{24,0},{28,4},{1,25},{... | collective-permute-start | bytes 479240 | tf_op jit(solution)/shard_map/ppermute | solution.py:19
  195.1 7.1 %collective-permute-start.45 = (bf16[1,96,768]{2,1,0:T(8,128)(2,1)S(1)}, bf16[1,96,768]{2,1,0:T(8,128)(2,1)S(1)}, u32[]{:S(2)}, u32[]{:S(2)}) collective-permute-start(bf16[1,96,768]{2,1,0:T(8,128)(2,1)S(1)} %get-tuple-element.288), channel_id=1, source_target_pairs={{0,24},{4,28},{8,16},{12,20},{16,8},{20,12},{24,0},{28,4},{1,25},{... | collective-permute-start | bytes 442376 | tf_op jit(solution)/shard_map/ppermute | solution.py:19
where the time goes:
time: 207 us; the launch traced here: 206 us
  waiting for transfers between devices  87.6 us (42%)
  Pallas kernels  59.4 us (29%)
  starting transfers between devices  45.5 us (22%)
  local copies, waits for them, and re-layouts  12.5 us (6%)
    ppermute x46, waiting for transfers between devices, swapped(): lax.ppermute(array, axis, [(i, i ^ mask) for i in range(lax.axis_size(axi...  87.6 us
    pallas_call x44, Pallas kernels, call(): pl.pallas_call(kernel, out_shape=tuple((jax.ShapeDtypeStruct(s, t) for s,...  59.4 us
    ppermute x46, starting transfers between devices, swapped(): lax.ppermute(array, axis, [(i, i ^ mask) for i in range(lax.axis_size(axi...  45.5 us
    unnamed x35, local copies, waits for them, and re-layouts  10.5 us
  transfers between devices with their start and end apart: 46, of which 25 were waited for; matrix products, arithmetic and copies ran while one was open for 2% of the time, Pallas kernels for 24%

commit v1 on v0

--- a/solution.py
+++ b/solution.py
@@ -62,7 +62,7 @@
     return jnp.stack([jnp.where(first, own, other), jnp.where(first, other, own)])
 
 
-def dp_scatter_sum(blocks, place):
+def dp_scatter_sum(blocks):
     steps, me = dp_steps(), lax.axis_index("dp")
     slots = jnp.stack([blocks[s] for s in slot_owners(steps)])
     for mask, kinds in reversed(steps):
@@ -124,18 +124,7 @@
     return lax.broadcasted_iota(jnp.int32, shape, dim)
 
 
-def call(kernel, outs, *args, scratch=(), mib=8, piped=False):
-    if piped:
-        whole = lambda shape: pl.BlockSpec(shape, lambda i: (0,) * len(shape))
-        return pl.pallas_call(
-            kernel,
-            out_shape=tuple(jax.ShapeDtypeStruct(s, t) for s, t in outs),
-            grid=(1,),
-            in_specs=[whole(a.shape) for a in args],
-            out_specs=tuple(pl.BlockSpec(memory_space=pltpu.VMEM) for _ in outs),
-            compiler_params=pltpu.CompilerParams(vmem_limit_bytes=mib << 20),
-            cost_estimate=pl.CostEstimate(flops=COST, bytes_accessed=0, transcendentals=0),
-        )(*args)
+def call(kernel, outs, *args, scratch=(), mib=8):
     spec = lambda a: pl.BlockSpec(
         memory_space=pltpu.SMEM if a.ndim == 1 and a.dtype == jnp.int32 else pltpu.VMEM
     )
@@ -318,15 +307,12 @@
     )
 
 
-def back_kernel(
-    chunk, place, starts, total, other, residual, cot_zero, cot_one, vecs, w_proj, q_ref, k_ref, v_ref, att, log, *rest,
+def norm_back_kernel(
+    chunk, total, other, residual, cot_zero, cot_one, vecs, w_proj, att,
+    grad_res_ref, branch_ref, gatt_ref, delta_ref, sums_ref,
 ):
-    keys_in, rest = (rest[:2], rest[2:]) if chunk else ((), rest)
-    grad_res_ref, branch_ref, dq_ref, dk_ref, dv_ref, sums_ref, dqt_ref, delta_ref, gatt_ref = rest
     half, width = residual.shape
     rows = half // 2
-    cols = q_ref.shape[1]
-    heads = cols // HD
     gain = vecs[3:4, :]
     sums = [0.0, 0.0, 0.0, 0.0]
     for rel, (ref, cot) in enumerate(((total, cot_zero), (other, cot_one))):
@@ -343,11 +329,36 @@
         sums_ref[k : k + 1, :] = sums[k]
     grad_att = dot(branch_ref[...], w_proj[...], 1, 0).astype(LOW)
     gatt_ref[...] = grad_att
-    head_of = iota((1, cols), 1) // HD
+    cols = att.shape[1]
     head_rows = (iota((8, cols), 0) == iota((8, cols), 1) // HD).astype(F32)
     delta_ref[...] = dot(
         head_rows, grad_att.astype(F32) * att[...].astype(F32), 1, 1, lax.Precision.HIGHEST
     )
+
+
+def branch_back(chunk, total, other, residual, cots, vecs, w_proj, att):
+    half, width = residual.shape
+    cols = att.shape[1]
+    return call(
+        functools.partial(norm_back_kernel, chunk),
+        (((half, width), F32), ((half, width), LOW), ((half, cols), LOW), ((8, half), F32), ((8, width), F32)),
+        total,
+        other,
+        residual,
+        *cots,
+        vecs,
+        w_proj,
+        att,
+    )
+
+
+def back_kernel(chunk, place, starts, q_ref, k_ref, v_ref, log, gatt_ref, delta_ref, *rest):
+    keys_in, rest = (rest[:2], rest[2:]) if chunk else ((), rest)
+    dq_ref, dk_ref, dv_ref, dqt_ref = rest
+    half, cols = gatt_ref.shape
+    rows = half // 2
+    heads = cols // HD
+    head_of = iota((1, cols), 1) // HD
     limits = query_limits(place, starts, chunk, rows)
     dqt_ref[...] = jnp.zeros_like(dqt_ref)
 
@@ -382,32 +393,22 @@
     dq_ref[...] = (dqt_ref[...] * 0.125).T.astype(LOW)
 
 
-def back(chunk, place, starts, total, other, residual, cots, vecs, w_proj, queries, keys, values, att, log, early):
-    length, cols = queries.shape
-    half, width = residual.shape
+def back(chunk, place, starts, queries, keys, values, log, grad_att, delta, early):
+    half, cols = grad_att.shape
     kind = (((half * (chunk + 1), cols), LOW if chunk else F32),) * 2
     return call(
         functools.partial(back_kernel, chunk),
-        (((half, width), F32), ((half, width), LOW), ((half, cols), LOW), *kind, ((8, width), F32)),
+        (((half, cols), LOW), *kind),
         place,
         starts,
-        total,
-        other,
-        residual,
-        *cots,
-        vecs,
-        w_proj,
         queries,
         keys,
         values,
-        att,
         log,
+        grad_att,
+        delta,
         *early,
-        scratch=(
-            pltpu.VMEM((cols, half), F32),
-            pltpu.VMEM((8, half), F32),
-            pltpu.VMEM((half, cols), LOW),
-        ),
+        scratch=(pltpu.VMEM((cols, half), F32),),
     )
 
 
@@ -498,43 +499,54 @@
     return call(add_kernel, ((a.shape, LOW),), a, b)[0]
 
 
-def to_slots(place, sum_ref, keep_ref, send_ref, rows):
+def to_slots(place, sum_ref, first, keep_ref, send_ref):
+    rows, cols = sum_ref.shape[0] // 8, keep_ref.shape[2]
     for slot, owner in enumerate((0, 6, 2, 4)):
-        mine = pl.multiple_of((owner ^ place[7]) * rows, rows)
-        rest = pl.multiple_of((owner ^ 1 ^ place[7]) * rows, rows)
-        keep_ref[slot, :rows, :] = sum_ref[pl.ds(mine, rows), :]
-        send_ref[slot, :rows, :] = sum_ref[pl.ds(rest, rows), :].astype(LOW)
+        mine = pl.ds(pl.multiple_of((owner ^ place[7]) * rows, rows), rows)
+        rest = pl.ds(pl.multiple_of((owner ^ 1 ^ place[7]) * rows, rows), rows)
+        keep_ref[slot, :rows, :] = sum_ref[mine, first : first + cols]
+        send_ref[slot, :rows, :] = sum_ref[rest, first : first + cols].astype(LOW)
+
+
+def all_slots(place, sum_ref, blocks):
+    first = 0
+    for keep_ref, send_ref in zip(blocks[::2], blocks[1::2]):
+        to_slots(place, sum_ref, first, keep_ref, send_ref)
+        first += keep_ref.shape[2]
 
 
 def product(left, right):
     return sum(dot(a[...], b[...], 0, 0) for a, b in zip(left, right))
 
 
-def grad_kernel(place, *refs):
-    *sides, keep_ref, send_ref, sum_ref = refs
-    half = len(sides) // 2
+def grad_kernel(count, place, *refs):
+    sides, blocks, sum_ref = refs[:count], refs[count:-1], refs[-1]
+    half = count // 2
     sum_ref[...] = product(sides[:half], sides[half:])
-    to_slots(place, sum_ref, keep_ref, send_ref, keep_ref.shape[1])
-
-
-def cot_grad_kernel(place, cot_zero, cot_one, hidden_zero, hidden_one, keep_ref, send_ref, sum_ref):
+    all_slots(place, sum_ref, blocks)
+
+
+def cot_grad_kernel(count, place, cot_zero, cot_one, hidden_zero, hidden_one, *refs):
+    blocks, sum_ref = refs[:-1], refs[-1]
     rows = cot_zero.shape[1]
     left = [c[upper] for upper in range(2) for c in (cot_zero, cot_one)]
     right = [h[k * rows : (k + 1) * rows, :] for h in (hidden_zero, hidden_one) for k in range(2)]
     sum_ref[...] = sum(dot(a, b, 0, 0) for a, b in zip(left, right))
-    to_slots(place, sum_ref, keep_ref, send_ref, keep_ref.shape[1])
-
-
-def last_kernel(normed, mixed, branch_zero, branch_one, att_zero, att_one, out_ref):
-    cols = mixed.shape[1]
-    out_ref[:, :cols] = dot(normed[...], mixed[...], 0, 0)
-    out_ref[:, cols:] = product((branch_zero, branch_one), (att_zero, att_one))
-
-
-def slot_kernel(place, sums, small, back_zero, back_one, up_zero, up_one, mixed_sums, keep_ref, send_ref, flat_ref):
+    all_slots(place, sum_ref, blocks)
+
+
+def last_kernel(place, normed, mixed, branch_zero, branch_one, att_zero, att_one, keep_ref, send_ref, rest_ref, sum_ref):
+    cols = att_zero.shape[1]
+    sum_ref[:, :cols] = product((branch_zero, branch_one), (att_zero, att_one))
+    sum_ref[:, cols:] = dot(normed[...], mixed[...], 0, 0)
+    to_slots(place, sum_ref, 0, keep_ref, send_ref)
+    rest_ref[...] = sum_ref[:, keep_ref.shape[2] :]
+
+
+def slot_kernel(place, rest, small, back_zero, back_one, up_zero, up_one, mixed_sums, keep_ref, send_ref, flat_ref):
+    to_slots(place, rest, 0, keep_ref, send_ref)
+    cols, wide_cols = mixed_sums.shape[1] // 3, keep_ref.shape[2]
     rows = keep_ref.shape[1] - 8
-    to_slots(place, sums, keep_ref, send_ref, rows)
-    cols = (mixed_sums.shape[1]) // 3
     count = small.shape[0] - 2
     back = back_zero[...] + back_one[...]
     wide = [small[count : count + 1, :], small[count + 1 :, :], back[2:3], back[0:1], back[1:2], back[3:4]]
@@ -544,26 +556,36 @@
         for v in wide:
             n = v.shape[1] // 8
             parts.append(v[:, owner * n : (owner + 1) * n])
-        parts.append(jnp.zeros((1, keep_ref.shape[2] - sum(p.shape[1] for p in parts)), F32))
+        parts.append(jnp.zeros((1, 2 * wide_cols - sum(p.shape[1] for p in parts)), F32))
         flat_ref[owner : owner + 1, :] = jnp.concatenate(parts, axis=1)
+    first = iota((8, wide_cols), 0) == 0
     for slot, owner in enumerate((0, 6, 2, 4)):
-        space = (8, keep_ref.shape[2])
-        keep_ref[slot, rows:, :] = jnp.broadcast_to(flat_ref[pl.ds(owner ^ place[7], 1), :], space)
-        send_ref[slot, rows:, :] = jnp.broadcast_to(flat_ref[pl.ds(owner ^ 1 ^ place[7], 1), :], space).astype(LOW)
-
-
-def finish_kernel(keep, got, in_ref, proj_ref, flat_ref):
+        mine, other = (flat_ref[pl.ds(owner ^ k ^ place[7], 1), :] for k in range(2))
+        keep_ref[slot, rows:, :] = jnp.where(first, mine[:, :wide_cols], mine[:, wide_cols:])
+        send_ref[slot, rows:, :] = jnp.where(first, other[:, :wide_cols], other[:, wide_cols:]).astype(LOW)
+
+
+def finish_kernel(one_keep, one_got, two_keep, two_got, in_ref, proj_ref, flat_ref):
     rows, cols = in_ref.shape[1:]
-    total = keep[0] + got[0].astype(F32)
-    for k in range(3):
-        in_ref[k] = total[:rows, k * cols : (k + 1) * cols]
-    proj_ref[...] = total[:rows, 3 * cols :].T
-    flat_ref[...] = total[rows : rows + 1, :]
-
-
-def pair_kernel(up_keep, up_got, down_keep, down_got, up_ref, down_ref):
-    up_ref[...] = up_keep[0] + up_got[0].astype(F32)
-    down_ref[...] = (down_keep[0] + down_got[0].astype(F32)).T
+    one = one_keep[0] + one_got[0].astype(F32)
+    two = two_keep[0] + two_got[0].astype(F32)
+    proj_ref[...] = one[:, :cols].T
+    in_ref[0] = one[:, cols:]
+    in_ref[1] = two[:rows, :cols]
+    in_ref[2] = two[:rows, cols:]
+    flat_ref[...] = jnp.concatenate([two[rows : rows + 1, :], two[rows + 1 : rows + 2, :]], axis=1)
+
+
+def pair_kernel(*refs):
+    *parts, out_ref = refs
+    out_ref[...] = jnp.concatenate(
+        [keep[0] + got[0].astype(F32) for keep, got in zip(parts[::2], parts[1::2])], axis=1
+    )
+
+
+def joined(*parts):
+    shape = (parts[0].shape[1], sum(p.shape[2] for p in parts[::2]))
+    return call(pair_kernel, ((shape, F32),), *parts)[0]
 
 
 def result_kernel(place, keep, got, res_zero, res_one, vecs, out_ref):
@@ -590,17 +612,19 @@
     return call(stack_kernel, (((2, *a.shape), a.dtype),), a, b)[0]
 
 
-def grad_blocks(kernel, place, shard_rows, *sides):
-    width, cols = 8 * shard_rows, sides[-1].shape[1]
-    shape = (4, shard_rows, cols)
+def grad_blocks(kernel, place, splits, *sides):
+    width, cols = sides[0].shape[-1], sides[-1].shape[1]
+    shapes = []
+    for n in splits:
+        shapes += [((4, width // 8, n), F32), ((4, width // 8, n), LOW)]
     scratch = (pltpu.VMEM((width, cols), F32),)
-    return call(kernel, ((shape, F32), (shape, LOW)), place, *sides, scratch=scratch, mib=12)
+    return call(functools.partial(kernel, len(sides)), shapes, place, *sides, scratch=scratch, mib=12)
 
 
 def plain_grad(shard_rows, *sides):
     half = len(sides) // 2
     total = sum(dot(a, b, 0, 0) for a, b in zip(sides[:half], sides[half:])).astype(LOW)
-    return dp_scatter_sum(total.reshape(-1, shard_rows, total.shape[1]), None)
+    return dp_scatter_sum(total.reshape(-1, shard_rows, total.shape[1]))
 
 
 def fast(shard_rows):
@@ -645,17 +669,37 @@
     place_pieces(masks, place, refs[:-1], write)
 
 
-def pack_kernel(w_qkv, w_proj, w_down, *refs):
-    *vectors, first_ref, down_ref = refs
+def pack_kernel(count, *refs):
+    sources, out_ref, held, sems = refs[:count], refs[count], refs[count + 1 : -1], refs[-1]
+    copies = [pltpu.make_async_copy(a, b, sems.at[k]) for k, (a, b) in enumerate(zip(sources, held))]
+    for c in copies:
+        c.start()
+    for c in copies:
+        c.wait()
+    w_qkv, w_proj, *vectors = held
     rows = w_qkv.shape[1]
-    parts = [w_qkv[0], w_qkv[1], w_qkv[2], w_proj[...].T]
-    first_ref[:rows, :] = jnp.concatenate(parts, axis=1)
+    out_ref[:rows, :] = jnp.concatenate([w_qkv[0], w_qkv[1], w_qkv[2], w_proj[...].T], axis=1)
     rows_of = [v[...].astype(F32) for v in vectors]
     rows_of = rows_of[:-1] + [rows_of[-1][0:1], rows_of[-1][1:2]]
     flat = jnp.concatenate(rows_of, axis=1)
-    flat = jnp.concatenate([flat, jnp.zeros((1, first_ref.shape[1] - flat.shape[1]), F32)], axis=1)
-    first_ref[rows:, :] = jnp.broadcast_to(flat, (8, flat.shape[1])).astype(LOW)
-    down_ref[...] = w_down[...].T
+    flat = jnp.concatenate([flat, jnp.zeros((1, out_ref.shape[1] - flat.shape[1]), F32)], axis=1)
+    out_ref[rows:, :] = jnp.broadcast_to(flat, (8, flat.shape[1])).astype(LOW)
+
+
+def first_pack(*args):
+    w_qkv, w_proj = args[:2]
+    return pl.pallas_call(
+        functools.partial(pack_kernel, len(args)),
+        out_shape=jax.ShapeDtypeStruct((w_qkv.shape[1] + 8, 3 * w_qkv.shape[2] + w_proj.shape[0]), LOW),
+        in_specs=[pl.BlockSpec(memory_space=pl.ANY) for _ in args],
+        out_specs=pl.BlockSpec(memory_space=pltpu.VMEM),
+        scratch_shapes=[
+            *(pltpu.VMEM(a.shape, a.dtype) for a in args),
+            pltpu.SemaphoreType.DMA((len(args),)),
+        ],
+        compiler_params=pltpu.CompilerParams(vmem_limit_bytes=63 << 20),
+        cost_estimate=pl.CostEstimate(flops=COST, bytes_accessed=0, transcendentals=0),
+    )(*args)
 
 
 def spans_of(vectors):
@@ -709,196 +753,73 @@
         send_ref[upper] = part[rows:].astype(LOW)
 
 
-def local(
-    x_embed,
-    thoughts,
-    thought_pos,
-    img_start,
-    pre_attn_gain,
-    pre_attn_bias,
-    w_qkv,
-    b_qv,
-    w_proj,
-    b_proj,
-    pre_mlp_gain,
-    pre_mlp_bias,
-    w_up,
-    b_up,
-    w_down,
-    b_down,
-    grad_out,
-):
+def local(x_embed, thoughts, thought_pos, img_start, *rest):
+    *params, grad_out = rest
     dp = lax.axis_size("dp")
-    tensor_rank = lax.axis_index("tensor")
-    dp_rank = lax.axis_index("dp")
-    _, rows, width = x_embed.shape
-    length, half = 4 * rows, 2 * rows
-    shard_rows = w_qkv.shape[1]
-    head_cols = w_qkv.shape[2]
-    qkv_cols = 3 * head_cols
-    hidden_cols = w_up.shape[1]
     table = []
     for d in range(dp):
         for t in range(4):
             table.append((t & 1, 0, 0, t >> 1, d, (d >> 1 ^ d >> 2) & 1, d >> 2 & 1, d & 1))
-    place = jnp.asarray(table, jnp.int32)[dp_rank * 4 + tensor_rank]
-    starts = img_start[0]
-
-    flat = [v.reshape(1, -1) for v in (pre_attn_gain, pre_attn_bias, b_proj, pre_mlp_gain, pre_mlp_bias, b_down, b_up)]
-    flat.append(b_qv)
-    sizes = (qkv_cols, head_cols, width)
-    quick = fast(shard_rows)
-
-    if quick:
-        pack_one, pack_three = call(
-            pack_kernel,
-            (((shard_rows + 8, qkv_cols + head_cols), LOW), ((shard_rows, hidden_cols), LOW)),
-            w_qkv,
-            w_proj,
-            w_down,
-            *flat,
-            piped=True,
-        )
-        x_far = swapped(x_embed[0], "tensor", 2)
-        far_one = swapped(pack_one, "dp", 6)
-        across_one = swapped(pack_one, "dp", 1)
-        across_two = swapped(w_up, "dp", 1)
-        x_far, far_one, across_one, across_two = together(x_far, far_one, across_one, across_two)
-
-        x_both = pick(place, x_embed[0], x_far)
-        cot_far = swapped(after(grad_out[0], x_far), "tensor", 2)
-        near_one = swapped(stacked(pack_one, far_one), "dp", 2)
-        far_across_one = swapped(far_one, "dp", 1)
-        across_three = swapped(after(pack_three, across_two), "dp", 1)
-        x_other = swapped(x_both, "tensor", 1)
-        near_one, far_across_one, across_three, x_other, cot_far = together(
-            near_one, far_across_one, across_three, x_other, cot_far
-        )
-
-        near_across_one = swapped(near_one, "dp", 1)
-        far_two = swapped(after(w_up, near_one), "dp", 6)
-        cot_both = pick(place, grad_out[0], cot_far)
-        cot_other = swapped(cot_both, "tensor", 1)
-        near_across_one, far_two, cot_other = together(near_across_one, far_two, cot_other)
-
-        pieces = (pack_one[None], across_one[None], far_one[None], near_one, far_across_one[None], near_across_one)
-        w_in, w_proj_t, vecs, up_bias, all_bias = first_unpacked(place, pieces, flat, *sizes)
-        near_two = swapped(stacked(w_up, far_two), "dp", 2)
-        far_across_two = swapped(far_two, "dp", 1)
-        x_rows, cots = (x_both, x_other), (cot_both, cot_other)
-    else:
-        x_rows, cots = rows_gather(x_embed[0]), rows_gather(grad_out[0])
-        first_pack = jnp.concatenate([w_qkv[0], w_qkv[1], w_qkv[2], w_proj.T], axis=1)
-        w_in, w_proj_t, vecs, up_bias, all_bias = plain_first(first_pack, flat, qkv_cols, width)
-        w_up_all = dp_gather(w_up).reshape(width, hidden_cols)
-        w_down_t = dp_gather(w_down.T).reshape(width, hidden_cols)
-
-    spliced, xhat_one, normed, queries, keys, values = call(
+    place = jnp.asarray(table, jnp.int32)[lax.axis_index("dp") * 4 + lax.axis_index("tensor")]
+    block = quick_block if fast(params[2].shape[1]) else plain_block
+    outs = block(place, img_start[0], x_embed[0], thoughts[0], thought_pos, params, grad_out[0])
+    vec, outs = outs[-1], outs[:-1]
+    sizes = [params[k].size for k in (0, 1, 5, 6, 7, 11, 9, 3)]
+    small, first = [], 0
+    for n in sizes:
+        small.append(vec[first : first + n])
+        first += n
+    gain_one, bias_one, proj_b, gain_two, bias_two, down_b, up_b, qv_b = small
+    block_out, grad_embed, grad_thoughts, grad_in, grad_proj, grad_up, grad_down = outs
+    return (
+        block_out[None],
+        grad_embed[None],
+        grad_thoughts[None],
+        gain_one,
+        bias_one,
+        grad_in,
+        qv_b.reshape(2, -1),
+        grad_proj,
+        proj_b,
+        gain_two,
+        bias_two,
+        grad_up,
+        up_b,
+        grad_down,
+        down_b,
+    )
+
+
+def vectors_of(params):
+    return [params[k].reshape(1, -1) for k in (0, 1, 5, 6, 7, 11, 9)] + [params[3]]
+
+
+def input_side(place, x_rows, thoughts, thought_pos, vecs, w_in, bias):
+    length, width = 4 * x_rows[0].shape[1], x_rows[0].shape[2]
+    return call(
         input_kernel,
-        (((length, width), LOW),) * 3 + (((length, head_cols), LOW),) * 3,
+        (((length, width), LOW),) * 3 + (((length, w_in.shape[1] // 3), LOW),) * 3,
         place,
         *x_rows,
-        thoughts[0],
+        thoughts,
         thought_pos,
         vecs,
         w_in,
-        all_bias,
-    )
-
-    def core_sum(keep, send):
-        return add_low(keep, swapped(send, "tensor", 1))
-
-    att_zero, log_zero, *part = attend(0, place, starts, queries, keys, values, w_proj_t)
-    if quick:
-        near_two, far_across_two, part[1] = together(near_two, far_across_two, part[1])
-    branch_zero = core_sum(*part)
-    far_zero = swapped(branch_zero, "tensor", 2)
-    if quick:
-        near_across_two = swapped(near_two, "dp", 1)
-        far_three = swapped(after(pack_three, near_two), "dp", 6)
-    att_one, log_one, *part = attend(1, after(place, branch_zero), starts, queries, keys, values, w_proj_t)
-    if quick:
-        near_across_two, far_three, part[1] = together(near_across_two, far_three, part[1])
-        near_three = swapped(stacked(pack_three, far_three), "dp", 2)
-        far_across_three = swapped(far_three, "dp", 1)
-    branch_one = core_sum(*part)
-    far_zero, branch_one = together(far_zero, branch_one)
-    far_one = swapped(branch_one, "tensor", 2)
-    total_zero = add_low(branch_zero, far_zero)
-    other_zero = swapped(total_zero, "tensor", 1)
-    if quick:
-        pieces = (w_up[None], across_two[None], far_two[None], near_two, far_across_two[None], near_across_two)
-        w_up_all = unpacked(after(place, other_zero), pieces)
-        near_three, far_across_three, w_up_all = together(near_three, far_across_three, w_up_all)
-        near_across_three = swapped(near_three, "dp", 1)
-        pieces = (pack_three[None], across_three[None], far_three[None], near_three, far_across_three[None], near_across_three)
-        w_down_t = unpacked(place, pieces)
-    total_one = add_low(branch_one, far_one)
-    other_one = swapped(total_one, "tensor", 1)
-    attended, logs = (att_zero, att_one), (log_zero, log_one)
-
-    weights = (vecs, up_bias, w_up_all, w_down_t)
-    fed_zero = feed(0, spliced, total_zero, other_zero, cots, *weights)
-    grad_zero = core_sum(*fed_zero[5:])
-    far_zero = swapped(grad_zero, "tensor", 2)
-    fed_one = feed(1, after(spliced, grad_zero), total_one, other_one, cots, *weights)
-    grad_one = core_sum(*fed_one[5:])
-    residual, normed_two, hidden, grad_hidden, up_sums = zip(fed_zero[:5], fed_one[:5])
-    ups = (*normed_two, *grad_hidden)
-    if quick:
-        up_keep, up_send = grad_blocks(grad_kernel, after(place, grad_one), shard_rows, *ups)
-        up_got = swapped(up_send, "dp", 1)
-        down_keep, down_send = grad_blocks(cot_grad_kernel, after(place, up_keep), shard_rows, *cots, *hidden)
-        far_zero, down_send = together(far_zero, down_send)
-    else:
-        downs = (cots_rows(cots, 0), cots_rows(cots, 1), *hidden)
-        out_up, out_down = plain_grad(shard_rows, *ups), plain_grad(shard_rows, *downs)
-    far_one = swapped(after(grad_one, far_zero), "tensor", 2)
-    total_zero = add_low(grad_zero, far_zero)
-    other_zero = swapped(total_zero, "tensor", 1)
-    mlp_keep, mlp_send = call(
-        down_kernel,
-        (((2, rows, width), F32), ((2, rows, width), LOW)),
-        after(hidden[0], total_zero),
-        hidden[1],
-        w_down_t,
-    )
-    mlp_got = swapped(mlp_send, "tensor", 1)
-
-    back_zero = back(
-        0, after(place, mlp_keep), starts, total_zero, other_zero, residual[0], cots, vecs, w_proj_t,
-        queries, keys, values, attended[0], logs[0], (),
-    )
-    if quick:
-        up_got, far_one, back_dk = together(up_got, far_one, back_zero[3])
-        back_zero = (*back_zero[:3], back_dk, *back_zero[4:])
-        up_keep, up_send = fold(5, place, up_keep, up_got)
-        up_got = swapped(up_send, "dp", 2)
-        down_got = swapped(after(down_send, up_got), "dp", 1)
-    total_one = add_low(grad_one, far_one)
-    other_one = swapped(total_one, "tensor", 1)
-    mlp_keep, mlp_send = fold(3, place, mlp_keep, mlp_got)
-    mlp_got = swapped(after(mlp_send, far_one), "tensor", 2)
-    back_one = back(
-        1, after(place, mlp_keep), starts, total_one, other_one, residual[1], cots, vecs, w_proj_t,
-        queries, keys, values, attended[1], logs[1], back_zero[3:5],
-    )
-    grad_residual, grad_branch, grad_queries = zip(back_zero[:3], back_one[:3])
-    grad_keys, grad_values = back_one[3:5]
-    if quick:
-        grad_keys, mlp_got, up_got = together(grad_keys, mlp_got, up_got)
-        up_keep, up_send = fold(6, place, up_keep, up_got)
-        up_got = swapped(up_send, "dp", 6)
-
-    count = thoughts.shape[1]
-    keep, send, grad_mixed, small, mixed_sums, picked = call(
+        bias,
+    )
+
+
+def input_back(place, thought_pos, grad_queries, grad_keys, grad_values, w_in, xhat, grad_residual):
+    length, width = xhat.shape
+    count = thought_pos.shape[1]
+    return call(
         input_back_kernel,
         (
-            ((2, rows, width), F32),
-            ((2, rows, width), LOW),
-            ((length, qkv_cols), LOW),
+            ((2, length // 4, width), F32),
+            ((2, length // 4, width), LOW),
+            ((length, w_in.shape[1]), LOW),
             ((-(-(count + 2) // 8) * 8, width), F32),
-            ((1, qkv_cols), F32),
+            ((1, w_in.shape[1]), F32),
             ((-(-count // 8) * 8, width), F32),
         ),
         place,
@@ -907,102 +828,299 @@
         grad_keys,
         grad_values,
         w_in,
-        xhat_one,
+        xhat,
         *grad_residual,
         scratch=(pltpu.VMEM((length, width), F32),),
     )
-    got = swapped(send, "tensor", 1)
-    small_got = swapped(small, "tensor", 1)
-    lasts = (normed, grad_mixed, *grad_branch, *attended)
-    if quick:
-        got, small_got = together(got, small_got)
-    keep, send = fold(3, place, keep, got)
-    got = swapped(send, "tensor", 2)
-    small = add_full(small, small_got)
-    small_got = swapped(small, "tensor", 2)
-    if quick:
-        last = call(last_kernel, (((width, qkv_cols + head_cols), F32),), after(normed, send, small), *lasts[1:])[0]
-        last, small_got = together(last, small_got)
-    small = add_full(small, small_got)
-    rest = (small, back_zero[5], back_one[5], *up_sums, mixed_sums)
-    if quick:
-        shape = (4, shard_rows + 8, qkv_cols + head_cols)
-        scratch = (pltpu.VMEM((8, qkv_cols + head_cols), F32),)
-        last_keep, last_send = call(slot_kernel, ((shape, F32), (shape, LOW)), place, last, *rest, scratch=scratch)
-        last_got = swapped(last_send, "dp", 1)
-        down_keep, down_send = fold(5, place, down_keep, after(down_got, last_send))
-        down_got = swapped(down_send, "dp", 2)
-        last_got, up_got = together(last_got, up_got)
-        last_keep, last_send = fold(5, place, last_keep, last_got)
-        last_got = swapped(last_send, "dp", 2)
-        down_keep, down_send = fold(6, place, down_keep, down_got)
-        down_got = swapped(down_send, "dp", 6)
-    mlp = (mlp_keep[0], mlp_got[0], *residual, vecs)
-    block_out = call(result_kernel, (((rows, width), LOW),), place, *mlp)[0]
-    grad_embed, grad_thoughts = call(
+
+
+def output_side(place, keep, got, spliced, grad_residual, vecs, thought_pos, thoughts, small, picked):
+    rows, width = keep.shape
+    return call(
         output_kernel,
-        (((rows, width), F32), ((count, width // 4), F32)),
+        (((rows, width), F32), ((thoughts.shape[0], width // 4), F32)),
         place,
-        keep[0],
-        got[0],
+        keep,
+        got,
         spliced,
         *grad_residual,
         vecs,
         thought_pos,
-        thoughts[0],
+        thoughts,
         small,
         picked,
     )
-    if quick:
-        last_keep, last_send = fold(6, place, last_keep, last_got)
-        last_got = swapped(last_send, "dp", 6)
-        out_up, out_down = call(
-            pair_kernel,
-            (((shard_rows, hidden_cols), F32), ((hidden_cols, shard_rows), F32)),
-            up_keep,
-            up_got,
-            down_keep,
-            down_got,
+
+
+def result(place, keep, got, residual, vecs):
+    return call(result_kernel, ((keep.shape, LOW),), place, keep, got, *residual, vecs)[0]
+
+
+def down_part(hidden, w_down_t):
+    shape = (2, hidden[0].shape[0] // 2, w_down_t.shape[0])
+    return call(down_kernel, ((shape, F32), (shape, LOW)), *hidden, w_down_t)
+
+
+def quick_block(place, starts, x_own, thoughts, thought_pos, params, cot_own):
+    across = lambda a: swapped(a, "dp", 1)
+    near = lambda a: swapped(a, "dp", 2)
+    far = lambda a: swapped(a, "dp", 6)
+    core = lambda a: swapped(a, "tensor", 1)
+    over = lambda a: swapped(a, "tensor", 2)
+    w_qkv, w_proj, w_up, w_down_own = params[2], params[4], params[8], params[10].T
+    shard_rows, head_cols = w_qkv.shape[1:]
+    width = x_own.shape[1]
+    vectors = vectors_of(params)
+
+    x_far = over(x_own)
+    pack = first_pack(w_qkv, w_proj, *vectors)
+    pack_far, pack_across, up_across = far(pack), across(pack), across(w_up)
+    x_far, pack_far, pack_across, up_across = together(x_far, pack_far, pack_across, up_across)
+
+    x_both = pick(place, x_own, x_far)
+    x_other = core(x_both)
+    pack_near, pack_far_across = near(stacked(pack, pack_far)), across(pack_far)
+    up_far = far(after(w_up, pack_far))
+    down_across = across(after(w_down_own, up_across))
+    cot_far = over(after(cot_own, x_far))
+    x_other, pack_near, pack_far_across, down_across, up_far, cot_far = together(
+        x_other, pack_near, pack_far_across, down_across, up_far, cot_far
+    )
+
+    pack_near_across = across(pack_near)
+    up_near = near(stacked(w_up, up_far))
+    down_far = far(after(w_down_own, up_far))
+    cot_both = pick(place, cot_own, cot_far)
+    cot_other = core(cot_both)
+    pieces = (pack[None], pack_across[None], pack_far[None], pack_near, pack_far_across[None], pack_near_across)
+    w_in, w_proj_t, vecs, up_bias, all_bias = first_unpacked(place, pieces, vectors, 3 * head_cols, head_cols, width)
+    spliced, xhat, normed, queries, keys, values = input_side(
+        place, (x_both, x_other), thoughts, thought_pos, vecs, w_in, all_bias
+    )
+    att_zero, log_zero, keep_zero, send_zero = attend(0, place, starts, queries, keys, values, w_proj_t)
+    send_zero, up_near, down_far, cot_other = together(send_zero, up_near, down_far, cot_other)
+    cots = (cot_both, cot_other)
+
+    mine_zero = add_low(keep_zero, core(send_zero))
+    far_zero = over(mine_zero)
+    up_far_across, up_near_across = across(after(up_far, send_zero)), across(up_near)
+    down_near = near(stacked(w_down_own, down_far))
+    att_one, log_one, keep_one, send_one = attend(1, after(place, mine_zero), starts, queries, keys, values, w_proj_t)
+    send_one, far_zero, up_far_across, up_near_across, down_near = together(
+        send_one, far_zero, up_far_across, up_near_across, down_near
+    )
+
+    mine_one = add_low(keep_one, core(send_one))
+    far_one = over(mine_one)
+    total_zero = add_low(mine_zero, far_zero)
+    other_zero = core(total_zero)
+    down_far_across, down_near_across = across(after(down_far, send_one)), across(down_near)
+    pieces = (w_up[None], up_across[None], up_far[None], up_near, up_far_across[None], up_near_across)
+    w_up_all = unpacked(place, pieces)
+    other_zero, down_far_across, down_near_across, w_up_all = together(
+        other_zero, down_far_across, down_near_across, w_up_all
+    )
+    pieces = (w_down_own[None], down_across[None], down_far[None], down_near, down_far_across[None], down_near_across)
+    w_down_t = unpacked(place, pieces)
+
+    weights = (vecs, up_bias, w_up_all, w_down_t)
+    residual_zero, normed_zero, hidden_zero, grad_zero, up_sum_zero, keep_zero, send_zero = feed(
+        0, spliced, total_zero, other_zero, cots, *weights
+    )
+    send_zero, far_one = together(send_zero, far_one)
+    total_one = add_low(mine_one, far_one)
+    other_one = core(total_one)
+    mine_zero = add_low(keep_zero, core(send_zero))
+    far_zero = over(mine_zero)
+    residual_one, normed_one, hidden_one, grad_one, up_sum_one, keep_one, send_one = feed(
+        1, after(spliced, mine_zero), total_one, other_one, cots, *weights
+    )
+    quarter = hidden_one.shape[1] // 3
+    a_keep, a_send, b_keep, b_send = grad_blocks(
+        grad_kernel, place, (quarter, 2 * quarter), normed_zero, normed_one, grad_zero, grad_one
+    )
+    a_got = across(a_send)
+    mine_one = add_low(keep_one, core(send_one))
+    c_keep, c_send = grad_blocks(
+        cot_grad_kernel, after(place, a_send), (3 * quarter,), *cots, hidden_zero, hidden_one
+    )
+    mlp_keep, mlp_send = down_part((hidden_zero, after(hidden_one, a_send)), w_down_t)
+    far_zero, mine_one, c_send, mlp_send, a_got = together(far_zero, mine_one, c_send, mlp_send, a_got)
+    residual = (residual_zero, residual_one)
+
+    far_one = over(mine_one)
+    b_got = across(after(b_send, a_got))
+    a_keep, a_send = fold(5, place, a_keep, a_got)
+    a_got = near(a_send)
+    mlp_got = core(mlp_send)
+    total_zero = add_low(mine_zero, far_zero)
+    res_zero, branch_zero, gatt_zero, delta_zero, sums_zero = branch_back(
+        0, total_zero, core(total_zero), residual_zero, cots, vecs, w_proj_t, att_zero
+    )
+    dq_zero, *early = back(0, place, starts, queries, keys, values, log_zero, gatt_zero, delta_zero, ())
+    early[0], far_one, mlp_got, a_got, b_got = together(early[0], far_one, mlp_got, a_got, b_got)
+
+    total_one = add_low(mine_one, far_one)
+    other_one = core(total_one)
+    c_got = across(after(c_send, b_got))
+    mlp_keep, mlp_send = fold(3, place, mlp_keep, mlp_got)
+    mlp_got = over(mlp_send)
+    a_keep, a_send = fold(6, place, a_keep, a_got)
+    a_got = far(a_send)
+    b_keep, b_send = fold(5, place, b_keep, b_got)
+    b_got = near(b_send)
+    res_one, branch_one, gatt_one, delta_one, sums_one = branch_back(
+        1, total_one, other_one, residual_one, cots, vecs, w_proj_t, att_one
+    )
+    dq_one, dk, dv = back(1, place, starts, queries, keys, values, log_one, gatt_one, delta_one, early)
+    dk, mlp_got, a_got, b_got, c_got = together(dk, mlp_got, a_got, b_got, c_got)
+
+    grad_residual = (res_zero, res_one)
+    c_keep, c_send = fold(5, place, c_keep, c_got)
+    c_got = near(c_send)
+    b_keep, b_send = fold(6, place, b_keep, b_got)
+    b_got = far(b_send)
+    keep, send, grad_mixed, small, mixed_sums, picked = input_back(
+        place, thought_pos, (dq_zero, dq_one), dk, dv, w_in, xhat, grad_residual
+    )
+    got, small_got = core(send), core(small)
+    shape = (4, shard_rows, 2 * head_cols)
+    d_keep, d_send, rest = call(
+        last_kernel,
+        ((shape, F32), (shape, LOW), ((width, 2 * head_cols), F32)),
+        place,
+        normed,
+        grad_mixed,
+        branch_zero,
+        branch_one,
+        att_zero,
+        att_one,
+        scratch=(pltpu.VMEM((width, 4 * head_cols), F32),),
+        mib=12,
+    )
+    got, small_got, d_send = together(got, small_got, d_send)
+    d_got = across(d_send)
+    keep, send = fold(3, place, keep, got)
+    got = over(send)
+    small = add_full(small, small_got)
+    small_got = over(small)
+    block_out = result(place, mlp_keep[0], mlp_got[0], residual, vecs)
+    small_got, b_got, c_got, block_out = together(small_got, b_got, c_got, block_out)
+    small = add_full(small, small_got)
+    c_keep, c_send = fold(6, place, c_keep, c_got)
+    c_got = far(c_send)
+    grad_up = joined(a_keep, a_got, b_keep, b_got)
+    shape = (4, shard_rows + 8, 2 * head_cols)
+    e_keep, e_send = call(
+        slot_kernel,
+        ((shape, F32), (shape, LOW)),
+        place,
+        rest,
+        small,
+        sums_zero,
+        sums_one,
+        up_sum_zero,
+        up_sum_one,
+        mixed_sums,
+        scratch=(pltpu.VMEM((8, 4 * head_cols), F32),),
+    )
+    e_send, d_got, grad_up = together(e_send, d_got, grad_up)
+    e_got = across(e_send)
+    d_keep, d_send = fold(5, place, d_keep, d_got)
+    d_got = near(d_send)
+    got, e_got, d_got, c_got = together(got, e_got, d_got, c_got)
+    e_keep, e_send = fold(5, place, e_keep, e_got)
+    e_got = near(e_send)
+    d_keep, d_send = fold(6, place, d_keep, d_got)
+    d_got = far(d_send)
+    grad_embed, grad_thoughts = output_side(
+        place, keep[0], got[0], spliced, grad_residual, vecs, thought_pos, thoughts, small, picked
+    )
+    grad_embed, d_got, e_got = together(grad_embed, d_got, e_got)
+    e_keep, e_send = fold(6, place, e_keep, e_got)
+    e_got = far(e_send)
+    grad_down = joined(c_keep, c_got)
+    grad_down, e_got = together(grad_down, e_got)
+    grad_in, grad_proj, vec = call(
+        finish_kernel,
+        (((3, shard_rows, head_cols), F32), ((head_cols, shard_rows), F32), ((1, 4 * head_cols), F32)),
+        d_keep,
+        d_got,
+        e_keep,
+        e_got,
+    )
+    return block_out, grad_embed, grad_thoughts, grad_in, grad_proj, grad_up, grad_down.T, vec[0]
+
+
+def plain_block(place, starts, x_own, thoughts, thought_pos, params, cot_own):
+    dp = lax.axis_size("dp")
+    w_qkv, w_proj, w_up, w_down_own = params[2], params[4], params[8], params[10].T
+    shard_rows, head_cols = w_qkv.shape[1:]
+    width = x_own.shape[1]
+    x_rows, cots = rows_gather(x_own), rows_gather(cot_own)
+    shard = jnp.concatenate([w_qkv[0], w_qkv[1], w_qkv[2], w_proj.T], axis=1)
+    w_in, w_proj_t, vecs, up_bias, all_bias = plain_first(shard, vectors_of(params), 3 * head_cols, width)
+    w_up_all = dp_gather(w_up).reshape(width, -1)
+    w_down_t = dp_gather(w_down_own).reshape(width, -1)
+    spliced, xhat, normed, queries, keys, values = input_side(
+        place, x_rows, thoughts, thought_pos, vecs, w_in, all_bias
+    )
+
+    def all_sum(keep, send):
+        mine = add_low(keep, swapped(send, "tensor", 1))
+        total = add_low(mine, swapped(mine, "tensor", 2))
+        return total, swapped(total, "tensor", 1)
+
+    def own_sum(keep, send):
+        keep, send = fold(3, place, keep, swapped(send, "tensor", 1))
+        return keep[0], swapped(send, "tensor", 2)[0]
+
+    atts, logs, feds, grad_twos = [], [], [], []
+    for chunk in range(2):
+        att, log, *part = attend(chunk, place, starts, queries, keys, values, w_proj_t)
+        feds.append(feed(chunk, spliced, *all_sum(*part), cots, vecs, up_bias, w_up_all, w_down_t))
+        grad_twos.append(all_sum(*feds[-1][5:]))
+        atts.append(att)
+        logs.append(log)
+    residual, normed_two, hidden, grad_hidden, up_sums = zip(feds[0][:5], feds[1][:5])
+    block_out = result(place, *own_sum(*down_part(hidden, w_down_t)), residual, vecs)
+    grad_up = plain_grad(shard_rows, *normed_two, *grad_hidden)
+    grad_down = plain_grad(shard_rows, cots_rows(cots, 0), cots_rows(cots, 1), *hidden)
+    branches, dqs, early = [], [], ()
+    for chunk in range(2):
+        branches.append(
+            branch_back(chunk, *grad_twos[chunk], residual[chunk], cots, vecs, w_proj_t, atts[chunk])
         )
-        out_in, out_proj, vec = call(
-            finish_kernel,
-            (((3, shard_rows, head_cols), F32), ((head_cols, shard_rows), F32), ((1, qkv_cols + head_cols), F32)),
-            last_keep,
-            last_got,
+        dq, *early = back(
+            chunk, place, starts, queries, keys, values, logs[chunk], *branches[-1][2:4], early
         )
-        vec = vec[0]
-    else:
-        out_in = plain_grad(shard_rows, *lasts[:2])
-        out_in = jnp.moveaxis(out_in.reshape(shard_rows, 3, head_cols), 1, 0)
-        out_proj = plain_grad(shard_rows, *lasts[2:]).T
-        out_down = out_down.T
-        two = back_zero[5] + back_one[5]
-        vec = (small[count], small[count + 1], two[2], two[0], two[1], two[3], up_sums[0] + up_sums[1])
-        vec += (mixed_sums[0, :head_cols], mixed_sums[0, 2 * head_cols :])
-        vec = jnp.concatenate([v.reshape(dp, -1) for v in vec], axis=1)
-        vec = dp_scatter_sum(vec[:, None, :], None)[0]
-    outs, first = [], 0
-    for n in (*(v.shape[1] for v in flat[:7]), b_qv.size):
-        outs.append(vec[first : first + n])
-        first += n
-    out_gain_one, out_bias_one, out_b_proj, out_gain_two, out_bias_two, out_b_down, out_b_up, out_qv = outs
-
+        dqs.append(dq)
+    grad_residual, grad_branch = zip(branches[0][:2], branches[1][:2])
+    keep, send, grad_mixed, small, mixed_sums, picked = input_back(
+        place, thought_pos, dqs, *early, w_in, xhat, grad_residual
+    )
+    small = small + swapped(small, "tensor", 1)
+    small = small + swapped(small, "tensor", 2)
+    grad_embed, grad_thoughts = output_side(
+        place, *own_sum(keep, send), spliced, grad_residual, vecs, thought_pos, thoughts, small, picked
+    )
+    grad_in = plain_grad(shard_rows, normed, grad_mixed).reshape(shard_rows, 3, head_cols)
+    grad_proj = plain_grad(shard_rows, *grad_branch, *atts)
+    two = branches[0][4] + branches[1][4]
+    count = small.shape[0] - 2
+    vec = (small[count], small[count + 1], two[2], two[0], two[1], two[3], up_sums[0] + up_sums[1])
+    vec += (mixed_sums[0, :head_cols], mixed_sums[0, 2 * head_cols :])
+    vec = jnp.concatenate([v.reshape(dp, -1) for v in vec], axis=1)
+    vec = dp_scatter_sum(vec[:, None, :])[0]
     return (
-        block_out[None],
-        grad_embed[None],
-        grad_thoughts[None],
-        out_gain_one,
-        out_bias_one,
-        out_in,
-        out_qv.reshape(2, -1),
-        out_proj,
-        out_b_proj,
-        out_gain_two,
-        out_bias_two,
-        out_up,
-        out_b_up,
-        out_down,
-        out_b_down,
+        block_out,
+        grad_embed,
+        grad_thoughts,
+        jnp.moveaxis(grad_in, 1, 0),
+        grad_proj.T,
+        grad_up,
+        grad_down.T,
+        vec,
     )
 
 

time: 207 us -> 184 us (0.89)
  waiting for transfers between devices: 87.6 us -> 62.8 us
  local copies, waits for them, and re-layouts: 12.5 us -> 3.97 us
  starting transfers between devices: 45.5 us -> 51.5 us
  Pallas kernels: 59.4 us -> 64.1 us
    ppermute x46 -> x52, waiting for transfers between devices: 87.6 us -> 62.8 us  [swapped(): lax.ppermute(array, axis, [(i, i ^ mask) for i in range(lax.axis_size(axi...]
    unnamed x35 -> x17, local copies, waits for them, and re-layouts: 10.5 us -> 1.94 us
    ppermute x46 -> x52, starting transfers between devices: 45.5 us -> 51.5 us  [swapped(): lax.ppermute(array, axis, [(i, i ^ mask) for i in range(lax.axis_size(axi...]
    pallas_call x44 -> x50, Pallas kernels: 59.4 us -> 62.3 us  [call(): pl.pallas_call(kernel, out_shape=tuple((jax.ShapeDtypeStruct(s, t) for s,...]
  transfers between devices with their start and end apart: 46 -> 52, of which waited for: 25 -> 19; matrix products, arithmetic and copies ran while one was open for 2% -> 1% of each run, Pallas kernels for 24% -> 30%
where the time goes in v1:
time: 184 us
  Pallas kernels  64.1 us (35%)
  waiting for transfers between devices  62.8 us (34%)
  starting transfers between devices  51.5 us (28%)
  local copies, waits for them, and re-layouts  3.97 us (2%)
    ppermute x52, waiting for transfers between devices, swapped(): lax.ppermute(array, axis, [(i, i ^ mask) for i in range(lax.axis_size(axi...  62.8 us
    pallas_call x50, Pallas kernels, call(): pl.pallas_call(kernel, out_shape=tuple((jax.ShapeDtypeStruct(s, t) for s,...  62.3 us
    ppermute x52, starting transfers between devices, swapped(): lax.ppermute(array, axis, [(i, i ^ mask) for i in range(lax.axis_size(axi...  51.5 us
  transfers between devices with their start and end apart: 52, of which 19 were waited for; matrix products, arithmetic and copies ran while one was open for 1% of the time, Pallas kernels for 30%

profile of v1, /device:TPU:0, one launch (start us, length us, event | category | flops | bytes accessed | tf_op | source)
XLA Modules:
  0.0 183.6 jit_solution(12097661070586660073)
XLA Ops:
  0.7 3.0 %collective-permute-start = (bf16[256,768]{1,0:T(8,128)(2,1)}, bf16[256,768]{1,0:T(8,128)(2,1)S(1)}, u32[]{:S(2)}, u32[]{:S(2)}) collective-permute-start(bf16[256,768]{1,0:T(8,128)(2,1)} %bitcast.63), channel_id=1, source_target_pairs={{0,2},{1,3},{2,0},{3,1},{4,6},{5,7},{6,4},{7,5},{8,10},{9,11},{10,... | collective-permute-start | bytes 1179656 | tf_op jit(solution)/shard_map/ppermute | solution.py:19
  3.7 1.8 shard_map.289.a
  5.5 3.7 %collective-permute-start.1 = (bf16[104,768]{1,0:T(8,128)(2,1)}, bf16[104,768]{1,0:T(8,128)(2,1)S(1)}, u32[]{:S(2)}, u32[]{:S(2)}) collective-permute-start(bf16[104,768]{1,0:T(8,128)(2,1)} %shard_map.289.a), channel_id=1, source_target_pairs={{0,24},{4,28},{8,16},{12,20},{16,8},{20,12},{24,0},{28,4},{1,25},{... | collective-permute-start | bytes 479240 | tf_op jit(solution)/shard_map/ppermute | solution.py:19
  9.2 1.5 collective-permute-start.2
  11.9 5.9 %collective-permute-done.3 = bf16[96,768]{1,0:T(8,128)(2,1)S(1)} collective-permute-done((bf16[96,768]{1,0:T(8,128)(2,1)}, bf16[96,768]{1,0:T(8,128)(2,1)S(1)}, u32[]{:S(2)}, u32[]{:S(2)}) %collective-permute-start.3) | collective-permute-done | bytes 147488 | tf_op jit(solution)/shard_map/ppermute | solution.py:19
  17.9 1.0 copy-done.3
  20.5 1.6 collective-permute-start.7
  22.6 4.7 %collective-permute-done.7 = bf16[96,768]{1,0:T(8,128)(2,1)S(1)} collective-permute-done((bf16[96,768]{1,0:T(8,128)(2,1)S(1)}, bf16[96,768]{1,0:T(8,128)(2,1)S(1)}, u32[]{:S(2)}, u32[]{:S(2)}) %collective-permute-start.7) | collective-permute-done | bytes 147488 | tf_op jit(solution)/shard_map/ppermute | solution.py:19
  27.3 0.9 collective-permute-start.8
  28.3 6.1 %collective-permute-done.8.b = bf16[96,768]{1,0:T(8,128)(2,1)S(1)} collective-permute-done((bf16[96,768]{1,0:T(8,128)(2,1)S(1)}, bf16[96,768]{1,0:T(8,128)(2,1)S(1)}, u32[]{:S(2)}, u32[]{:S(2)}) %collective-permute-start.8) | collective-permute-done | bytes 147488 | tf_op jit(solution)/shard_map/ppermute | solution.py:19
  35.1 1.6 collective-permute-start.10
  36.7 1.7 collective-permute-start.11
  38.4 1.2 collective-permute-start.12
  39.6 5.4 %collective-permute-done.10.refs_5_ = bf16[2,104,768]{2,1,0:T(8,128)(2,1)S(1)} collective-permute-done((bf16[2,104,768]{2,1,0:T(8,128)(2,1)S(1)}, bf16[2,104,768]{2,1,0:T(8,128)(2,1)S(1)}, u32[]{:S(2)}, u32[]{:S(2)}) %collective-permute-start.10) | collective-permute-done | bytes 319520 | tf_op jit(solution)/shard_map/ppermute | solution.py:19
  45.0 0.8 shard_map.292
  45.9 3.8 %shard_map.293 = (bf16[1024,768]{1,0:T(8,128)(2,1)S(1)}, bf16[1024,768]{1,0:T(8,128)(2,1)S(1)}, bf16[1024,768]{1,0:T(8,128)(2,1)S(1)}, bf16[1024,192]{1,0:T(8,12...) custom-call(s32[8]{0:T(128)S(1)} %dynamic-slice_bitcast_fusion.place, ...), custom_call_target="tpu_custom_call" | custom-call | flops 1000 | tf_op jit(solution)/shard_map/pallas_call | solution.py:131
  49.7 3.6 %shard_map.294 = (bf16[512,192]{1,0:T(8,128)(2,1)S(1)}, f32[8,512]{1,0:T(8,128)S(1)}, f32[256,768]{1,0:T(8,128)S(1)}, bf16[256,768]{1,0:T(8,128)(2,1)S(1)}) custom-call(s32[8]{0:T(128)S(1)} %dynamic-slice_bitcast_fusion.place, s32[2]{0:T(128)S(1)} %bitcast.76, bf16[1024,192]{1,0:T(8,128)(2,1)S(1)} %get-tuple-element.196.q_ref, ...), custom_call_target="tpu_custom_call" | custom-call | flops 1000 | tf_op jit(solution)/shard_map/pallas_call | solution.py:131
  53.4 1.7 collective-permute-done.14.b
  55.2 1.6 collective-permute-start.15
  56.8 1.7 collective-permute-start.18
  58.5 1.5 collective-permute-start.17
  60.5 6.4 %shard_map.298 = (bf16[512,192]{1,0:T(8,128)(2,1)S(1)}, f32[8,512]{1,0:T(8,128)S(1)}, f32[256,768]{1,0:T(8,128)S(1)}, bf16[256,768]{1,0:T(8,128)(2,1)S(1)}) custom-call(s32[8]{0:T(128)S(1)} %dynamic-slice_bitcast_fusion.place, s32[2]{0:T(128)S(1)} %bitcast.77, bf16[1024,192]{1,0:T(8,128)(2,1)S(1)} %get-tuple-element.196.q_ref, ...), custom_call_target="tpu_custom_call" | custom-call | flops 1000 | tf_op jit(solution)/shard_map/pallas_call | solution.py:131
  66.9 3.3 %collective-permute-done.16 = bf16[96,768]{1,0:T(8,128)(2,1)S(1)} collective-permute-done((bf16[96,768]{1,0:T(8,128)(2,1)S(1)}, bf16[96,768]{1,0:T(8,128)(2,1)S(1)}, u32[]{:S(2)}, u32[]{:S(2)}) %collective-permute-start.16) | collective-permute-done | bytes 147488 | tf_op jit(solution)/shard_map/ppermute | solution.py:19
  70.9 1.1 collective-permute-done.22.b
  72.6 1.5 collective-permute-start.21
  75.3 9.3 %collective-permute-done.20 = bf16[96,768]{1,0:T(8,128)(2,1)S(1)} collective-permute-done((bf16[96,768]{1,0:T(8,128)(2,1)S(1)}, bf16[96,768]{1,0:T(8,128)(2,1)S(1)}, u32[]{:S(2)}, u32[]{:S(2)}) %collective-permute-start.20) | collective-permute-done | bytes 147488 | tf_op jit(solution)/shard_map/ppermute | solution.py:19
  85.2 2.7 %shard_map.303 = (f32[512,768]{1,0:T(8,128)S(1)}, bf16[512,768]{1,0:T(8,128)(2,1)S(1)}, bf16[512,768]{1,0:T(8,128)(2,1)S(1)}, bf16[512,768]{1,0:T(8,128)(2,1)S(1...) custom-call(bf16[1024,768]{1,0:T(8,128)(2,1)S(1)} %get-tuple-element.230.spliced, ...), custom_call_target="tpu_custom_call" | custom-call | flops 1000 | tf_op jit(solution)/shard_map/pallas_call | solution.py:131
  88.6 1.1 collective-permute-done.24.b
  90.3 2.7 %shard_map.307 = (f32[512,768]{1,0:T(8,128)S(1)}, bf16[512,768]{1,0:T(8,128)(2,1)S(1)}, bf16[512,768]{1,0:T(8,128)(2,1)S(1)}, bf16[512,768]{1,0:T(8,128)(2,1)S(1...) custom-call(bf16[1024,768]{1,0:T(8,128)(2,1)S(1)} %get-tuple-element.230.spliced, ...), custom_call_target="tpu_custom_call" | custom-call | flops 1000 | tf_op jit(solution)/shard_map/pallas_call | solution.py:131
  93.2 1.5 collective-permute-start.25
  94.7 2.1 %shard_map.309 = (f32[4,96,256]{2,1,0:T(8,128)S(1)}, bf16[4,96,256]{2,1,0:T(8,128)(2,1)S(1)}, f32[4,96,512]{2,1,0:T(8,128)S(1)}, bf16[4,96,512]{2,1,0:T(8,128)(2,1)S(1)}) custom-call(s32[8]{0:T(128)S(1)} %dynamic-slice_bitcast_fusion.place, bf16[512,768]{1,0:T(8,128)(2,1)S(1)} %get-tuple-element.234.refs_0_, ...), custom_call_target="tpu_custom_call" | custom-call | flops 1000 | tf_op jit(solution)/shard_map/pallas_call | solution.py:131
  96.8 1.6 collective-permute-start.28
  98.4 1.4 shard_map.311
  99.8 2.1 %shard_map.310 = (f32[4,96,768]{2,1,0:T(8,128)S(1)}, bf16[4,96,768]{2,1,0:T(8,128)(2,1)S(1)}) custom-call(s32[8]{0:T(128)S(1)} %dynamic-slice_bitcast_fusion.place, bf16[2,256,768]{2,1,0:T(8,128)(2,1)S(1)} %shard_map.296.cot_zero, bf16[2,256,768]{2,1,0:T(8,128)(2,1)S(1)} %collective-permute-done.13.cot_one, ...), custom_call_target="tpu_custom_call" | custom-call | flops 1000 | tf_op jit(solution)/shard_map/pallas_call | solution.py:131
  102.0 1.7 collective-permute-done.28.got
  103.7 0.8 collective-permute-done.25.b
  105.3 1.5 collective-permute-start.33
  106.8 1.5 collective-permute-start.30
  109.3 2.3 %shard_map.313 = (f32[512,768]{1,0:T(8,128)S(1)}, bf16[512,768]{1,0:T(8,128)(2,1)S(1)}, bf16[512,192]{1,0:T(8,128)(2,1)S(1)}, f32[8,512]{1,0:T(8,128)S(1)}, f32[8,768]{1,0:T(8,128)S(1)}) custom-call(bf16[256,768]{1,0:T(8,128)(2,1)S(1)} %shard_map.312.total, bf16[256,768]{1,0:T(8,128)(2,1)S(1)} %collective-permute-done.29.other, ...), custom_call_target="tpu_custom_call" | custom-call | flops 1000 | tf_op jit(solution)/shard_map/pallas_call | solution.py:131
  111.6 3.6 %shard_map.314 = (bf16[512,192]{1,0:T(8,128)(2,1)S(1)}, f32[512,192]{1,0:T(8,128)S(1)}, f32[512,192]{1,0:T(8,128)S(1)}) custom-call(s32[8]{0:T(128)S(1)} %dynamic-slice_bitcast_fusion.place, s32[2]{0:T(128)S(1)} %bitcast.78, bf16[1024,192]{1,0:T(8,128)(2,1)S(1)} %get-tuple-element.196.q_ref, bf16[1024,192]{1,0:T(8,128)(2,1)S(1)} %get-tuple-element.197.k_ref, ...), custom_call_target="tpu_custom_call" | custom-call | flops 1000 | tf_op jit(solution)/shard_map/pallas_call | solution.py:131
  115.2 1.1 collective-permute-done.33.got
  116.4 1.2 collective-permute-done.30.b
  119.0 1.6 collective-permute-start.35
  122.2 1.2 collective-permute-start.36
  123.4 2.0 %shard_map.317 = (f32[512,768]{1,0:T(8,128)S(1)}, bf16[512,768]{1,0:T(8,128)(2,1)S(1)}, bf16[512,192]{1,0:T(8,128)(2,1)S(1)}, f32[8,512]{1,0:T(8,128)S(1)}, f32[8,768]{1,0:T(8,128)S(1)}) custom-call(bf16[256,768]{1,0:T(8,128)(2,1)S(1)} %shard_map.316.total, bf16[256,768]{1,0:T(8,128)(2,1)S(1)} %collective-permute-done.34.other, ...), custom_call_target="tpu_custom_call" | custom-call | flops 1000 | tf_op jit(solution)/shard_map/pallas_call | solution.py:131
  125.5 6.8 %shard_map.318 = (bf16[512,192]{1,0:T(8,128)(2,1)S(1)}, bf16[1024,192]{1,0:T(8,128)(2,1)S(1)}, bf16[1024,192]{1,0:T(8,128)(2,1)S(1)}) custom-call(s32[8]{0:T(128)S(1)} %dynamic-slice_bitcast_fusion.place, s32[2]{0:T(128)S(1)} %bitcast.79, bf16[1024,192]{1,0:T(8,128)(2,1)S(1)} %get-tuple-element.196.q_ref, bf16[1024,192]{1,0:T(8,128)(2,1)S(1)} %get-tuple-element.197.k_ref, ...), custom_call_target="tpu_custom_call" | custom-call | flops 1000 | tf_op jit(solution)/shard_map/pallas_call | solution.py:131
  132.3 2.2 %shard_map.322 = (f32[2,256,768]{2,1,0:T(8,128)S(1)}, bf16[2,256,768]{2,1,0:T(8,128)(2,1)S(1)}, bf16[1024,576]{1,0:T(8,128)(2,1)S(1)}, f32[8,768]{1,0:T(8,128)S(...) custom-call(s32[8]{0:T(128)S(1)} %dynamic-slice_bitcast_fusion.place, s32[6]{0:T(128)S(1)} %bitcast.80, ...), custom_call_target="tpu_custom_call" | custom-call | flops 1000 | tf_op jit(solution)/shard_map/pallas_call | solution.py:131
  135.7 0.8 collective-permute-start.43
  136.6 2.6 %shard_map.323 = (f32[4,96,384]{2,1,0:T(8,128)S(1)}, bf16[4,96,384]{2,1,0:T(8,128)(2,1)S(1)}, f32[768,384]{1,0:T(8,128)S(1)}) custom-call(s32[8]{0:T(128)S(1)} %dynamic-slice_bitcast_fusion.place, bf16[1024,768]{1,0:T(8,128)(2,1)S(1)} %get-tuple-element.287.normed, bf16[1024,576]{1,0:T(8,128)(2,1)S(1)} %get-tuple-element.288.mixed, ...), custom_call_target="tpu_custom_call" | custom-call | flops 1000 | tf_op jit(solution)/shard_map/pallas_call | solution.py:131
  139.2 1.6 collective-permute-start.45
  141.4 2.7 %collective-permute-start.42 = (bf16[1,96,512]{2,1,0:T(8,128)(2,1)S(1)}, bf16[1,96,512]{2,1,0:T(8,128)(2,1)S(1)}, u32[]{:S(2)}, u32[]{:S(2)}) collective-permute-start(bf16[1,96,512]{2,1,0:T(8,128)(2,1)S(1)} %get-tuple-element.295), channel_id=1, source_target_pairs={{0,24},{4,28},{8,16},{12,20},{16,8},{20,12},{24,0},{28,4},{1,25},{... | collective-permute-start | bytes 294920 | tf_op jit(solution)/shard_map/ppermute | solution.py:19
  145.3 1.5 collective-permute-start.41
  146.9 1.5 shard_map.327
  148.4 7.2 %collective-permute-done.41.b = f32[8,768]{1,0:T(8,128)S(1)} collective-permute-done((f32[8,768]{1,0:T(8,128)S(1)}, f32[8,768]{1,0:T(8,128)S(1)}, u32[]{:S(2)}, u32[]{:S(2)}) %collective-permute-start.41) | collective-permute-done | bytes 24608 | tf_op jit(solution)/shard_map/ppermute | solution.py:19
  155.6 0.7 shard_map.331
  158.3 1.2 collective-permute-start.48
  160.2 5.4 %collective-permute-done.48.refs_1_ = bf16[1,96,768]{2,1,0:T(8,128)(2,1)S(1)} collective-permute-done((bf16[1,96,768]{2,1,0:T(8,128)(2,1)S(1)}, bf16[1,96,768]{2,1,0:T(8,128)(2,1)S(1)}, u32[]{:S(2)}, u32[]{:S(2)}) %collective-permute-start.48) | collective-permute-done | bytes 147488 | tf_op jit(solution)/shard_map/ppermute | solution.py:19
  165.6 1.3 collective-permute-done.47.got
  168.2 2.2 %collective-permute-start.49 = (bf16[1,96,384]{2,1,0:T(8,128)(2,1)S(1)}, bf16[1,96,384]{2,1,0:T(8,128)(2,1)S(1)}, u32[]{:S(2)}, u32[]{:S(2)}) collective-permute-start(bf16[1,96,384]{2,1,0:T(8,128)(2,1)S(1)} %get-tuple-element.331), channel_id=1, source_target_pairs={{0,24},{4,28},{8,16},{12,20},{16,8},{20,12},{24,0},{28,4},{1,25},{... | collective-permute-start | bytes 221192 | tf_op jit(solution)/shard_map/ppermute | solution.py:19
  170.4 2.0 %shard_map.334 = (f32[256,768]{1,0:T(8,128)}, f32[6,192]{1,0:T(8,128)S(1)}) custom-call(s32[8]{0:T(128)S(1)} %dynamic-slice_bitcast_fusion.place, f32[256,768]{1,0:T(8,128)S(1)} %bitcast.52, bf16[256,768]{1,0:T(8,128)(2,1)S(1)} %bitcast.62, bf16[1024,768]{1,0:T(8,128)(2,1)S(1)} %get-tuple-element.230.spliced, f32[512,768]{1,0:T(8,128)S(1)} %get-tuple-element.283.res_zero, ...), custom_call_target="tpu_custom_call" | custom-call | flops 1000 | tf_op jit(solution)/shard_map/pallas_call | solution.py:131
  172.5 2.0 %collective-permute-done.49.one_got = bf16[1,96,384]{2,1,0:T(8,128)(2,1)S(1)} collective-permute-done((bf16[1,96,384]{2,1,0:T(8,128)(2,1)S(1)}, bf16[1,96,384]{2,1,0:T(8,128)(2,1)S(1)}, u32[]{:S(2)}, u32[]{:S(2)}) %collective-permute-start.49) | collective-permute-done | bytes 73760 | tf_op jit(solution)/shard_map/ppermute | solution.py:19
  175.1 2.2 %collective-permute-start.51 = (bf16[1,104,384]{2,1,0:T(8,128)(2,1)S(1)}, bf16[1,104,384]{2,1,0:T(8,128)(2,1)S(1)}, u32[]{:S(2)}, u32[]{:S(2)}) collective-permute-start(bf16[1,104,384]{2,1,0:T(8,128)(2,1)S(1)} %get-tuple-element.344), channel_id=1, source_target_pairs={{0,24},{4,28},{8,16},{12,20},{16,8},{20,12},{24,0},{28,4},{1,25},{... | collective-permute-start | bytes 239624 | tf_op jit(solution)/shard_map/ppermute | solution.py:19
  178.7 2.7 %collective-permute-done.51.two_got = bf16[1,104,384]{2,1,0:T(8,128)(2,1)S(1)} collective-permute-done((bf16[1,104,384]{2,1,0:T(8,128)(2,1)S(1)}, bf16[1,104,384]{2,1,0:T(8,128)(2,1)S(1)}, u32[]{:S(2)}, u32[]{:S(2)}) %collective-permute-start.51) | collective-permute-done | bytes 79904 | tf_op jit(solution)/shard_map/ppermute | solution.py:19
  181.4 0.9 shard_map.339
  (112 shorter events, 24.4 us)
Async XLA Ops:
  0.7 26.7 %copy-start.1 = (bf16[96,768]{1,0:T(8,128)(2,1)S(1)}, bf16[96,768]{1,0:T(8,128)(2,1)}, u32[]{:S(2)}) copy-start(bf16[96,768]{1,0:T(8,128)(2,1)} %a.1) | copy-start | bytes 442372
  0.7 19.8 %copy-start.2 = (bf16[768,96]{0,1:T(8,128)(2,1)S(1)}, bf16[768,96]{0,1:T(8,128)(2,1)}, u32[]{:S(2)}) copy-start(bf16[768,96]{0,1:T(8,128)(2,1)} %param.32) | copy-start | bytes 442372
  0.7 17.2 %collective-permute-start = (bf16[256,768]{1,0:T(8,128)(2,1)}, bf16[256,768]{1,0:T(8,128)(2,1)S(1)}, u32[]{:S(2)}, u32[]{:S(2)}) collective-permute-start(bf16[256,768]{1,0:T(8,128)(2,1)} %bitcast.63), channel_id=1, source_target_pairs={{0,2},{1,3},{2,0},{3,1},{4,6},{5,7},{6,4},{7,5},{8,10},{9,11},{10,... | collective-permute-start | bytes 1179656 | tf_op jit(solution)/shard_map/ppermute | solution.py:19
  5.5 14.9 %copy-start = (bf16[104,768]{1,0:T(8,128)(2,1)S(1)}, bf16[104,768]{1,0:T(8,128)(2,1)}, u32[]{:S(2)}) copy-start(bf16[104,768]{1,0:T(8,128)(2,1)} %shard_map.289.a) | copy-start | bytes 479236
  5.5 12.3 %collective-permute-start.1 = (bf16[104,768]{1,0:T(8,128)(2,1)}, bf16[104,768]{1,0:T(8,128)(2,1)S(1)}, u32[]{:S(2)}, u32[]{:S(2)}) collective-permute-start(bf16[104,768]{1,0:T(8,128)(2,1)} %shard_map.289.a), channel_id=1, source_target_pairs={{0,24},{4,28},{8,16},{12,20},{16,8},{20,12},{24,0},{28,4},{1,25},{... | collective-permute-start | bytes 479240 | tf_op jit(solution)/shard_map/ppermute | solution.py:19
  9.2 8.7 %collective-permute-start.2 = (bf16[104,768]{1,0:T(8,128)(2,1)}, bf16[104,768]{1,0:T(8,128)(2,1)S(1)}, u32[]{:S(2)}, u32[]{:S(2)}) collective-permute-start(bf16[104,768]{1,0:T(8,128)(2,1)} %shard_map.289.a), channel_id=1, source_target_pairs={{0,4},{4,0},{8,12},{12,8},{16,20},{20,16},{24,28},{28,24},{1,5},{5... | collective-permute-start | bytes 479240 | tf_op jit(solution)/shard_map/ppermute | solution.py:19
  10.7 7.1 %collective-permute-start.3 = (bf16[96,768]{1,0:T(8,128)(2,1)}, bf16[96,768]{1,0:T(8,128)(2,1)S(1)}, u32[]{:S(2)}, u32[]{:S(2)}) collective-permute-start(bf16[96,768]{1,0:T(8,128)(2,1)} %a.1), channel_id=1, source_target_pairs={{0,4},{4,0},{8,12},{12,8},{16,20},{20,16},{24,28},{28,24},{1,5},{5... | collective-permute-start | bytes 442376 | tf_op jit(solution)/shard_map/ppermute | solution.py:19
  17.9 1.0 copy-start.3
  18.9 1.0 copy-start.4
  19.5 14.9 %collective-permute-start.4 = (bf16[2,256,768]{2,1,0:T(8,128)(2,1)S(1)}, bf16[2,256,768]{2,1,0:T(8,128)(2,1)S(1)}, u32[]{:S(2)}, u32[]{:S(2)}) collective-permute-start(bf16[2,256,768]{2,1,0:T(8,128)(2,1)S(1)} %shard_map.290.x_zero), channel_id=1, source_target_pairs={{0,1},{1,0},{2,3},{3,2},{4,5},{5,4},{6,7},{7,6},{8,9},{9,8},{10,11... | collective-permute-start | bytes 2359304 | tf_op jit(solution)/shard_map/ppermute | solution.py:19
  19.9 14.5 %collective-permute-start.9 = (bf16[256,768]{1,0:T(8,128)(2,1)S(1)}, bf16[256,768]{1,0:T(8,128)(2,1)S(1)}, u32[]{:S(2)}, u32[]{:S(2)}) collective-permute-start(bf16[256,768]{1,0:T(8,128)(2,1)S(1)} %bitcast.65), channel_id=1, source_target_pairs={{0,2},{1,3},{2,0},{3,1},{4,6},{5,7},{6,4},{7,5},{8,10},{9,11},{10,... | collective-permute-start | bytes 1179656 | tf_op jit(solution)/shard_map/ppermute | solution.py:19
  20.4 14.0 %collective-permute-start.5 = (bf16[2,104,768]{2,1,0:T(8,128)(2,1)S(1)}, bf16[2,104,768]{2,1,0:T(8,128)(2,1)S(1)}, u32[]{:S(2)}, u32[]{:S(2)}) collective-permute-start(bf16[2,104,768]{2,1,0:T(8,128)(2,1)S(1)} %shard_map.291), channel_id=1, source_target_pairs={{0,8},{4,12},{8,0},{12,4},{16,24},{20,28},{24,16},{28,20},{1,9},{5... | collective-permute-start | bytes 958472 | tf_op jit(solution)/shard_map/ppermute | solution.py:19
  20.5 25.4 %copy-start.5 = (bf16[1,6,768]{2,1,0:T(8,128)(2,1)S(1)}, bf16[1,6,768]{2,1,0:T(8,128)(2,1)}, u32[]{:S(2)}) copy-start(bf16[1,6,768]{2,1,0:T(8,128)(2,1)} %param.19) | copy-start | bytes 27652
  20.5 25.4 %copy-start.7 = (s32[1,6]{1,0:T(1,128)S(1)}, s32[1,6]{1,0:T(1,128)}, u32[]{:S(2)}) copy-start(s32[1,6]{1,0:T(1,128)} %thought_pos.3) | copy-start | bytes 76
  20.5 6.8 %collective-permute-start.7 = (bf16[96,768]{1,0:T(8,128)(2,1)S(1)}, bf16[96,768]{1,0:T(8,128)(2,1)S(1)}, u32[]{:S(2)}, u32[]{:S(2)}) collective-permute-start(bf16[96,768]{1,0:T(8,128)(2,1)S(1)} %bitcast.55), channel_id=1, source_target_pairs={{0,4},{4,0},{8,12},{12,8},{16,20},{20,16},{24,28},{28,24},{1,5},{5... | collective-permute-start | bytes 442376 | tf_op jit(solution)/shard_map/ppermute | solution.py:19
  22.1 12.3 %collective-permute-start.6 = (bf16[104,768]{1,0:T(8,128)(2,1)S(1)}, bf16[104,768]{1,0:T(8,128)(2,1)S(1)}, u32[]{:S(2)}, u32[]{:S(2)}) collective-permute-start(bf16[104,768]{1,0:T(8,128)(2,1)S(1)} %collective-permute-done.1.b), channel_id=1, source_target_pairs={{0,4},{4,0},{8,12},{12,8},{16,20},{20,16},{24,28},{28,24},{1,5},{5... | collective-permute-start | bytes 479240 | tf_op jit(solution)/shard_map/ppermute | solution.py:19
  27.3 7.0 %collective-permute-start.8 = (bf16[96,768]{1,0:T(8,128)(2,1)S(1)}, bf16[96,768]{1,0:T(8,128)(2,1)S(1)}, u32[]{:S(2)}, u32[]{:S(2)}) collective-permute-start(bf16[96,768]{1,0:T(8,128)(2,1)S(1)} %copy-done.1), channel_id=1, source_target_pairs={{0,24},{4,28},{8,16},{12,20},{16,8},{20,12},{24,0},{28,4},{1,25},{... | collective-permute-start | bytes 442376 | tf_op jit(solution)/shard_map/ppermute | solution.py:19
  35.0 18.3 %collective-permute-start.13 = (bf16[2,256,768]{2,1,0:T(8,128)(2,1)S(1)}, bf16[2,256,768]{2,1,0:T(8,128)(2,1)S(1)}, u32[]{:S(2)}, u32[]{:S(2)}) collective-permute-start(bf16[2,256,768]{2,1,0:T(8,128)(2,1)S(1)} %shard_map.296.cot_zero), channel_id=1, source_target_pairs={{0,1},{1,0},{2,3},{3,2},{4,5},{5,4},{6,7},{7,6},{8,9},{9,8},{10,11... | collective-permute-start | bytes 2359304 | tf_op jit(solution)/shard_map/ppermute | solution.py:19
  35.1 10.0 %collective-permute-start.10 = (bf16[2,104,768]{2,1,0:T(8,128)(2,1)S(1)}, bf16[2,104,768]{2,1,0:T(8,128)(2,1)S(1)}, u32[]{:S(2)}, u32[]{:S(2)}) collective-permute-start(bf16[2,104,768]{2,1,0:T(8,128)(2,1)S(1)} %collective-permute-done.5.refs_3_), channel_id=1, source_target_pairs={{0,4},{4,0},{8,12},{12,8},{16,20},{20,16},{24,28},{28,24},{1,5},{5... | collective-permute-start | bytes 958472 | tf_op jit(solution)/shard_map/ppermute | solution.py:19
  36.7 16.6 %collective-permute-start.11 = (bf16[2,96,768]{2,1,0:T(8,128)(2,1)S(1)}, bf16[2,96,768]{2,1,0:T(8,128)(2,1)S(1)}, u32[]{:S(2)}, u32[]{:S(2)}) collective-permute-start(bf16[2,96,768]{2,1,0:T(8,128)(2,1)S(1)} %shard_map.295), channel_id=1, source_target_pairs={{0,8},{4,12},{8,0},{12,4},{16,24},{20,28},{24,16},{28,20},{1,9},{5... | collective-permute-start | bytes 884744 | tf_op jit(solution)/shard_map/ppermute | solution.py:19
  38.4 14.9 %collective-permute-start.12 = (bf16[96,768]{1,0:T(8,128)(2,1)S(1)}, bf16[96,768]{1,0:T(8,128)(2,1)S(1)}, u32[]{:S(2)}, u32[]{:S(2)}) collective-permute-start(bf16[96,768]{1,0:T(8,128)(2,1)S(1)} %bitcast.56), channel_id=1, source_target_pairs={{0,24},{4,28},{8,16},{12,20},{16,8},{20,12},{24,0},{28,4},{1,25},{... | collective-permute-start | bytes 442376 | tf_op jit(solution)/shard_map/ppermute | solution.py:19
  45.9 3.8 %copy-start.6 = (s32[1,2]{1,0:T(1,128)S(1)}, s32[1,2]{1,0:T(1,128)}, u32[]{:S(2)}) copy-start(s32[1,2]{1,0:T(1,128)} %param.21) | copy-start | bytes 28
  53.3 1.8 collective-permute-start.14
  55.2 14.9 %collective-permute-start.15 = (bf16[256,768]{1,0:T(8,128)(2,1)S(1)}, bf16[256,768]{1,0:T(8,128)(2,1)S(1)}, u32[]{:S(2)}, u32[]{:S(2)}) collective-permute-start(bf16[256,768]{1,0:T(8,128)(2,1)S(1)} %shard_map.297.a), channel_id=1, source_target_pairs={{0,2},{1,3},{2,0},{3,1},{4,6},{5,7},{6,4},{7,5},{8,10},{9,11},{10,... | collective-permute-start | bytes 1179656 | tf_op jit(solution)/shard_map/ppermute | solution.py:19
  56.8 13.3 %collective-permute-start.18 = (bf16[2,96,768]{2,1,0:T(8,128)(2,1)S(1)}, bf16[2,96,768]{2,1,0:T(8,128)(2,1)S(1)}, u32[]{:S(2)}, u32[]{:S(2)}) collective-permute-start(bf16[2,96,768]{2,1,0:T(8,128)(2,1)S(1)} %shard_map.299), channel_id=1, source_target_pairs={{0,8},{4,12},{8,0},{12,4},{16,24},{20,28},{24,16},{28,20},{1,9},{5... | collective-permute-start | bytes 884744 | tf_op jit(solution)/shard_map/ppermute | solution.py:19
  58.5 11.7 %collective-permute-start.17 = (bf16[2,96,768]{2,1,0:T(8,128)(2,1)S(1)}, bf16[2,96,768]{2,1,0:T(8,128)(2,1)S(1)}, u32[]{:S(2)}, u32[]{:S(2)}) collective-permute-start(bf16[2,96,768]{2,1,0:T(8,128)(2,1)S(1)} %collective-permute-done.11.refs_3_), channel_id=1, source_target_pairs={{0,4},{4,0},{8,12},{12,8},{16,20},{20,16},{24,28},{28,24},{1,5},{5... | collective-permute-start | bytes 884744 | tf_op jit(solution)/shard_map/ppermute | solution.py:19
  60.0 10.1 %collective-permute-start.16 = (bf16[96,768]{1,0:T(8,128)(2,1)S(1)}, bf16[96,768]{1,0:T(8,128)(2,1)S(1)}, u32[]{:S(2)}, u32[]{:S(2)}) collective-permute-start(bf16[96,768]{1,0:T(8,128)(2,1)S(1)} %collective-permute-done.8.b), channel_id=1, source_target_pairs={{0,4},{4,0},{8,12},{12,8},{16,20},{20,16},{24,28},{28,24},{1,5},{5... | collective-permute-start | bytes 442376 | tf_op jit(solution)/shard_map/ppermute | solution.py:19
  70.1 1.8 collective-permute-start.22
  70.3 14.2 %collective-permute-start.19 = (bf16[256,768]{1,0:T(8,128)(2,1)S(1)}, bf16[256,768]{1,0:T(8,128)(2,1)S(1)}, u32[]{:S(2)}, u32[]{:S(2)}) collective-permute-start(bf16[256,768]{1,0:T(8,128)(2,1)S(1)} %shard_map.300.total), channel_id=1, source_target_pairs={{0,1},{1,0},{2,3},{3,2},{4,5},{5,4},{6,7},{7,6},{8,9},{9,8},{10,11... | collective-permute-start | bytes 1179656 | tf_op jit(solution)/shard_map/ppermute | solution.py:19
  72.0 15.9 %collective-permute-start.23 = (bf16[256,768]{1,0:T(8,128)(2,1)S(1)}, bf16[256,768]{1,0:T(8,128)(2,1)S(1)}, u32[]{:S(2)}, u32[]{:S(2)}) collective-permute-start(bf16[256,768]{1,0:T(8,128)(2,1)S(1)} %shard_map.304.a), channel_id=1, source_target_pairs={{0,2},{1,3},{2,0},{3,1},{4,6},{5,7},{6,4},{7,5},{8,10},{9,11},{10,... | collective-permute-start | bytes 1179656 | tf_op jit(solution)/shard_map/ppermute | solution.py:19
  72.6 11.9 %collective-permute-start.21 = (bf16[2,96,768]{2,1,0:T(8,128)(2,1)S(1)}, bf16[2,96,768]{2,1,0:T(8,128)(2,1)S(1)}, u32[]{:S(2)}, u32[]{:S(2)}) collective-permute-start(bf16[2,96,768]{2,1,0:T(8,128)(2,1)S(1)} %collective-permute-done.18.refs_3_), channel_id=1, source_target_pairs={{0,4},{4,0},{8,12},{12,8},{16,20},{20,16},{24,28},{28,24},{1,5},{5... | collective-permute-start | bytes 884744 | tf_op jit(solution)/shard_map/ppermute | solution.py:19
  74.1 10.4 %collective-permute-start.20 = (bf16[96,768]{1,0:T(8,128)(2,1)S(1)}, bf16[96,768]{1,0:T(8,128)(2,1)S(1)}, u32[]{:S(2)}, u32[]{:S(2)}) collective-permute-start(bf16[96,768]{1,0:T(8,128)(2,1)S(1)} %collective-permute-done.12.b), channel_id=1, source_target_pairs={{0,4},{4,0},{8,12},{12,8},{16,20},{20,16},{24,28},{28,24},{1,5},{5... | collective-permute-start | bytes 442376 | tf_op jit(solution)/shard_map/ppermute | solution.py:19
  87.9 1.8 collective-permute-start.24
  88.1 2.2 %collective-permute-start.26 = (bf16[256,768]{1,0:T(8,128)(2,1)S(1)}, bf16[256,768]{1,0:T(8,128)(2,1)S(1)}, u32[]{:S(2)}, u32[]{:S(2)}) collective-permute-start(bf16[256,768]{1,0:T(8,128)(2,1)S(1)} %shard_map.306.total), channel_id=1, source_target_pairs={{0,1},{1,0},{2,3},{3,2},{4,5},{5,4},{6,7},{7,6},{8,9},{9,8},{10,11... | collective-permute-start | bytes 1179656 | tf_op jit(solution)/shard_map/ppermute | solution.py:19
  93.0 9.0 %collective-permute-start.27 = (bf16[256,768]{1,0:T(8,128)(2,1)S(1)}, bf16[256,768]{1,0:T(8,128)(2,1)S(1)}, u32[]{:S(2)}, u32[]{:S(2)}) collective-permute-start(bf16[256,768]{1,0:T(8,128)(2,1)S(1)} %get-tuple-element.233), channel_id=1, source_target_pairs={{0,1},{1,0},{2,3},{3,2},{4,5},{5,4},{6,7},{7,6},{8,9},{9,8},{10,11... | collective-permute-start | bytes 1179656 | tf_op jit(solution)/shard_map/ppermute | solution.py:19
  93.2 11.4 %collective-permute-start.25 = (bf16[256,768]{1,0:T(8,128)(2,1)S(1)}, bf16[256,768]{1,0:T(8,128)(2,1)S(1)}, u32[]{:S(2)}, u32[]{:S(2)}) collective-permute-start(bf16[256,768]{1,0:T(8,128)(2,1)S(1)} %shard_map.305.a), channel_id=1, source_target_pairs={{0,2},{1,3},{2,0},{3,1},{4,6},{5,7},{6,4},{7,5},{8,10},{9,11},{10,... | collective-permute-start | bytes 1179656 | tf_op jit(solution)/shard_map/ppermute | solution.py:19
  96.8 7.0 %collective-permute-start.28 = (bf16[4,96,256]{2,1,0:T(8,128)(2,1)S(1)}, bf16[4,96,256]{2,1,0:T(8,128)(2,1)S(1)}, u32[]{:S(2)}, u32[]{:S(2)}) collective-permute-start(bf16[4,96,256]{2,1,0:T(8,128)(2,1)S(1)} %get-tuple-element.238), channel_id=1, source_target_pairs={{0,4},{4,0},{8,12},{12,8},{16,20},{20,16},{24,28},{28,24},{1,5},{5... | collective-permute-start | bytes 589832 | tf_op jit(solution)/shard_map/ppermute | solution.py:19
  104.6 13.0 %collective-permute-start.31 = (bf16[2,256,768]{2,1,0:T(8,128)(2,1)S(1)}, bf16[2,256,768]{2,1,0:T(8,128)(2,1)S(1)}, u32[]{:S(2)}, u32[]{:S(2)}) collective-permute-start(bf16[2,256,768]{2,1,0:T(8,128)(2,1)S(1)} %get-tuple-element.254), channel_id=1, source_target_pairs={{0,1},{1,0},{2,3},{3,2},{4,5},{5,4},{6,7},{7,6},{8,9},{9,8},{10,11... | collective-permute-start | bytes 2359304 | tf_op jit(solution)/shard_map/ppermute | solution.py:19
  104.7 4.6 %collective-permute-start.29 = (bf16[256,768]{1,0:T(8,128)(2,1)S(1)}, bf16[256,768]{1,0:T(8,128)(2,1)S(1)}, u32[]{:S(2)}, u32[]{:S(2)}) collective-permute-start(bf16[256,768]{1,0:T(8,128)(2,1)S(1)} %shard_map.312.total), channel_id=1, source_target_pairs={{0,1},{1,0},{2,3},{3,2},{4,5},{5,4},{6,7},{7,6},{8,9},{9,8},{10,11... | collective-permute-start | bytes 1179656 | tf_op jit(solution)/shard_map/ppermute | solution.py:19
  105.3 11.1 %collective-permute-start.33 = (bf16[4,96,512]{2,1,0:T(8,128)(2,1)S(1)}, bf16[4,96,512]{2,1,0:T(8,128)(2,1)S(1)}, u32[]{:S(2)}, u32[]{:S(2)}) collective-permute-start(bf16[4,96,512]{2,1,0:T(8,128)(2,1)S(1)} %get-tuple-element.259), channel_id=1, source_target_pairs={{0,4},{4,0},{8,12},{12,8},{16,20},{20,16},{24,28},{28,24},{1,5},{5... | collective-permute-start | bytes 1179656 | tf_op jit(solution)/shard_map/ppermute | solution.py:19
  106.8 10.8 %collective-permute-start.30 = (bf16[256,768]{1,0:T(8,128)(2,1)S(1)}, bf16[256,768]{1,0:T(8,128)(2,1)S(1)}, u32[]{:S(2)}, u32[]{:S(2)}) collective-permute-start(bf16[256,768]{1,0:T(8,128)(2,1)S(1)} %shard_map.308.a), channel_id=1, source_target_pairs={{0,2},{1,3},{2,0},{3,1},{4,6},{5,7},{6,4},{7,5},{8,10},{9,11},{10,... | collective-permute-start | bytes 1179656 | tf_op jit(solution)/shard_map/ppermute | solution.py:19
  108.9 6.4 %collective-permute-start.32 = (bf16[2,96,256]{2,1,0:T(8,128)(2,1)S(1)}, bf16[2,96,256]{2,1,0:T(8,128)(2,1)S(1)}, u32[]{:S(2)}, u32[]{:S(2)}) collective-permute-start(bf16[2,96,256]{2,1,0:T(8,128)(2,1)S(1)} %get-tuple-element.257), channel_id=1, source_target_pairs={{0,8},{4,12},{8,0},{12,4},{16,24},{20,28},{24,16},{28,20},{1,9},{5... | collective-permute-start | bytes 294920 | tf_op jit(solution)/shard_map/ppermute | solution.py:19
  117.6 14.7 %collective-permute-start.38 = (bf16[4,96,768]{2,1,0:T(8,128)(2,1)S(1)}, bf16[4,96,768]{2,1,0:T(8,128)(2,1)S(1)}, u32[]{:S(2)}, u32[]{:S(2)}) collective-permute-start(bf16[4,96,768]{2,1,0:T(8,128)(2,1)S(1)} %get-tuple-element.279), channel_id=1, source_target_pairs={{0,4},{4,0},{8,12},{12,8},{16,20},{20,16},{24,28},{28,24},{1,5},{5... | collective-permute-start | bytes 1769480 | tf_op jit(solution)/shard_map/ppermute | solution.py:19
  118.2 5.2 %collective-permute-start.34 = (bf16[256,768]{1,0:T(8,128)(2,1)S(1)}, bf16[256,768]{1,0:T(8,128)(2,1)S(1)}, u32[]{:S(2)}, u32[]{:S(2)}) collective-permute-start(bf16[256,768]{1,0:T(8,128)(2,1)S(1)} %shard_map.316.total), channel_id=1, source_target_pairs={{0,1},{1,0},{2,3},{3,2},{4,5},{5,4},{6,7},{7,6},{8,9},{9,8},{10,11... | collective-permute-start | bytes 1179656 | tf_op jit(solution)/shard_map/ppermute | solution.py:19
  119.0 13.3 %collective-permute-start.35 = (bf16[1,256,768]{2,1,0:T(8,128)(2,1)S(1)}, bf16[1,256,768]{2,1,0:T(8,128)(2,1)S(1)}, u32[]{:S(2)}, u32[]{:S(2)}) collective-permute-start(bf16[1,256,768]{2,1,0:T(8,128)(2,1)S(1)} %get-tuple-element.271), channel_id=1, source_target_pairs={{0,2},{1,3},{2,0},{3,1},{4,6},{5,7},{6,4},{7,5},{8,10},{9,11},{10,... | collective-permute-start | bytes 1179656 | tf_op jit(solution)/shard_map/ppermute | solution.py:19
  121.2 11.1 %collective-permute-start.37 = (bf16[2,96,512]{2,1,0:T(8,128)(2,1)S(1)}, bf16[2,96,512]{2,1,0:T(8,128)(2,1)S(1)}, u32[]{:S(2)}, u32[]{:S(2)}) collective-permute-start(bf16[2,96,512]{2,1,0:T(8,128)(2,1)S(1)} %get-tuple-element.277), channel_id=1, source_target_pairs={{0,8},{4,12},{8,0},{12,4},{16,24},{20,28},{24,16},{28,20},{1,9},{5... | collective-permute-start | bytes 589832 | tf_op jit(solution)/shard_map/ppermute | solution.py:19
  122.2 10.0 %collective-permute-start.36 = (bf16[1,96,256]{2,1,0:T(8,128)(2,1)S(1)}, bf16[1,96,256]{2,1,0:T(8,128)(2,1)S(1)}, u32[]{:S(2)}, u32[]{:S(2)}) collective-permute-start(bf16[1,96,256]{2,1,0:T(8,128)(2,1)S(1)} %get-tuple-element.274), channel_id=1, source_target_pairs={{0,24},{4,28},{8,16},{12,20},{16,8},{20,12},{24,0},{28,4},{1,25},{... | collective-permute-start | bytes 147464 | tf_op jit(solution)/shard_map/ppermute | solution.py:19
  134.5 4.7 %collective-permute-start.39 = (bf16[2,256,768]{2,1,0:T(8,128)(2,1)S(1)}, bf16[2,256,768]{2,1,0:T(8,128)(2,1)S(1)}, u32[]{:S(2)}, u32[]{:S(2)}) collective-permute-start(bf16[2,256,768]{2,1,0:T(8,128)(2,1)S(1)} %get-tuple-element.286), channel_id=1, source_target_pairs={{0,1},{1,0},{2,3},{3,2},{4,5},{5,4},{6,7},{7,6},{8,9},{9,8},{10,11... | collective-permute-start | bytes 2359304 | tf_op jit(solution)/shard_map/ppermute | solution.py:19
  134.6 4.6 %collective-permute-start.40 = (f32[8,768]{1,0:T(8,128)S(1)}, f32[8,768]{1,0:T(8,128)S(1)}, u32[]{:S(2)}, u32[]{:S(2)}) collective-permute-start(f32[8,768]{1,0:T(8,128)S(1)} %get-tuple-element.285.a), channel_id=1, source_target_pairs={{0,1},{1,0},{2,3},{3,2},{4,5},{5,4},{6,7},{7,6},{8,9},{9,8},{10,11... | collective-permute-start | bytes 73736 | tf_op jit(solution)/shard_map/ppermute | solution.py:19
  135.7 12.6 %collective-permute-start.43 = (bf16[2,96,768]{2,1,0:T(8,128)(2,1)S(1)}, bf16[2,96,768]{2,1,0:T(8,128)(2,1)S(1)}, u32[]{:S(2)}, u32[]{:S(2)}) collective-permute-start(bf16[2,96,768]{2,1,0:T(8,128)(2,1)S(1)} %get-tuple-element.298), channel_id=1, source_target_pairs={{0,8},{4,12},{8,0},{12,4},{16,24},{20,28},{24,16},{28,20},{1,9},{5... | collective-permute-start | bytes 884744 | tf_op jit(solution)/shard_map/ppermute | solution.py:19
  139.2 17.9 %collective-permute-start.45 = (bf16[4,96,384]{2,1,0:T(8,128)(2,1)S(1)}, bf16[4,96,384]{2,1,0:T(8,128)(2,1)S(1)}, u32[]{:S(2)}, u32[]{:S(2)}) collective-permute-start(bf16[4,96,384]{2,1,0:T(8,128)(2,1)S(1)} %get-tuple-element.314), channel_id=1, source_target_pairs={{0,4},{4,0},{8,12},{12,8},{16,20},{20,16},{24,28},{28,24},{1,5},{5... | collective-permute-start | bytes 884744 | tf_op jit(solution)/shard_map/ppermute | solution.py:19
  141.4 7.0 %collective-permute-start.42 = (bf16[1,96,512]{2,1,0:T(8,128)(2,1)S(1)}, bf16[1,96,512]{2,1,0:T(8,128)(2,1)S(1)}, u32[]{:S(2)}, u32[]{:S(2)}) collective-permute-start(bf16[1,96,512]{2,1,0:T(8,128)(2,1)S(1)} %get-tuple-element.295), channel_id=1, source_target_pairs={{0,24},{4,28},{8,16},{12,20},{16,8},{20,12},{24,0},{28,4},{1,25},{... | collective-permute-start | bytes 294920 | tf_op jit(solution)/shard_map/ppermute | solution.py:19
  144.8 20.9 %collective-permute-start.44 = (bf16[1,256,768]{2,1,0:T(8,128)(2,1)S(1)}, bf16[1,256,768]{2,1,0:T(8,128)(2,1)S(1)}, u32[]{:S(2)}, u32[]{:S(2)}) collective-permute-start(bf16[1,256,768]{2,1,0:T(8,128)(2,1)S(1)} %get-tuple-element.305), channel_id=1, source_target_pairs={{0,2},{1,3},{2,0},{3,1},{4,6},{5,7},{6,4},{7,5},{8,10},{9,11},{10,... | collective-permute-start | bytes 1179656 | tf_op jit(solution)/shard_map/ppermute | solution.py:19
  145.3 10.3 %collective-permute-start.41 = (f32[8,768]{1,0:T(8,128)S(1)}, f32[8,768]{1,0:T(8,128)S(1)}, u32[]{:S(2)}, u32[]{:S(2)}) collective-permute-start(f32[8,768]{1,0:T(8,128)S(1)} %shard_map.324.a), channel_id=1, source_target_pairs={{0,2},{1,3},{2,0},{3,1},{4,6},{5,7},{6,4},{7,5},{8,10},{9,11},{10,... | collective-permute-start | bytes 73736 | tf_op jit(solution)/shard_map/ppermute | solution.py:19
  157.1 9.8 %collective-permute-start.46 = (bf16[4,104,384]{2,1,0:T(8,128)(2,1)S(1)}, bf16[4,104,384]{2,1,0:T(8,128)(2,1)S(1)}, u32[]{:S(2)}, u32[]{:S(2)}) collective-permute-start(bf16[4,104,384]{2,1,0:T(8,128)(2,1)S(1)} %get-tuple-element.319), channel_id=1, source_target_pairs={{0,4},{4,0},{8,12},{12,8},{16,20},{20,16},{24,28},{28,24},{1,5},{5... | collective-permute-start | bytes 958472 | tf_op jit(solution)/shard_map/ppermute | solution.py:19
  158.3 7.3 %collective-permute-start.48 = (bf16[1,96,768]{2,1,0:T(8,128)(2,1)S(1)}, bf16[1,96,768]{2,1,0:T(8,128)(2,1)S(1)}, u32[]{:S(2)}, u32[]{:S(2)}) collective-permute-start(bf16[1,96,768]{2,1,0:T(8,128)(2,1)S(1)} %get-tuple-element.325), channel_id=1, source_target_pairs={{0,24},{4,28},{8,16},{12,20},{16,8},{20,12},{24,0},{28,4},{1,25},{... | collective-permute-start | bytes 442376 | tf_op jit(solution)/shard_map/ppermute | solution.py:19
  160.1 6.8 %collective-permute-start.47 = (bf16[2,96,384]{2,1,0:T(8,128)(2,1)S(1)}, bf16[2,96,384]{2,1,0:T(8,128)(2,1)S(1)}, u32[]{:S(2)}, u32[]{:S(2)}) collective-permute-start(bf16[2,96,384]{2,1,0:T(8,128)(2,1)S(1)} %get-tuple-element.322), channel_id=1, source_target_pairs={{0,8},{4,12},{8,0},{12,4},{16,24},{20,28},{24,16},{28,20},{1,9},{5... | collective-permute-start | bytes 442376 | tf_op jit(solution)/shard_map/ppermute | solution.py:19
  167.5 7.0 %collective-permute-start.50 = (bf16[2,104,384]{2,1,0:T(8,128)(2,1)S(1)}, bf16[2,104,384]{2,1,0:T(8,128)(2,1)S(1)}, u32[]{:S(2)}, u32[]{:S(2)}) collective-permute-start(bf16[2,104,384]{2,1,0:T(8,128)(2,1)S(1)} %get-tuple-element.334), channel_id=1, source_target_pairs={{0,8},{4,12},{8,0},{12,4},{16,24},{20,28},{24,16},{28,20},{1,9},{5... | collective-permute-start | bytes 479240 | tf_op jit(solution)/shard_map/ppermute | solution.py:19
  168.2 6.3 %collective-permute-start.49 = (bf16[1,96,384]{2,1,0:T(8,128)(2,1)S(1)}, bf16[1,96,384]{2,1,0:T(8,128)(2,1)S(1)}, u32[]{:S(2)}, u32[]{:S(2)}) collective-permute-start(bf16[1,96,384]{2,1,0:T(8,128)(2,1)S(1)} %get-tuple-element.331), channel_id=1, source_target_pairs={{0,24},{4,28},{8,16},{12,20},{16,8},{20,12},{24,0},{28,4},{1,25},{... | collective-permute-start | bytes 221192 | tf_op jit(solution)/shard_map/ppermute | solution.py:19
  175.1 6.3 %collective-permute-start.51 = (bf16[1,104,384]{2,1,0:T(8,128)(2,1)S(1)}, bf16[1,104,384]{2,1,0:T(8,128)(2,1)S(1)}, u32[]{:S(2)}, u32[]{:S(2)}) collective-permute-start(bf16[1,104,384]{2,1,0:T(8,128)(2,1)S(1)} %get-tuple-element.344), channel_id=1, source_target_pairs={{0,24},{4,28},{8,16},{12,20},{16,8},{20,12},{24,0},{28,4},{1,25},{... | collective-permute-start | bytes 239624 | tf_op jit(solution)/shard_map/ppermute | solution.py:19

commit v2 on v1

--- a/solution.py
+++ b/solution.py
@@ -19,42 +19,31 @@
     return lax.ppermute(array, axis, [(i, i ^ mask) for i in range(lax.axis_size(axis))])
 
 
-def dp_steps():
-    size = lax.axis_size("dp")
-    if size == 8:
-        return ((6, 4), (2, 6), (1, 1))
-    return tuple((1 << b, 1 << b) for b in reversed(range(size.bit_length() - 1)))
-
-
-def parity(index, mask):
-    bit = jnp.int32(0)
-    for b in range(mask.bit_length()):
-        if mask >> b & 1:
-            bit = bit ^ ((index >> b) & 1)
-    return bit
-
-
-def slot_owners(steps):
+def dp_masks():
+    return [1 << b for b in reversed(range(lax.axis_size("dp").bit_length() - 1))]
+
+
+def slot_owners(masks):
     owners = [0]
-    for mask, _ in steps:
+    for mask in masks:
         owners = owners + [o ^ mask for o in owners]
     return owners
 
 
 def dp_gather(shard):
-    steps, me = dp_steps(), lax.axis_index("dp")
+    masks, me = dp_masks(), lax.axis_index("dp")
     slots = shard[None]
-    for mask, kinds in steps:
+    for mask in masks:
         other = swapped(slots, "dp", mask)
-        first = parity(me, kinds) == 0
+        first = (me & mask) == 0
         slots = jnp.where(
             first, jnp.concatenate([slots, other]), jnp.concatenate([other, slots])
         )
-    owners = slot_owners(steps)
+    owners = slot_owners(masks)
     return jnp.stack([slots[owners.index(s)] for s in range(len(owners))])
 
 
-MASKS = ((0,), (1,), (6,), (2, 4), (7,), (3, 5))
+MASKS = ((0,), (1,), (4,), (2, 6), (5,), (3, 7))
 
 
 def rows_pick(own, other):
@@ -63,11 +52,11 @@
 
 
 def dp_scatter_sum(blocks):
-    steps, me = dp_steps(), lax.axis_index("dp")
-    slots = jnp.stack([blocks[s] for s in slot_owners(steps)])
-    for mask, kinds in reversed(steps):
+    masks, me = dp_masks(), lax.axis_index("dp")
+    slots = jnp.stack([blocks[s] for s in slot_owners(masks)])
+    for mask in reversed(masks):
         half = slots.shape[0] // 2
-        first = parity(me, kinds) == 0
+        first = (me & mask) == 0
         keep = jnp.where(first, slots[:half], slots[half:])
         send = jnp.where(first, slots[half:], slots[:half])
         slots = keep.astype(F32) + swapped(send, "dp", mask).astype(F32)
@@ -139,14 +128,9 @@
     )(*args)
 
 
-def input_kernel(
-    place, x_zero, x_one, thoughts, thought_pos, vecs, w_in, bias,
-    spliced_ref, xhat_ref, normed_ref, q_ref, k_ref, v_ref,
-):
+def splice_kernel(place, x_zero, x_one, thoughts, thought_pos, spliced_ref, xhat_ref):
     core = place[0]
     rows = x_zero.shape[1]
-    cols = q_ref.shape[1]
-    gain, shift = vecs[0:1, :], vecs[1:2, :]
     for upper in range(2):
         for rel, ref in enumerate((x_zero, x_one)):
             first = upper * 2 * rows + (core ^ rel) * rows
@@ -155,15 +139,21 @@
             covered = jnp.sum(match.astype(F32), axis=1, keepdims=True) > 0.0
             picked = dot(match.astype(LOW), thoughts[...], 1, 0)
             spliced = jnp.where(covered, picked, ref[upper].astype(F32))
-            xhat, _ = normalised(spliced)
             spliced_ref[part, :] = spliced.astype(LOW)
-            xhat_ref[part, :] = xhat.astype(LOW)
-            normed = (xhat * gain + shift).astype(LOW)
-            normed_ref[part, :] = normed
-            mixed = (dot(normed, w_in[...], 1, 0) + bias[...]).astype(LOW)
-            q_ref[part, :] = mixed[:, :cols]
-            k_ref[part, :] = mixed[:, cols : 2 * cols]
-            v_ref[part, :] = mixed[:, 2 * cols :]
+            xhat_ref[part, :] = normalised(spliced)[0]
+
+
+def input_kernel(xhat, vecs, w_in, bias, normed_ref, q_ref, k_ref, v_ref):
+    rows = xhat.shape[0] // 4
+    cols = q_ref.shape[1]
+    for k in range(4):
+        part = slice(k * rows, (k + 1) * rows)
+        normed = (xhat[part, :] * vecs[0:1, :] + vecs[1:2, :]).astype(LOW)
+        normed_ref[part, :] = normed
+        mixed = (dot(normed, w_in[...], 1, 0) + bias[...]).astype(LOW)
+        q_ref[part, :] = mixed[:, :cols]
+        k_ref[part, :] = mixed[:, cols : 2 * cols]
+        v_ref[part, :] = mixed[:, 2 * cols :]
 
 
 def query_limits(place, starts, chunk, rows):
@@ -414,7 +404,7 @@
 
 def input_back_kernel(
     place, thought_pos, dq_zero, dq_one, dk, dv, w_in, xhat, res_zero, res_one,
-    keep_ref, send_ref, mixed_ref, small_ref, colsum_ref, picked_ref, grad_ref,
+    keep_ref, send_ref, small_ref, colsum_ref, picked_ref, grad_ref,
 ):
     half, cols = dq_zero.shape
     rows = half // 2
@@ -425,14 +415,13 @@
             mixed = jnp.concatenate(
                 [dq[rel * rows : (rel + 1) * rows, :], dk[part, :], dv[part, :]], axis=1
             )
-            mixed_ref[part, :] = mixed
             grad = dot(mixed, w_in[...], 1, 1)
             grad_ref[part, :] = grad
             if rel:
                 send_ref[upper] = grad.astype(LOW)
             else:
                 keep_ref[upper] = grad
-            terms = (grad * xhat[part, :].astype(F32), grad, mixed.astype(F32))
+            terms = (grad * xhat[part, :], grad, mixed.astype(F32))
             sums = [a + jnp.sum(b, axis=0, keepdims=True) for a, b in zip(sums, terms)]
     small_ref[...] = jnp.zeros_like(small_ref)
     picked_ref[...] = jnp.zeros_like(picked_ref)
@@ -449,7 +438,8 @@
     colsum_ref[...] = sums[2]
 
 
-def output_kernel(place, keep, got, spliced, res_zero, res_one, vecs, thought_pos, thoughts, small, picked, embed_ref, rows_ref):
+def output_kernel(place, keep, got, spliced, res_zero, res_one, vecs, thought_pos, thoughts, small, picked, *rest):
+    pairs, (embed_ref, rows_ref, *more) = rest[: 2 * ((len(rest) - 2) // 3)], rest[2 * ((len(rest) - 2) // 3) :]
     rows = keep.shape[0]
     gain = vecs[0:1, :]
     own = pl.ds(pl.multiple_of(place[3] * (2 * rows), 2 * rows), rows)
@@ -462,25 +452,39 @@
     count = thoughts.shape[0]
     xhat, inverse = normalised(thoughts[...].astype(F32))
     grad = norm_back(small[:count, :], xhat, inverse, gain) + picked[:count, :]
-    cols = rows_ref.shape[1]
+    cols = rows_ref.shape[2]
     rank = 2 * place[3] + place[0]
-    rows_ref[...] = sum(
-        jnp.where(rank == k, 1.0, 0.0) * grad[:, k * cols : (k + 1) * cols] for k in range(4)
-    )
-
-
-def fold_kernel(bit, place, keep, got, keep_ref, send_ref):
+    grad = sum(jnp.where(rank == k, 1.0, 0.0) * grad[:, k * cols : (k + 1) * cols] for k in range(4))
+    for k in range(count):
+        rows_ref[k] = grad[k : k + 1, :]
+    for ref, keep, got in zip(more, pairs[::2], pairs[1::2]):
+        ref[...] = keep[0] + got[0].astype(F32)
+
+
+def fold_kernel(bit, place, *refs):
+    *parts, keep_ref, send_ref = refs
     half = keep_ref.shape[0]
     mine = place[bit] * half
     rest = half - mine
-    for k in range(half):
-        keep_ref[k] = keep[mine + k] + got[mine + k].astype(F32)
-        send_ref[k] = (keep[rest + k] + got[rest + k].astype(F32)).astype(LOW)
-
-
-def fold(bit, place, keep, got):
-    shape = (keep.shape[0] // 2, *keep.shape[1:])
-    return call(functools.partial(fold_kernel, bit), ((shape, F32), (shape, LOW)), place, keep, got)
+    first = 0
+    for keep, got in zip(parts[::2], parts[1::2]):
+        rows, cols = keep.shape[1:]
+        below = rows < 16 and first > 0
+        if below:
+            at = (slice(keep_ref.shape[1] - rows, None), slice(0, cols))
+        else:
+            at = (slice(0, rows), slice(first, first + cols))
+            first += cols
+        for k in range(half):
+            keep_ref[(k, *at)] = keep[mine + k] + got[mine + k].astype(F32)
+            send_ref[(k, *at)] = (keep[rest + k] + got[rest + k].astype(F32)).astype(LOW)
+
+
+def fold(bit, place, *parts):
+    under = [p.shape[1] for p in parts[2::2] if p.shape[1] < 16]
+    cols = sum(p.shape[2] for k, p in enumerate(parts[::2]) if k == 0 or p.shape[1] >= 16)
+    shape = (parts[0].shape[0] // 2, parts[0].shape[1] + sum(under), cols)
+    return call(functools.partial(fold_kernel, bit), ((shape, F32), (shape, LOW)), place, *parts)
 
 
 def add_kernel(a, b, out):
@@ -499,11 +503,12 @@
     return call(add_kernel, ((a.shape, LOW),), a, b)[0]
 
 
-def to_slots(place, sum_ref, first, keep_ref, send_ref):
+def to_slots(place, sum_ref, first, keep_ref, send_ref, bit=0):
     rows, cols = sum_ref.shape[0] // 8, keep_ref.shape[2]
-    for slot, owner in enumerate((0, 6, 2, 4)):
-        mine = pl.ds(pl.multiple_of((owner ^ place[7]) * rows, rows), rows)
-        rest = pl.ds(pl.multiple_of((owner ^ 1 ^ place[7]) * rows, rows), rows)
+    here = place[(7, 5, 6)[bit]] << bit
+    for slot, owner in enumerate(((0, 4, 2, 6), (0, 1, 4, 5))[bit]):
+        mine = pl.ds(pl.multiple_of((owner ^ here) * rows, rows), rows)
+        rest = pl.ds(pl.multiple_of((owner ^ here ^ (1 << bit)) * rows, rows), rows)
         keep_ref[slot, :rows, :] = sum_ref[mine, first : first + cols]
         send_ref[slot, :rows, :] = sum_ref[rest, first : first + cols].astype(LOW)
 
@@ -535,18 +540,18 @@
     all_slots(place, sum_ref, blocks)
 
 
-def last_kernel(place, normed, mixed, branch_zero, branch_one, att_zero, att_one, keep_ref, send_ref, rest_ref, sum_ref):
-    cols = att_zero.shape[1]
+def last_kernel(place, normed, dq_zero, dq_one, dk, dv, branch_zero, branch_one, att_zero, att_one, *refs):
+    *blocks, sum_ref = refs
+    half, cols = att_zero.shape
     sum_ref[:, :cols] = product((branch_zero, branch_one), (att_zero, att_one))
-    sum_ref[:, cols:] = dot(normed[...], mixed[...], 0, 0)
-    to_slots(place, sum_ref, 0, keep_ref, send_ref)
-    rest_ref[...] = sum_ref[:, keep_ref.shape[2] :]
-
-
-def slot_kernel(place, rest, small, back_zero, back_one, up_zero, up_one, mixed_sums, keep_ref, send_ref, flat_ref):
-    to_slots(place, rest, 0, keep_ref, send_ref)
+    sum_ref[:, cols : 2 * cols] = dot(normed[:half, :], dq_zero[...], 0, 0) + dot(normed[half:, :], dq_one[...], 0, 0)
+    sum_ref[:, 2 * cols : 3 * cols] = dot(normed[...], dk[...], 0, 0)
+    sum_ref[:, 3 * cols :] = dot(normed[...], dv[...], 0, 0)
+    all_slots(place, sum_ref, blocks)
+
+
+def slot_kernel(place, small, back_zero, back_one, up_zero, up_one, mixed_sums, keep_ref, send_ref, flat_ref):
     cols, wide_cols = mixed_sums.shape[1] // 3, keep_ref.shape[2]
-    rows = keep_ref.shape[1] - 8
     count = small.shape[0] - 2
     back = back_zero[...] + back_one[...]
     wide = [small[count : count + 1, :], small[count + 1 :, :], back[2:3], back[0:1], back[1:2], back[3:4]]
@@ -559,39 +564,50 @@
         parts.append(jnp.zeros((1, 2 * wide_cols - sum(p.shape[1] for p in parts)), F32))
         flat_ref[owner : owner + 1, :] = jnp.concatenate(parts, axis=1)
     first = iota((8, wide_cols), 0) == 0
-    for slot, owner in enumerate((0, 6, 2, 4)):
+    for slot, owner in enumerate((0, 4, 2, 6)):
         mine, other = (flat_ref[pl.ds(owner ^ k ^ place[7], 1), :] for k in range(2))
-        keep_ref[slot, rows:, :] = jnp.where(first, mine[:, :wide_cols], mine[:, wide_cols:])
-        send_ref[slot, rows:, :] = jnp.where(first, other[:, :wide_cols], other[:, wide_cols:]).astype(LOW)
-
-
-def finish_kernel(one_keep, one_got, two_keep, two_got, in_ref, proj_ref, flat_ref):
+        keep_ref[slot] = jnp.where(first, mine[:, :wide_cols], mine[:, wide_cols:])
+        send_ref[slot] = jnp.where(first, other[:, :wide_cols], other[:, wide_cols:]).astype(LOW)
+
+
+def finish_kernel(
+    d_keep, d_got, e_keep, e_got, in_ref, proj_ref, gain_one, bias_one, proj_b, gain_two, bias_two, down_b, up_b, qv_b
+):
     rows, cols = in_ref.shape[1:]
-    one = one_keep[0] + one_got[0].astype(F32)
-    two = two_keep[0] + two_got[0].astype(F32)
+    one = d_keep[0] + d_got[0].astype(F32)
+    two = e_keep[0] + e_got[0].astype(F32)
     proj_ref[...] = one[:, :cols].T
     in_ref[0] = one[:, cols:]
     in_ref[1] = two[:rows, :cols]
     in_ref[2] = two[:rows, cols:]
-    flat_ref[...] = jnp.concatenate([two[rows : rows + 1, :], two[rows + 1 : rows + 2, :]], axis=1)
-
-
-def pair_kernel(*refs):
-    *parts, out_ref = refs
-    out_ref[...] = jnp.concatenate(
-        [keep[0] + got[0].astype(F32) for keep, got in zip(parts[::2], parts[1::2])], axis=1
-    )
-
-
-def joined(*parts):
-    shape = (parts[0].shape[1], sum(p.shape[2] for p in parts[::2]))
-    return call(pair_kernel, ((shape, F32),), *parts)[0]
+    flat = jnp.concatenate([two[rows : rows + 1, :], two[rows + 1 : rows + 2, :]], axis=1)
+    first = 0
+    for ref in (gain_one, bias_one, proj_b, gain_two, bias_two, down_b, up_b):
+        ref[...] = flat[:, first : first + ref.shape[1]]
+        first += ref.shape[1]
+    count = qv_b.shape[1]
+    qv_b[...] = jnp.concatenate([flat[:, first : first + count], flat[:, first + count : first + 2 * count]])
+
+
+def parts_kernel(keep, got, one_ref, two_ref):
+    cols = one_ref.shape[1]
+    one_ref[...] = keep[0, :, :cols] + got[0, :, :cols].astype(F32)
+    two_ref[...] = keep[0, :, cols:] + got[0, :, cols:].astype(F32)
+
+
+def parted(keep, got):
+    shape = (keep.shape[1], keep.shape[2] // 2)
+    return call(parts_kernel, ((shape, F32),) * 2, keep, got)
+
+
+def result_of(place, keep, got, res_zero, res_one, vecs):
+    rows = keep.shape[0]
+    residual = jnp.where(place[3] == 0, res_zero[:rows, :], res_one[:rows, :])
+    return (residual + (keep[...] + got[...].astype(F32)) + vecs[5:6, :]).astype(LOW)
 
 
 def result_kernel(place, keep, got, res_zero, res_one, vecs, out_ref):
-    rows = out_ref.shape[0]
-    residual = jnp.where(place[3] == 0, res_zero[:rows, :], res_one[:rows, :])
-    out_ref[...] = (residual + (keep[...] + got[...].astype(F32)) + vecs[5:6, :]).astype(LOW)
+    out_ref[...] = result_of(place, keep, got, res_zero, res_one, vecs)
 
 
 def pick_kernel(place, own, other, out_ref):
@@ -601,6 +617,16 @@
 
 def pick(place, own, other):
     return call(pick_kernel, (((2, *own.shape), own.dtype),), place, own, other)[0]
+
+
+def copy_kernel(*refs):
+    half = len(refs) // 2
+    for a, b in zip(refs[:half], refs[half:]):
+        b[...] = a[...]
+
+
+def brought(*arrays):
+    return call(copy_kernel, tuple((a.shape, a.dtype) for a in arrays), *arrays)
 
 
 def stack_kernel(a, b, out_ref):
@@ -759,34 +785,30 @@
     table = []
     for d in range(dp):
         for t in range(4):
-            table.append((t & 1, 0, 0, t >> 1, d, (d >> 1 ^ d >> 2) & 1, d >> 2 & 1, d & 1))
+            table.append((t & 1, 0, 0, t >> 1, d, d >> 1 & 1, d >> 2 & 1, d & 1))
     place = jnp.asarray(table, jnp.int32)[lax.axis_index("dp") * 4 + lax.axis_index("tensor")]
     block = quick_block if fast(params[2].shape[1]) else plain_block
-    outs = block(place, img_start[0], x_embed[0], thoughts[0], thought_pos, params, grad_out[0])
-    vec, outs = outs[-1], outs[:-1]
-    sizes = [params[k].size for k in (0, 1, 5, 6, 7, 11, 9, 3)]
-    small, first = [], 0
-    for n in sizes:
-        small.append(vec[first : first + n])
-        first += n
+    block_out, grad_embed, grad_thoughts, grad_in, grad_proj, grad_up, grad_down, small = block(
+        place, img_start[0], x_embed[0], thoughts[0], thought_pos, params, grad_out[0]
+    )
     gain_one, bias_one, proj_b, gain_two, bias_two, down_b, up_b, qv_b = small
-    block_out, grad_embed, grad_thoughts, grad_in, grad_proj, grad_up, grad_down = outs
+    flat = lambda a: a.reshape(-1)
     return (
         block_out[None],
         grad_embed[None],
-        grad_thoughts[None],
-        gain_one,
-        bias_one,
+        grad_thoughts,
+        flat(gain_one),
+        flat(bias_one),
         grad_in,
         qv_b.reshape(2, -1),
         grad_proj,
-        proj_b,
-        gain_two,
-        bias_two,
+        flat(proj_b),
+        flat(gain_two),
+        flat(bias_two),
         grad_up,
-        up_b,
+        flat(up_b),
         grad_down,
-        down_b,
+        flat(down_b),
     )
 
 
@@ -794,19 +816,15 @@
     return [params[k].reshape(1, -1) for k in (0, 1, 5, 6, 7, 11, 9)] + [params[3]]
 
 
-def input_side(place, x_rows, thoughts, thought_pos, vecs, w_in, bias):
-    length, width = 4 * x_rows[0].shape[1], x_rows[0].shape[2]
-    return call(
-        input_kernel,
-        (((length, width), LOW),) * 3 + (((length, w_in.shape[1] // 3), LOW),) * 3,
-        place,
-        *x_rows,
-        thoughts,
-        thought_pos,
-        vecs,
-        w_in,
-        bias,
-    )
+def splice_side(place, x_rows, thoughts, thought_pos):
+    shape = (4 * x_rows[0].shape[1], x_rows[0].shape[2])
+    return call(splice_kernel, ((shape, LOW), (shape, F32)), place, *x_rows, thoughts, thought_pos)
+
+
+def input_side(xhat, vecs, w_in, bias):
+    length, width = xhat.shape
+    kinds = (((length, width), LOW),) + (((length, w_in.shape[1] // 3), LOW),) * 3
+    return call(input_kernel, kinds, xhat, vecs, w_in, bias)
 
 
 def input_back(place, thought_pos, grad_queries, grad_keys, grad_values, w_in, xhat, grad_residual):
@@ -817,7 +835,6 @@
         (
             ((2, length // 4, width), F32),
             ((2, length // 4, width), LOW),
-            ((length, w_in.shape[1]), LOW),
             ((-(-(count + 2) // 8) * 8, width), F32),
             ((1, w_in.shape[1]), F32),
             ((-(-count // 8) * 8, width), F32),
@@ -834,11 +851,15 @@
     )
 
 
-def output_side(place, keep, got, spliced, grad_residual, vecs, thought_pos, thoughts, small, picked):
+def output_side(place, keep, got, spliced, grad_residual, vecs, thought_pos, thoughts, small, picked, *pairs):
     rows, width = keep.shape
-    return call(
+    embed, own, *more = call(
         output_kernel,
-        (((rows, width), F32), ((thoughts.shape[0], width // 4), F32)),
+        (
+            ((rows, width), F32),
+            ((thoughts.shape[0], 1, width // 4), F32),
+            *((p.shape[1:], F32) for p in pairs[::2]),
+        ),
         place,
         keep,
         got,
@@ -849,7 +870,9 @@
         thoughts,
         small,
         picked,
-    )
+        *pairs,
+    )
+    return embed, jnp.moveaxis(own, 1, 0), *more
 
 
 def result(place, keep, got, residual, vecs):
@@ -864,7 +887,7 @@
 def quick_block(place, starts, x_own, thoughts, thought_pos, params, cot_own):
     across = lambda a: swapped(a, "dp", 1)
     near = lambda a: swapped(a, "dp", 2)
-    far = lambda a: swapped(a, "dp", 6)
+    far = lambda a: swapped(a, "dp", 4)
     core = lambda a: swapped(a, "tensor", 1)
     over = lambda a: swapped(a, "tensor", 2)
     w_qkv, w_proj, w_up, w_down_own = params[2], params[4], params[8], params[10].T
@@ -872,54 +895,55 @@
     width = x_own.shape[1]
     vectors = vectors_of(params)
 
-    x_far = over(x_own)
     pack = first_pack(w_qkv, w_proj, *vectors)
-    pack_far, pack_across, up_across = far(pack), across(pack), across(w_up)
-    x_far, pack_far, pack_across, up_across = together(x_far, pack_far, pack_across, up_across)
-
-    x_both = pick(place, x_own, x_far)
-    x_other = core(x_both)
-    pack_near, pack_far_across = near(stacked(pack, pack_far)), across(pack_far)
-    up_far = far(after(w_up, pack_far))
-    down_across = across(after(w_down_own, up_across))
+    pack_far, pack_across = far(pack), across(pack)
+    x_far = over(after(x_own, pack))
+    pack_here, x_here = brought(pack, after(x_own, pack))
+    x_far, pack_far, pack_across, pack_here, x_here = together(x_far, pack_far, pack_across, pack_here, x_here)
+
+    pack_near, pack_far_across = near(stacked(pack_here, pack_far)), across(pack_far)
+    up_far, up_across = far(after(w_up, pack_far)), across(after(w_up, pack_far))
     cot_far = over(after(cot_own, x_far))
-    x_other, pack_near, pack_far_across, down_across, up_far, cot_far = together(
-        x_other, pack_near, pack_far_across, down_across, up_far, cot_far
+    pack_near, pack_far_across, up_far, up_across, cot_far = together(
+        pack_near, pack_far_across, up_far, up_across, cot_far
     )
 
     pack_near_across = across(pack_near)
     up_near = near(stacked(w_up, up_far))
     down_far = far(after(w_down_own, up_far))
-    cot_both = pick(place, cot_own, cot_far)
-    cot_other = core(cot_both)
-    pieces = (pack[None], pack_across[None], pack_far[None], pack_near, pack_far_across[None], pack_near_across)
+    x_both = pick(place, x_here, after(x_far, up_far))
+    x_other = core(x_both)
+    spliced, xhat = splice_side(place, (x_both, x_other), thoughts, thought_pos)
+    pack_near_across, xhat = together(pack_near_across, xhat)
+    up_far_across, down_across = across(after(up_far, pack_near_across)), across(after(w_down_own, pack_near_across))
+    pieces = (pack_here[None], pack_across[None], pack_far[None], pack_near, pack_far_across[None], pack_near_across)
     w_in, w_proj_t, vecs, up_bias, all_bias = first_unpacked(place, pieces, vectors, 3 * head_cols, head_cols, width)
-    spliced, xhat, normed, queries, keys, values = input_side(
-        place, (x_both, x_other), thoughts, thought_pos, vecs, w_in, all_bias
-    )
+    normed, queries, keys, values = input_side(xhat, vecs, w_in, all_bias)
     att_zero, log_zero, keep_zero, send_zero = attend(0, place, starts, queries, keys, values, w_proj_t)
-    send_zero, up_near, down_far, cot_other = together(send_zero, up_near, down_far, cot_other)
-    cots = (cot_both, cot_other)
+    send_zero, up_near, down_far, up_far_across, down_across = together(
+        send_zero, up_near, down_far, up_far_across, down_across
+    )
 
     mine_zero = add_low(keep_zero, core(send_zero))
     far_zero = over(mine_zero)
-    up_far_across, up_near_across = across(after(up_far, send_zero)), across(up_near)
+    up_near_across, down_far_across = across(up_near), across(down_far)
     down_near = near(stacked(w_down_own, down_far))
     att_one, log_one, keep_one, send_one = attend(1, after(place, mine_zero), starts, queries, keys, values, w_proj_t)
-    send_one, far_zero, up_far_across, up_near_across, down_near = together(
-        send_one, far_zero, up_far_across, up_near_across, down_near
+    send_one, far_zero, up_near_across, down_far_across, down_near = together(
+        send_one, far_zero, up_near_across, down_far_across, down_near
     )
 
     mine_one = add_low(keep_one, core(send_one))
     far_one = over(mine_one)
     total_zero = add_low(mine_zero, far_zero)
     other_zero = core(total_zero)
-    down_far_across, down_near_across = across(after(down_far, send_one)), across(down_near)
+    down_near_across = across(down_near)
     pieces = (w_up[None], up_across[None], up_far[None], up_near, up_far_across[None], up_near_across)
     w_up_all = unpacked(place, pieces)
-    other_zero, down_far_across, down_near_across, w_up_all = together(
-        other_zero, down_far_across, down_near_across, w_up_all
-    )
+    cot_both = pick(place, cot_own, cot_far)
+    cot_other = core(cot_both)
+    other_zero, down_near_across, w_up_all, cot_other = together(other_zero, down_near_across, w_up_all, cot_other)
+    cots = (cot_both, cot_other)
     pieces = (w_down_own[None], down_across[None], down_far[None], down_near, down_far_across[None], down_near_across)
     w_down_t = unpacked(place, pieces)
 
@@ -945,52 +969,44 @@
         cot_grad_kernel, after(place, a_send), (3 * quarter,), *cots, hidden_zero, hidden_one
     )
     mlp_keep, mlp_send = down_part((hidden_zero, after(hidden_one, a_send)), w_down_t)
-    far_zero, mine_one, c_send, mlp_send, a_got = together(far_zero, mine_one, c_send, mlp_send, a_got)
+    total_zero = add_low(after(mine_zero, a_got, c_send, mlp_send), far_zero)
+    other_zero = core(total_zero)
+    other_zero, mine_one = together(other_zero, mine_one)
     residual = (residual_zero, residual_one)
 
     far_one = over(mine_one)
-    b_got = across(after(b_send, a_got))
-    a_keep, a_send = fold(5, place, a_keep, a_got)
-    a_got = near(a_send)
-    mlp_got = core(mlp_send)
-    total_zero = add_low(mine_zero, far_zero)
+    b_got = across(after(b_send, other_zero))
+    mlp_got = core(after(mlp_send, other_zero))
     res_zero, branch_zero, gatt_zero, delta_zero, sums_zero = branch_back(
-        0, total_zero, core(total_zero), residual_zero, cots, vecs, w_proj_t, att_zero
+        0, total_zero, other_zero, residual_zero, cots, vecs, w_proj_t, att_zero
     )
     dq_zero, *early = back(0, place, starts, queries, keys, values, log_zero, gatt_zero, delta_zero, ())
-    early[0], far_one, mlp_got, a_got, b_got = together(early[0], far_one, mlp_got, a_got, b_got)
+    early[0], far_one, b_got, mlp_got = together(early[0], far_one, b_got, mlp_got)
 
     total_one = add_low(mine_one, far_one)
     other_one = core(total_one)
     c_got = across(after(c_send, b_got))
     mlp_keep, mlp_send = fold(3, place, mlp_keep, mlp_got)
     mlp_got = over(mlp_send)
-    a_keep, a_send = fold(6, place, a_keep, a_got)
-    a_got = far(a_send)
-    b_keep, b_send = fold(5, place, b_keep, b_got)
+    b_keep, b_send = fold(5, place, a_keep, a_got, b_keep, b_got)
     b_got = near(b_send)
     res_one, branch_one, gatt_one, delta_one, sums_one = branch_back(
         1, total_one, other_one, residual_one, cots, vecs, w_proj_t, att_one
     )
     dq_one, dk, dv = back(1, place, starts, queries, keys, values, log_one, gatt_one, delta_one, early)
-    dk, mlp_got, a_got, b_got, c_got = together(dk, mlp_got, a_got, b_got, c_got)
+    dk, b_got, c_got, mlp_got = together(dk, b_got, c_got, mlp_got)
 
     grad_residual = (res_zero, res_one)
-    c_keep, c_send = fold(5, place, c_keep, c_got)
-    c_got = near(c_send)
-    b_keep, b_send = fold(6, place, b_keep, b_got)
-    b_got = far(b_send)
-    keep, send, grad_mixed, small, mixed_sums, picked = input_back(
-        place, thought_pos, (dq_zero, dq_one), dk, dv, w_in, xhat, grad_residual
-    )
-    got, small_got = core(send), core(small)
-    shape = (4, shard_rows, 2 * head_cols)
-    d_keep, d_send, rest = call(
+    shapes = (((4, shard_rows, 2 * head_cols), F32), ((4, shard_rows, 2 * head_cols), LOW)) * 2
+    d_keep, d_send, e_keep, e_send = call(
         last_kernel,
-        ((shape, F32), (shape, LOW), ((width, 2 * head_cols), F32)),
+        shapes,
         place,
         normed,
-        grad_mixed,
+        dq_zero,
+        dq_one,
+        dk,
+        dv,
         branch_zero,
         branch_one,
         att_zero,
@@ -998,24 +1014,30 @@
         scratch=(pltpu.VMEM((width, 4 * head_cols), F32),),
         mib=12,
     )
-    got, small_got, d_send = together(got, small_got, d_send)
     d_got = across(d_send)
+    c_keep, c_send = fold(5, place, c_keep, after(c_got, d_send))
+    c_got = near(c_send)
+    keep, send, small, mixed_sums, picked = input_back(
+        place, thought_pos, (dq_zero, dq_one), after(dk, d_send), dv, w_in, xhat, grad_residual
+    )
+    small = add_full(small, core(small))
+    small_got = over(small)
+    small_got, d_got, c_got = together(small_got, d_got, c_got)
+
+    e_got = across(after(e_send, d_got))
+    got = core(after(send, d_got))
     keep, send = fold(3, place, keep, got)
     got = over(send)
     small = add_full(small, small_got)
-    small_got = over(small)
-    block_out = result(place, mlp_keep[0], mlp_got[0], residual, vecs)
-    small_got, b_got, c_got, block_out = together(small_got, b_got, c_got, block_out)
-    small = add_full(small, small_got)
-    c_keep, c_send = fold(6, place, c_keep, c_got)
-    c_got = far(c_send)
-    grad_up = joined(a_keep, a_got, b_keep, b_got)
-    shape = (4, shard_rows + 8, 2 * head_cols)
-    e_keep, e_send = call(
+    d_keep, d_send = fold(5, place, d_keep, d_got)
+    d_got = near(d_send)
+    b_keep, b_send = fold(6, place, b_keep, after(b_got, c_got), c_keep, c_got)
+    b_got = far(b_send)
+    shape = (4, 8, 2 * head_cols)
+    vec_keep, vec_send = call(
         slot_kernel,
         ((shape, F32), (shape, LOW)),
         place,
-        rest,
         small,
         sums_zero,
         sums_one,
@@ -1024,32 +1046,36 @@
         mixed_sums,
         scratch=(pltpu.VMEM((8, 4 * head_cols), F32),),
     )
-    e_send, d_got, grad_up = together(e_send, d_got, grad_up)
-    e_got = across(e_send)
-    d_keep, d_send = fold(5, place, d_keep, d_got)
-    d_got = near(d_send)
-    got, e_got, d_got, c_got = together(got, e_got, d_got, c_got)
-    e_keep, e_send = fold(5, place, e_keep, e_got)
+    vec_got = across(vec_send)
+    block_out = result(place, mlp_keep[0], mlp_got[0], residual, vecs)
+    e_got, d_got, vec_got, block_out = together(e_got, d_got, vec_got, block_out)
+
+    e_keep, e_send = fold(5, place, e_keep, e_got, vec_keep, vec_got)
     e_got = near(e_send)
     d_keep, d_send = fold(6, place, d_keep, d_got)
     d_got = far(d_send)
     grad_embed, grad_thoughts = output_side(
         place, keep[0], got[0], spliced, grad_residual, vecs, thought_pos, thoughts, small, picked
     )
-    grad_embed, d_got, e_got = together(grad_embed, d_got, e_got)
+    grad_embed, e_got, d_got, b_got = together(grad_embed, e_got, d_got, b_got)
+
     e_keep, e_send = fold(6, place, e_keep, e_got)
     e_got = far(e_send)
-    grad_down = joined(c_keep, c_got)
+    grad_up, grad_down = parted(b_keep, b_got)
     grad_down, e_got = together(grad_down, e_got)
-    grad_in, grad_proj, vec = call(
+    grad_in, grad_proj, *small = call(
         finish_kernel,
-        (((3, shard_rows, head_cols), F32), ((head_cols, shard_rows), F32), ((1, 4 * head_cols), F32)),
+        (
+            ((3, shard_rows, head_cols), F32),
+            ((head_cols, shard_rows), F32),
+            *((v.shape, F32) for v in vectors),
+        ),
         d_keep,
         d_got,
         e_keep,
         e_got,
     )
-    return block_out, grad_embed, grad_thoughts, grad_in, grad_proj, grad_up, grad_down.T, vec[0]
+    return block_out, grad_embed, grad_thoughts, grad_in, grad_proj, grad_up, grad_down.T, small
 
 
 def plain_block(place, starts, x_own, thoughts, thought_pos, params, cot_own):
@@ -1062,9 +1088,8 @@
     w_in, w_proj_t, vecs, up_bias, all_bias = plain_first(shard, vectors_of(params), 3 * head_cols, width)
     w_up_all = dp_gather(w_up).reshape(width, -1)
     w_down_t = dp_gather(w_down_own).reshape(width, -1)
-    spliced, xhat, normed, queries, keys, values = input_side(
-        place, x_rows, thoughts, thought_pos, vecs, w_in, all_bias
-    )
+    spliced, xhat = splice_side(place, x_rows, thoughts, thought_pos)
+    normed, queries, keys, values = input_side(xhat, vecs, w_in, all_bias)
 
     def all_sum(keep, send):
         mine = add_low(keep, swapped(send, "tensor", 1))
@@ -1096,9 +1121,10 @@
         )
         dqs.append(dq)
     grad_residual, grad_branch = zip(branches[0][:2], branches[1][:2])
-    keep, send, grad_mixed, small, mixed_sums, picked = input_back(
+    keep, send, small, mixed_sums, picked = input_back(
         place, thought_pos, dqs, *early, w_in, xhat, grad_residual
     )
+    grad_mixed = jnp.concatenate([jnp.concatenate(dqs), *early], axis=1)
     small = small + swapped(small, "tensor", 1)
     small = small + swapped(small, "tensor", 2)
     grad_embed, grad_thoughts = output_side(
@@ -1112,6 +1138,10 @@
     vec += (mixed_sums[0, :head_cols], mixed_sums[0, 2 * head_cols :])
     vec = jnp.concatenate([v.reshape(dp, -1) for v in vec], axis=1)
     vec = dp_scatter_sum(vec[:, None, :])[0]
+    small, first = [], 0
+    for n in (params[k].size for k in (0, 1, 5, 6, 7, 11, 9, 3)):
+        small.append(vec[first : first + n])
+        first += n
     return (
         block_out,
         grad_embed,
@@ -1120,7 +1150,7 @@
         grad_proj.T,
         grad_up,
         grad_down.T,
-        vec,
+        small,
     )
 
 

time: 184 us -> 170 us (0.924)
  waiting for transfers between devices: 62.8 us -> 56.3 us
  starting transfers between devices: 51.5 us -> 47.7 us
  Pallas kernels: 64.1 us -> 61.8 us
    ppermute x52 -> x50, waiting for transfers between devices: 62.8 us -> 56.3 us  [swapped(): lax.ppermute(array, axis, [(i, i ^ mask) for i in range(lax.axis_size(axi...]
    ppermute x52 -> x50, starting transfers between devices: 51.5 us -> 47.7 us  [swapped(): lax.ppermute(array, axis, [(i, i ^ mask) for i in range(lax.axis_size(axi...]
    pallas_call x50 -> x48, Pallas kernels: 62.3 us -> 60 us  [call(): pl.pallas_call(kernel, out_shape=tuple((jax.ShapeDtypeStruct(s, t) for s,...]
  transfers between devices with their start and end apart: 52 -> 50, of which waited for: 19 -> 24; matrix products, arithmetic and copies ran while one was open for 1% -> 0% of each run, Pallas kernels for 30% -> 32%
where the time goes in v2:
time: 170 us
  Pallas kernels  61.8 us (36%)
  waiting for transfers between devices  56.3 us (33%)
  starting transfers between devices  47.7 us (28%)
  local copies, waits for them, and re-layouts  2.67 us (2%)
    pallas_call x48, Pallas kernels, call(): pl.pallas_call(kernel, out_shape=tuple((jax.ShapeDtypeStruct(s, t) for s,...  60 us
    ppermute x50, waiting for transfers between devices, swapped(): lax.ppermute(array, axis, [(i, i ^ mask) for i in range(lax.axis_size(axi...  56.3 us
    ppermute x50, starting transfers between devices, swapped(): lax.ppermute(array, axis, [(i, i ^ mask) for i in range(lax.axis_size(axi...  47.7 us
  transfers between devices with their start and end apart: 50, of which 24 were waited for; matrix products, arithmetic and copies ran while one was open for 0% of the time, Pallas kernels for 32%

profile of v2, /device:TPU:0, one launch (start us, length us, event | category | flops | bytes accessed | tf_op | source)
XLA Modules:
  0.0 169.7 jit_solution(11697313453893015131)
XLA Ops:
  0.7 1.9 %shard_map.289.refs_0_ = bf16[104,768]{1,0:T(8,128)(2,1)} custom-call(bf16[3,96,192]{2,1,0:T(8,128)(2,1)} %refs_0_.1, bf16[192,96]{1,0:T(8,128)(2,1)} %refs_1_.1, bf16[1,96]{1,0:T(2,128)(2,1)} %bitcast.74, bf16[1,96]{1,0:T(2,128)(2,1)} %bitcast.75, bf16[1,96]{1,0:T(2,128)(2,1)} %bitcast.76, bf16[1,96]{1,0:T(2,128)(2,1)} %bitcast.77, bf16[1,96]{1,0:T(2,128)(2,1)} %bitcast.78, ...), custom_call_target="tpu_custom_call" | custom-call | flops 1000 | tf_op jit(solution)/shard_map/pallas_call | solution.py:717
  2.6 3.0 %collective-permute-start = (bf16[256,768]{1,0:T(8,128)(2,1)}, bf16[256,768]{1,0:T(8,128)(2,1)S(1)}, u32[]{:S(2)}, u32[]{:S(2)}) collective-permute-start(bf16[256,768]{1,0:T(8,128)(2,1)} %bitcast.56), channel_id=1, source_target_pairs={{0,2},{1,3},{2,0},{3,1},{4,6},{5,7},{6,4},{7,5},{8,10},{9,11},{10,... | collective-permute-start | bytes 1179656 | tf_op jit(solution)/shard_map/ppermute | solution.py:19
  5.6 1.5 collective-permute-start.2
  7.1 2.6 %collective-permute-start.1 = (bf16[104,768]{1,0:T(8,128)(2,1)}, bf16[104,768]{1,0:T(8,128)(2,1)S(1)}, u32[]{:S(2)}, u32[]{:S(2)}) collective-permute-start(bf16[104,768]{1,0:T(8,128)(2,1)} %shard_map.289.refs_0_), channel_id=1, source_target_pairs={{0,16},{4,20},{8,24},{12,28},{16,0},{20,4},{24,8},{28,12},{1,17},{... | collective-permute-start | bytes 479240 | tf_op jit(solution)/shard_map/ppermute | solution.py:19
  9.7 0.9 copy-done
  10.6 1.0 copy-done.3
  11.7 5.3 %collective-permute-done.1.b = bf16[104,768]{1,0:T(8,128)(2,1)S(1)} collective-permute-done((bf16[104,768]{1,0:T(8,128)(2,1)}, bf16[104,768]{1,0:T(8,128)(2,1)S(1)}, u32[]{:S(2)}, u32[]{:S(2)}) %collective-permute-start.1) | collective-permute-done | bytes 159776 | tf_op jit(solution)/shard_map/ppermute | solution.py:19
  17.5 0.8 collective-permute-start.3
  18.3 1.5 collective-permute-start.4
  20.4 3.3 %collective-permute-start.5 = (bf16[96,768]{1,0:T(8,128)(2,1)S(1)}, bf16[96,768]{1,0:T(8,128)(2,1)S(1)}, u32[]{:S(2)}, u32[]{:S(2)}) collective-permute-start(bf16[96,768]{1,0:T(8,128)(2,1)S(1)} %copy-done.1), channel_id=1, source_target_pairs={{0,16},{4,20},{8,24},{12,28},{16,0},{20,4},{24,8},{28,12},{1,17},{... | collective-permute-start | bytes 442376 | tf_op jit(solution)/shard_map/ppermute | solution.py:19
  24.3 2.6 %collective-permute-done.6 = bf16[96,768]{1,0:T(8,128)(2,1)S(1)} collective-permute-done((bf16[96,768]{1,0:T(8,128)(2,1)S(1)}, bf16[96,768]{1,0:T(8,128)(2,1)S(1)}, u32[]{:S(2)}, u32[]{:S(2)}) %collective-permute-start.6) | collective-permute-done | bytes 147488 | tf_op jit(solution)/shard_map/ppermute | solution.py:19
  27.0 1.2 collective-permute-done.5.b
  30.3 3.2 %collective-permute-start.10 = (bf16[2,96,768]{2,1,0:T(8,128)(2,1)S(1)}, bf16[2,96,768]{2,1,0:T(8,128)(2,1)S(1)}, u32[]{:S(2)}, u32[]{:S(2)}) collective-permute-start(bf16[2,96,768]{2,1,0:T(8,128)(2,1)S(1)} %shard_map.297), channel_id=1, source_target_pairs={{0,8},{4,12},{8,0},{12,4},{16,24},{20,28},{24,16},{28,20},{1,9},{5... | collective-permute-start | bytes 884744 | tf_op jit(solution)/shard_map/ppermute | solution.py:19
  33.6 1.7 %collective-permute-start.11 = (bf16[96,768]{1,0:T(8,128)(2,1)S(1)}, bf16[96,768]{1,0:T(8,128)(2,1)S(1)}, u32[]{:S(2)}, u32[]{:S(2)}) collective-permute-start(bf16[96,768]{1,0:T(8,128)(2,1)S(1)} %bitcast.48), channel_id=1, source_target_pairs={{0,16},{4,20},{8,24},{12,28},{16,0},{20,4},{24,8},{28,12},{1,17},{... | collective-permute-start | bytes 442376 | tf_op jit(solution)/shard_map/ppermute | solution.py:19
  35.3 1.8 %shard_map.293 = (bf16[1024,768]{1,0:T(8,128)(2,1)S(1)}, f32[1024,768]{1,0:T(8,128)S(1)}) custom-call(s32[8]{0:T(128)S(1)} %dynamic-slice_bitcast_fusion.place, bf16[2,256,768]{2,1,0:T(8,128)(2,1)S(1)} %shard_map.292.x_zero, bf16[2,256,768]{2,1,0:T(8,128)(2,1)S(1)} %collective-permute-done.9.x_one, bf16[6,768]{1,0:T(8,128)(2,1)S(1)} %bitcast.66, ...), custom_call_target="tpu_custom_call" | custom-call | flops 1000 | tf_op jit(solution)/shard_map/pallas_call | solution.py:120
  37.1 2.4 %collective-permute-done.8.refs_5_ = bf16[2,104,768]{2,1,0:T(8,128)(2,1)S(1)} collective-permute-done((bf16[2,104,768]{2,1,0:T(8,128)(2,1)S(1)}, bf16[2,104,768]{2,1,0:T(8,128)(2,1)S(1)}, u32[]{:S(2)}, u32[]{:S(2)}) %collective-permute-start.8) | collective-permute-done | bytes 319520 | tf_op jit(solution)/shard_map/ppermute | solution.py:19
  40.2 1.4 collective-permute-start.13
  41.6 0.8 shard_map.294
  42.4 1.4 shard_map.295
  43.9 3.6 %shard_map.296 = (bf16[512,192]{1,0:T(8,128)(2,1)S(1)}, f32[8,512]{1,0:T(8,128)S(1)}, f32[256,768]{1,0:T(8,128)S(1)}, bf16[256,768]{1,0:T(8,128)(2,1)S(1)}) custom-call(s32[8]{0:T(128)S(1)} %dynamic-slice_bitcast_fusion.place, s32[2]{0:T(128)S(1)} %bitcast.68, bf16[1024,192]{1,0:T(8,128)(2,1)S(1)} %get-tuple-element.209.q_ref, ...), custom_call_target="tpu_custom_call" | custom-call | flops 1000 | tf_op jit(solution)/shard_map/pallas_call | solution.py:120
  48.1 1.7 %collective-permute-done.14.b = bf16[256,768]{1,0:T(8,128)(2,1)S(1)} collective-permute-done((bf16[256,768]{1,0:T(8,128)(2,1)S(1)}, bf16[256,768]{1,0:T(8,128)(2,1)S(1)}, u32[]{:S(2)}, u32[]{:S(2)}) %collective-permute-start.14) | collective-permute-done | bytes 393248 | tf_op jit(solution)/shard_map/ppermute | solution.py:19
  50.0 1.6 collective-permute-start.15
  51.5 3.3 %collective-permute-start.18 = (bf16[2,96,768]{2,1,0:T(8,128)(2,1)S(1)}, bf16[2,96,768]{2,1,0:T(8,128)(2,1)S(1)}, u32[]{:S(2)}, u32[]{:S(2)}) collective-permute-start(bf16[2,96,768]{2,1,0:T(8,128)(2,1)S(1)} %shard_map.300), channel_id=1, source_target_pairs={{0,8},{4,12},{8,0},{12,4},{16,24},{20,28},{24,16},{28,20},{1,9},{5... | collective-permute-start | bytes 884744 | tf_op jit(solution)/shard_map/ppermute | solution.py:19
  55.4 1.5 collective-permute-start.17
  57.6 6.4 %shard_map.299 = (bf16[512,192]{1,0:T(8,128)(2,1)S(1)}, f32[8,512]{1,0:T(8,128)S(1)}, f32[256,768]{1,0:T(8,128)S(1)}, bf16[256,768]{1,0:T(8,128)(2,1)S(1)}) custom-call(s32[8]{0:T(128)S(1)} %dynamic-slice_bitcast_fusion.place, s32[2]{0:T(128)S(1)} %bitcast.69, bf16[1024,192]{1,0:T(8,128)(2,1)S(1)} %get-tuple-element.209.q_ref, ...), custom_call_target="tpu_custom_call" | custom-call | flops 1000 | tf_op jit(solution)/shard_map/pallas_call | solution.py:120
  64.0 2.6 %collective-permute-done.17 = bf16[96,768]{1,0:T(8,128)(2,1)S(1)} collective-permute-done((bf16[96,768]{1,0:T(8,128)(2,1)S(1)}, bf16[96,768]{1,0:T(8,128)(2,1)S(1)}, u32[]{:S(2)}, u32[]{:S(2)}) %collective-permute-start.17) | collective-permute-done | bytes 147488 | tf_op jit(solution)/shard_map/ppermute | solution.py:19
  67.3 1.1 collective-permute-done.22.b
  70.2 7.6 %collective-permute-done.20.refs_5_ = bf16[2,96,768]{2,1,0:T(8,128)(2,1)S(1)} collective-permute-done((bf16[2,96,768]{2,1,0:T(8,128)(2,1)S(1)}, bf16[2,96,768]{2,1,0:T(8,128)(2,1)S(1)}, u32[]{:S(2)}, u32[]{:S(2)}) %collective-permute-start.20) | collective-permute-done | bytes 294944 | tf_op jit(solution)/shard_map/ppermute | solution.py:19
  78.4 2.8 %shard_map.305 = (f32[512,768]{1,0:T(8,128)S(1)}, bf16[512,768]{1,0:T(8,128)(2,1)S(1)}, bf16[512,768]{1,0:T(8,128)(2,1)S(1)}, bf16[512,768]{1,0:T(8,128)(2,1)S(1...) custom-call(bf16[1024,768]{1,0:T(8,128)(2,1)S(1)} %get-tuple-element.244.spliced, ...), custom_call_target="tpu_custom_call" | custom-call | flops 1000 | tf_op jit(solution)/shard_map/pallas_call | solution.py:120
  82.0 1.1 collective-permute-done.24.b
  83.1 1.6 collective-permute-start.27
  84.6 2.8 %shard_map.309 = (f32[512,768]{1,0:T(8,128)S(1)}, bf16[512,768]{1,0:T(8,128)(2,1)S(1)}, bf16[512,768]{1,0:T(8,128)(2,1)S(1)}, bf16[512,768]{1,0:T(8,128)(2,1)S(1...) custom-call(bf16[1024,768]{1,0:T(8,128)(2,1)S(1)} %get-tuple-element.244.spliced, ...), custom_call_target="tpu_custom_call" | custom-call | flops 1000 | tf_op jit(solution)/shard_map/pallas_call | solution.py:120
  87.5 2.1 %shard_map.310 = (f32[4,96,256]{2,1,0:T(8,128)S(1)}, bf16[4,96,256]{2,1,0:T(8,128)(2,1)S(1)}, f32[4,96,512]{2,1,0:T(8,128)S(1)}, bf16[4,96,512]{2,1,0:T(8,128)(2,1)S(1)}) custom-call(s32[8]{0:T(128)S(1)} %dynamic-slice_bitcast_fusion.place, bf16[512,768]{1,0:T(8,128)(2,1)S(1)} %get-tuple-element.243.refs_0_, ...), custom_call_target="tpu_custom_call" | custom-call | flops 1000 | tf_op jit(solution)/shard_map/pallas_call | solution.py:120
  90.1 1.4 shard_map.312
  91.6 2.1 %shard_map.311 = (f32[4,96,768]{2,1,0:T(8,128)S(1)}, bf16[4,96,768]{2,1,0:T(8,128)(2,1)S(1)}) custom-call(s32[8]{0:T(128)S(1)} %dynamic-slice_bitcast_fusion.place, bf16[2,256,768]{2,1,0:T(8,128)(2,1)S(1)} %shard_map.303.cot_zero, bf16[2,256,768]{2,1,0:T(8,128)(2,1)S(1)} %collective-permute-done.21.cot_one, ...), custom_call_target="tpu_custom_call" | custom-call | flops 1000 | tf_op jit(solution)/shard_map/pallas_call | solution.py:120
  93.7 2.6 %collective-permute-done.26.refs_1_ = bf16[4,96,256]{2,1,0:T(8,128)(2,1)S(1)} collective-permute-done((bf16[4,96,256]{2,1,0:T(8,128)(2,1)S(1)}, bf16[4,96,256]{2,1,0:T(8,128)(2,1)S(1)}, u32[]{:S(2)}, u32[]{:S(2)}) %collective-permute-start.26) | collective-permute-done | bytes 196640 | tf_op jit(solution)/shard_map/ppermute | solution.py:19
  96.6 1.6 collective-permute-done.28.other
  99.5 2.3 %shard_map.315 = (f32[512,768]{1,0:T(8,128)S(1)}, bf16[512,768]{1,0:T(8,128)(2,1)S(1)}, bf16[512,192]{1,0:T(8,128)(2,1)S(1)}, f32[8,512]{1,0:T(8,128)S(1)}, f32[8,768]{1,0:T(8,128)S(1)}) custom-call(bf16[256,768]{1,0:T(8,128)(2,1)S(1)} %shard_map.313.total, bf16[256,768]{1,0:T(8,128)(2,1)S(1)} %collective-permute-done.28.other, ...), custom_call_target="tpu_custom_call" | custom-call | flops 1000 | tf_op jit(solution)/shard_map/pallas_call | solution.py:120
  101.8 3.6 %shard_map.316 = (bf16[512,192]{1,0:T(8,128)(2,1)S(1)}, f32[512,192]{1,0:T(8,128)S(1)}, f32[512,192]{1,0:T(8,128)S(1)}) custom-call(s32[8]{0:T(128)S(1)} %dynamic-slice_bitcast_fusion.place, s32[2]{0:T(128)S(1)} %bitcast.70, bf16[1024,192]{1,0:T(8,128)(2,1)S(1)} %get-tuple-element.209.q_ref, bf16[1024,192]{1,0:T(8,128)(2,1)S(1)} %get-tuple-element.210.k_ref, ...), custom_call_target="tpu_custom_call" | custom-call | flops 1000 | tf_op jit(solution)/shard_map/pallas_call | solution.py:120
  105.5 4.2 %collective-permute-done.31.refs_3_ = bf16[4,96,512]{2,1,0:T(8,128)(2,1)S(1)} collective-permute-done((bf16[4,96,512]{2,1,0:T(8,128)(2,1)S(1)}, bf16[4,96,512]{2,1,0:T(8,128)(2,1)S(1)}, u32[]{:S(2)}, u32[]{:S(2)}) %collective-permute-start.31) | collective-permute-done | bytes 393248 | tf_op jit(solution)/shard_map/ppermute | solution.py:19
  109.9 1.5 collective-permute-start.35
  112.4 0.8 collective-permute-start.36
  114.2 2.1 %shard_map.318 = (f32[512,768]{1,0:T(8,128)S(1)}, bf16[512,768]{1,0:T(8,128)(2,1)S(1)}, bf16[512,192]{1,0:T(8,128)(2,1)S(1)}, f32[8,512]{1,0:T(8,128)S(1)}, f32[8,768]{1,0:T(8,128)S(1)}) custom-call(bf16[256,768]{1,0:T(8,128)(2,1)S(1)} %shard_map.317.total, bf16[256,768]{1,0:T(8,128)(2,1)S(1)} %collective-permute-done.33.other, ...), custom_call_target="tpu_custom_call" | custom-call | flops 1000 | tf_op jit(solution)/shard_map/pallas_call | solution.py:120
  116.3 6.8 %shard_map.319 = (bf16[512,192]{1,0:T(8,128)(2,1)S(1)}, bf16[1024,192]{1,0:T(8,128)(2,1)S(1)}, bf16[1024,192]{1,0:T(8,128)(2,1)S(1)}) custom-call(s32[8]{0:T(128)S(1)} %dynamic-slice_bitcast_fusion.place, s32[2]{0:T(128)S(1)} %bitcast.71, bf16[1024,192]{1,0:T(8,128)(2,1)S(1)} %get-tuple-element.209.q_ref, bf16[1024,192]{1,0:T(8,128)(2,1)S(1)} %get-tuple-element.210.k_ref, ...), custom_call_target="tpu_custom_call" | custom-call | flops 1000 | tf_op jit(solution)/shard_map/pallas_call | solution.py:120
  123.1 0.8 collective-permute-done.36
  124.5 2.8 %shard_map.322 = (f32[4,96,384]{2,1,0:T(8,128)S(1)}, bf16[4,96,384]{2,1,0:T(8,128)(2,1)S(1)}, f32[4,96,384]{2,1,0:T(8,128)S(1)}, bf16[4,96,384]{2,1,0:T(8,128)(2,1)S(1)}) custom-call(s32[8]{0:T(128)S(1)} %dynamic-slice_bitcast_fusion.place, bf16[1024,768]{1,0:T(8,128)(2,1)S(1)} %get-tuple-element.208.normed, ...), custom_call_target="tpu_custom_call" | custom-call | flops 1000 | tf_op jit(solution)/shard_map/pallas_call | solution.py:120
  128.5 1.4 collective-permute-start.39
  129.9 2.1 %shard_map.323 = (f32[2,256,768]{2,1,0:T(8,128)S(1)}, bf16[2,256,768]{2,1,0:T(8,128)(2,1)S(1)}, f32[8,768]{1,0:T(8,128)S(1)}, f32[1,576]{1,0:T(1,128)S(1)}, f32[8,768]{1,0:T(8,128)S(1)}) custom-call(s32[8]{0:T(128)S(1)} %dynamic-slice_bitcast_fusion.place, s32[6]{0:T(128)S(1)} %bitcast.72, bf16[512,192]{1,0:T(8,128)(2,1)S(1)} %get-tuple-element.264.dq_zero, ...), custom_call_target="tpu_custom_call" | custom-call | flops 1000 | tf_op jit(solution)/shard_map/pallas_call | solution.py:120
  132.1 1.2 collective-permute-done.37.b
  134.0 3.1 %collective-permute-done.38.b = f32[8,768]{1,0:T(8,128)S(1)} collective-permute-done((f32[8,768]{1,0:T(8,128)S(1)}, f32[8,768]{1,0:T(8,128)S(1)}, u32[]{:S(2)}, u32[]{:S(2)}) %collective-permute-start.38) | collective-permute-done | bytes 24608 | tf_op jit(solution)/shard_map/ppermute | solution.py:19
  137.8 1.6 collective-permute-done.44.refs_1_
  140.1 1.2 collective-permute-start.45
  141.9 1.3 collective-permute-start.42
  143.8 1.8 %collective-permute-start.48 = (bf16[1,96,1536]{2,1,0:T(8,128)(2,1)S(1)}, bf16[1,96,1536]{2,1,0:T(8,128)(2,1)S(1)}, u32[]{:S(2)}, u32[]{:S(2)}) collective-permute-start(bf16[1,96,1536]{2,1,0:T(8,128)(2,1)S(1)} %get-tuple-element.336), channel_id=1, source_target_pairs={{0,16},{4,20},{8,24},{12,28},{16,0},{20,4},{24,8},{28,12},{1,17},{... | collective-permute-start | bytes 884744 | tf_op jit(solution)/shard_map/ppermute | solution.py:19
  147.0 1.4 shard_map.329
  148.5 1.8 %collective-permute-done.43.refs_3_ = bf16[4,8,384]{2,1,0:T(8,128)(2,1)S(1)} collective-permute-done((bf16[4,8,384]{2,1,0:T(8,128)(2,1)S(1)}, bf16[4,8,384]{2,1,0:T(8,128)(2,1)S(1)}, u32[]{:S(2)}, u32[]{:S(2)}) %collective-permute-start.43) | collective-permute-done | bytes 24608 | tf_op jit(solution)/shard_map/ppermute | solution.py:19
  150.9 0.9 collective-permute-start.46
  152.4 1.3 collective-permute-start.47
  153.6 2.1 %shard_map.331 = (f32[256,768]{1,0:T(8,128)}, f32[6,1,192]{2,1,0:T(1,128)}) custom-call(s32[8]{0:T(128)S(1)} %dynamic-slice_bitcast_fusion.place, f32[256,768]{1,0:T(8,128)S(1)} %bitcast.44, bf16[256,768]{1,0:T(8,128)(2,1)S(1)} %bitcast.55, bf16[1024,768]{1,0:T(8,128)(2,1)S(1)} %get-tuple-element.244.spliced, f32[512,768]{1,0:T(8,128)S(1)} %get-tuple-element.295.res_zero, ...), custom_call_target="tpu_custom_call" | custom-call | flops 1000 | tf_op jit(solution)/shard_map/pallas_call | solution.py:120
  155.7 6.3 %collective-permute-done.48.got = bf16[1,96,1536]{2,1,0:T(8,128)(2,1)S(1)} collective-permute-done((bf16[1,96,1536]{2,1,0:T(8,128)(2,1)S(1)}, bf16[1,96,1536]{2,1,0:T(8,128)(2,1)S(1)}, u32[]{:S(2)}, u32[]{:S(2)}) %collective-permute-start.48) | collective-permute-done | bytes 294944 | tf_op jit(solution)/shard_map/ppermute | solution.py:19
  162.0 0.8 collective-permute-done.47.d_got
  163.5 0.9 shard_map.336
  164.4 4.4 %collective-permute-done.49.e_got = bf16[1,104,384]{2,1,0:T(8,128)(2,1)S(1)} collective-permute-done((bf16[1,104,384]{2,1,0:T(8,128)(2,1)S(1)}, bf16[1,104,384]{2,1,0:T(8,128)(2,1)S(1)}, u32[]{:S(2)}, u32[]{:S(2)}) %collective-permute-start.49) | collective-permute-done | bytes 79904 | tf_op jit(solution)/shard_map/ppermute | solution.py:19
  168.8 0.9 shard_map.337
  (102 shorter events, 23.1 us)
Async XLA Ops:
  0.7 19.2 %copy-start.1 = (bf16[96,768]{1,0:T(8,128)(2,1)S(1)}, bf16[96,768]{1,0:T(8,128)(2,1)}, u32[]{:S(2)}) copy-start(bf16[96,768]{1,0:T(8,128)(2,1)} %a.1) | copy-start | bytes 442372
  0.7 32.9 %copy-start.2 = (bf16[768,96]{0,1:T(8,128)(2,1)S(1)}, bf16[768,96]{0,1:T(8,128)(2,1)}, u32[]{:S(2)}) copy-start(bf16[768,96]{0,1:T(8,128)(2,1)} %param.32) | copy-start | bytes 442372
  0.7 34.6 %copy-start.5 = (bf16[1,6,768]{2,1,0:T(8,128)(2,1)S(1)}, bf16[1,6,768]{2,1,0:T(8,128)(2,1)}, u32[]{:S(2)}) copy-start(bf16[1,6,768]{2,1,0:T(8,128)(2,1)} %param.19) | copy-start | bytes 27652
  2.6 32.7 %copy-start.7 = (s32[1,6]{1,0:T(1,128)S(1)}, s32[1,6]{1,0:T(1,128)}, u32[]{:S(2)}) copy-start(s32[1,6]{1,0:T(1,128)} %thought_pos.3) | copy-start | bytes 76
  2.6 14.4 %collective-permute-start = (bf16[256,768]{1,0:T(8,128)(2,1)}, bf16[256,768]{1,0:T(8,128)(2,1)S(1)}, u32[]{:S(2)}, u32[]{:S(2)}) collective-permute-start(bf16[256,768]{1,0:T(8,128)(2,1)} %bitcast.56), channel_id=1, source_target_pairs={{0,2},{1,3},{2,0},{3,1},{4,6},{5,7},{6,4},{7,5},{8,10},{9,11},{10,... | collective-permute-start | bytes 1179656 | tf_op jit(solution)/shard_map/ppermute | solution.py:19
  5.6 6.1 %collective-permute-start.2 = (bf16[104,768]{1,0:T(8,128)(2,1)}, bf16[104,768]{1,0:T(8,128)(2,1)S(1)}, u32[]{:S(2)}, u32[]{:S(2)}) collective-permute-start(bf16[104,768]{1,0:T(8,128)(2,1)} %shard_map.289.refs_0_), channel_id=1, source_target_pairs={{0,4},{4,0},{8,12},{12,8},{16,20},{20,16},{24,28},{28,24},{1,5},{5... | collective-permute-start | bytes 479240 | tf_op jit(solution)/shard_map/ppermute | solution.py:19
  7.1 9.8 %collective-permute-start.1 = (bf16[104,768]{1,0:T(8,128)(2,1)}, bf16[104,768]{1,0:T(8,128)(2,1)S(1)}, u32[]{:S(2)}, u32[]{:S(2)}) collective-permute-start(bf16[104,768]{1,0:T(8,128)(2,1)} %shard_map.289.refs_0_), channel_id=1, source_target_pairs={{0,16},{4,20},{8,24},{12,28},{16,0},{20,4},{24,8},{28,12},{1,17},{... | collective-permute-start | bytes 479240 | tf_op jit(solution)/shard_map/ppermute | solution.py:19
  9.7 0.9 copy-start
  10.6 1.0 copy-start.3
  16.9 12.0 %collective-permute-start.7 = (bf16[256,768]{1,0:T(8,128)(2,1)}, bf16[256,768]{1,0:T(8,128)(2,1)S(1)}, u32[]{:S(2)}, u32[]{:S(2)}) collective-permute-start(bf16[256,768]{1,0:T(8,128)(2,1)} %bitcast.58), channel_id=1, source_target_pairs={{0,2},{1,3},{2,0},{3,1},{4,6},{5,7},{6,4},{7,5},{8,10},{9,11},{10,... | collective-permute-start | bytes 1179656 | tf_op jit(solution)/shard_map/ppermute | solution.py:19
  17.5 11.4 %collective-permute-start.3 = (bf16[2,104,768]{2,1,0:T(8,128)(2,1)S(1)}, bf16[2,104,768]{2,1,0:T(8,128)(2,1)S(1)}, u32[]{:S(2)}, u32[]{:S(2)}) collective-permute-start(bf16[2,104,768]{2,1,0:T(8,128)(2,1)S(1)} %shard_map.291), channel_id=1, source_target_pairs={{0,8},{4,12},{8,0},{12,4},{16,24},{20,28},{24,16},{28,20},{1,9},{5... | collective-permute-start | bytes 958472 | tf_op jit(solution)/shard_map/ppermute | solution.py:19
  18.3 9.9 %collective-permute-start.4 = (bf16[104,768]{1,0:T(8,128)(2,1)S(1)}, bf16[104,768]{1,0:T(8,128)(2,1)S(1)}, u32[]{:S(2)}, u32[]{:S(2)}) collective-permute-start(bf16[104,768]{1,0:T(8,128)(2,1)S(1)} %collective-permute-done.1.b), channel_id=1, source_target_pairs={{0,4},{4,0},{8,12},{12,8},{16,20},{20,16},{24,28},{28,24},{1,5},{5... | collective-permute-start | bytes 479240 | tf_op jit(solution)/shard_map/ppermute | solution.py:19
  19.8 7.1 %collective-permute-start.6 = (bf16[96,768]{1,0:T(8,128)(2,1)S(1)}, bf16[96,768]{1,0:T(8,128)(2,1)S(1)}, u32[]{:S(2)}, u32[]{:S(2)}) collective-permute-start(bf16[96,768]{1,0:T(8,128)(2,1)S(1)} %copy-done.1), channel_id=1, source_target_pairs={{0,4},{4,0},{8,12},{12,8},{16,20},{20,16},{24,28},{28,24},{1,5},{5... | collective-permute-start | bytes 442376 | tf_op jit(solution)/shard_map/ppermute | solution.py:19
  20.4 7.8 %collective-permute-start.5 = (bf16[96,768]{1,0:T(8,128)(2,1)S(1)}, bf16[96,768]{1,0:T(8,128)(2,1)S(1)}, u32[]{:S(2)}, u32[]{:S(2)}) collective-permute-start(bf16[96,768]{1,0:T(8,128)(2,1)S(1)} %copy-done.1), channel_id=1, source_target_pairs={{0,16},{4,20},{8,24},{12,28},{16,0},{20,4},{24,8},{28,12},{1,17},{... | collective-permute-start | bytes 442376 | tf_op jit(solution)/shard_map/ppermute | solution.py:19
  29.5 5.8 %collective-permute-start.9 = (bf16[2,256,768]{2,1,0:T(8,128)(2,1)S(1)}, bf16[2,256,768]{2,1,0:T(8,128)(2,1)S(1)}, u32[]{:S(2)}, u32[]{:S(2)}) collective-permute-start(bf16[2,256,768]{2,1,0:T(8,128)(2,1)S(1)} %shard_map.292.x_zero), channel_id=1, source_target_pairs={{0,1},{1,0},{2,3},{3,2},{4,5},{5,4},{6,7},{7,6},{8,9},{9,8},{10,11... | collective-permute-start | bytes 2359304 | tf_op jit(solution)/shard_map/ppermute | solution.py:19
  29.6 10.0 %collective-permute-start.8 = (bf16[2,104,768]{2,1,0:T(8,128)(2,1)S(1)}, bf16[2,104,768]{2,1,0:T(8,128)(2,1)S(1)}, u32[]{:S(2)}, u32[]{:S(2)}) collective-permute-start(bf16[2,104,768]{2,1,0:T(8,128)(2,1)S(1)} %collective-permute-done.3.refs_3_), channel_id=1, source_target_pairs={{0,4},{4,0},{8,12},{12,8},{16,20},{20,16},{24,28},{28,24},{1,5},{5... | collective-permute-start | bytes 958472 | tf_op jit(solution)/shard_map/ppermute | solution.py:19
  30.3 17.2 %collective-permute-start.10 = (bf16[2,96,768]{2,1,0:T(8,128)(2,1)S(1)}, bf16[2,96,768]{2,1,0:T(8,128)(2,1)S(1)}, u32[]{:S(2)}, u32[]{:S(2)}) collective-permute-start(bf16[2,96,768]{2,1,0:T(8,128)(2,1)S(1)} %shard_map.297), channel_id=1, source_target_pairs={{0,8},{4,12},{8,0},{12,4},{16,24},{20,28},{24,16},{28,20},{1,9},{5... | collective-permute-start | bytes 884744 | tf_op jit(solution)/shard_map/ppermute | solution.py:19
  33.6 13.9 %collective-permute-start.11 = (bf16[96,768]{1,0:T(8,128)(2,1)S(1)}, bf16[96,768]{1,0:T(8,128)(2,1)S(1)}, u32[]{:S(2)}, u32[]{:S(2)}) collective-permute-start(bf16[96,768]{1,0:T(8,128)(2,1)S(1)} %bitcast.48), channel_id=1, source_target_pairs={{0,16},{4,20},{8,24},{12,28},{16,0},{20,4},{24,8},{28,12},{1,17},{... | collective-permute-start | bytes 442376 | tf_op jit(solution)/shard_map/ppermute | solution.py:19
  39.6 7.9 %collective-permute-start.12 = (bf16[96,768]{1,0:T(8,128)(2,1)S(1)}, bf16[96,768]{1,0:T(8,128)(2,1)S(1)}, u32[]{:S(2)}, u32[]{:S(2)}) collective-permute-start(bf16[96,768]{1,0:T(8,128)(2,1)S(1)} %collective-permute-done.5.b), channel_id=1, source_target_pairs={{0,4},{4,0},{8,12},{12,8},{16,20},{20,16},{24,28},{28,24},{1,5},{5... | collective-permute-start | bytes 442376 | tf_op jit(solution)/shard_map/ppermute | solution.py:19
  40.2 8.0 %collective-permute-start.13 = (bf16[96,768]{1,0:T(8,128)(2,1)S(1)}, bf16[96,768]{1,0:T(8,128)(2,1)S(1)}, u32[]{:S(2)}, u32[]{:S(2)}) collective-permute-start(bf16[96,768]{1,0:T(8,128)(2,1)S(1)} %bitcast.49), channel_id=1, source_target_pairs={{0,4},{4,0},{8,12},{12,8},{16,20},{20,16},{24,28},{28,24},{1,5},{5... | collective-permute-start | bytes 442376 | tf_op jit(solution)/shard_map/ppermute | solution.py:19
  42.4 1.4 copy-start.6
  47.5 9.4 %copy-start.4 = (bf16[1,256,768]{2,1,0:T(8,128)(2,1)S(1)}, bf16[1,256,768]{2,1,0:T(8,128)(2,1)}, u32[]{:S(2)}) copy-start(bf16[1,256,768]{2,1,0:T(8,128)(2,1)} %param.34) | copy-start | bytes 1179652
  48.1 1.7 %collective-permute-start.14 = (bf16[256,768]{1,0:T(8,128)(2,1)S(1)}, bf16[256,768]{1,0:T(8,128)(2,1)S(1)}, u32[]{:S(2)}, u32[]{:S(2)}) collective-permute-start(bf16[256,768]{1,0:T(8,128)(2,1)S(1)} %get-tuple-element.220), channel_id=1, source_target_pairs={{0,1},{1,0},{2,3},{3,2},{4,5},{5,4},{6,7},{7,6},{8,9},{9,8},{10,11... | collective-permute-start | bytes 1179656 | tf_op jit(solution)/shard_map/ppermute | solution.py:19
  50.0 16.6 %collective-permute-start.15 = (bf16[256,768]{1,0:T(8,128)(2,1)S(1)}, bf16[256,768]{1,0:T(8,128)(2,1)S(1)}, u32[]{:S(2)}, u32[]{:S(2)}) collective-permute-start(bf16[256,768]{1,0:T(8,128)(2,1)S(1)} %shard_map.298.a), channel_id=1, source_target_pairs={{0,2},{1,3},{2,0},{3,1},{4,6},{5,7},{6,4},{7,5},{8,10},{9,11},{10,... | collective-permute-start | bytes 1179656 | tf_op jit(solution)/shard_map/ppermute | solution.py:19
  51.5 15.0 %collective-permute-start.18 = (bf16[2,96,768]{2,1,0:T(8,128)(2,1)S(1)}, bf16[2,96,768]{2,1,0:T(8,128)(2,1)S(1)}, u32[]{:S(2)}, u32[]{:S(2)}) collective-permute-start(bf16[2,96,768]{2,1,0:T(8,128)(2,1)S(1)} %shard_map.300), channel_id=1, source_target_pairs={{0,8},{4,12},{8,0},{12,4},{16,24},{20,28},{24,16},{28,20},{1,9},{5... | collective-permute-start | bytes 884744 | tf_op jit(solution)/shard_map/ppermute | solution.py:19
  54.9 11.7 %collective-permute-start.16 = (bf16[2,96,768]{2,1,0:T(8,128)(2,1)S(1)}, bf16[2,96,768]{2,1,0:T(8,128)(2,1)S(1)}, u32[]{:S(2)}, u32[]{:S(2)}) collective-permute-start(bf16[2,96,768]{2,1,0:T(8,128)(2,1)S(1)} %collective-permute-done.10.refs_3_), channel_id=1, source_target_pairs={{0,4},{4,0},{8,12},{12,8},{16,20},{20,16},{24,28},{28,24},{1,5},{5... | collective-permute-start | bytes 884744 | tf_op jit(solution)/shard_map/ppermute | solution.py:19
  55.4 11.1 %collective-permute-start.17 = (bf16[96,768]{1,0:T(8,128)(2,1)S(1)}, bf16[96,768]{1,0:T(8,128)(2,1)S(1)}, u32[]{:S(2)}, u32[]{:S(2)}) collective-permute-start(bf16[96,768]{1,0:T(8,128)(2,1)S(1)} %collective-permute-done.11.b), channel_id=1, source_target_pairs={{0,4},{4,0},{8,12},{12,8},{16,20},{20,16},{24,28},{28,24},{1,5},{5... | collective-permute-start | bytes 442376 | tf_op jit(solution)/shard_map/ppermute | solution.py:19
  57.5 12.6 %collective-permute-start.21 = (bf16[2,256,768]{2,1,0:T(8,128)(2,1)S(1)}, bf16[2,256,768]{2,1,0:T(8,128)(2,1)S(1)}, u32[]{:S(2)}, u32[]{:S(2)}) collective-permute-start(bf16[2,256,768]{2,1,0:T(8,128)(2,1)S(1)} %shard_map.303.cot_zero), channel_id=1, source_target_pairs={{0,1},{1,0},{2,3},{3,2},{4,5},{5,4},{6,7},{7,6},{8,9},{9,8},{10,11... | collective-permute-start | bytes 2359304 | tf_op jit(solution)/shard_map/ppermute | solution.py:19
  66.5 1.8 %collective-permute-start.22 = (bf16[256,768]{1,0:T(8,128)(2,1)S(1)}, bf16[256,768]{1,0:T(8,128)(2,1)S(1)}, u32[]{:S(2)}, u32[]{:S(2)}) collective-permute-start(bf16[256,768]{1,0:T(8,128)(2,1)S(1)} %get-tuple-element.241), channel_id=1, source_target_pairs={{0,1},{1,0},{2,3},{3,2},{4,5},{5,4},{6,7},{7,6},{8,9},{9,8},{10,11... | collective-permute-start | bytes 1179656 | tf_op jit(solution)/shard_map/ppermute | solution.py:19
  66.7 11.1 %collective-permute-start.19 = (bf16[256,768]{1,0:T(8,128)(2,1)S(1)}, bf16[256,768]{1,0:T(8,128)(2,1)S(1)}, u32[]{:S(2)}, u32[]{:S(2)}) collective-permute-start(bf16[256,768]{1,0:T(8,128)(2,1)S(1)} %shard_map.301.total), channel_id=1, source_target_pairs={{0,1},{1,0},{2,3},{3,2},{4,5},{5,4},{6,7},{7,6},{8,9},{9,8},{10,11... | collective-permute-start | bytes 1179656 | tf_op jit(solution)/shard_map/ppermute | solution.py:19
  68.4 12.8 %collective-permute-start.23 = (bf16[256,768]{1,0:T(8,128)(2,1)S(1)}, bf16[256,768]{1,0:T(8,128)(2,1)S(1)}, u32[]{:S(2)}, u32[]{:S(2)}) collective-permute-start(bf16[256,768]{1,0:T(8,128)(2,1)S(1)} %shard_map.306.a), channel_id=1, source_target_pairs={{0,2},{1,3},{2,0},{3,1},{4,6},{5,7},{6,4},{7,5},{8,10},{9,11},{10,... | collective-permute-start | bytes 1179656 | tf_op jit(solution)/shard_map/ppermute | solution.py:19
  69.0 8.8 %collective-permute-start.20 = (bf16[2,96,768]{2,1,0:T(8,128)(2,1)S(1)}, bf16[2,96,768]{2,1,0:T(8,128)(2,1)S(1)}, u32[]{:S(2)}, u32[]{:S(2)}) collective-permute-start(bf16[2,96,768]{2,1,0:T(8,128)(2,1)S(1)} %collective-permute-done.18.refs_3_), channel_id=1, source_target_pairs={{0,4},{4,0},{8,12},{12,8},{16,20},{20,16},{24,28},{28,24},{1,5},{5... | collective-permute-start | bytes 884744 | tf_op jit(solution)/shard_map/ppermute | solution.py:19
  81.2 1.8 %collective-permute-start.24 = (bf16[256,768]{1,0:T(8,128)(2,1)S(1)}, bf16[256,768]{1,0:T(8,128)(2,1)S(1)}, u32[]{:S(2)}, u32[]{:S(2)}) collective-permute-start(bf16[256,768]{1,0:T(8,128)(2,1)S(1)} %get-tuple-element.242), channel_id=1, source_target_pairs={{0,1},{1,0},{2,3},{3,2},{4,5},{5,4},{6,7},{7,6},{8,9},{9,8},{10,11... | collective-permute-start | bytes 1179656 | tf_op jit(solution)/shard_map/ppermute | solution.py:19
  81.4 3.2 %collective-permute-start.25 = (bf16[256,768]{1,0:T(8,128)(2,1)S(1)}, bf16[256,768]{1,0:T(8,128)(2,1)S(1)}, u32[]{:S(2)}, u32[]{:S(2)}) collective-permute-start(bf16[256,768]{1,0:T(8,128)(2,1)S(1)} %shard_map.308.total), channel_id=1, source_target_pairs={{0,1},{1,0},{2,3},{3,2},{4,5},{5,4},{6,7},{7,6},{8,9},{9,8},{10,11... | collective-permute-start | bytes 1179656 | tf_op jit(solution)/shard_map/ppermute | solution.py:19
  83.1 13.2 %collective-permute-start.27 = (bf16[256,768]{1,0:T(8,128)(2,1)S(1)}, bf16[256,768]{1,0:T(8,128)(2,1)S(1)}, u32[]{:S(2)}, u32[]{:S(2)}) collective-permute-start(bf16[256,768]{1,0:T(8,128)(2,1)S(1)} %shard_map.307.a), channel_id=1, source_target_pairs={{0,2},{1,3},{2,0},{3,1},{4,6},{5,7},{6,4},{7,5},{8,10},{9,11},{10,... | collective-permute-start | bytes 1179656 | tf_op jit(solution)/shard_map/ppermute | solution.py:19
  89.6 6.7 %collective-permute-start.26 = (bf16[4,96,256]{2,1,0:T(8,128)(2,1)S(1)}, bf16[4,96,256]{2,1,0:T(8,128)(2,1)S(1)}, u32[]{:S(2)}, u32[]{:S(2)}) collective-permute-start(bf16[4,96,256]{2,1,0:T(8,128)(2,1)S(1)} %get-tuple-element.249), channel_id=1, source_target_pairs={{0,4},{4,0},{8,12},{12,8},{16,20},{20,16},{24,28},{28,24},{1,5},{5... | collective-permute-start | bytes 589832 | tf_op jit(solution)/shard_map/ppermute | solution.py:19
  90.1 6.3 %collective-permute-start.29 = (bf16[256,768]{1,0:T(8,128)(2,1)S(1)}, bf16[256,768]{1,0:T(8,128)(2,1)S(1)}, u32[]{:S(2)}, u32[]{:S(2)}) collective-permute-start(bf16[256,768]{1,0:T(8,128)(2,1)S(1)} %get-tuple-element.258), channel_id=1, source_target_pairs={{0,1},{1,0},{2,3},{3,2},{4,5},{5,4},{6,7},{7,6},{8,9},{9,8},{10,11... | collective-permute-start | bytes 1179656 | tf_op jit(solution)/shard_map/ppermute | solution.py:19
  96.4 1.8 %collective-permute-start.28 = (bf16[256,768]{1,0:T(8,128)(2,1)S(1)}, bf16[256,768]{1,0:T(8,128)(2,1)S(1)}, u32[]{:S(2)}, u32[]{:S(2)}) collective-permute-start(bf16[256,768]{1,0:T(8,128)(2,1)S(1)} %shard_map.313.total), channel_id=1, source_target_pairs={{0,1},{1,0},{2,3},{3,2},{4,5},{5,4},{6,7},{7,6},{8,9},{9,8},{10,11... | collective-permute-start | bytes 1179656 | tf_op jit(solution)/shard_map/ppermute | solution.py:19
  98.2 11.8 %collective-permute-start.32 = (bf16[2,256,768]{2,1,0:T(8,128)(2,1)S(1)}, bf16[2,256,768]{2,1,0:T(8,128)(2,1)S(1)}, u32[]{:S(2)}, u32[]{:S(2)}) collective-permute-start(bf16[2,256,768]{2,1,0:T(8,128)(2,1)S(1)} %get-tuple-element.270), channel_id=1, source_target_pairs={{0,1},{1,0},{2,3},{3,2},{4,5},{5,4},{6,7},{7,6},{8,9},{9,8},{10,11... | collective-permute-start | bytes 2359304 | tf_op jit(solution)/shard_map/ppermute | solution.py:19
  98.3 11.4 %collective-permute-start.31 = (bf16[4,96,512]{2,1,0:T(8,128)(2,1)S(1)}, bf16[4,96,512]{2,1,0:T(8,128)(2,1)S(1)}, u32[]{:S(2)}, u32[]{:S(2)}) collective-permute-start(bf16[4,96,512]{2,1,0:T(8,128)(2,1)S(1)} %get-tuple-element.269), channel_id=1, source_target_pairs={{0,4},{4,0},{8,12},{12,8},{16,20},{20,16},{24,28},{28,24},{1,5},{5... | collective-permute-start | bytes 1179656 | tf_op jit(solution)/shard_map/ppermute | solution.py:19
  98.8 11.1 %collective-permute-start.30 = (bf16[256,768]{1,0:T(8,128)(2,1)S(1)}, bf16[256,768]{1,0:T(8,128)(2,1)S(1)}, u32[]{:S(2)}, u32[]{:S(2)}) collective-permute-start(bf16[256,768]{1,0:T(8,128)(2,1)S(1)} %shard_map.314.a), channel_id=1, source_target_pairs={{0,2},{1,3},{2,0},{3,1},{4,6},{5,7},{6,4},{7,5},{8,10},{9,11},{10,... | collective-permute-start | bytes 1179656 | tf_op jit(solution)/shard_map/ppermute | solution.py:19
  109.9 14.6 %collective-permute-start.35 = (bf16[4,96,768]{2,1,0:T(8,128)(2,1)S(1)}, bf16[4,96,768]{2,1,0:T(8,128)(2,1)S(1)}, u32[]{:S(2)}, u32[]{:S(2)}) collective-permute-start(bf16[4,96,768]{2,1,0:T(8,128)(2,1)S(1)} %get-tuple-element.284), channel_id=1, source_target_pairs={{0,4},{4,0},{8,12},{12,8},{16,20},{20,16},{24,28},{28,24},{1,5},{5... | collective-permute-start | bytes 1769480 | tf_op jit(solution)/shard_map/ppermute | solution.py:19
  111.6 2.7 %collective-permute-start.33 = (bf16[256,768]{1,0:T(8,128)(2,1)S(1)}, bf16[256,768]{1,0:T(8,128)(2,1)S(1)}, u32[]{:S(2)}, u32[]{:S(2)}) collective-permute-start(bf16[256,768]{1,0:T(8,128)(2,1)S(1)} %shard_map.317.total), channel_id=1, source_target_pairs={{0,1},{1,0},{2,3},{3,2},{4,5},{5,4},{6,7},{7,6},{8,9},{9,8},{10,11... | collective-permute-start | bytes 1179656 | tf_op jit(solution)/shard_map/ppermute | solution.py:19
  112.4 11.6 %collective-permute-start.36 = (bf16[1,256,768]{2,1,0:T(8,128)(2,1)S(1)}, bf16[1,256,768]{2,1,0:T(8,128)(2,1)S(1)}, u32[]{:S(2)}, u32[]{:S(2)}) collective-permute-start(bf16[1,256,768]{2,1,0:T(8,128)(2,1)S(1)} %get-tuple-element.287), channel_id=1, source_target_pairs={{0,2},{1,3},{2,0},{3,1},{4,6},{5,7},{6,4},{7,5},{8,10},{9,11},{10,... | collective-permute-start | bytes 1179656 | tf_op jit(solution)/shard_map/ppermute | solution.py:19
  113.8 9.3 %collective-permute-start.34 = (bf16[2,96,768]{2,1,0:T(8,128)(2,1)S(1)}, bf16[2,96,768]{2,1,0:T(8,128)(2,1)S(1)}, u32[]{:S(2)}, u32[]{:S(2)}) collective-permute-start(bf16[2,96,768]{2,1,0:T(8,128)(2,1)S(1)} %get-tuple-element.283), channel_id=1, source_target_pairs={{0,8},{4,12},{8,0},{12,4},{16,24},{20,28},{24,16},{28,20},{1,9},{5... | collective-permute-start | bytes 884744 | tf_op jit(solution)/shard_map/ppermute | solution.py:19
  128.0 9.1 %collective-permute-start.40 = (bf16[2,96,768]{2,1,0:T(8,128)(2,1)S(1)}, bf16[2,96,768]{2,1,0:T(8,128)(2,1)S(1)}, u32[]{:S(2)}, u32[]{:S(2)}) collective-permute-start(bf16[2,96,768]{2,1,0:T(8,128)(2,1)S(1)} %get-tuple-element.301), channel_id=1, source_target_pairs={{0,8},{4,12},{8,0},{12,4},{16,24},{20,28},{24,16},{28,20},{1,9},{5... | collective-permute-start | bytes 884744 | tf_op jit(solution)/shard_map/ppermute | solution.py:19
  128.5 8.6 %collective-permute-start.39 = (bf16[4,96,384]{2,1,0:T(8,128)(2,1)S(1)}, bf16[4,96,384]{2,1,0:T(8,128)(2,1)S(1)}, u32[]{:S(2)}, u32[]{:S(2)}) collective-permute-start(bf16[4,96,384]{2,1,0:T(8,128)(2,1)S(1)} %get-tuple-element.293), channel_id=1, source_target_pairs={{0,4},{4,0},{8,12},{12,8},{16,20},{20,16},{24,28},{28,24},{1,5},{5... | collective-permute-start | bytes 884744 | tf_op jit(solution)/shard_map/ppermute | solution.py:19
  132.0 1.3 collective-permute-start.37
  133.3 3.8 %collective-permute-start.38 = (f32[8,768]{1,0:T(8,128)S(1)}, f32[8,768]{1,0:T(8,128)S(1)}, u32[]{:S(2)}, u32[]{:S(2)}) collective-permute-start(f32[8,768]{1,0:T(8,128)S(1)} %shard_map.324.a), channel_id=1, source_target_pairs={{0,2},{1,3},{2,0},{3,1},{4,6},{5,7},{6,4},{7,5},{8,10},{9,11},{10,... | collective-permute-start | bytes 73736 | tf_op jit(solution)/shard_map/ppermute | solution.py:19
  137.1 2.3 %collective-permute-start.44 = (bf16[2,256,768]{2,1,0:T(8,128)(2,1)S(1)}, bf16[2,256,768]{2,1,0:T(8,128)(2,1)S(1)}, u32[]{:S(2)}, u32[]{:S(2)}) collective-permute-start(bf16[2,256,768]{2,1,0:T(8,128)(2,1)S(1)} %get-tuple-element.318), channel_id=1, source_target_pairs={{0,1},{1,0},{2,3},{3,2},{4,5},{5,4},{6,7},{7,6},{8,9},{9,8},{10,11... | collective-permute-start | bytes 2359304 | tf_op jit(solution)/shard_map/ppermute | solution.py:19
  137.1 13.1 %collective-permute-start.41 = (bf16[4,96,384]{2,1,0:T(8,128)(2,1)S(1)}, bf16[4,96,384]{2,1,0:T(8,128)(2,1)S(1)}, u32[]{:S(2)}, u32[]{:S(2)}) collective-permute-start(bf16[4,96,384]{2,1,0:T(8,128)(2,1)S(1)} %get-tuple-element.303), channel_id=1, source_target_pairs={{0,4},{4,0},{8,12},{12,8},{16,20},{20,16},{24,28},{28,24},{1,5},{5... | collective-permute-start | bytes 884744 | tf_op jit(solution)/shard_map/ppermute | solution.py:19
  140.1 13.5 %collective-permute-start.45 = (bf16[1,256,768]{2,1,0:T(8,128)(2,1)S(1)}, bf16[1,256,768]{2,1,0:T(8,128)(2,1)S(1)}, u32[]{:S(2)}, u32[]{:S(2)}) collective-permute-start(bf16[1,256,768]{2,1,0:T(8,128)(2,1)S(1)} %get-tuple-element.320), channel_id=1, source_target_pairs={{0,2},{1,3},{2,0},{3,1},{4,6},{5,7},{6,4},{7,5},{8,10},{9,11},{10,... | collective-permute-start | bytes 1179656 | tf_op jit(solution)/shard_map/ppermute | solution.py:19
  141.9 8.3 %collective-permute-start.42 = (bf16[2,96,384]{2,1,0:T(8,128)(2,1)S(1)}, bf16[2,96,384]{2,1,0:T(8,128)(2,1)S(1)}, u32[]{:S(2)}, u32[]{:S(2)}) collective-permute-start(bf16[2,96,384]{2,1,0:T(8,128)(2,1)S(1)} %get-tuple-element.305), channel_id=1, source_target_pairs={{0,8},{4,12},{8,0},{12,4},{16,24},{20,28},{24,16},{28,20},{1,9},{5... | collective-permute-start | bytes 442376 | tf_op jit(solution)/shard_map/ppermute | solution.py:19
  143.8 18.2 %collective-permute-start.48 = (bf16[1,96,1536]{2,1,0:T(8,128)(2,1)S(1)}, bf16[1,96,1536]{2,1,0:T(8,128)(2,1)S(1)}, u32[]{:S(2)}, u32[]{:S(2)}) collective-permute-start(bf16[1,96,1536]{2,1,0:T(8,128)(2,1)S(1)} %get-tuple-element.336), channel_id=1, source_target_pairs={{0,16},{4,20},{8,24},{12,28},{16,0},{20,4},{24,8},{28,12},{1,17},{... | collective-permute-start | bytes 884744 | tf_op jit(solution)/shard_map/ppermute | solution.py:19
  146.4 3.9 %collective-permute-start.43 = (bf16[4,8,384]{2,1,0:T(8,128)(2,1)S(1)}, bf16[4,8,384]{2,1,0:T(8,128)(2,1)S(1)}, u32[]{:S(2)}, u32[]{:S(2)}) collective-permute-start(bf16[4,8,384]{2,1,0:T(8,128)(2,1)S(1)} %get-tuple-element.312), channel_id=1, source_target_pairs={{0,4},{4,0},{8,12},{12,8},{16,20},{20,16},{24,28},{28,24},{1,5},{5... | collective-permute-start | bytes 73736 | tf_op jit(solution)/shard_map/ppermute | solution.py:19
  150.9 11.9 %collective-permute-start.46 = (bf16[2,104,384]{2,1,0:T(8,128)(2,1)S(1)}, bf16[2,104,384]{2,1,0:T(8,128)(2,1)S(1)}, u32[]{:S(2)}, u32[]{:S(2)}) collective-permute-start(bf16[2,104,384]{2,1,0:T(8,128)(2,1)S(1)} %get-tuple-element.327), channel_id=1, source_target_pairs={{0,8},{4,12},{8,0},{12,4},{16,24},{20,28},{24,16},{28,20},{1,9},{5... | collective-permute-start | bytes 479240 | tf_op jit(solution)/shard_map/ppermute | solution.py:19
  152.4 10.5 %collective-permute-start.47 = (bf16[1,96,384]{2,1,0:T(8,128)(2,1)S(1)}, bf16[1,96,384]{2,1,0:T(8,128)(2,1)S(1)}, u32[]{:S(2)}, u32[]{:S(2)}) collective-permute-start(bf16[1,96,384]{2,1,0:T(8,128)(2,1)S(1)} %get-tuple-element.330), channel_id=1, source_target_pairs={{0,16},{4,20},{8,24},{12,28},{16,0},{20,4},{24,8},{28,12},{1,17},{... | collective-permute-start | bytes 221192 | tf_op jit(solution)/shard_map/ppermute | solution.py:19
  163.4 5.4 %collective-permute-start.49 = (bf16[1,104,384]{2,1,0:T(8,128)(2,1)S(1)}, bf16[1,104,384]{2,1,0:T(8,128)(2,1)S(1)}, u32[]{:S(2)}, u32[]{:S(2)}) collective-permute-start(bf16[1,104,384]{2,1,0:T(8,128)(2,1)S(1)} %get-tuple-element.347), channel_id=1, source_target_pairs={{0,16},{4,20},{8,24},{12,28},{16,0},{20,4},{24,8},{28,12},{1,17},{... | collective-permute-start | bytes 239624 | tf_op jit(solution)/shard_map/ppermute | solution.py:19

commit v3 on v2

--- a/solution.py
+++ b/solution.py
@@ -113,7 +113,7 @@
     return lax.broadcasted_iota(jnp.int32, shape, dim)
 
 
-def call(kernel, outs, *args, scratch=(), mib=8):
+def call(kernel, outs, *args, scratch=(), mib=8, cost=0):
     spec = lambda a: pl.BlockSpec(
         memory_space=pltpu.SMEM if a.ndim == 1 and a.dtype == jnp.int32 else pltpu.VMEM
     )
@@ -124,7 +124,7 @@
         out_specs=tuple(pl.BlockSpec(memory_space=pltpu.VMEM) for _ in outs),
         scratch_shapes=scratch,
         compiler_params=pltpu.CompilerParams(vmem_limit_bytes=mib << 20),
-        cost_estimate=pl.CostEstimate(flops=COST, bytes_accessed=0, transcendentals=0),
+        cost_estimate=pl.CostEstimate(flops=COST + cost, bytes_accessed=0, transcendentals=0),
     )(*args)
 
 
@@ -404,7 +404,7 @@
 
 def input_back_kernel(
     place, thought_pos, dq_zero, dq_one, dk, dv, w_in, xhat, res_zero, res_one,
-    keep_ref, send_ref, small_ref, colsum_ref, picked_ref, grad_ref,
+    keep_ref, low_ref, high_ref, small_ref, colsum_ref, picked_ref, grad_ref,
 ):
     half, cols = dq_zero.shape
     rows = half // 2
@@ -418,7 +418,7 @@
             grad = dot(mixed, w_in[...], 1, 1)
             grad_ref[part, :] = grad
             if rel:
-                send_ref[upper] = grad.astype(LOW)
+                (low_ref, high_ref)[upper][...] = grad.astype(LOW)
             else:
                 keep_ref[upper] = grad
             terms = (grad * xhat[part, :], grad, mixed.astype(F32))
@@ -487,6 +487,18 @@
     return call(functools.partial(fold_kernel, bit), ((shape, F32), (shape, LOW)), place, *parts)
 
 
+def fold_two_kernel(bit, place, keep, low, high, keep_ref, send_ref):
+    first = place[bit] == 0
+    low, high = keep[0] + low[...].astype(F32), keep[1] + high[...].astype(F32)
+    keep_ref[...] = jnp.where(first, low, high)
+    send_ref[...] = jnp.where(first, high, low).astype(LOW)
+
+
+def fold_two(bit, place, keep, low, high):
+    kinds = ((low.shape, F32), (low.shape, LOW))
+    return call(functools.partial(fold_two_kernel, bit), kinds, place, keep, low, high)
+
+
 def add_kernel(a, b, out):
     out[...] = (a[...].astype(F32) + b[...].astype(F32)).astype(LOW)
 
@@ -499,8 +511,8 @@
     return call(add_full_kernel, ((a.shape, F32),), a, b)[0]
 
 
-def add_low(a, b):
-    return call(add_kernel, ((a.shape, LOW),), a, b)[0]
+def add_low(a, b, cost=0):
+    return call(add_kernel, ((a.shape, LOW),), a, b, cost=cost)[0]
 
 
 def to_slots(place, sum_ref, first, keep_ref, send_ref, bit=0):
@@ -540,18 +552,22 @@
     all_slots(place, sum_ref, blocks)
 
 
-def last_kernel(place, normed, dq_zero, dq_one, dk, dv, branch_zero, branch_one, att_zero, att_one, *refs):
+def last_kernel_one(place, normed, dq_zero, dq_one, branch_zero, branch_one, att_zero, att_one, *refs):
     *blocks, sum_ref = refs
     half, cols = att_zero.shape
     sum_ref[:, :cols] = product((branch_zero, branch_one), (att_zero, att_one))
-    sum_ref[:, cols : 2 * cols] = dot(normed[:half, :], dq_zero[...], 0, 0) + dot(normed[half:, :], dq_one[...], 0, 0)
-    sum_ref[:, 2 * cols : 3 * cols] = dot(normed[...], dk[...], 0, 0)
-    sum_ref[:, 3 * cols :] = dot(normed[...], dv[...], 0, 0)
+    sum_ref[:, cols:] = dot(normed[:half, :], dq_zero[...], 0, 0) + dot(normed[half:, :], dq_one[...], 0, 0)
     all_slots(place, sum_ref, blocks)
 
 
-def slot_kernel(place, small, back_zero, back_one, up_zero, up_one, mixed_sums, keep_ref, send_ref, flat_ref):
-    cols, wide_cols = mixed_sums.shape[1] // 3, keep_ref.shape[2]
+def last_kernel_two(
+    place, normed, dk, dv, small, back_zero, back_one, up_zero, up_one, mixed_sums, keep_ref, send_ref, sum_ref, flat_ref
+):
+    cols = dk.shape[1]
+    sum_ref[:, :cols] = dot(normed[...], dk[...], 0, 0)
+    sum_ref[:, cols:] = dot(normed[...], dv[...], 0, 0)
+    to_slots(place, sum_ref, 0, keep_ref, send_ref)
+    rows, wide_cols = keep_ref.shape[1] - 8, keep_ref.shape[2]
     count = small.shape[0] - 2
     back = back_zero[...] + back_one[...]
     wide = [small[count : count + 1, :], small[count + 1 :, :], back[2:3], back[0:1], back[1:2], back[3:4]]
@@ -566,8 +582,8 @@
     first = iota((8, wide_cols), 0) == 0
     for slot, owner in enumerate((0, 4, 2, 6)):
         mine, other = (flat_ref[pl.ds(owner ^ k ^ place[7], 1), :] for k in range(2))
-        keep_ref[slot] = jnp.where(first, mine[:, :wide_cols], mine[:, wide_cols:])
-        send_ref[slot] = jnp.where(first, other[:, :wide_cols], other[:, wide_cols:]).astype(LOW)
+        keep_ref[slot, rows:, :] = jnp.where(first, mine[:, :wide_cols], mine[:, wide_cols:])
+        send_ref[slot, rows:, :] = jnp.where(first, other[:, :wide_cols], other[:, wide_cols:]).astype(LOW)
 
 
 def finish_kernel(
@@ -589,17 +605,6 @@
     qv_b[...] = jnp.concatenate([flat[:, first : first + count], flat[:, first + count : first + 2 * count]])
 
 
-def parts_kernel(keep, got, one_ref, two_ref):
-    cols = one_ref.shape[1]
-    one_ref[...] = keep[0, :, :cols] + got[0, :, :cols].astype(F32)
-    two_ref[...] = keep[0, :, cols:] + got[0, :, cols:].astype(F32)
-
-
-def parted(keep, got):
-    shape = (keep.shape[1], keep.shape[2] // 2)
-    return call(parts_kernel, ((shape, F32),) * 2, keep, got)
-
-
 def result_of(place, keep, got, res_zero, res_one, vecs):
     rows = keep.shape[0]
     residual = jnp.where(place[3] == 0, res_zero[:rows, :], res_one[:rows, :])
@@ -625,8 +630,8 @@
         b[...] = a[...]
 
 
-def brought(*arrays):
-    return call(copy_kernel, tuple((a.shape, a.dtype) for a in arrays), *arrays)
+def brought(*arrays, cost=0):
+    return call(copy_kernel, tuple((a.shape, a.dtype) for a in arrays), *arrays, cost=cost)
 
 
 def stack_kernel(a, b, out_ref):
@@ -685,14 +690,13 @@
     bias_ref[...] = jnp.concatenate([joined[7], jnp.zeros_like(joined[7]), joined[8]], axis=1)
 
 
-def plain_kernel(masks, place, *refs):
-    out_ref = refs[-1]
+def plain_kernel(masks, second, place, *refs):
+    *pieces, out_ref = refs
     rows = out_ref.shape[0] // 8
-
-    def write(owner, piece, k):
-        out_ref[pl.ds(pl.multiple_of(owner * rows, rows), rows), :] = piece[k]
-
-    place_pieces(masks, place, refs[:-1], write)
+    for number, (piece, owners) in enumerate(zip(pieces, masks)):
+        for k, mask in enumerate(owners):
+            at = pl.ds(pl.multiple_of((place[4] ^ mask) * rows, rows), rows)
+            out_ref[at, :] = piece[second if number == 1 else k]
 
 
 def pack_kernel(count, *refs):
@@ -752,9 +756,9 @@
     )
 
 
-def unpacked(place, pieces):
+def unpacked(place, pieces, second):
     rows, cols = pieces[0].shape[1:]
-    return call(functools.partial(plain_kernel, MASKS), (((8 * rows, cols), LOW),), place, *pieces)[0]
+    return call(functools.partial(plain_kernel, MASKS, second), (((8 * rows, cols), LOW),), place, *pieces)[0]
 
 
 def plain_first(shard, vectors, qkv_cols, width):
@@ -834,7 +838,8 @@
         input_back_kernel,
         (
             ((2, length // 4, width), F32),
-            ((2, length // 4, width), LOW),
+            ((length // 4, width), LOW),
+            ((length // 4, width), LOW),
             ((-(-(count + 2) // 8) * 8, width), F32),
             ((1, w_in.shape[1]), F32),
             ((-(-count // 8) * 8, width), F32),
@@ -896,16 +901,21 @@
     vectors = vectors_of(params)
 
     pack = first_pack(w_qkv, w_proj, *vectors)
-    pack_far, pack_across = far(pack), across(pack)
+    pack_across = across(pack)
+    pack_far = far(pack)
     x_far = over(after(x_own, pack))
     pack_here, x_here = brought(pack, after(x_own, pack))
-    x_far, pack_far, pack_across, pack_here, x_here = together(x_far, pack_far, pack_across, pack_here, x_here)
+    both = stacked(after(w_up, pack), w_down_own)
+    x_far, pack_far, pack_across, pack_here, x_here, both = together(
+        x_far, pack_far, pack_across, pack_here, x_here, both
+    )
 
     pack_near, pack_far_across = near(stacked(pack_here, pack_far)), across(pack_far)
-    up_far, up_across = far(after(w_up, pack_far)), across(after(w_up, pack_far))
+    up_far = far(after(w_up, pack_far))
+    both_across = across(both)
     cot_far = over(after(cot_own, x_far))
-    pack_near, pack_far_across, up_far, up_across, cot_far = together(
-        pack_near, pack_far_across, up_far, up_across, cot_far
+    pack_near, pack_far_across, up_far, both_across, cot_far = together(
+        pack_near, pack_far_across, up_far, both_across, cot_far
     )
 
     pack_near_across = across(pack_near)
@@ -915,19 +925,18 @@
     x_other = core(x_both)
     spliced, xhat = splice_side(place, (x_both, x_other), thoughts, thought_pos)
     pack_near_across, xhat = together(pack_near_across, xhat)
-    up_far_across, down_across = across(after(up_far, pack_near_across)), across(after(w_down_own, pack_near_across))
+    up_far_across = across(after(up_far, pack_near_across))
     pieces = (pack_here[None], pack_across[None], pack_far[None], pack_near, pack_far_across[None], pack_near_across)
     w_in, w_proj_t, vecs, up_bias, all_bias = first_unpacked(place, pieces, vectors, 3 * head_cols, head_cols, width)
     normed, queries, keys, values = input_side(xhat, vecs, w_in, all_bias)
     att_zero, log_zero, keep_zero, send_zero = attend(0, place, starts, queries, keys, values, w_proj_t)
-    send_zero, up_near, down_far, up_far_across, down_across = together(
-        send_zero, up_near, down_far, up_far_across, down_across
-    )
+    send_zero, up_near, down_far, up_far_across = together(send_zero, up_near, down_far, up_far_across)
 
     mine_zero = add_low(keep_zero, core(send_zero))
     far_zero = over(mine_zero)
-    up_near_across, down_far_across = across(up_near), across(down_far)
     down_near = near(stacked(w_down_own, down_far))
+    down_far_across = across(down_far)
+    up_near_across = across(up_near)
     att_one, log_one, keep_one, send_one = attend(1, after(place, mine_zero), starts, queries, keys, values, w_proj_t)
     send_one, far_zero, up_near_across, down_far_across, down_near = together(
         send_one, far_zero, up_near_across, down_far_across, down_near
@@ -938,14 +947,14 @@
     total_zero = add_low(mine_zero, far_zero)
     other_zero = core(total_zero)
     down_near_across = across(down_near)
-    pieces = (w_up[None], up_across[None], up_far[None], up_near, up_far_across[None], up_near_across)
-    w_up_all = unpacked(place, pieces)
+    pieces = (w_up[None], both_across, up_far[None], up_near, up_far_across[None], up_near_across)
+    w_up_all = unpacked(place, pieces, 0)
     cot_both = pick(place, cot_own, cot_far)
     cot_other = core(cot_both)
     other_zero, down_near_across, w_up_all, cot_other = together(other_zero, down_near_across, w_up_all, cot_other)
     cots = (cot_both, cot_other)
-    pieces = (w_down_own[None], down_across[None], down_far[None], down_near, down_far_across[None], down_near_across)
-    w_down_t = unpacked(place, pieces)
+    pieces = (w_down_own[None], both_across, down_far[None], down_near, down_far_across[None], down_near_across)
+    w_down_t = unpacked(place, pieces, 1)
 
     weights = (vecs, up_bias, w_up_all, w_down_t)
     residual_zero, normed_zero, hidden_zero, grad_zero, up_sum_zero, keep_zero, send_zero = feed(
@@ -959,110 +968,93 @@
     residual_one, normed_one, hidden_one, grad_one, up_sum_one, keep_one, send_one = feed(
         1, after(spliced, mine_zero), total_one, other_one, cots, *weights
     )
-    quarter = hidden_one.shape[1] // 3
-    a_keep, a_send, b_keep, b_send = grad_blocks(
-        grad_kernel, place, (quarter, 2 * quarter), normed_zero, normed_one, grad_zero, grad_one
-    )
-    a_got = across(a_send)
+    hidden_cols = hidden_one.shape[1]
     mine_one = add_low(keep_one, core(send_one))
+    far_one = over(mine_one)
+    b_keep, b_send = grad_blocks(
+        grad_kernel, place, (hidden_cols,), normed_zero, normed_one, grad_zero, grad_one
+    )
+    b_got = across(b_send)
     c_keep, c_send = grad_blocks(
-        cot_grad_kernel, after(place, a_send), (3 * quarter,), *cots, hidden_zero, hidden_one
-    )
-    mlp_keep, mlp_send = down_part((hidden_zero, after(hidden_one, a_send)), w_down_t)
-    total_zero = add_low(after(mine_zero, a_got, c_send, mlp_send), far_zero)
+        cot_grad_kernel, after(place, b_send), (hidden_cols,), *cots, hidden_zero, hidden_one
+    )
+    mlp_keep, mlp_send = down_part((hidden_zero, after(hidden_one, b_send)), w_down_t)
+    total_zero = add_low(after(mine_zero, c_send, mlp_send), far_zero, cost=0)
     other_zero = core(total_zero)
-    other_zero, mine_one = together(other_zero, mine_one)
     residual = (residual_zero, residual_one)
 
-    far_one = over(mine_one)
-    b_got = across(after(b_send, other_zero))
-    mlp_got = core(after(mlp_send, other_zero))
     res_zero, branch_zero, gatt_zero, delta_zero, sums_zero = branch_back(
         0, total_zero, other_zero, residual_zero, cots, vecs, w_proj_t, att_zero
     )
     dq_zero, *early = back(0, place, starts, queries, keys, values, log_zero, gatt_zero, delta_zero, ())
-    early[0], far_one, b_got, mlp_got = together(early[0], far_one, b_got, mlp_got)
-
-    total_one = add_low(mine_one, far_one)
+    c_got = across(after(c_send, other_zero))
+    total_one = add_low(after(mine_one, early[0], b_got), far_one)
     other_one = core(total_one)
-    c_got = across(after(c_send, b_got))
-    mlp_keep, mlp_send = fold(3, place, mlp_keep, mlp_got)
-    mlp_got = over(mlp_send)
-    b_keep, b_send = fold(5, place, a_keep, a_got, b_keep, b_got)
+    b_keep, b_send = fold(5, place, b_keep, after(b_got, total_one))
     b_got = near(b_send)
+    mlp_keep, mlp_send = fold(3, place, mlp_keep, core(after(mlp_send, other_zero)))
+    mlp_got = over(after(mlp_send, total_one))
     res_one, branch_one, gatt_one, delta_one, sums_one = branch_back(
         1, total_one, other_one, residual_one, cots, vecs, w_proj_t, att_one
     )
     dq_one, dk, dv = back(1, place, starts, queries, keys, values, log_one, gatt_one, delta_one, early)
-    dk, b_got, c_got, mlp_got = together(dk, b_got, c_got, mlp_got)
+    dk, b_got = together(dk, b_got)
 
     grad_residual = (res_zero, res_one)
-    shapes = (((4, shard_rows, 2 * head_cols), F32), ((4, shard_rows, 2 * head_cols), LOW)) * 2
-    d_keep, d_send, e_keep, e_send = call(
-        last_kernel,
-        shapes,
+    kinds = (((4, shard_rows, 2 * head_cols), F32), ((4, shard_rows, 2 * head_cols), LOW))
+    scratch = (pltpu.VMEM((width, 2 * head_cols), F32),)
+    d_keep, d_send = call(
+        last_kernel_one, kinds, place, normed, dq_zero, dq_one, branch_zero, branch_one, att_zero, att_one, scratch=scratch
+    )
+    d_got = across(after(d_send, dk))
+    c_keep, c_send = fold(5, place, c_keep, c_got)
+    c_got = near(c_send)
+    b_keep, b_send = fold(6, place, b_keep, b_got)
+    b_got = far(b_send)
+    keep, send_low, send_high, small, mixed_sums, picked = input_back(
+        place, thought_pos, (dq_zero, dq_one), dk, dv, w_in, xhat, grad_residual
+    )
+    got_low, got_high = core(send_low), core(send_high)
+    small = add_full(small, core(small))
+    small = add_full(small, over(small))
+    shape = (4, shard_rows + 8, 2 * head_cols)
+    e_keep, e_send = call(
+        last_kernel_two,
+        ((shape, F32), (shape, LOW)),
         place,
-        normed,
-        dq_zero,
-        dq_one,
+        after(normed, b_got),
         dk,
         dv,
-        branch_zero,
-        branch_one,
-        att_zero,
-        att_one,
-        scratch=(pltpu.VMEM((width, 4 * head_cols), F32),),
-        mib=12,
-    )
-    d_got = across(d_send)
-    c_keep, c_send = fold(5, place, c_keep, after(c_got, d_send))
-    c_got = near(c_send)
-    keep, send, small, mixed_sums, picked = input_back(
-        place, thought_pos, (dq_zero, dq_one), after(dk, d_send), dv, w_in, xhat, grad_residual
-    )
-    small = add_full(small, core(small))
-    small_got = over(small)
-    small_got, d_got, c_got = together(small_got, d_got, c_got)
-
-    e_got = across(after(e_send, d_got))
-    got = core(after(send, d_got))
-    keep, send = fold(3, place, keep, got)
-    got = over(send)
-    small = add_full(small, small_got)
-    d_keep, d_send = fold(5, place, d_keep, d_got)
-    d_got = near(d_send)
-    b_keep, b_send = fold(6, place, b_keep, after(b_got, c_got), c_keep, c_got)
-    b_got = far(b_send)
-    shape = (4, 8, 2 * head_cols)
-    vec_keep, vec_send = call(
-        slot_kernel,
-        ((shape, F32), (shape, LOW)),
-        place,
         small,
         sums_zero,
         sums_one,
         up_sum_zero,
         up_sum_one,
         mixed_sums,
-        scratch=(pltpu.VMEM((8, 4 * head_cols), F32),),
-    )
-    vec_got = across(vec_send)
+        scratch=(*scratch, pltpu.VMEM((8, 4 * head_cols), F32)),
+    )
+    e_got = across(e_send)
+    keep, send = fold_two(3, place, keep, got_low, got_high)
+    got = over(after(send, small))
+    d_keep, d_send = fold(5, place, d_keep, after(d_got, c_got))
+    d_got = near(d_send)
+    c_keep, c_send = fold(6, place, c_keep, after(c_got, d_send))
+    c_got = far(c_send)
+    e_got, d_got = together(e_got, d_got)
+
+    e_keep, e_send = fold(5, place, e_keep, e_got)
+    e_got = near(e_send)
+    d_keep, d_send = fold(6, place, d_keep, after(d_got, c_got))
+    d_got = far(d_send)
+
+    e_keep, e_send = fold(6, place, e_keep, after(e_got, d_got))
+    e_got = far(e_send)
     block_out = result(place, mlp_keep[0], mlp_got[0], residual, vecs)
-    e_got, d_got, vec_got, block_out = together(e_got, d_got, vec_got, block_out)
-
-    e_keep, e_send = fold(5, place, e_keep, e_got, vec_keep, vec_got)
-    e_got = near(e_send)
-    d_keep, d_send = fold(6, place, d_keep, d_got)
-    d_got = far(d_send)
-    grad_embed, grad_thoughts = output_side(
-        place, keep[0], got[0], spliced, grad_residual, vecs, thought_pos, thoughts, small, picked
-    )
-    grad_embed, e_got, d_got, b_got = together(grad_embed, e_got, d_got, b_got)
-
-    e_keep, e_send = fold(6, place, e_keep, e_got)
-    e_got = far(e_send)
-    grad_up, grad_down = parted(b_keep, b_got)
-    grad_down, e_got = together(grad_down, e_got)
+    grad_embed, grad_thoughts, grad_up, grad_down = output_side(
+        place, keep, got, spliced, grad_residual, vecs, thought_pos, thoughts, small, picked,
+        b_keep, b_got, c_keep, c_got,
+    )
+    grad_embed, block_out, e_got, d_got = together(grad_embed, block_out, e_got, d_got)
     grad_in, grad_proj, *small = call(
         finish_kernel,
         (
@@ -1121,14 +1113,14 @@
         )
         dqs.append(dq)
     grad_residual, grad_branch = zip(branches[0][:2], branches[1][:2])
-    keep, send, small, mixed_sums, picked = input_back(
+    keep, *send, small, mixed_sums, picked = input_back(
         place, thought_pos, dqs, *early, w_in, xhat, grad_residual
     )
     grad_mixed = jnp.concatenate([jnp.concatenate(dqs), *early], axis=1)
     small = small + swapped(small, "tensor", 1)
     small = small + swapped(small, "tensor", 2)
     grad_embed, grad_thoughts = output_side(
-        place, *own_sum(keep, send), spliced, grad_residual, vecs, thought_pos, thoughts, small, picked
+        place, *own_sum(keep, jnp.stack(send)), spliced, grad_residual, vecs, thought_pos, thoughts, small, picked
     )
     grad_in = plain_grad(shard_rows, normed, grad_mixed).reshape(shard_rows, 3, head_cols)
     grad_proj = plain_grad(shard_rows, *grad_branch, *atts)

time: 170 us -> 160 us (0.941)
  waiting for transfers between devices: 56.3 us -> 45.6 us
  local copies, waits for them, and re-layouts: 2.67 us -> 4.48 us
    ppermute x50 -> x49, waiting for transfers between devices: 56.3 us -> 45.6 us  [swapped(): lax.ppermute(array, axis, [(i, i ^ mask) for i in range(lax.axis_size(axi...]
    unnamed x16 -> x20, local copies, waits for them, and re-layouts: 1.97 us -> 3.79 us
    ppermute x50 -> x49, starting transfers between devices: 47.7 us -> 46.5 us  [swapped(): lax.ppermute(array, axis, [(i, i ^ mask) for i in range(lax.axis_size(axi...]
    pallas_call x48 -> x49, Pallas kernels: 60 us -> 60.1 us  [call(): pl.pallas_call(kernel, out_shape=tuple((jax.ShapeDtypeStruct(s, t) for s,...]
  transfers between devices with their start and end apart: 50 -> 49, of which waited for: 24 -> 21; matrix products, arithmetic and copies ran while one was open for 0% -> 0% of each run, Pallas kernels for 32% -> 37%
where the time goes in v3:
time: 160 us
  Pallas kernels  61.9 us (39%)
  starting transfers between devices  46.5 us (29%)
  waiting for transfers between devices  45.6 us (28%)
  local copies, waits for them, and re-layouts  4.48 us (3%)
    pallas_call x49, Pallas kernels, call(): pl.pallas_call(kernel, out_shape=tuple((jax.ShapeDtypeStruct(s, t) for s,...  60.1 us
    ppermute x49, starting transfers between devices, swapped(): lax.ppermute(array, axis, [(i, i ^ mask) for i in range(lax.axis_size(axi...  46.5 us
    ppermute x49, waiting for transfers between devices, swapped(): lax.ppermute(array, axis, [(i, i ^ mask) for i in range(lax.axis_size(axi...  45.6 us
    unnamed x20, local copies, waits for them, and re-layouts  3.79 us
  transfers between devices with their start and end apart: 49, of which 21 were waited for; matrix products, arithmetic and copies ran while one was open for 0% of the time, Pallas kernels for 37%

profile of v3, /device:TPU:0, one launch (start us, length us, event | category | flops | bytes accessed | tf_op | source)
XLA Modules:
  0.0 159.7 jit_solution(6053622155743840796)
XLA Ops:
  0.7 1.9 %shard_map.289.refs_0_ = bf16[104,768]{1,0:T(8,128)(2,1)} custom-call(bf16[3,96,192]{2,1,0:T(8,128)(2,1)} %refs_0_.1, bf16[192,96]{1,0:T(8,128)(2,1)} %refs_1_.1, bf16[1,96]{1,0:T(2,128)(2,1)} %bitcast.65, bf16[1,96]{1,0:T(2,128)(2,1)} %bitcast.66, bf16[1,96]{1,0:T(2,128)(2,1)} %bitcast.67, bf16[1,96]{1,0:T(2,128)(2,1)} %bitcast.68, bf16[1,96]{1,0:T(2,128)(2,1)} %bitcast.69, ...), custom_call_target="tpu_custom_call" | custom-call | flops 1000 | tf_op jit(solution)/shard_map/pallas_call | solution.py:721
  2.5 3.0 %collective-permute-start = (bf16[256,768]{1,0:T(8,128)(2,1)}, bf16[256,768]{1,0:T(8,128)(2,1)S(1)}, u32[]{:S(2)}, u32[]{:S(2)}) collective-permute-start(bf16[256,768]{1,0:T(8,128)(2,1)} %bitcast.50), channel_id=1, source_target_pairs={{0,2},{1,3},{2,0},{3,1},{4,6},{5,7},{6,4},{7,5},{8,10},{9,11},{10,... | collective-permute-start | bytes 1179656 | tf_op jit(solution)/shard_map/ppermute | solution.py:19
  5.5 1.5 collective-permute-start.2
  7.1 2.6 %collective-permute-start.1 = (bf16[104,768]{1,0:T(8,128)(2,1)}, bf16[104,768]{1,0:T(8,128)(2,1)S(1)}, u32[]{:S(2)}, u32[]{:S(2)}) collective-permute-start(bf16[104,768]{1,0:T(8,128)(2,1)} %shard_map.289.refs_0_), channel_id=1, source_target_pairs={{0,16},{4,20},{8,24},{12,28},{16,0},{20,4},{24,8},{28,12},{1,17},{... | collective-permute-start | bytes 479240 | tf_op jit(solution)/shard_map/ppermute | solution.py:19
  9.7 0.9 copy-done.4
  10.6 1.0 copy-done.5
  11.6 0.9 copy-done
  12.5 0.9 copy-done.2
  13.5 3.4 %collective-permute-done.1.b = bf16[104,768]{1,0:T(8,128)(2,1)S(1)} collective-permute-done((bf16[104,768]{1,0:T(8,128)(2,1)}, bf16[104,768]{1,0:T(8,128)(2,1)S(1)}, u32[]{:S(2)}, u32[]{:S(2)}) %collective-permute-start.1) | collective-permute-done | bytes 159776 | tf_op jit(solution)/shard_map/ppermute | solution.py:19
  18.3 1.5 collective-permute-start.6
  20.3 3.3 %collective-permute-start.5 = (bf16[96,768]{1,0:T(8,128)(2,1)S(1)}, bf16[96,768]{1,0:T(8,128)(2,1)S(1)}, u32[]{:S(2)}, u32[]{:S(2)}) collective-permute-start(bf16[96,768]{1,0:T(8,128)(2,1)S(1)} %copy-done.1), channel_id=1, source_target_pairs={{0,16},{4,20},{8,24},{12,28},{16,0},{20,4},{24,8},{28,12},{1,17},{... | collective-permute-start | bytes 442376 | tf_op jit(solution)/shard_map/ppermute | solution.py:19
  24.3 3.9 %collective-permute-done.5.b = bf16[96,768]{1,0:T(8,128)(2,1)S(1)} collective-permute-done((bf16[96,768]{1,0:T(8,128)(2,1)S(1)}, bf16[96,768]{1,0:T(8,128)(2,1)S(1)}, u32[]{:S(2)}, u32[]{:S(2)}) %collective-permute-start.5) | collective-permute-done | bytes 147488 | tf_op jit(solution)/shard_map/ppermute | solution.py:19
  28.1 2.0 %collective-permute-done.4 = bf16[104,768]{1,0:T(8,128)(2,1)} collective-permute-done((bf16[104,768]{1,0:T(8,128)(2,1)S(1)}, bf16[104,768]{1,0:T(8,128)(2,1)}, u32[]{:S(2)}, u32[]{:S(2)}) %collective-permute-start.4) | collective-permute-done | bytes 159776 | tf_op jit(solution)/shard_map/ppermute | solution.py:19
  31.5 2.0 %collective-permute-start.10 = (bf16[2,96,768]{2,1,0:T(8,128)(2,1)S(1)}, bf16[2,96,768]{2,1,0:T(8,128)(2,1)S(1)}, u32[]{:S(2)}, u32[]{:S(2)}) collective-permute-start(bf16[2,96,768]{2,1,0:T(8,128)(2,1)S(1)} %shard_map.298), channel_id=1, source_target_pairs={{0,8},{4,12},{8,0},{12,4},{16,24},{20,28},{24,16},{28,20},{1,9},{5... | collective-permute-start | bytes 884744 | tf_op jit(solution)/shard_map/ppermute | solution.py:19
  33.5 1.7 %collective-permute-start.11 = (bf16[96,768]{1,0:T(8,128)(2,1)S(1)}, bf16[96,768]{1,0:T(8,128)(2,1)S(1)}, u32[]{:S(2)}, u32[]{:S(2)}) collective-permute-start(bf16[96,768]{1,0:T(8,128)(2,1)S(1)} %bitcast.41), channel_id=1, source_target_pairs={{0,16},{4,20},{8,24},{12,28},{16,0},{20,4},{24,8},{28,12},{1,17},{... | collective-permute-start | bytes 442376 | tf_op jit(solution)/shard_map/ppermute | solution.py:19
  35.3 1.8 %shard_map.294 = (bf16[1024,768]{1,0:T(8,128)(2,1)S(1)}, f32[1024,768]{1,0:T(8,128)S(1)}) custom-call(s32[8]{0:T(128)S(1)} %dynamic-slice_bitcast_fusion.place, bf16[2,256,768]{2,1,0:T(8,128)(2,1)S(1)} %shard_map.293.x_zero, bf16[2,256,768]{2,1,0:T(8,128)(2,1)S(1)} %collective-permute-done.9.x_one, bf16[6,768]{1,0:T(8,128)(2,1)S(1)} %bitcast.57, ...), custom_call_target="tpu_custom_call" | custom-call | flops 1000 | tf_op jit(solution)/shard_map/pallas_call | solution.py:120
  37.1 3.8 %collective-permute-done.8.refs_5_ = bf16[2,104,768]{2,1,0:T(8,128)(2,1)S(1)} collective-permute-done((bf16[2,104,768]{2,1,0:T(8,128)(2,1)S(1)}, bf16[2,104,768]{2,1,0:T(8,128)(2,1)S(1)}, u32[]{:S(2)}, u32[]{:S(2)}) %collective-permute-start.8) | collective-permute-done | bytes 319520 | tf_op jit(solution)/shard_map/ppermute | solution.py:19
  41.3 1.2 shard_map.295
  42.6 1.4 shard_map.296
  44.0 3.6 %shard_map.297 = (bf16[512,192]{1,0:T(8,128)(2,1)S(1)}, f32[8,512]{1,0:T(8,128)S(1)}, f32[256,768]{1,0:T(8,128)S(1)}, bf16[256,768]{1,0:T(8,128)(2,1)S(1)}) custom-call(s32[8]{0:T(128)S(1)} %dynamic-slice_bitcast_fusion.place, s32[2]{0:T(128)S(1)} %bitcast.59, bf16[1024,192]{1,0:T(8,128)(2,1)S(1)} %get-tuple-element.198.q_ref, ...), custom_call_target="tpu_custom_call" | custom-call | flops 1000 | tf_op jit(solution)/shard_map/pallas_call | solution.py:120
  47.7 1.7 %collective-permute-done.13.b = bf16[256,768]{1,0:T(8,128)(2,1)S(1)} collective-permute-done((bf16[256,768]{1,0:T(8,128)(2,1)S(1)}, bf16[256,768]{1,0:T(8,128)(2,1)S(1)}, u32[]{:S(2)}, u32[]{:S(2)}) %collective-permute-start.13) | collective-permute-done | bytes 393248 | tf_op jit(solution)/shard_map/ppermute | solution.py:19
  49.5 1.6 collective-permute-start.14
  51.1 2.0 %collective-permute-start.17 = (bf16[2,96,768]{2,1,0:T(8,128)(2,1)S(1)}, bf16[2,96,768]{2,1,0:T(8,128)(2,1)S(1)}, u32[]{:S(2)}, u32[]{:S(2)}) collective-permute-start(bf16[2,96,768]{2,1,0:T(8,128)(2,1)S(1)} %shard_map.301), channel_id=1, source_target_pairs={{0,8},{4,12},{8,0},{12,4},{16,24},{20,28},{24,16},{28,20},{1,9},{5... | collective-permute-start | bytes 884744 | tf_op jit(solution)/shard_map/ppermute | solution.py:19
  53.2 1.5 collective-permute-start.15
  55.9 6.4 %shard_map.300 = (bf16[512,192]{1,0:T(8,128)(2,1)S(1)}, f32[8,512]{1,0:T(8,128)S(1)}, f32[256,768]{1,0:T(8,128)S(1)}, bf16[256,768]{1,0:T(8,128)(2,1)S(1)}) custom-call(s32[8]{0:T(128)S(1)} %dynamic-slice_bitcast_fusion.place, s32[2]{0:T(128)S(1)} %bitcast.60, bf16[1024,192]{1,0:T(8,128)(2,1)S(1)} %get-tuple-element.198.q_ref, ...), custom_call_target="tpu_custom_call" | custom-call | flops 1000 | tf_op jit(solution)/shard_map/pallas_call | solution.py:120
  62.2 2.6 %collective-permute-done.16 = bf16[96,768]{1,0:T(8,128)(2,1)S(1)} collective-permute-done((bf16[96,768]{1,0:T(8,128)(2,1)S(1)}, bf16[96,768]{1,0:T(8,128)(2,1)S(1)}, u32[]{:S(2)}, u32[]{:S(2)}) %collective-permute-start.16) | collective-permute-done | bytes 147488 | tf_op jit(solution)/shard_map/ppermute | solution.py:19
  65.6 1.1 collective-permute-done.21.b
  67.3 1.5 collective-permute-start.19
  69.5 6.6 %collective-permute-done.19.refs_5_ = bf16[2,96,768]{2,1,0:T(8,128)(2,1)S(1)} collective-permute-done((bf16[2,96,768]{2,1,0:T(8,128)(2,1)S(1)}, bf16[2,96,768]{2,1,0:T(8,128)(2,1)S(1)}, u32[]{:S(2)}, u32[]{:S(2)}) %collective-permute-start.19) | collective-permute-done | bytes 294944 | tf_op jit(solution)/shard_map/ppermute | solution.py:19
  76.7 2.8 %shard_map.306 = (f32[512,768]{1,0:T(8,128)S(1)}, bf16[512,768]{1,0:T(8,128)(2,1)S(1)}, bf16[512,768]{1,0:T(8,128)(2,1)S(1)}, bf16[512,768]{1,0:T(8,128)(2,1)S(1...) custom-call(bf16[1024,768]{1,0:T(8,128)(2,1)S(1)} %get-tuple-element.231.spliced, ...), custom_call_target="tpu_custom_call" | custom-call | flops 1000 | tf_op jit(solution)/shard_map/pallas_call | solution.py:120
  80.3 1.0 collective-permute-done.23.b
  81.4 1.5 collective-permute-start.25
  82.9 2.8 %shard_map.310 = (f32[512,768]{1,0:T(8,128)S(1)}, bf16[512,768]{1,0:T(8,128)(2,1)S(1)}, bf16[512,768]{1,0:T(8,128)(2,1)S(1)}, bf16[512,768]{1,0:T(8,128)(2,1)S(1...) custom-call(bf16[1024,768]{1,0:T(8,128)(2,1)S(1)} %get-tuple-element.231.spliced, ...), custom_call_target="tpu_custom_call" | custom-call | flops 1000 | tf_op jit(solution)/shard_map/pallas_call | solution.py:120
  85.8 2.1 %shard_map.311 = (f32[4,96,768]{2,1,0:T(8,128)S(1)}, bf16[4,96,768]{2,1,0:T(8,128)(2,1)S(1)}) custom-call(s32[8]{0:T(128)S(1)} %dynamic-slice_bitcast_fusion.place, bf16[512,768]{1,0:T(8,128)(2,1)S(1)} %get-tuple-element.230.refs_0_, bf16[512,768]{1,0:T(8,128)(2,1)S(1)} %get-tuple-element.233.refs_1_, bf16[512,768]{1,0:T(8,128)(2,1)S(1)} %get-tuple-element.234.refs_2_, ...), custom_call_target="tpu_custom_call" | custom-call | flops 1000 | tf_op jit(solution)/shard_map/pallas_call | solution.py:120
  87.9 1.6 collective-permute-start.28
  89.5 1.4 shard_map.313
  90.9 2.1 %shard_map.312 = (f32[4,96,768]{2,1,0:T(8,128)S(1)}, bf16[4,96,768]{2,1,0:T(8,128)(2,1)S(1)}) custom-call(s32[8]{0:T(128)S(1)} %dynamic-slice_bitcast_fusion.place, bf16[2,256,768]{2,1,0:T(8,128)(2,1)S(1)} %shard_map.304.cot_zero, bf16[2,256,768]{2,1,0:T(8,128)(2,1)S(1)} %collective-permute-done.20.cot_one, ...), custom_call_target="tpu_custom_call" | custom-call | flops 1000 | tf_op jit(solution)/shard_map/pallas_call | solution.py:120
  93.5 0.9 collective-permute-start.29
  95.2 1.0 collective-permute-start.38
  96.2 2.2 %shard_map.315 = (f32[512,768]{1,0:T(8,128)S(1)}, bf16[512,768]{1,0:T(8,128)(2,1)S(1)}, bf16[512,192]{1,0:T(8,128)(2,1)S(1)}, f32[8,512]{1,0:T(8,128)S(1)}, f32[8,768]{1,0:T(8,128)S(1)}) custom-call(bf16[256,768]{1,0:T(8,128)(2,1)S(1)} %shard_map.314.total, bf16[256,768]{1,0:T(8,128)(2,1)S(1)} %collective-permute-done.26.other, ...), custom_call_target="tpu_custom_call" | custom-call | flops 1000 | tf_op jit(solution)/shard_map/pallas_call | solution.py:120
  98.4 3.6 %shard_map.316 = (bf16[512,192]{1,0:T(8,128)(2,1)S(1)}, f32[512,192]{1,0:T(8,128)S(1)}, f32[512,192]{1,0:T(8,128)S(1)}) custom-call(s32[8]{0:T(128)S(1)} %dynamic-slice_bitcast_fusion.place, s32[2]{0:T(128)S(1)} %bitcast.61, bf16[1024,192]{1,0:T(8,128)(2,1)S(1)} %get-tuple-element.198.q_ref, bf16[1024,192]{1,0:T(8,128)(2,1)S(1)} %get-tuple-element.199.k_ref, ...), custom_call_target="tpu_custom_call" | custom-call | flops 1000 | tf_op jit(solution)/shard_map/pallas_call | solution.py:120
  102.0 2.1 %collective-permute-done.28.refs_1_ = bf16[4,96,768]{2,1,0:T(8,128)(2,1)S(1)} collective-permute-done((bf16[4,96,768]{2,1,0:T(8,128)(2,1)S(1)}, bf16[4,96,768]{2,1,0:T(8,128)(2,1)S(1)}, u32[]{:S(2)}, u32[]{:S(2)}) %collective-permute-start.28) | collective-permute-done | bytes 589856 | tf_op jit(solution)/shard_map/ppermute | solution.py:19
  106.8 2.1 %shard_map.319 = (f32[512,768]{1,0:T(8,128)S(1)}, bf16[512,768]{1,0:T(8,128)(2,1)S(1)}, bf16[512,192]{1,0:T(8,128)(2,1)S(1)}, f32[8,512]{1,0:T(8,128)S(1)}, f32[8,768]{1,0:T(8,128)S(1)}) custom-call(bf16[256,768]{1,0:T(8,128)(2,1)S(1)} %shard_map.318.total, bf16[256,768]{1,0:T(8,128)(2,1)S(1)} %collective-permute-done.30.other, ...), custom_call_target="tpu_custom_call" | custom-call | flops 1000 | tf_op jit(solution)/shard_map/pallas_call | solution.py:120
  108.8 6.5 %shard_map.320 = (bf16[512,192]{1,0:T(8,128)(2,1)S(1)}, bf16[1024,192]{1,0:T(8,128)(2,1)S(1)}, bf16[1024,192]{1,0:T(8,128)(2,1)S(1)}) custom-call(s32[8]{0:T(128)S(1)} %dynamic-slice_bitcast_fusion.place, s32[2]{0:T(128)S(1)} %bitcast.62, bf16[1024,192]{1,0:T(8,128)(2,1)S(1)} %get-tuple-element.198.q_ref, bf16[1024,192]{1,0:T(8,128)(2,1)S(1)} %get-tuple-element.199.k_ref, ...), custom_call_target="tpu_custom_call" | custom-call | flops 1000 | tf_op jit(solution)/shard_map/pallas_call | solution.py:120
  115.9 2.4 %collective-permute-start.37 = (bf16[1,96,768]{2,1,0:T(8,128)(2,1)S(1)}, bf16[1,96,768]{2,1,0:T(8,128)(2,1)S(1)}, u32[]{:S(2)}, u32[]{:S(2)}) collective-permute-start(bf16[1,96,768]{2,1,0:T(8,128)(2,1)S(1)} %get-tuple-element.279), channel_id=1, source_target_pairs={{0,16},{4,20},{8,24},{12,28},{16,0},{20,4},{24,8},{28,12},{1,17},{... | collective-permute-start | bytes 442376 | tf_op jit(solution)/shard_map/ppermute | solution.py:19
  118.4 2.2 %shard_map.322 = (f32[2,256,768]{2,1,0:T(8,128)S(1)}, bf16[256,768]{1,0:T(8,128)(2,1)S(1)}, bf16[256,768]{1,0:T(8,128)(2,1)S(1)}, f32[8,768]{1,0:T(8,128)S(1)}, ...) custom-call(s32[8]{0:T(128)S(1)} %dynamic-slice_bitcast_fusion.place, s32[6]{0:T(128)S(1)} %bitcast.63, ...), custom_call_target="tpu_custom_call" | custom-call | flops 1000 | tf_op jit(solution)/shard_map/pallas_call | solution.py:120
  122.0 1.1 collective-permute-start.35
  123.1 1.7 %shard_map.328 = (f32[4,96,384]{2,1,0:T(8,128)S(1)}, bf16[4,96,384]{2,1,0:T(8,128)(2,1)S(1)}) custom-call(s32[8]{0:T(128)S(1)} %dynamic-slice_bitcast_fusion.place, bf16[1024,768]{1,0:T(8,128)(2,1)S(1)} %get-tuple-element.301.normed, bf16[512,192]{1,0:T(8,128)(2,1)S(1)} %get-tuple-element.248.dq_zero, bf16[512,192]{1,0:T(8,128)(2,1)S(1)} %get-tuple-element.259.dq_one, ...), custom_call_target="tpu_custom_call" | custom-call | flops 1000 | tf_op jit(solution)/shard_map/pallas_call | solution.py:120
  125.9 1.2 collective-permute-start.40
  127.1 1.0 collective-permute-start.39
  128.1 1.9 %shard_map.334 = (f32[4,104,384]{2,1,0:T(8,128)S(1)}, bf16[4,104,384]{2,1,0:T(8,128)(2,1)S(1)}) custom-call(s32[8]{0:T(128)S(1)} %dynamic-slice_bitcast_fusion.place, bf16[1024,768]{1,0:T(8,128)(2,1)S(1)} %get-tuple-element.301.normed, bf16[1024,192]{1,0:T(8,128)(2,1)S(1)} %get-tuple-element.264.dk, bf16[1024,192]{1,0:T(8,128)(2,1)S(1)} %get-tuple-element.265.dv, ...), custom_call_target="tpu_custom_call" | custom-call | flops 1000 | tf_op jit(solution)/shard_map/pallas_call | solution.py:120
  131.5 1.1 collective-permute-start.43
  133.4 1.1 collective-permute-start.36
  134.4 1.4 collective-permute-done.40.refs_1_
  136.4 1.0 collective-permute-start.45
  138.1 1.0 collective-permute-start.41
  139.0 2.4 %collective-permute-done.44.refs_1_ = bf16[4,104,384]{2,1,0:T(8,128)(2,1)S(1)} collective-permute-done((bf16[4,104,384]{2,1,0:T(8,128)(2,1)S(1)}, bf16[4,104,384]{2,1,0:T(8,128)(2,1)S(1)}, u32[]{:S(2)}, u32[]{:S(2)}) %collective-permute-start.44) | collective-permute-done | bytes 319520 | tf_op jit(solution)/shard_map/ppermute | solution.py:19
  141.4 1.6 collective-permute-done.45.refs_1_
  144.4 2.3 %collective-permute-done.41.rest_3_ = bf16[1,96,768]{2,1,0:T(8,128)(2,1)S(1)} collective-permute-done((bf16[1,96,768]{2,1,0:T(8,128)(2,1)S(1)}, bf16[1,96,768]{2,1,0:T(8,128)(2,1)S(1)}, u32[]{:S(2)}, u32[]{:S(2)}) %collective-permute-start.41) | collective-permute-done | bytes 147488 | tf_op jit(solution)/shard_map/ppermute | solution.py:19
  147.5 5.2 %collective-permute-done.47.d_got = bf16[1,96,384]{2,1,0:T(8,128)(2,1)S(1)} collective-permute-done((bf16[1,96,384]{2,1,0:T(8,128)(2,1)S(1)}, bf16[1,96,384]{2,1,0:T(8,128)(2,1)S(1)}, u32[]{:S(2)}, u32[]{:S(2)}) %collective-permute-start.47) | collective-permute-done | bytes 73760 | tf_op jit(solution)/shard_map/ppermute | solution.py:19
  153.5 1.5 shard_map.333
  155.0 2.3 %shard_map.331 = (f32[256,768]{1,0:T(8,128)}, f32[6,1,192]{2,1,0:T(1,128)}, f32[96,768]{1,0:T(8,128)}, f32[96,768]{1,0:T(8,128)}) custom-call(s32[8]{0:T(128)S(1)} %dynamic-slice_bitcast_fusion.place, f32[256,768]{1,0:T(8,128)S(1)} %get-tuple-element.271.keep, bf16[256,768]{1,0:T(8,128)(2,1)S(1)} %collective-permute-done.36.got, ...), custom_call_target="tpu_custom_call" | custom-call | flops 1000 | tf_op jit(solution)/shard_map/pallas_call | solution.py:120
  157.2 1.5 collective-permute-done.48.e_got
  158.8 0.9 shard_map.338
  (105 shorter events, 22.8 us)
Async XLA Ops:
  0.6 19.7 %copy-start.1 = (bf16[96,768]{1,0:T(8,128)(2,1)S(1)}, bf16[96,768]{1,0:T(8,128)(2,1)}, u32[]{:S(2)}) copy-start(bf16[96,768]{1,0:T(8,128)(2,1)} %a.2) | copy-start | bytes 442372
  2.5 14.4 %collective-permute-start = (bf16[256,768]{1,0:T(8,128)(2,1)}, bf16[256,768]{1,0:T(8,128)(2,1)S(1)}, u32[]{:S(2)}, u32[]{:S(2)}) collective-permute-start(bf16[256,768]{1,0:T(8,128)(2,1)} %bitcast.50), channel_id=1, source_target_pairs={{0,2},{1,3},{2,0},{3,1},{4,6},{5,7},{6,4},{7,5},{8,10},{9,11},{10,... | collective-permute-start | bytes 1179656 | tf_op jit(solution)/shard_map/ppermute | solution.py:19
  5.5 8.0 %collective-permute-start.2 = (bf16[104,768]{1,0:T(8,128)(2,1)}, bf16[104,768]{1,0:T(8,128)(2,1)S(1)}, u32[]{:S(2)}, u32[]{:S(2)}) collective-permute-start(bf16[104,768]{1,0:T(8,128)(2,1)} %shard_map.289.refs_0_), channel_id=1, source_target_pairs={{0,4},{4,0},{8,12},{12,8},{16,20},{20,16},{24,28},{28,24},{1,5},{5... | collective-permute-start | bytes 479240 | tf_op jit(solution)/shard_map/ppermute | solution.py:19
  7.1 9.8 %collective-permute-start.1 = (bf16[104,768]{1,0:T(8,128)(2,1)}, bf16[104,768]{1,0:T(8,128)(2,1)S(1)}, u32[]{:S(2)}, u32[]{:S(2)}) collective-permute-start(bf16[104,768]{1,0:T(8,128)(2,1)} %shard_map.289.refs_0_), channel_id=1, source_target_pairs={{0,16},{4,20},{8,24},{12,28},{16,0},{20,4},{24,8},{28,12},{1,17},{... | collective-permute-start | bytes 479240 | tf_op jit(solution)/shard_map/ppermute | solution.py:19
  9.6 0.9 copy-start.4
  10.6 1.0 copy-start.5
  11.6 0.9 copy-start
  12.5 0.9 copy-start.2
  13.5 20.1 %copy-start.3 = (bf16[768,96]{0,1:T(8,128)(2,1)S(1)}, bf16[768,96]{0,1:T(8,128)(2,1)}, u32[]{:S(2)}) copy-start(bf16[768,96]{0,1:T(8,128)(2,1)} %param.32) | copy-start | bytes 442372
  13.5 21.8 %copy-start.7 = (bf16[1,6,768]{2,1,0:T(8,128)(2,1)S(1)}, bf16[1,6,768]{2,1,0:T(8,128)(2,1)}, u32[]{:S(2)}) copy-start(bf16[1,6,768]{2,1,0:T(8,128)(2,1)} %param.19) | copy-start | bytes 27652
  13.5 21.8 %copy-start.9 = (s32[1,6]{1,0:T(1,128)S(1)}, s32[1,6]{1,0:T(1,128)}, u32[]{:S(2)}) copy-start(s32[1,6]{1,0:T(1,128)} %thought_pos.3) | copy-start | bytes 76
  16.9 13.3 %collective-permute-start.7 = (bf16[256,768]{1,0:T(8,128)(2,1)}, bf16[256,768]{1,0:T(8,128)(2,1)S(1)}, u32[]{:S(2)}, u32[]{:S(2)}) collective-permute-start(bf16[256,768]{1,0:T(8,128)(2,1)} %bitcast.52), channel_id=1, source_target_pairs={{0,2},{1,3},{2,0},{3,1},{4,6},{5,7},{6,4},{7,5},{8,10},{9,11},{10,... | collective-permute-start | bytes 1179656 | tf_op jit(solution)/shard_map/ppermute | solution.py:19
  17.5 12.7 %collective-permute-start.3 = (bf16[2,104,768]{2,1,0:T(8,128)(2,1)S(1)}, bf16[2,104,768]{2,1,0:T(8,128)(2,1)S(1)}, u32[]{:S(2)}, u32[]{:S(2)}) collective-permute-start(bf16[2,104,768]{2,1,0:T(8,128)(2,1)S(1)} %shard_map.292), channel_id=1, source_target_pairs={{0,8},{4,12},{8,0},{12,4},{16,24},{20,28},{24,16},{28,20},{1,9},{5... | collective-permute-start | bytes 958472 | tf_op jit(solution)/shard_map/ppermute | solution.py:19
  18.3 11.9 %collective-permute-start.6 = (bf16[2,96,768]{2,1,0:T(8,128)(2,1)S(1)}, bf16[2,96,768]{2,1,0:T(8,128)(2,1)S(1)}, u32[]{:S(2)}, u32[]{:S(2)}) collective-permute-start(bf16[2,96,768]{2,1,0:T(8,128)(2,1)S(1)} %shard_map.291), channel_id=1, source_target_pairs={{0,4},{4,0},{8,12},{12,8},{16,20},{20,16},{24,28},{28,24},{1,5},{5... | collective-permute-start | bytes 884744 | tf_op jit(solution)/shard_map/ppermute | solution.py:19
  19.8 10.4 %collective-permute-start.4 = (bf16[104,768]{1,0:T(8,128)(2,1)S(1)}, bf16[104,768]{1,0:T(8,128)(2,1)}, u32[]{:S(2)}, u32[]{:S(2)}) collective-permute-start(bf16[104,768]{1,0:T(8,128)(2,1)S(1)} %collective-permute-done.1.b), channel_id=1, source_target_pairs={{0,4},{4,0},{8,12},{12,8},{16,20},{20,16},{24,28},{28,24},{1,5},{5... | collective-permute-start | bytes 479240 | tf_op jit(solution)/shard_map/ppermute | solution.py:19
  20.3 7.8 %collective-permute-start.5 = (bf16[96,768]{1,0:T(8,128)(2,1)S(1)}, bf16[96,768]{1,0:T(8,128)(2,1)S(1)}, u32[]{:S(2)}, u32[]{:S(2)}) collective-permute-start(bf16[96,768]{1,0:T(8,128)(2,1)S(1)} %copy-done.1), channel_id=1, source_target_pairs={{0,16},{4,20},{8,24},{12,28},{16,0},{20,4},{24,8},{28,12},{1,17},{... | collective-permute-start | bytes 442376 | tf_op jit(solution)/shard_map/ppermute | solution.py:19
  30.8 4.4 %collective-permute-start.9 = (bf16[2,256,768]{2,1,0:T(8,128)(2,1)S(1)}, bf16[2,256,768]{2,1,0:T(8,128)(2,1)S(1)}, u32[]{:S(2)}, u32[]{:S(2)}) collective-permute-start(bf16[2,256,768]{2,1,0:T(8,128)(2,1)S(1)} %shard_map.293.x_zero), channel_id=1, source_target_pairs={{0,1},{1,0},{2,3},{3,2},{4,5},{5,4},{6,7},{7,6},{8,9},{9,8},{10,11... | collective-permute-start | bytes 2359304 | tf_op jit(solution)/shard_map/ppermute | solution.py:19
  30.9 10.0 %collective-permute-start.8 = (bf16[2,104,768]{2,1,0:T(8,128)(2,1)S(1)}, bf16[2,104,768]{2,1,0:T(8,128)(2,1)S(1)}, u32[]{:S(2)}, u32[]{:S(2)}) collective-permute-start(bf16[2,104,768]{2,1,0:T(8,128)(2,1)S(1)} %collective-permute-done.3.refs_3_), channel_id=1, source_target_pairs={{0,4},{4,0},{8,12},{12,8},{16,20},{20,16},{24,28},{28,24},{1,5},{5... | collective-permute-start | bytes 958472 | tf_op jit(solution)/shard_map/ppermute | solution.py:19
  31.5 16.2 %collective-permute-start.10 = (bf16[2,96,768]{2,1,0:T(8,128)(2,1)S(1)}, bf16[2,96,768]{2,1,0:T(8,128)(2,1)S(1)}, u32[]{:S(2)}, u32[]{:S(2)}) collective-permute-start(bf16[2,96,768]{2,1,0:T(8,128)(2,1)S(1)} %shard_map.298), channel_id=1, source_target_pairs={{0,8},{4,12},{8,0},{12,4},{16,24},{20,28},{24,16},{28,20},{1,9},{5... | collective-permute-start | bytes 884744 | tf_op jit(solution)/shard_map/ppermute | solution.py:19
  33.5 14.1 %collective-permute-start.11 = (bf16[96,768]{1,0:T(8,128)(2,1)S(1)}, bf16[96,768]{1,0:T(8,128)(2,1)S(1)}, u32[]{:S(2)}, u32[]{:S(2)}) collective-permute-start(bf16[96,768]{1,0:T(8,128)(2,1)S(1)} %bitcast.41), channel_id=1, source_target_pairs={{0,16},{4,20},{8,24},{12,28},{16,0},{20,4},{24,8},{28,12},{1,17},{... | collective-permute-start | bytes 442376 | tf_op jit(solution)/shard_map/ppermute | solution.py:19
  40.8 6.8 %collective-permute-start.12 = (bf16[96,768]{1,0:T(8,128)(2,1)S(1)}, bf16[96,768]{1,0:T(8,128)(2,1)S(1)}, u32[]{:S(2)}, u32[]{:S(2)}) collective-permute-start(bf16[96,768]{1,0:T(8,128)(2,1)S(1)} %collective-permute-done.5.b), channel_id=1, source_target_pairs={{0,4},{4,0},{8,12},{12,8},{16,20},{20,16},{24,28},{28,24},{1,5},{5... | collective-permute-start | bytes 442376 | tf_op jit(solution)/shard_map/ppermute | solution.py:19
  42.6 1.4 copy-start.8
  47.6 7.6 %copy-start.6 = (bf16[1,256,768]{2,1,0:T(8,128)(2,1)S(1)}, bf16[1,256,768]{2,1,0:T(8,128)(2,1)}, u32[]{:S(2)}) copy-start(bf16[1,256,768]{2,1,0:T(8,128)(2,1)} %param.34) | copy-start | bytes 1179652
  47.7 1.8 %collective-permute-start.13 = (bf16[256,768]{1,0:T(8,128)(2,1)S(1)}, bf16[256,768]{1,0:T(8,128)(2,1)S(1)}, u32[]{:S(2)}, u32[]{:S(2)}) collective-permute-start(bf16[256,768]{1,0:T(8,128)(2,1)S(1)} %get-tuple-element.208), channel_id=1, source_target_pairs={{0,1},{1,0},{2,3},{3,2},{4,5},{5,4},{6,7},{7,6},{8,9},{9,8},{10,11... | collective-permute-start | bytes 1179656 | tf_op jit(solution)/shard_map/ppermute | solution.py:19
  49.5 15.3 %collective-permute-start.14 = (bf16[256,768]{1,0:T(8,128)(2,1)S(1)}, bf16[256,768]{1,0:T(8,128)(2,1)S(1)}, u32[]{:S(2)}, u32[]{:S(2)}) collective-permute-start(bf16[256,768]{1,0:T(8,128)(2,1)S(1)} %shard_map.299.a), channel_id=1, source_target_pairs={{0,2},{1,3},{2,0},{3,1},{4,6},{5,7},{6,4},{7,5},{8,10},{9,11},{10,... | collective-permute-start | bytes 1179656 | tf_op jit(solution)/shard_map/ppermute | solution.py:19
  51.1 13.7 %collective-permute-start.17 = (bf16[2,96,768]{2,1,0:T(8,128)(2,1)S(1)}, bf16[2,96,768]{2,1,0:T(8,128)(2,1)S(1)}, u32[]{:S(2)}, u32[]{:S(2)}) collective-permute-start(bf16[2,96,768]{2,1,0:T(8,128)(2,1)S(1)} %shard_map.301), channel_id=1, source_target_pairs={{0,8},{4,12},{8,0},{12,4},{16,24},{20,28},{24,16},{28,20},{1,9},{5... | collective-permute-start | bytes 884744 | tf_op jit(solution)/shard_map/ppermute | solution.py:19
  53.2 11.7 %collective-permute-start.15 = (bf16[2,96,768]{2,1,0:T(8,128)(2,1)S(1)}, bf16[2,96,768]{2,1,0:T(8,128)(2,1)S(1)}, u32[]{:S(2)}, u32[]{:S(2)}) collective-permute-start(bf16[2,96,768]{2,1,0:T(8,128)(2,1)S(1)} %collective-permute-done.10.refs_3_), channel_id=1, source_target_pairs={{0,4},{4,0},{8,12},{12,8},{16,20},{20,16},{24,28},{28,24},{1,5},{5... | collective-permute-start | bytes 884744 | tf_op jit(solution)/shard_map/ppermute | solution.py:19
  54.7 10.1 %collective-permute-start.16 = (bf16[96,768]{1,0:T(8,128)(2,1)S(1)}, bf16[96,768]{1,0:T(8,128)(2,1)S(1)}, u32[]{:S(2)}, u32[]{:S(2)}) collective-permute-start(bf16[96,768]{1,0:T(8,128)(2,1)S(1)} %collective-permute-done.11.b), channel_id=1, source_target_pairs={{0,4},{4,0},{8,12},{12,8},{16,20},{20,16},{24,28},{28,24},{1,5},{5... | collective-permute-start | bytes 442376 | tf_op jit(solution)/shard_map/ppermute | solution.py:19
  55.8 13.7 %collective-permute-start.20 = (bf16[2,256,768]{2,1,0:T(8,128)(2,1)S(1)}, bf16[2,256,768]{2,1,0:T(8,128)(2,1)S(1)}, u32[]{:S(2)}, u32[]{:S(2)}) collective-permute-start(bf16[2,256,768]{2,1,0:T(8,128)(2,1)S(1)} %shard_map.304.cot_zero), channel_id=1, source_target_pairs={{0,1},{1,0},{2,3},{3,2},{4,5},{5,4},{6,7},{7,6},{8,9},{9,8},{10,11... | collective-permute-start | bytes 2359304 | tf_op jit(solution)/shard_map/ppermute | solution.py:19
  64.8 1.8 %collective-permute-start.21 = (bf16[256,768]{1,0:T(8,128)(2,1)S(1)}, bf16[256,768]{1,0:T(8,128)(2,1)S(1)}, u32[]{:S(2)}, u32[]{:S(2)}) collective-permute-start(bf16[256,768]{1,0:T(8,128)(2,1)S(1)} %get-tuple-element.228), channel_id=1, source_target_pairs={{0,1},{1,0},{2,3},{3,2},{4,5},{5,4},{6,7},{7,6},{8,9},{9,8},{10,11... | collective-permute-start | bytes 1179656 | tf_op jit(solution)/shard_map/ppermute | solution.py:19
  65.0 11.1 %collective-permute-start.18 = (bf16[256,768]{1,0:T(8,128)(2,1)S(1)}, bf16[256,768]{1,0:T(8,128)(2,1)S(1)}, u32[]{:S(2)}, u32[]{:S(2)}) collective-permute-start(bf16[256,768]{1,0:T(8,128)(2,1)S(1)} %shard_map.302.total), channel_id=1, source_target_pairs={{0,1},{1,0},{2,3},{3,2},{4,5},{5,4},{6,7},{7,6},{8,9},{9,8},{10,11... | collective-permute-start | bytes 1179656 | tf_op jit(solution)/shard_map/ppermute | solution.py:19
  66.7 12.8 %collective-permute-start.22 = (bf16[256,768]{1,0:T(8,128)(2,1)S(1)}, bf16[256,768]{1,0:T(8,128)(2,1)S(1)}, u32[]{:S(2)}, u32[]{:S(2)}) collective-permute-start(bf16[256,768]{1,0:T(8,128)(2,1)S(1)} %shard_map.307.a), channel_id=1, source_target_pairs={{0,2},{1,3},{2,0},{3,1},{4,6},{5,7},{6,4},{7,5},{8,10},{9,11},{10,... | collective-permute-start | bytes 1179656 | tf_op jit(solution)/shard_map/ppermute | solution.py:19
  67.3 8.8 %collective-permute-start.19 = (bf16[2,96,768]{2,1,0:T(8,128)(2,1)S(1)}, bf16[2,96,768]{2,1,0:T(8,128)(2,1)S(1)}, u32[]{:S(2)}, u32[]{:S(2)}) collective-permute-start(bf16[2,96,768]{2,1,0:T(8,128)(2,1)S(1)} %collective-permute-done.17.refs_3_), channel_id=1, source_target_pairs={{0,4},{4,0},{8,12},{12,8},{16,20},{20,16},{24,28},{28,24},{1,5},{5... | collective-permute-start | bytes 884744 | tf_op jit(solution)/shard_map/ppermute | solution.py:19
  79.5 1.8 %collective-permute-start.23 = (bf16[256,768]{1,0:T(8,128)(2,1)S(1)}, bf16[256,768]{1,0:T(8,128)(2,1)S(1)}, u32[]{:S(2)}, u32[]{:S(2)}) collective-permute-start(bf16[256,768]{1,0:T(8,128)(2,1)S(1)} %get-tuple-element.229), channel_id=1, source_target_pairs={{0,1},{1,0},{2,3},{3,2},{4,5},{5,4},{6,7},{7,6},{8,9},{9,8},{10,11... | collective-permute-start | bytes 1179656 | tf_op jit(solution)/shard_map/ppermute | solution.py:19
  79.7 3.2 %collective-permute-start.24 = (bf16[256,768]{1,0:T(8,128)(2,1)S(1)}, bf16[256,768]{1,0:T(8,128)(2,1)S(1)}, u32[]{:S(2)}, u32[]{:S(2)}) collective-permute-start(bf16[256,768]{1,0:T(8,128)(2,1)S(1)} %shard_map.309.total), channel_id=1, source_target_pairs={{0,1},{1,0},{2,3},{3,2},{4,5},{5,4},{6,7},{7,6},{8,9},{9,8},{10,11... | collective-permute-start | bytes 1179656 | tf_op jit(solution)/shard_map/ppermute | solution.py:19
  81.4 11.7 %collective-permute-start.25 = (bf16[256,768]{1,0:T(8,128)(2,1)S(1)}, bf16[256,768]{1,0:T(8,128)(2,1)S(1)}, u32[]{:S(2)}, u32[]{:S(2)}) collective-permute-start(bf16[256,768]{1,0:T(8,128)(2,1)S(1)} %shard_map.308.a), channel_id=1, source_target_pairs={{0,2},{1,3},{2,0},{3,1},{4,6},{5,7},{6,4},{7,5},{8,10},{9,11},{10,... | collective-permute-start | bytes 1179656 | tf_op jit(solution)/shard_map/ppermute | solution.py:19
  85.7 7.7 %collective-permute-start.27 = (bf16[256,768]{1,0:T(8,128)(2,1)S(1)}, bf16[256,768]{1,0:T(8,128)(2,1)S(1)}, u32[]{:S(2)}, u32[]{:S(2)}) collective-permute-start(bf16[256,768]{1,0:T(8,128)(2,1)S(1)} %get-tuple-element.251), channel_id=1, source_target_pairs={{0,1},{1,0},{2,3},{3,2},{4,5},{5,4},{6,7},{7,6},{8,9},{9,8},{10,11... | collective-permute-start | bytes 1179656 | tf_op jit(solution)/shard_map/ppermute | solution.py:19
  87.9 16.2 %collective-permute-start.28 = (bf16[4,96,768]{2,1,0:T(8,128)(2,1)S(1)}, bf16[4,96,768]{2,1,0:T(8,128)(2,1)S(1)}, u32[]{:S(2)}, u32[]{:S(2)}) collective-permute-start(bf16[4,96,768]{2,1,0:T(8,128)(2,1)S(1)} %get-tuple-element.236), channel_id=1, source_target_pairs={{0,4},{4,0},{8,12},{12,8},{16,20},{20,16},{24,28},{28,24},{1,5},{5... | collective-permute-start | bytes 1769480 | tf_op jit(solution)/shard_map/ppermute | solution.py:19
  93.1 1.8 %collective-permute-start.26 = (bf16[256,768]{1,0:T(8,128)(2,1)S(1)}, bf16[256,768]{1,0:T(8,128)(2,1)S(1)}, u32[]{:S(2)}, u32[]{:S(2)}) collective-permute-start(bf16[256,768]{1,0:T(8,128)(2,1)S(1)} %shard_map.314.total), channel_id=1, source_target_pairs={{0,1},{1,0},{2,3},{3,2},{4,5},{5,4},{6,7},{7,6},{8,9},{9,8},{10,11... | collective-permute-start | bytes 1179656 | tf_op jit(solution)/shard_map/ppermute | solution.py:19
  93.5 11.4 %collective-permute-start.29 = (bf16[256,768]{1,0:T(8,128)(2,1)S(1)}, bf16[256,768]{1,0:T(8,128)(2,1)S(1)}, u32[]{:S(2)}, u32[]{:S(2)}) collective-permute-start(bf16[256,768]{1,0:T(8,128)(2,1)S(1)} %shard_map.317.a), channel_id=1, source_target_pairs={{0,2},{1,3},{2,0},{3,1},{4,6},{5,7},{6,4},{7,5},{8,10},{9,11},{10,... | collective-permute-start | bytes 1179656 | tf_op jit(solution)/shard_map/ppermute | solution.py:19
  94.9 35.0 %collective-permute-start.42 = (bf16[2,256,768]{2,1,0:T(8,128)(2,1)S(1)}, bf16[2,256,768]{2,1,0:T(8,128)(2,1)S(1)}, u32[]{:S(2)}, u32[]{:S(2)}) collective-permute-start(bf16[2,256,768]{2,1,0:T(8,128)(2,1)S(1)} %get-tuple-element.297), channel_id=1, source_target_pairs={{0,1},{1,0},{2,3},{3,2},{4,5},{5,4},{6,7},{7,6},{8,9},{9,8},{10,11... | collective-permute-start | bytes 2359304 | tf_op jit(solution)/shard_map/ppermute | solution.py:19
  95.2 26.8 %collective-permute-start.38 = (bf16[4,96,768]{2,1,0:T(8,128)(2,1)S(1)}, bf16[4,96,768]{2,1,0:T(8,128)(2,1)S(1)}, u32[]{:S(2)}, u32[]{:S(2)}) collective-permute-start(bf16[4,96,768]{2,1,0:T(8,128)(2,1)S(1)} %get-tuple-element.281), channel_id=1, source_target_pairs={{0,4},{4,0},{8,12},{12,8},{16,20},{20,16},{24,28},{28,24},{1,5},{5... | collective-permute-start | bytes 1769480 | tf_op jit(solution)/shard_map/ppermute | solution.py:19
  105.0 1.8 %collective-permute-start.30 = (bf16[256,768]{1,0:T(8,128)(2,1)S(1)}, bf16[256,768]{1,0:T(8,128)(2,1)S(1)}, u32[]{:S(2)}, u32[]{:S(2)}) collective-permute-start(bf16[256,768]{1,0:T(8,128)(2,1)S(1)} %shard_map.318.total), channel_id=1, source_target_pairs={{0,1},{1,0},{2,3},{3,2},{4,5},{5,4},{6,7},{7,6},{8,9},{9,8},{10,11... | collective-permute-start | bytes 1179656 | tf_op jit(solution)/shard_map/ppermute | solution.py:19
  105.7 9.6 %collective-permute-start.31 = (bf16[2,96,768]{2,1,0:T(8,128)(2,1)S(1)}, bf16[2,96,768]{2,1,0:T(8,128)(2,1)S(1)}, u32[]{:S(2)}, u32[]{:S(2)}) collective-permute-start(bf16[2,96,768]{2,1,0:T(8,128)(2,1)S(1)} %get-tuple-element.263), channel_id=1, source_target_pairs={{0,8},{4,12},{8,0},{12,4},{16,24},{20,28},{24,16},{28,20},{1,9},{5... | collective-permute-start | bytes 884744 | tf_op jit(solution)/shard_map/ppermute | solution.py:19
  115.9 11.2 %collective-permute-start.37 = (bf16[1,96,768]{2,1,0:T(8,128)(2,1)S(1)}, bf16[1,96,768]{2,1,0:T(8,128)(2,1)S(1)}, u32[]{:S(2)}, u32[]{:S(2)}) collective-permute-start(bf16[1,96,768]{2,1,0:T(8,128)(2,1)S(1)} %get-tuple-element.279), channel_id=1, source_target_pairs={{0,16},{4,20},{8,24},{12,28},{16,0},{20,4},{24,8},{28,12},{1,17},{... | collective-permute-start | bytes 442376 | tf_op jit(solution)/shard_map/ppermute | solution.py:19
  120.5 1.3 collective-permute-start.34
  120.6 10.9 %collective-permute-start.32 = (bf16[256,768]{1,0:T(8,128)(2,1)S(1)}, bf16[256,768]{1,0:T(8,128)(2,1)S(1)}, u32[]{:S(2)}, u32[]{:S(2)}) collective-permute-start(bf16[256,768]{1,0:T(8,128)(2,1)S(1)} %get-tuple-element.269), channel_id=1, source_target_pairs={{0,1},{1,0},{2,3},{3,2},{4,5},{5,4},{6,7},{7,6},{8,9},{9,8},{10,11... | collective-permute-start | bytes 1179656 | tf_op jit(solution)/shard_map/ppermute | solution.py:19
  121.8 10.8 %collective-permute-start.33 = (bf16[256,768]{1,0:T(8,128)(2,1)S(1)}, bf16[256,768]{1,0:T(8,128)(2,1)S(1)}, u32[]{:S(2)}, u32[]{:S(2)}) collective-permute-start(bf16[256,768]{1,0:T(8,128)(2,1)S(1)} %get-tuple-element.270), channel_id=1, source_target_pairs={{0,1},{1,0},{2,3},{3,2},{4,5},{5,4},{6,7},{7,6},{8,9},{9,8},{10,11... | collective-permute-start | bytes 1179656 | tf_op jit(solution)/shard_map/ppermute | solution.py:19
  122.0 3.9 %collective-permute-start.35 = (f32[8,768]{1,0:T(8,128)S(1)}, f32[8,768]{1,0:T(8,128)S(1)}, u32[]{:S(2)}, u32[]{:S(2)}) collective-permute-start(f32[8,768]{1,0:T(8,128)S(1)} %shard_map.324.a), channel_id=1, source_target_pairs={{0,2},{1,3},{2,0},{3,1},{4,6},{5,7},{6,4},{7,5},{8,10},{9,11},{10,... | collective-permute-start | bytes 73736 | tf_op jit(solution)/shard_map/ppermute | solution.py:19
  125.9 9.9 %collective-permute-start.40 = (bf16[4,96,384]{2,1,0:T(8,128)(2,1)S(1)}, bf16[4,96,384]{2,1,0:T(8,128)(2,1)S(1)}, u32[]{:S(2)}, u32[]{:S(2)}) collective-permute-start(bf16[4,96,384]{2,1,0:T(8,128)(2,1)S(1)} %get-tuple-element.289), channel_id=1, source_target_pairs={{0,4},{4,0},{8,12},{12,8},{16,20},{20,16},{24,28},{28,24},{1,5},{5... | collective-permute-start | bytes 884744 | tf_op jit(solution)/shard_map/ppermute | solution.py:19
  127.1 8.7 %collective-permute-start.39 = (bf16[2,96,768]{2,1,0:T(8,128)(2,1)S(1)}, bf16[2,96,768]{2,1,0:T(8,128)(2,1)S(1)}, u32[]{:S(2)}, u32[]{:S(2)}) collective-permute-start(bf16[2,96,768]{2,1,0:T(8,128)(2,1)S(1)} %get-tuple-element.283), channel_id=1, source_target_pairs={{0,8},{4,12},{8,0},{12,4},{16,24},{20,28},{24,16},{28,20},{1,9},{5... | collective-permute-start | bytes 884744 | tf_op jit(solution)/shard_map/ppermute | solution.py:19
  129.9 11.5 %collective-permute-start.44 = (bf16[4,104,384]{2,1,0:T(8,128)(2,1)S(1)}, bf16[4,104,384]{2,1,0:T(8,128)(2,1)S(1)}, u32[]{:S(2)}, u32[]{:S(2)}) collective-permute-start(bf16[4,104,384]{2,1,0:T(8,128)(2,1)S(1)} %get-tuple-element.308), channel_id=1, source_target_pairs={{0,4},{4,0},{8,12},{12,8},{16,20},{20,16},{24,28},{28,24},{1,5},{5... | collective-permute-start | bytes 958472 | tf_op jit(solution)/shard_map/ppermute | solution.py:19
  131.5 22.0 %collective-permute-start.43 = (bf16[1,256,768]{2,1,0:T(8,128)(2,1)S(1)}, bf16[1,256,768]{2,1,0:T(8,128)(2,1)S(1)}, u32[]{:S(2)}, u32[]{:S(2)}) collective-permute-start(bf16[1,256,768]{2,1,0:T(8,128)(2,1)S(1)} %get-tuple-element.300), channel_id=1, source_target_pairs={{0,2},{1,3},{2,0},{3,1},{4,6},{5,7},{6,4},{7,5},{8,10},{9,11},{10,... | collective-permute-start | bytes 1179656 | tf_op jit(solution)/shard_map/ppermute | solution.py:19
  133.4 21.6 %collective-permute-start.36 = (bf16[256,768]{1,0:T(8,128)(2,1)S(1)}, bf16[256,768]{1,0:T(8,128)(2,1)S(1)}, u32[]{:S(2)}, u32[]{:S(2)}) collective-permute-start(bf16[256,768]{1,0:T(8,128)(2,1)S(1)} %get-tuple-element.274), channel_id=1, source_target_pairs={{0,2},{1,3},{2,0},{3,1},{4,6},{5,7},{6,4},{7,5},{8,10},{9,11},{10,... | collective-permute-start | bytes 1179656 | tf_op jit(solution)/shard_map/ppermute | solution.py:19
  136.4 6.6 %collective-permute-start.45 = (bf16[2,96,384]{2,1,0:T(8,128)(2,1)S(1)}, bf16[2,96,384]{2,1,0:T(8,128)(2,1)S(1)}, u32[]{:S(2)}, u32[]{:S(2)}) collective-permute-start(bf16[2,96,384]{2,1,0:T(8,128)(2,1)S(1)} %get-tuple-element.291), channel_id=1, source_target_pairs={{0,8},{4,12},{8,0},{12,4},{16,24},{20,28},{24,16},{28,20},{1,9},{5... | collective-permute-start | bytes 442376 | tf_op jit(solution)/shard_map/ppermute | solution.py:19
  138.1 8.6 %collective-permute-start.41 = (bf16[1,96,768]{2,1,0:T(8,128)(2,1)S(1)}, bf16[1,96,768]{2,1,0:T(8,128)(2,1)S(1)}, u32[]{:S(2)}, u32[]{:S(2)}) collective-permute-start(bf16[1,96,768]{2,1,0:T(8,128)(2,1)S(1)} %get-tuple-element.294), channel_id=1, source_target_pairs={{0,16},{4,20},{8,24},{12,28},{16,0},{20,4},{24,8},{28,12},{1,17},{... | collective-permute-start | bytes 442376 | tf_op jit(solution)/shard_map/ppermute | solution.py:19
  143.6 9.1 %collective-permute-start.46 = (bf16[2,104,384]{2,1,0:T(8,128)(2,1)S(1)}, bf16[2,104,384]{2,1,0:T(8,128)(2,1)S(1)}, u32[]{:S(2)}, u32[]{:S(2)}) collective-permute-start(bf16[2,104,384]{2,1,0:T(8,128)(2,1)S(1)} %get-tuple-element.311), channel_id=1, source_target_pairs={{0,8},{4,12},{8,0},{12,4},{16,24},{20,28},{24,16},{28,20},{1,9},{5... | collective-permute-start | bytes 479240 | tf_op jit(solution)/shard_map/ppermute | solution.py:19
  147.3 5.5 %collective-permute-start.47 = (bf16[1,96,384]{2,1,0:T(8,128)(2,1)S(1)}, bf16[1,96,384]{2,1,0:T(8,128)(2,1)S(1)}, u32[]{:S(2)}, u32[]{:S(2)}) collective-permute-start(bf16[1,96,384]{2,1,0:T(8,128)(2,1)S(1)} %get-tuple-element.315), channel_id=1, source_target_pairs={{0,16},{4,20},{8,24},{12,28},{16,0},{20,4},{24,8},{28,12},{1,17},{... | collective-permute-start | bytes 221192 | tf_op jit(solution)/shard_map/ppermute | solution.py:19
  153.3 5.5 %collective-permute-start.48 = (bf16[1,104,384]{2,1,0:T(8,128)(2,1)S(1)}, bf16[1,104,384]{2,1,0:T(8,128)(2,1)S(1)}, u32[]{:S(2)}, u32[]{:S(2)}) collective-permute-start(bf16[1,104,384]{2,1,0:T(8,128)(2,1)S(1)} %get-tuple-element.317), channel_id=1, source_target_pairs={{0,16},{4,20},{8,24},{12,28},{16,0},{20,4},{24,8},{28,12},{1,17},{... | collective-permute-start | bytes 239624 | tf_op jit(solution)/shard_map/ppermute | solution.py:19

commit v4 on v3

--- a/solution.py
+++ b/solution.py
@@ -342,33 +342,56 @@
     )
 
 
-def back_kernel(chunk, place, starts, q_ref, k_ref, v_ref, log, gatt_ref, delta_ref, *rest):
+def probs_kernel(chunk, place, starts, q_ref, k_ref, log, out_ref):
+    heads, _, half = out_ref.shape
+    cols = q_ref.shape[1]
+    rows = half // 2
+    head_of = iota((1, cols), 1) // HD
+    limits = query_limits(place, starts, chunk, rows)
+
+    @pl.loop(0, 2 * chunk + 2)
+    def _(block):
+        span = pl.ds(pl.multiple_of(block * rows, rows), rows)
+        keys = k_ref[span, :]
+        queries = q_ref[chunk * half : (chunk + 1) * half, :] * LOW(0.125)
+        allowed = key_positions(place, block, rows) <= limits
+        for head in range(heads):
+            scores = dot(jnp.where(head_of == head, keys, LOW(0)), queries, 1, 1)
+            probs = jnp.exp(jnp.where(allowed, scores, -1e30) - log[head : head + 1, :])
+            out_ref[head, span, :] = probs.astype(LOW)
+
+
+def probs_of(chunk, place, starts, queries, keys, log):
+    length, cols = queries.shape
+    half = length // 2
+    shape = (cols // HD, half * (chunk + 1), half)
+    return call(functools.partial(probs_kernel, chunk), ((shape, LOW),), place, starts, queries, keys, log)[0]
+
+
+def back_kernel(chunk, place, q_ref, k_ref, v_ref, probs_ref, gatt_ref, delta_ref, *rest):
     keys_in, rest = (rest[:2], rest[2:]) if chunk else ((), rest)
     dq_ref, dk_ref, dv_ref, dqt_ref = rest
     half, cols = gatt_ref.shape
     rows = half // 2
     heads = cols // HD
     head_of = iota((1, cols), 1) // HD
-    limits = query_limits(place, starts, chunk, rows)
     dqt_ref[...] = jnp.zeros_like(dqt_ref)
 
     @pl.loop(0, 2 * chunk + 2)
     def _(block):
         span = pl.ds(pl.multiple_of(block * rows, rows), rows)
-        keys, values = k_ref[span, :], v_ref[span, :]
-        keys_t = keys.T
+        values = v_ref[span, :]
+        keys_t = k_ref[span, :].T
         queries = q_ref[chunk * half : (chunk + 1) * half, :] * LOW(0.125)
         grad_att = gatt_ref[...]
-        allowed = key_positions(place, block, rows) <= limits
         dk = jnp.zeros((rows, cols), F32)
         dv = jnp.zeros((rows, cols), F32)
         for head in range(heads):
             mine = head_of == head
-            scores = dot(jnp.where(mine, keys, LOW(0)), queries, 1, 1)
-            probs = jnp.exp(jnp.where(allowed, scores, -1e30) - log[head : head + 1, :])
+            probs = probs_ref[head, span, :]
             grad_probs = dot(jnp.where(mine, values, LOW(0)), grad_att, 1, 1)
-            grad_scores = (probs * (grad_probs - delta_ref[head : head + 1, :])).astype(LOW)
-            dv = dv + dot(probs.astype(LOW), jnp.where(mine, grad_att, LOW(0)), 1, 0)
+            grad_scores = (probs.astype(F32) * (grad_probs - delta_ref[head : head + 1, :])).astype(LOW)
+            dv = dv + dot(probs, jnp.where(mine, grad_att, LOW(0)), 1, 0)
             dk = dk + dot(grad_scores, jnp.where(mine, queries, LOW(0)), 1, 0)
             part = slice(head * HD, (head + 1) * HD)
             dqt_ref[part, :] = dqt_ref[part, :] + dot(keys_t[part, :], grad_scores, 1, 0)
@@ -383,18 +406,17 @@
     dq_ref[...] = (dqt_ref[...] * 0.125).T.astype(LOW)
 
 
-def back(chunk, place, starts, queries, keys, values, log, grad_att, delta, early):
+def back(chunk, place, queries, keys, values, probs, grad_att, delta, early):
     half, cols = grad_att.shape
     kind = (((half * (chunk + 1), cols), LOW if chunk else F32),) * 2
     return call(
         functools.partial(back_kernel, chunk),
         (((half, cols), LOW), *kind),
         place,
-        starts,
         queries,
         keys,
         values,
-        log,
+        probs,
         grad_att,
         delta,
         *early,
@@ -615,6 +637,16 @@
     out_ref[...] = result_of(place, keep, got, res_zero, res_one, vecs)
 
 
+def stack_three_kernel(pair, one, out_ref):
+    out_ref[0] = pair[0]
+    out_ref[1] = pair[1]
+    out_ref[2] = one[...]
+
+
+def stacked_three(pair, one):
+    return call(stack_three_kernel, (((3, *one.shape), one.dtype),), pair, one)[0]
+
+
 def pick_kernel(place, own, other, out_ref):
     out_ref[place[3]] = own[...]
     out_ref[1 - place[3]] = other[...]
@@ -690,13 +722,13 @@
     bias_ref[...] = jnp.concatenate([joined[7], jnp.zeros_like(joined[7]), joined[8]], axis=1)
 
 
-def plain_kernel(masks, second, place, *refs):
+def plain_kernel(masks, firsts, place, *refs):
     *pieces, out_ref = refs
     rows = out_ref.shape[0] // 8
     for number, (piece, owners) in enumerate(zip(pieces, masks)):
         for k, mask in enumerate(owners):
             at = pl.ds(pl.multiple_of((place[4] ^ mask) * rows, rows), rows)
-            out_ref[at, :] = piece[second if number == 1 else k]
+            out_ref[at, :] = piece[firsts[number] + k]
 
 
 def pack_kernel(count, *refs):
@@ -756,9 +788,9 @@
     )
 
 
-def unpacked(place, pieces, second):
+def unpacked(place, pieces, firsts):
     rows, cols = pieces[0].shape[1:]
-    return call(functools.partial(plain_kernel, MASKS, second), (((8 * rows, cols), LOW),), place, *pieces)[0]
+    return call(functools.partial(plain_kernel, MASKS, firsts), (((8 * rows, cols), LOW),), place, *pieces)[0]
 
 
 def plain_first(shard, vectors, qkv_cols, width):
@@ -931,36 +963,37 @@
     normed, queries, keys, values = input_side(xhat, vecs, w_in, all_bias)
     att_zero, log_zero, keep_zero, send_zero = attend(0, place, starts, queries, keys, values, w_proj_t)
     send_zero, up_near, down_far, up_far_across = together(send_zero, up_near, down_far, up_far_across)
+    near_and_far = stacked_three(up_near, down_far)
 
     mine_zero = add_low(keep_zero, core(send_zero))
     far_zero = over(mine_zero)
     down_near = near(stacked(w_down_own, down_far))
-    down_far_across = across(down_far)
-    up_near_across = across(up_near)
+    three_across = across(near_and_far)
     att_one, log_one, keep_one, send_one = attend(1, after(place, mine_zero), starts, queries, keys, values, w_proj_t)
-    send_one, far_zero, up_near_across, down_far_across, down_near = together(
-        send_one, far_zero, up_near_across, down_far_across, down_near
-    )
+    send_one, far_zero, three_across, down_near = together(send_one, far_zero, three_across, down_near)
+    down_near_across = across(down_near)
 
     mine_one = add_low(keep_one, core(send_one))
     far_one = over(mine_one)
     total_zero = add_low(mine_zero, far_zero)
     other_zero = core(total_zero)
-    down_near_across = across(down_near)
-    pieces = (w_up[None], both_across, up_far[None], up_near, up_far_across[None], up_near_across)
-    w_up_all = unpacked(place, pieces, 0)
+    pieces = (w_up[None], both_across, up_far[None], up_near, up_far_across[None], three_across)
+    w_up_all = unpacked(place, pieces, (0, 0, 0, 0, 0, 0))
     cot_both = pick(place, cot_own, cot_far)
     cot_other = core(cot_both)
-    other_zero, down_near_across, w_up_all, cot_other = together(other_zero, down_near_across, w_up_all, cot_other)
+    other_zero, cot_other, w_up_all, down_near_across = together(other_zero, cot_other, w_up_all, down_near_across)
     cots = (cot_both, cot_other)
-    pieces = (w_down_own[None], both_across, down_far[None], down_near, down_far_across[None], down_near_across)
-    w_down_t = unpacked(place, pieces, 1)
+    pieces = (w_down_own[None], both_across, down_far[None], down_near, three_across, down_near_across)
+    probs_one = probs_of(1, after(place, mine_one), starts, queries, keys, log_one)
+    probs_zero = probs_of(0, after(place, mine_one), starts, queries, keys, log_zero)
+    probs_one, probs_zero, w_pieces = together(probs_one, probs_zero, pieces[0])
+    pieces = (w_pieces, *pieces[1:])
+    w_down_t = unpacked(place, pieces, (0, 1, 0, 0, 2, 0))
 
     weights = (vecs, up_bias, w_up_all, w_down_t)
     residual_zero, normed_zero, hidden_zero, grad_zero, up_sum_zero, keep_zero, send_zero = feed(
         0, spliced, total_zero, other_zero, cots, *weights
     )
-    send_zero, far_one = together(send_zero, far_one)
     total_one = add_low(mine_one, far_one)
     other_one = core(total_one)
     mine_zero = add_low(keep_zero, core(send_zero))
@@ -986,7 +1019,7 @@
     res_zero, branch_zero, gatt_zero, delta_zero, sums_zero = branch_back(
         0, total_zero, other_zero, residual_zero, cots, vecs, w_proj_t, att_zero
     )
-    dq_zero, *early = back(0, place, starts, queries, keys, values, log_zero, gatt_zero, delta_zero, ())
+    dq_zero, *early = back(0, place, queries, keys, values, probs_zero, gatt_zero, delta_zero, ())
     c_got = across(after(c_send, other_zero))
     total_one = add_low(after(mine_one, early[0], b_got), far_one)
     other_one = core(total_one)
@@ -997,8 +1030,8 @@
     res_one, branch_one, gatt_one, delta_one, sums_one = branch_back(
         1, total_one, other_one, residual_one, cots, vecs, w_proj_t, att_one
     )
-    dq_one, dk, dv = back(1, place, starts, queries, keys, values, log_one, gatt_one, delta_one, early)
-    dk, b_got = together(dk, b_got)
+    dq_one, dk, dv = back(1, place, queries, keys, values, probs_one, gatt_one, delta_one, early)
+    dk, b_got, c_got = together(dk, b_got, c_got)
 
     grad_residual = (res_zero, res_one)
     kinds = (((4, shard_rows, 2 * head_cols), F32), ((4, shard_rows, 2 * head_cols), LOW))
@@ -1022,7 +1055,7 @@
         last_kernel_two,
         ((shape, F32), (shape, LOW)),
         place,
-        after(normed, b_got),
+        normed,
         dk,
         dv,
         small,
@@ -1040,14 +1073,14 @@
     d_got = near(d_send)
     c_keep, c_send = fold(6, place, c_keep, after(c_got, d_send))
     c_got = far(c_send)
-    e_got, d_got = together(e_got, d_got)
+    e_got, d_got, b_got = together(e_got, d_got, b_got)
 
     e_keep, e_send = fold(5, place, e_keep, e_got)
     e_got = near(e_send)
-    d_keep, d_send = fold(6, place, d_keep, after(d_got, c_got))
+    d_keep, d_send = fold(6, place, d_keep, d_got)
     d_got = far(d_send)
 
-    e_keep, e_send = fold(6, place, e_keep, after(e_got, d_got))
+    e_keep, e_send = fold(6, place, e_keep, e_got)
     e_got = far(e_send)
     block_out = result(place, mlp_keep[0], mlp_got[0], residual, vecs)
     grad_embed, grad_thoughts, grad_up, grad_down = output_side(
@@ -1108,8 +1141,9 @@
         branches.append(
             branch_back(chunk, *grad_twos[chunk], residual[chunk], cots, vecs, w_proj_t, atts[chunk])
         )
+        probs = probs_of(chunk, place, starts, queries, keys, logs[chunk])
         dq, *early = back(
-            chunk, place, starts, queries, keys, values, logs[chunk], *branches[-1][2:4], early
+            chunk, place, queries, keys, values, probs, *branches[-1][2:4], early
         )
         dqs.append(dq)
     grad_residual, grad_branch = zip(branches[0][:2], branches[1][:2])

time: 160 us -> 154 us (0.963)
  waiting for transfers between devices: 45.6 us -> 31.1 us
  starting transfers between devices: 46.5 us -> 52.8 us
  Pallas kernels: 61.9 us -> 64.5 us
    ppermute x49 -> x48, waiting for transfers between devices: 45.6 us -> 31.1 us  [swapped(): lax.ppermute(array, axis, [(i, i ^ mask) for i in range(lax.axis_size(axi...]
    ppermute x49 -> x48, starting transfers between devices: 46.5 us -> 52.8 us  [swapped(): lax.ppermute(array, axis, [(i, i ^ mask) for i in range(lax.axis_size(axi...]
    pallas_call x49 -> x52, Pallas kernels: 60.1 us -> 62.6 us  [call(): pl.pallas_call(kernel, out_shape=tuple((jax.ShapeDtypeStruct(s, t) for s,...]
  transfers between devices with their start and end apart: 49 -> 48, of which waited for: 21 -> 19; matrix products, arithmetic and copies ran while one was open for 0% -> 0% of each run, Pallas kernels for 37% -> 40%
where the time goes in v4:
time: 154 us
  Pallas kernels  64.5 us (42%)
  starting transfers between devices  52.8 us (34%)
  waiting for transfers between devices  31.1 us (20%)
  local copies, waits for them, and re-layouts  4.48 us (3%)
    pallas_call x52, Pallas kernels, call(): pl.pallas_call(kernel, out_shape=tuple((jax.ShapeDtypeStruct(s, t) for s,...  62.6 us
    ppermute x48, starting transfers between devices, swapped(): lax.ppermute(array, axis, [(i, i ^ mask) for i in range(lax.axis_size(axi...  52.8 us
    ppermute x48, waiting for transfers between devices, swapped(): lax.ppermute(array, axis, [(i, i ^ mask) for i in range(lax.axis_size(axi...  31.1 us
    unnamed x20, local copies, waits for them, and re-layouts  3.79 us
  transfers between devices with their start and end apart: 48, of which 19 were waited for; matrix products, arithmetic and copies ran while one was open for 0% of the time, Pallas kernels for 40%

profile of v4, /device:TPU:0, one launch (start us, length us, event | category | flops | bytes accessed | tf_op | source)
XLA Modules:
  0.0 154.1 jit_solution(15864292331083520251)
XLA Ops:
  0.7 1.9 %shard_map.289.refs_0_ = bf16[104,768]{1,0:T(8,128)(2,1)} custom-call(bf16[3,96,192]{2,1,0:T(8,128)(2,1)} %refs_0_.1, bf16[192,96]{1,0:T(8,128)(2,1)} %refs_1_.1, bf16[1,96]{1,0:T(2,128)(2,1)} %bitcast.63, bf16[1,96]{1,0:T(2,128)(2,1)} %bitcast.64, bf16[1,96]{1,0:T(2,128)(2,1)} %bitcast.65, bf16[1,96]{1,0:T(2,128)(2,1)} %bitcast.66, bf16[1,96]{1,0:T(2,128)(2,1)} %bitcast.67, ...), custom_call_target="tpu_custom_call" | custom-call | flops 1000 | tf_op jit(solution)/shard_map/pallas_call | solution.py:753
  2.5 3.0 %collective-permute-start = (bf16[256,768]{1,0:T(8,128)(2,1)}, bf16[256,768]{1,0:T(8,128)(2,1)S(1)}, u32[]{:S(2)}, u32[]{:S(2)}) collective-permute-start(bf16[256,768]{1,0:T(8,128)(2,1)} %bitcast.49), channel_id=1, source_target_pairs={{0,2},{1,3},{2,0},{3,1},{4,6},{5,7},{6,4},{7,5},{8,10},{9,11},{10,... | collective-permute-start | bytes 1179656 | tf_op jit(solution)/shard_map/ppermute | solution.py:19
  5.5 1.5 collective-permute-start.2
  7.1 2.6 %collective-permute-start.1 = (bf16[104,768]{1,0:T(8,128)(2,1)}, bf16[104,768]{1,0:T(8,128)(2,1)S(1)}, u32[]{:S(2)}, u32[]{:S(2)}) collective-permute-start(bf16[104,768]{1,0:T(8,128)(2,1)} %shard_map.289.refs_0_), channel_id=1, source_target_pairs={{0,16},{4,20},{8,24},{12,28},{16,0},{20,4},{24,8},{28,12},{1,17},{... | collective-permute-start | bytes 479240 | tf_op jit(solution)/shard_map/ppermute | solution.py:19
  9.7 0.9 copy-done.4
  10.6 1.0 copy-done.5
  11.6 0.9 copy-done
  12.5 0.9 copy-done.2
  13.5 3.4 %collective-permute-done.1.b = bf16[104,768]{1,0:T(8,128)(2,1)S(1)} collective-permute-done((bf16[104,768]{1,0:T(8,128)(2,1)}, bf16[104,768]{1,0:T(8,128)(2,1)S(1)}, u32[]{:S(2)}, u32[]{:S(2)}) %collective-permute-start.1) | collective-permute-done | bytes 159776 | tf_op jit(solution)/shard_map/ppermute | solution.py:19
  17.5 0.8 collective-permute-start.3
  18.3 1.5 collective-permute-start.6
  20.3 3.3 %collective-permute-start.5 = (bf16[96,768]{1,0:T(8,128)(2,1)S(1)}, bf16[96,768]{1,0:T(8,128)(2,1)S(1)}, u32[]{:S(2)}, u32[]{:S(2)}) collective-permute-start(bf16[96,768]{1,0:T(8,128)(2,1)S(1)} %copy-done.1), channel_id=1, source_target_pairs={{0,16},{4,20},{8,24},{12,28},{16,0},{20,4},{24,8},{28,12},{1,17},{... | collective-permute-start | bytes 442376 | tf_op jit(solution)/shard_map/ppermute | solution.py:19
  24.3 3.9 %collective-permute-done.5.b = bf16[96,768]{1,0:T(8,128)(2,1)S(1)} collective-permute-done((bf16[96,768]{1,0:T(8,128)(2,1)S(1)}, bf16[96,768]{1,0:T(8,128)(2,1)S(1)}, u32[]{:S(2)}, u32[]{:S(2)}) %collective-permute-start.5) | collective-permute-done | bytes 147488 | tf_op jit(solution)/shard_map/ppermute | solution.py:19
  28.1 2.0 %collective-permute-done.4 = bf16[104,768]{1,0:T(8,128)(2,1)} collective-permute-done((bf16[104,768]{1,0:T(8,128)(2,1)S(1)}, bf16[104,768]{1,0:T(8,128)(2,1)}, u32[]{:S(2)}, u32[]{:S(2)}) %collective-permute-start.4) | collective-permute-done | bytes 159776 | tf_op jit(solution)/shard_map/ppermute | solution.py:19
  31.5 2.0 %collective-permute-start.10 = (bf16[2,96,768]{2,1,0:T(8,128)(2,1)S(1)}, bf16[2,96,768]{2,1,0:T(8,128)(2,1)S(1)}, u32[]{:S(2)}, u32[]{:S(2)}) collective-permute-start(bf16[2,96,768]{2,1,0:T(8,128)(2,1)S(1)} %shard_map.298), channel_id=1, source_target_pairs={{0,8},{4,12},{8,0},{12,4},{16,24},{20,28},{24,16},{28,20},{1,9},{5... | collective-permute-start | bytes 884744 | tf_op jit(solution)/shard_map/ppermute | solution.py:19
  33.5 1.7 %collective-permute-start.11 = (bf16[96,768]{1,0:T(8,128)(2,1)S(1)}, bf16[96,768]{1,0:T(8,128)(2,1)S(1)}, u32[]{:S(2)}, u32[]{:S(2)}) collective-permute-start(bf16[96,768]{1,0:T(8,128)(2,1)S(1)} %bitcast.41), channel_id=1, source_target_pairs={{0,16},{4,20},{8,24},{12,28},{16,0},{20,4},{24,8},{28,12},{1,17},{... | collective-permute-start | bytes 442376 | tf_op jit(solution)/shard_map/ppermute | solution.py:19
  35.3 1.8 %shard_map.294 = (bf16[1024,768]{1,0:T(8,128)(2,1)S(1)}, f32[1024,768]{1,0:T(8,128)S(1)}) custom-call(s32[8]{0:T(128)S(1)} %dynamic-slice_bitcast_fusion.place, bf16[2,256,768]{2,1,0:T(8,128)(2,1)S(1)} %shard_map.293.x_zero, bf16[2,256,768]{2,1,0:T(8,128)(2,1)S(1)} %collective-permute-done.9.x_one, bf16[6,768]{1,0:T(8,128)(2,1)S(1)} %bitcast.55, ...), custom_call_target="tpu_custom_call" | custom-call | flops 1000 | tf_op jit(solution)/shard_map/pallas_call | solution.py:120
  37.1 3.8 %collective-permute-done.8.refs_5_ = bf16[2,104,768]{2,1,0:T(8,128)(2,1)S(1)} collective-permute-done((bf16[2,104,768]{2,1,0:T(8,128)(2,1)S(1)}, bf16[2,104,768]{2,1,0:T(8,128)(2,1)S(1)}, u32[]{:S(2)}, u32[]{:S(2)}) %collective-permute-start.8) | collective-permute-done | bytes 319520 | tf_op jit(solution)/shard_map/ppermute | solution.py:19
  41.3 1.2 shard_map.295
  42.6 1.4 shard_map.296
  44.0 3.6 %shard_map.297 = (bf16[512,192]{1,0:T(8,128)(2,1)S(1)}, f32[8,512]{1,0:T(8,128)S(1)}, f32[256,768]{1,0:T(8,128)S(1)}, bf16[256,768]{1,0:T(8,128)(2,1)S(1)}) custom-call(s32[8]{0:T(128)S(1)} %dynamic-slice_bitcast_fusion.place, s32[2]{0:T(128)S(1)} %bitcast.57, bf16[1024,192]{1,0:T(8,128)(2,1)S(1)} %get-tuple-element.198.q_ref, ...), custom_call_target="tpu_custom_call" | custom-call | flops 1000 | tf_op jit(solution)/shard_map/pallas_call | solution.py:120
  47.8 1.6 %collective-permute-start.15 = (bf16[3,96,768]{2,1,0:T(8,128)(2,1)S(1)}, bf16[3,96,768]{2,1,0:T(8,128)(2,1)S(1)}, u32[]{:S(2)}, u32[]{:S(2)}) collective-permute-start(bf16[3,96,768]{2,1,0:T(8,128)(2,1)S(1)} %shard_map.301), channel_id=1, source_target_pairs={{0,4},{4,0},{8,12},{12,8},{16,20},{20,16},{24,28},{28,24},{1,5},{5... | collective-permute-start | bytes 1327112 | tf_op jit(solution)/shard_map/ppermute | solution.py:19
  49.5 1.6 %collective-permute-start.14 = (bf16[256,768]{1,0:T(8,128)(2,1)S(1)}, bf16[256,768]{1,0:T(8,128)(2,1)S(1)}, u32[]{:S(2)}, u32[]{:S(2)}) collective-permute-start(bf16[256,768]{1,0:T(8,128)(2,1)S(1)} %shard_map.299.a), channel_id=1, source_target_pairs={{0,2},{1,3},{2,0},{3,1},{4,6},{5,7},{6,4},{7,5},{8,10},{9,11},{10,... | collective-permute-start | bytes 1179656 | tf_op jit(solution)/shard_map/ppermute | solution.py:19
  51.1 2.0 %collective-permute-start.16 = (bf16[2,96,768]{2,1,0:T(8,128)(2,1)S(1)}, bf16[2,96,768]{2,1,0:T(8,128)(2,1)S(1)}, u32[]{:S(2)}, u32[]{:S(2)}) collective-permute-start(bf16[2,96,768]{2,1,0:T(8,128)(2,1)S(1)} %shard_map.302), channel_id=1, source_target_pairs={{0,8},{4,12},{8,0},{12,4},{16,24},{20,28},{24,16},{28,20},{1,9},{5... | collective-permute-start | bytes 884744 | tf_op jit(solution)/shard_map/ppermute | solution.py:19
  53.8 6.2 %shard_map.300 = (bf16[512,192]{1,0:T(8,128)(2,1)S(1)}, f32[8,512]{1,0:T(8,128)S(1)}, f32[256,768]{1,0:T(8,128)S(1)}, bf16[256,768]{1,0:T(8,128)(2,1)S(1)}) custom-call(s32[8]{0:T(128)S(1)} %dynamic-slice_bitcast_fusion.place, s32[2]{0:T(128)S(1)} %bitcast.58, bf16[1024,192]{1,0:T(8,128)(2,1)S(1)} %get-tuple-element.198.q_ref, ...), custom_call_target="tpu_custom_call" | custom-call | flops 1000 | tf_op jit(solution)/shard_map/pallas_call | solution.py:120
  61.4 1.5 collective-permute-start.20
  63.0 1.6 %collective-permute-start.22 = (bf16[256,768]{1,0:T(8,128)(2,1)S(1)}, bf16[256,768]{1,0:T(8,128)(2,1)S(1)}, u32[]{:S(2)}, u32[]{:S(2)}) collective-permute-start(bf16[256,768]{1,0:T(8,128)(2,1)S(1)} %shard_map.303.a), channel_id=1, source_target_pairs={{0,2},{1,3},{2,0},{3,1},{4,6},{5,7},{6,4},{7,5},{8,10},{9,11},{10,... | collective-permute-start | bytes 1179656 | tf_op jit(solution)/shard_map/ppermute | solution.py:19
  65.2 1.5 %shard_map.305.probs_ref = bf16[3,512,512]{2,1,0:T(8,128)(2,1)S(1)} custom-call(s32[8]{0:T(128)S(1)} %dynamic-slice_bitcast_fusion.place, s32[2]{0:T(128)S(1)} %bitcast.59, bf16[1024,192]{1,0:T(8,128)(2,1)S(1)} %get-tuple-element.198.q_ref, bf16[1024,192]{1,0:T(8,128)(2,1)S(1)} %get-tuple-element.199.k_ref, f32[8,512]{1,0:T(8,128)S(1)} %get-tuple-element.215.log), custom_call_target="tpu_custom_call" | custom-call | flops 1000 | tf_op jit(solution)/shard_map/pallas_call | solution.py:120
  66.8 2.7 %shard_map.304.probs_ref = bf16[3,1024,512]{2,1,0:T(8,128)(2,1)S(1)} custom-call(s32[8]{0:T(128)S(1)} %dynamic-slice_bitcast_fusion.place, s32[2]{0:T(128)S(1)} %bitcast.60, bf16[1024,192]{1,0:T(8,128)(2,1)S(1)} %get-tuple-element.198.q_ref, bf16[1024,192]{1,0:T(8,128)(2,1)S(1)} %get-tuple-element.199.k_ref, f32[8,512]{1,0:T(8,128)S(1)} %get-tuple-element.214.log), custom_call_target="tpu_custom_call" | custom-call | flops 1000 | tf_op jit(solution)/shard_map/pallas_call | solution.py:120
  69.5 0.9 collective-permute-done.20.refs_5_
  71.0 2.8 %shard_map.310 = (f32[512,768]{1,0:T(8,128)S(1)}, bf16[512,768]{1,0:T(8,128)(2,1)S(1)}, bf16[512,768]{1,0:T(8,128)(2,1)S(1)}, bf16[512,768]{1,0:T(8,128)(2,1)S(1...) custom-call(bf16[1024,768]{1,0:T(8,128)(2,1)S(1)} %get-tuple-element.233.spliced, ...), custom_call_target="tpu_custom_call" | custom-call | flops 1000 | tf_op jit(solution)/shard_map/pallas_call | solution.py:120
  74.6 1.0 collective-permute-done.21.b
  75.7 1.6 %collective-permute-start.24 = (bf16[256,768]{1,0:T(8,128)(2,1)S(1)}, bf16[256,768]{1,0:T(8,128)(2,1)S(1)}, u32[]{:S(2)}, u32[]{:S(2)}) collective-permute-start(bf16[256,768]{1,0:T(8,128)(2,1)S(1)} %shard_map.311.a), channel_id=1, source_target_pairs={{0,2},{1,3},{2,0},{3,1},{4,6},{5,7},{6,4},{7,5},{8,10},{9,11},{10,... | collective-permute-start | bytes 1179656 | tf_op jit(solution)/shard_map/ppermute | solution.py:19
  77.2 2.8 %shard_map.313 = (f32[512,768]{1,0:T(8,128)S(1)}, bf16[512,768]{1,0:T(8,128)(2,1)S(1)}, bf16[512,768]{1,0:T(8,128)(2,1)S(1)}, bf16[512,768]{1,0:T(8,128)(2,1)S(1...) custom-call(bf16[1024,768]{1,0:T(8,128)(2,1)S(1)} %get-tuple-element.233.spliced, ...), custom_call_target="tpu_custom_call" | custom-call | flops 1000 | tf_op jit(solution)/shard_map/pallas_call | solution.py:120
  80.1 2.1 %shard_map.314 = (f32[4,96,768]{2,1,0:T(8,128)S(1)}, bf16[4,96,768]{2,1,0:T(8,128)(2,1)S(1)}) custom-call(s32[8]{0:T(128)S(1)} %dynamic-slice_bitcast_fusion.place, bf16[512,768]{1,0:T(8,128)(2,1)S(1)} %get-tuple-element.232.refs_0_, bf16[512,768]{1,0:T(8,128)(2,1)S(1)} %get-tuple-element.234.refs_1_, bf16[512,768]{1,0:T(8,128)(2,1)S(1)} %get-tuple-element.235.refs_2_, ...), custom_call_target="tpu_custom_call" | custom-call | flops 1000 | tf_op jit(solution)/shard_map/pallas_call | solution.py:120
  82.2 1.6 %collective-permute-start.27 = (bf16[4,96,768]{2,1,0:T(8,128)(2,1)S(1)}, bf16[4,96,768]{2,1,0:T(8,128)(2,1)S(1)}, u32[]{:S(2)}, u32[]{:S(2)}) collective-permute-start(bf16[4,96,768]{2,1,0:T(8,128)(2,1)S(1)} %get-tuple-element.237), channel_id=1, source_target_pairs={{0,4},{4,0},{8,12},{12,8},{16,20},{20,16},{24,28},{28,24},{1,5},{5... | collective-permute-start | bytes 1769480 | tf_op jit(solution)/shard_map/ppermute | solution.py:19
  83.8 1.4 shard_map.316
  85.2 2.1 %shard_map.315 = (f32[4,96,768]{2,1,0:T(8,128)S(1)}, bf16[4,96,768]{2,1,0:T(8,128)(2,1)S(1)}) custom-call(s32[8]{0:T(128)S(1)} %dynamic-slice_bitcast_fusion.place, bf16[2,256,768]{2,1,0:T(8,128)(2,1)S(1)} %shard_map.307.cot_zero, bf16[2,256,768]{2,1,0:T(8,128)(2,1)S(1)} %collective-permute-done.19.cot_one, ...), custom_call_target="tpu_custom_call" | custom-call | flops 1000 | tf_op jit(solution)/shard_map/pallas_call | solution.py:120
  87.8 0.9 collective-permute-start.28
  89.3 1.0 collective-permute-start.31
  90.3 2.0 %shard_map.318 = (f32[512,768]{1,0:T(8,128)S(1)}, bf16[512,768]{1,0:T(8,128)(2,1)S(1)}, bf16[512,192]{1,0:T(8,128)(2,1)S(1)}, f32[8,512]{1,0:T(8,128)S(1)}, f32[8,768]{1,0:T(8,128)S(1)}) custom-call(bf16[256,768]{1,0:T(8,128)(2,1)S(1)} %shard_map.317.total, bf16[256,768]{1,0:T(8,128)(2,1)S(1)} %collective-permute-done.25.other, ...), custom_call_target="tpu_custom_call" | custom-call | flops 1000 | tf_op jit(solution)/shard_map/pallas_call | solution.py:120
  92.3 3.3 %shard_map.319 = (bf16[512,192]{1,0:T(8,128)(2,1)S(1)}, f32[512,192]{1,0:T(8,128)S(1)}, f32[512,192]{1,0:T(8,128)S(1)}) custom-call(s32[8]{0:T(128)S(1)} %dynamic-slice_bitcast_fusion.place, bf16[1024,192]{1,0:T(8,128)(2,1)S(1)} %get-tuple-element.198.q_ref, bf16[1024,192]{1,0:T(8,128)(2,1)S(1)} %get-tuple-element.199.k_ref, ...), custom_call_target="tpu_custom_call" | custom-call | flops 1000 | tf_op jit(solution)/shard_map/pallas_call | solution.py:120
  95.7 2.8 %collective-permute-done.27.refs_1_ = bf16[4,96,768]{2,1,0:T(8,128)(2,1)S(1)} collective-permute-done((bf16[4,96,768]{2,1,0:T(8,128)(2,1)S(1)}, bf16[4,96,768]{2,1,0:T(8,128)(2,1)S(1)}, u32[]{:S(2)}, u32[]{:S(2)}) %collective-permute-start.27) | collective-permute-done | bytes 589856 | tf_op jit(solution)/shard_map/ppermute | solution.py:19
  100.1 2.0 %collective-permute-start.30 = (bf16[2,96,768]{2,1,0:T(8,128)(2,1)S(1)}, bf16[2,96,768]{2,1,0:T(8,128)(2,1)S(1)}, u32[]{:S(2)}, u32[]{:S(2)}) collective-permute-start(bf16[2,96,768]{2,1,0:T(8,128)(2,1)S(1)} %get-tuple-element.264), channel_id=1, source_target_pairs={{0,8},{4,12},{8,0},{12,4},{16,24},{20,28},{24,16},{28,20},{1,9},{5... | collective-permute-start | bytes 884744 | tf_op jit(solution)/shard_map/ppermute | solution.py:19
  102.1 2.1 %shard_map.322 = (f32[512,768]{1,0:T(8,128)S(1)}, bf16[512,768]{1,0:T(8,128)(2,1)S(1)}, bf16[512,192]{1,0:T(8,128)(2,1)S(1)}, f32[8,512]{1,0:T(8,128)S(1)}, f32[8,768]{1,0:T(8,128)S(1)}) custom-call(bf16[256,768]{1,0:T(8,128)(2,1)S(1)} %shard_map.321.total, bf16[256,768]{1,0:T(8,128)(2,1)S(1)} %collective-permute-done.29.other, ...), custom_call_target="tpu_custom_call" | custom-call | flops 1000 | tf_op jit(solution)/shard_map/pallas_call | solution.py:120
  104.2 5.5 %shard_map.323 = (bf16[512,192]{1,0:T(8,128)(2,1)S(1)}, bf16[1024,192]{1,0:T(8,128)(2,1)S(1)}, bf16[1024,192]{1,0:T(8,128)(2,1)S(1)}) custom-call(s32[8]{0:T(128)S(1)} %dynamic-slice_bitcast_fusion.place, bf16[1024,192]{1,0:T(8,128)(2,1)S(1)} %get-tuple-element.198.q_ref, bf16[1024,192]{1,0:T(8,128)(2,1)S(1)} %get-tuple-element.199.k_ref, ...), custom_call_target="tpu_custom_call" | custom-call | flops 1000 | tf_op jit(solution)/shard_map/pallas_call | solution.py:120
  109.7 1.0 collective-permute-done.31.refs_1_
  110.7 2.1 %shard_map.325 = (f32[2,256,768]{2,1,0:T(8,128)S(1)}, bf16[256,768]{1,0:T(8,128)(2,1)S(1)}, bf16[256,768]{1,0:T(8,128)(2,1)S(1)}, f32[8,768]{1,0:T(8,128)S(1)}, ...) custom-call(s32[8]{0:T(128)S(1)} %dynamic-slice_bitcast_fusion.place, s32[6]{0:T(128)S(1)} %bitcast.61, ...), custom_call_target="tpu_custom_call" | custom-call | flops 1000 | tf_op jit(solution)/shard_map/pallas_call | solution.py:120
  113.5 1.7 %collective-permute-done.34.b = f32[8,768]{1,0:T(8,128)S(1)} collective-permute-done((f32[8,768]{1,0:T(8,128)S(1)}, f32[8,768]{1,0:T(8,128)S(1)}, u32[]{:S(2)}, u32[]{:S(2)}) %collective-permute-start.34) | collective-permute-done | bytes 24608 | tf_op jit(solution)/shard_map/ppermute | solution.py:19
  115.7 1.7 %shard_map.331 = (f32[4,96,384]{2,1,0:T(8,128)S(1)}, bf16[4,96,384]{2,1,0:T(8,128)(2,1)S(1)}) custom-call(s32[8]{0:T(128)S(1)} %dynamic-slice_bitcast_fusion.place, bf16[1024,768]{1,0:T(8,128)(2,1)S(1)} %get-tuple-element.281.normed, bf16[512,192]{1,0:T(8,128)(2,1)S(1)} %get-tuple-element.249.dq_zero, bf16[512,192]{1,0:T(8,128)(2,1)S(1)} %get-tuple-element.260.dq_one, ...), custom_call_target="tpu_custom_call" | custom-call | flops 1000 | tf_op jit(solution)/shard_map/pallas_call | solution.py:120
  117.5 1.6 %collective-permute-start.38 = (bf16[4,96,384]{2,1,0:T(8,128)(2,1)S(1)}, bf16[4,96,384]{2,1,0:T(8,128)(2,1)S(1)}, u32[]{:S(2)}, u32[]{:S(2)}) collective-permute-start(bf16[4,96,384]{2,1,0:T(8,128)(2,1)S(1)} %get-tuple-element.292), channel_id=1, source_target_pairs={{0,4},{4,0},{8,12},{12,8},{16,20},{20,16},{24,28},{28,24},{1,5},{5... | collective-permute-start | bytes 884744 | tf_op jit(solution)/shard_map/ppermute | solution.py:19
  119.7 2.1 %collective-permute-start.39 = (bf16[2,96,768]{2,1,0:T(8,128)(2,1)S(1)}, bf16[2,96,768]{2,1,0:T(8,128)(2,1)S(1)}, u32[]{:S(2)}, u32[]{:S(2)}) collective-permute-start(bf16[2,96,768]{2,1,0:T(8,128)(2,1)S(1)} %get-tuple-element.295), channel_id=1, source_target_pairs={{0,8},{4,12},{8,0},{12,4},{16,24},{20,28},{24,16},{28,20},{1,9},{5... | collective-permute-start | bytes 884744 | tf_op jit(solution)/shard_map/ppermute | solution.py:19
  121.8 1.9 %shard_map.330 = (f32[4,104,384]{2,1,0:T(8,128)S(1)}, bf16[4,104,384]{2,1,0:T(8,128)(2,1)S(1)}) custom-call(s32[8]{0:T(128)S(1)} %dynamic-slice_bitcast_fusion.place, bf16[1024,768]{1,0:T(8,128)(2,1)S(1)} %get-tuple-element.281.normed, bf16[1024,192]{1,0:T(8,128)(2,1)S(1)} %get-tuple-element.266.dk, bf16[1024,192]{1,0:T(8,128)(2,1)S(1)} %get-tuple-element.267.dv, ...), custom_call_target="tpu_custom_call" | custom-call | flops 1000 | tf_op jit(solution)/shard_map/pallas_call | solution.py:120
  125.2 1.3 collective-permute-start.44
  127.3 0.9 collective-permute-start.36
  128.8 1.9 %collective-permute-start.41 = (bf16[1,96,768]{2,1,0:T(8,128)(2,1)S(1)}, bf16[1,96,768]{2,1,0:T(8,128)(2,1)S(1)}, u32[]{:S(2)}, u32[]{:S(2)}) collective-permute-start(bf16[1,96,768]{2,1,0:T(8,128)(2,1)S(1)} %get-tuple-element.298), channel_id=1, source_target_pairs={{0,16},{4,20},{8,24},{12,28},{16,0},{20,4},{24,8},{28,12},{1,17},{... | collective-permute-start | bytes 442376 | tf_op jit(solution)/shard_map/ppermute | solution.py:19
  131.3 1.5 collective-permute-start.40
  132.8 4.1 %collective-permute-done.41.rest_1_ = bf16[1,96,768]{2,1,0:T(8,128)(2,1)S(1)} collective-permute-done((bf16[1,96,768]{2,1,0:T(8,128)(2,1)S(1)}, bf16[1,96,768]{2,1,0:T(8,128)(2,1)S(1)}, u32[]{:S(2)}, u32[]{:S(2)}) %collective-permute-start.41) | collective-permute-done | bytes 147488 | tf_op jit(solution)/shard_map/ppermute | solution.py:19
  139.4 2.2 %collective-permute-start.42 = (bf16[1,96,768]{2,1,0:T(8,128)(2,1)S(1)}, bf16[1,96,768]{2,1,0:T(8,128)(2,1)S(1)}, u32[]{:S(2)}, u32[]{:S(2)}) collective-permute-start(bf16[1,96,768]{2,1,0:T(8,128)(2,1)S(1)} %get-tuple-element.303), channel_id=1, source_target_pairs={{0,16},{4,20},{8,24},{12,28},{16,0},{20,4},{24,8},{28,12},{1,17},{... | collective-permute-start | bytes 442376 | tf_op jit(solution)/shard_map/ppermute | solution.py:19
  141.6 3.4 %collective-permute-done.45.refs_1_ = bf16[2,104,384]{2,1,0:T(8,128)(2,1)S(1)} collective-permute-done((bf16[2,104,384]{2,1,0:T(8,128)(2,1)S(1)}, bf16[2,104,384]{2,1,0:T(8,128)(2,1)S(1)}, u32[]{:S(2)}, u32[]{:S(2)}) %collective-permute-start.45) | collective-permute-done | bytes 159776 | tf_op jit(solution)/shard_map/ppermute | solution.py:19
  146.7 2.5 %collective-permute-start.47 = (bf16[1,96,384]{2,1,0:T(8,128)(2,1)S(1)}, bf16[1,96,384]{2,1,0:T(8,128)(2,1)S(1)}, u32[]{:S(2)}, u32[]{:S(2)}) collective-permute-start(bf16[1,96,384]{2,1,0:T(8,128)(2,1)S(1)} %get-tuple-element.317), channel_id=1, source_target_pairs={{0,16},{4,20},{8,24},{12,28},{16,0},{20,4},{24,8},{28,12},{1,17},{... | collective-permute-start | bytes 221192 | tf_op jit(solution)/shard_map/ppermute | solution.py:19
  149.2 1.5 shard_map.337
  150.9 2.3 %shard_map.335 = (f32[256,768]{1,0:T(8,128)}, f32[6,1,192]{2,1,0:T(1,128)}, f32[96,768]{1,0:T(8,128)}, f32[96,768]{1,0:T(8,128)}) custom-call(s32[8]{0:T(128)S(1)} %dynamic-slice_bitcast_fusion.place, f32[256,768]{1,0:T(8,128)S(1)} %get-tuple-element.273.keep, bf16[256,768]{1,0:T(8,128)(2,1)S(1)} %collective-permute-done.36.got, ...), custom_call_target="tpu_custom_call" | custom-call | flops 1000 | tf_op jit(solution)/shard_map/pallas_call | solution.py:120
  153.2 0.9 shard_map.341
  (106 shorter events, 20.5 us)
Async XLA Ops:
  0.6 19.7 %copy-start.1 = (bf16[96,768]{1,0:T(8,128)(2,1)S(1)}, bf16[96,768]{1,0:T(8,128)(2,1)}, u32[]{:S(2)}) copy-start(bf16[96,768]{1,0:T(8,128)(2,1)} %a.2) | copy-start | bytes 442372
  2.5 14.4 %collective-permute-start = (bf16[256,768]{1,0:T(8,128)(2,1)}, bf16[256,768]{1,0:T(8,128)(2,1)S(1)}, u32[]{:S(2)}, u32[]{:S(2)}) collective-permute-start(bf16[256,768]{1,0:T(8,128)(2,1)} %bitcast.49), channel_id=1, source_target_pairs={{0,2},{1,3},{2,0},{3,1},{4,6},{5,7},{6,4},{7,5},{8,10},{9,11},{10,... | collective-permute-start | bytes 1179656 | tf_op jit(solution)/shard_map/ppermute | solution.py:19
  5.5 8.0 %collective-permute-start.2 = (bf16[104,768]{1,0:T(8,128)(2,1)}, bf16[104,768]{1,0:T(8,128)(2,1)S(1)}, u32[]{:S(2)}, u32[]{:S(2)}) collective-permute-start(bf16[104,768]{1,0:T(8,128)(2,1)} %shard_map.289.refs_0_), channel_id=1, source_target_pairs={{0,4},{4,0},{8,12},{12,8},{16,20},{20,16},{24,28},{28,24},{1,5},{5... | collective-permute-start | bytes 479240 | tf_op jit(solution)/shard_map/ppermute | solution.py:19
  7.1 9.8 %collective-permute-start.1 = (bf16[104,768]{1,0:T(8,128)(2,1)}, bf16[104,768]{1,0:T(8,128)(2,1)S(1)}, u32[]{:S(2)}, u32[]{:S(2)}) collective-permute-start(bf16[104,768]{1,0:T(8,128)(2,1)} %shard_map.289.refs_0_), channel_id=1, source_target_pairs={{0,16},{4,20},{8,24},{12,28},{16,0},{20,4},{24,8},{28,12},{1,17},{... | collective-permute-start | bytes 479240 | tf_op jit(solution)/shard_map/ppermute | solution.py:19
  9.6 0.9 copy-start.4
  10.6 1.0 copy-start.5
  11.6 0.9 copy-start
  12.5 0.9 copy-start.2
  13.5 20.1 %copy-start.3 = (bf16[768,96]{0,1:T(8,128)(2,1)S(1)}, bf16[768,96]{0,1:T(8,128)(2,1)}, u32[]{:S(2)}) copy-start(bf16[768,96]{0,1:T(8,128)(2,1)} %param.32) | copy-start | bytes 442372
  13.5 21.8 %copy-start.7 = (bf16[1,6,768]{2,1,0:T(8,128)(2,1)S(1)}, bf16[1,6,768]{2,1,0:T(8,128)(2,1)}, u32[]{:S(2)}) copy-start(bf16[1,6,768]{2,1,0:T(8,128)(2,1)} %param.19) | copy-start | bytes 27652
  13.5 21.8 %copy-start.9 = (s32[1,6]{1,0:T(1,128)S(1)}, s32[1,6]{1,0:T(1,128)}, u32[]{:S(2)}) copy-start(s32[1,6]{1,0:T(1,128)} %thought_pos.3) | copy-start | bytes 76
  16.9 13.3 %collective-permute-start.7 = (bf16[256,768]{1,0:T(8,128)(2,1)}, bf16[256,768]{1,0:T(8,128)(2,1)S(1)}, u32[]{:S(2)}, u32[]{:S(2)}) collective-permute-start(bf16[256,768]{1,0:T(8,128)(2,1)} %bitcast.51), channel_id=1, source_target_pairs={{0,2},{1,3},{2,0},{3,1},{4,6},{5,7},{6,4},{7,5},{8,10},{9,11},{10,... | collective-permute-start | bytes 1179656 | tf_op jit(solution)/shard_map/ppermute | solution.py:19
  17.5 12.7 %collective-permute-start.3 = (bf16[2,104,768]{2,1,0:T(8,128)(2,1)S(1)}, bf16[2,104,768]{2,1,0:T(8,128)(2,1)S(1)}, u32[]{:S(2)}, u32[]{:S(2)}) collective-permute-start(bf16[2,104,768]{2,1,0:T(8,128)(2,1)S(1)} %shard_map.292), channel_id=1, source_target_pairs={{0,8},{4,12},{8,0},{12,4},{16,24},{20,28},{24,16},{28,20},{1,9},{5... | collective-permute-start | bytes 958472 | tf_op jit(solution)/shard_map/ppermute | solution.py:19
  18.3 11.9 %collective-permute-start.6 = (bf16[2,96,768]{2,1,0:T(8,128)(2,1)S(1)}, bf16[2,96,768]{2,1,0:T(8,128)(2,1)S(1)}, u32[]{:S(2)}, u32[]{:S(2)}) collective-permute-start(bf16[2,96,768]{2,1,0:T(8,128)(2,1)S(1)} %shard_map.291), channel_id=1, source_target_pairs={{0,4},{4,0},{8,12},{12,8},{16,20},{20,16},{24,28},{28,24},{1,5},{5... | collective-permute-start | bytes 884744 | tf_op jit(solution)/shard_map/ppermute | solution.py:19
  19.8 10.4 %collective-permute-start.4 = (bf16[104,768]{1,0:T(8,128)(2,1)S(1)}, bf16[104,768]{1,0:T(8,128)(2,1)}, u32[]{:S(2)}, u32[]{:S(2)}) collective-permute-start(bf16[104,768]{1,0:T(8,128)(2,1)S(1)} %collective-permute-done.1.b), channel_id=1, source_target_pairs={{0,4},{4,0},{8,12},{12,8},{16,20},{20,16},{24,28},{28,24},{1,5},{5... | collective-permute-start | bytes 479240 | tf_op jit(solution)/shard_map/ppermute | solution.py:19
  20.3 7.8 %collective-permute-start.5 = (bf16[96,768]{1,0:T(8,128)(2,1)S(1)}, bf16[96,768]{1,0:T(8,128)(2,1)S(1)}, u32[]{:S(2)}, u32[]{:S(2)}) collective-permute-start(bf16[96,768]{1,0:T(8,128)(2,1)S(1)} %copy-done.1), channel_id=1, source_target_pairs={{0,16},{4,20},{8,24},{12,28},{16,0},{20,4},{24,8},{28,12},{1,17},{... | collective-permute-start | bytes 442376 | tf_op jit(solution)/shard_map/ppermute | solution.py:19
  30.8 4.4 %collective-permute-start.9 = (bf16[2,256,768]{2,1,0:T(8,128)(2,1)S(1)}, bf16[2,256,768]{2,1,0:T(8,128)(2,1)S(1)}, u32[]{:S(2)}, u32[]{:S(2)}) collective-permute-start(bf16[2,256,768]{2,1,0:T(8,128)(2,1)S(1)} %shard_map.293.x_zero), channel_id=1, source_target_pairs={{0,1},{1,0},{2,3},{3,2},{4,5},{5,4},{6,7},{7,6},{8,9},{9,8},{10,11... | collective-permute-start | bytes 2359304 | tf_op jit(solution)/shard_map/ppermute | solution.py:19
  30.9 10.0 %collective-permute-start.8 = (bf16[2,104,768]{2,1,0:T(8,128)(2,1)S(1)}, bf16[2,104,768]{2,1,0:T(8,128)(2,1)S(1)}, u32[]{:S(2)}, u32[]{:S(2)}) collective-permute-start(bf16[2,104,768]{2,1,0:T(8,128)(2,1)S(1)} %collective-permute-done.3.refs_3_), channel_id=1, source_target_pairs={{0,4},{4,0},{8,12},{12,8},{16,20},{20,16},{24,28},{28,24},{1,5},{5... | collective-permute-start | bytes 958472 | tf_op jit(solution)/shard_map/ppermute | solution.py:19
  31.5 16.1 %collective-permute-start.10 = (bf16[2,96,768]{2,1,0:T(8,128)(2,1)S(1)}, bf16[2,96,768]{2,1,0:T(8,128)(2,1)S(1)}, u32[]{:S(2)}, u32[]{:S(2)}) collective-permute-start(bf16[2,96,768]{2,1,0:T(8,128)(2,1)S(1)} %shard_map.298), channel_id=1, source_target_pairs={{0,8},{4,12},{8,0},{12,4},{16,24},{20,28},{24,16},{28,20},{1,9},{5... | collective-permute-start | bytes 884744 | tf_op jit(solution)/shard_map/ppermute | solution.py:19
  33.5 14.1 %collective-permute-start.11 = (bf16[96,768]{1,0:T(8,128)(2,1)S(1)}, bf16[96,768]{1,0:T(8,128)(2,1)S(1)}, u32[]{:S(2)}, u32[]{:S(2)}) collective-permute-start(bf16[96,768]{1,0:T(8,128)(2,1)S(1)} %bitcast.41), channel_id=1, source_target_pairs={{0,16},{4,20},{8,24},{12,28},{16,0},{20,4},{24,8},{28,12},{1,17},{... | collective-permute-start | bytes 442376 | tf_op jit(solution)/shard_map/ppermute | solution.py:19
  40.8 6.8 %collective-permute-start.12 = (bf16[96,768]{1,0:T(8,128)(2,1)S(1)}, bf16[96,768]{1,0:T(8,128)(2,1)S(1)}, u32[]{:S(2)}, u32[]{:S(2)}) collective-permute-start(bf16[96,768]{1,0:T(8,128)(2,1)S(1)} %collective-permute-done.5.b), channel_id=1, source_target_pairs={{0,4},{4,0},{8,12},{12,8},{16,20},{20,16},{24,28},{28,24},{1,5},{5... | collective-permute-start | bytes 442376 | tf_op jit(solution)/shard_map/ppermute | solution.py:19
  42.6 1.4 copy-start.8
  47.6 5.5 %copy-start.6 = (bf16[1,256,768]{2,1,0:T(8,128)(2,1)S(1)}, bf16[1,256,768]{2,1,0:T(8,128)(2,1)}, u32[]{:S(2)}) copy-start(bf16[1,256,768]{2,1,0:T(8,128)(2,1)} %param.34) | copy-start | bytes 1179652
  47.6 1.8 %collective-permute-start.13 = (bf16[256,768]{1,0:T(8,128)(2,1)S(1)}, bf16[256,768]{1,0:T(8,128)(2,1)S(1)}, u32[]{:S(2)}, u32[]{:S(2)}) collective-permute-start(bf16[256,768]{1,0:T(8,128)(2,1)S(1)} %get-tuple-element.206), channel_id=1, source_target_pairs={{0,1},{1,0},{2,3},{3,2},{4,5},{5,4},{6,7},{7,6},{8,9},{9,8},{10,11... | collective-permute-start | bytes 1179656 | tf_op jit(solution)/shard_map/ppermute | solution.py:19
  47.8 12.6 %collective-permute-start.15 = (bf16[3,96,768]{2,1,0:T(8,128)(2,1)S(1)}, bf16[3,96,768]{2,1,0:T(8,128)(2,1)S(1)}, u32[]{:S(2)}, u32[]{:S(2)}) collective-permute-start(bf16[3,96,768]{2,1,0:T(8,128)(2,1)S(1)} %shard_map.301), channel_id=1, source_target_pairs={{0,4},{4,0},{8,12},{12,8},{16,20},{20,16},{24,28},{28,24},{1,5},{5... | collective-permute-start | bytes 1327112 | tf_op jit(solution)/shard_map/ppermute | solution.py:19
  49.5 11.2 %collective-permute-start.14 = (bf16[256,768]{1,0:T(8,128)(2,1)S(1)}, bf16[256,768]{1,0:T(8,128)(2,1)S(1)}, u32[]{:S(2)}, u32[]{:S(2)}) collective-permute-start(bf16[256,768]{1,0:T(8,128)(2,1)S(1)} %shard_map.299.a), channel_id=1, source_target_pairs={{0,2},{1,3},{2,0},{3,1},{4,6},{5,7},{6,4},{7,5},{8,10},{9,11},{10,... | collective-permute-start | bytes 1179656 | tf_op jit(solution)/shard_map/ppermute | solution.py:19
  51.1 9.1 %collective-permute-start.16 = (bf16[2,96,768]{2,1,0:T(8,128)(2,1)S(1)}, bf16[2,96,768]{2,1,0:T(8,128)(2,1)S(1)}, u32[]{:S(2)}, u32[]{:S(2)}) collective-permute-start(bf16[2,96,768]{2,1,0:T(8,128)(2,1)S(1)} %shard_map.302), channel_id=1, source_target_pairs={{0,8},{4,12},{8,0},{12,4},{16,24},{20,28},{24,16},{28,20},{1,9},{5... | collective-permute-start | bytes 884744 | tf_op jit(solution)/shard_map/ppermute | solution.py:19
  53.7 15.7 %collective-permute-start.19 = (bf16[2,256,768]{2,1,0:T(8,128)(2,1)S(1)}, bf16[2,256,768]{2,1,0:T(8,128)(2,1)S(1)}, u32[]{:S(2)}, u32[]{:S(2)}) collective-permute-start(bf16[2,256,768]{2,1,0:T(8,128)(2,1)S(1)} %shard_map.307.cot_zero), channel_id=1, source_target_pairs={{0,1},{1,0},{2,3},{3,2},{4,5},{5,4},{6,7},{7,6},{8,9},{9,8},{10,11... | collective-permute-start | bytes 2359304 | tf_op jit(solution)/shard_map/ppermute | solution.py:19
  60.7 2.2 %collective-permute-start.17 = (bf16[256,768]{1,0:T(8,128)(2,1)S(1)}, bf16[256,768]{1,0:T(8,128)(2,1)S(1)}, u32[]{:S(2)}, u32[]{:S(2)}) collective-permute-start(bf16[256,768]{1,0:T(8,128)(2,1)S(1)} %get-tuple-element.212), channel_id=1, source_target_pairs={{0,1},{1,0},{2,3},{3,2},{4,5},{5,4},{6,7},{7,6},{8,9},{9,8},{10,11... | collective-permute-start | bytes 1179656 | tf_op jit(solution)/shard_map/ppermute | solution.py:19
  60.8 9.6 %collective-permute-start.18 = (bf16[256,768]{1,0:T(8,128)(2,1)S(1)}, bf16[256,768]{1,0:T(8,128)(2,1)S(1)}, u32[]{:S(2)}, u32[]{:S(2)}) collective-permute-start(bf16[256,768]{1,0:T(8,128)(2,1)S(1)} %shard_map.306.total), channel_id=1, source_target_pairs={{0,1},{1,0},{2,3},{3,2},{4,5},{5,4},{6,7},{7,6},{8,9},{9,8},{10,11... | collective-permute-start | bytes 1179656 | tf_op jit(solution)/shard_map/ppermute | solution.py:19
  61.4 9.0 %collective-permute-start.20 = (bf16[2,96,768]{2,1,0:T(8,128)(2,1)S(1)}, bf16[2,96,768]{2,1,0:T(8,128)(2,1)S(1)}, u32[]{:S(2)}, u32[]{:S(2)}) collective-permute-start(bf16[2,96,768]{2,1,0:T(8,128)(2,1)S(1)} %collective-permute-done.16.refs_3_), channel_id=1, source_target_pairs={{0,4},{4,0},{8,12},{12,8},{16,20},{20,16},{24,28},{28,24},{1,5},{5... | collective-permute-start | bytes 884744 | tf_op jit(solution)/shard_map/ppermute | solution.py:19
  63.0 10.9 %collective-permute-start.22 = (bf16[256,768]{1,0:T(8,128)(2,1)S(1)}, bf16[256,768]{1,0:T(8,128)(2,1)S(1)}, u32[]{:S(2)}, u32[]{:S(2)}) collective-permute-start(bf16[256,768]{1,0:T(8,128)(2,1)S(1)} %shard_map.303.a), channel_id=1, source_target_pairs={{0,2},{1,3},{2,0},{3,1},{4,6},{5,7},{6,4},{7,5},{8,10},{9,11},{10,... | collective-permute-start | bytes 1179656 | tf_op jit(solution)/shard_map/ppermute | solution.py:19
  73.8 1.8 %collective-permute-start.21 = (bf16[256,768]{1,0:T(8,128)(2,1)S(1)}, bf16[256,768]{1,0:T(8,128)(2,1)S(1)}, u32[]{:S(2)}, u32[]{:S(2)}) collective-permute-start(bf16[256,768]{1,0:T(8,128)(2,1)S(1)} %get-tuple-element.231), channel_id=1, source_target_pairs={{0,1},{1,0},{2,3},{3,2},{4,5},{5,4},{6,7},{7,6},{8,9},{9,8},{10,11... | collective-permute-start | bytes 1179656 | tf_op jit(solution)/shard_map/ppermute | solution.py:19
  74.0 3.2 %collective-permute-start.23 = (bf16[256,768]{1,0:T(8,128)(2,1)S(1)}, bf16[256,768]{1,0:T(8,128)(2,1)S(1)}, u32[]{:S(2)}, u32[]{:S(2)}) collective-permute-start(bf16[256,768]{1,0:T(8,128)(2,1)S(1)} %shard_map.312.total), channel_id=1, source_target_pairs={{0,1},{1,0},{2,3},{3,2},{4,5},{5,4},{6,7},{7,6},{8,9},{9,8},{10,11... | collective-permute-start | bytes 1179656 | tf_op jit(solution)/shard_map/ppermute | solution.py:19
  75.7 11.7 %collective-permute-start.24 = (bf16[256,768]{1,0:T(8,128)(2,1)S(1)}, bf16[256,768]{1,0:T(8,128)(2,1)S(1)}, u32[]{:S(2)}, u32[]{:S(2)}) collective-permute-start(bf16[256,768]{1,0:T(8,128)(2,1)S(1)} %shard_map.311.a), channel_id=1, source_target_pairs={{0,2},{1,3},{2,0},{3,1},{4,6},{5,7},{6,4},{7,5},{8,10},{9,11},{10,... | collective-permute-start | bytes 1179656 | tf_op jit(solution)/shard_map/ppermute | solution.py:19
  80.0 7.7 %collective-permute-start.26 = (bf16[256,768]{1,0:T(8,128)(2,1)S(1)}, bf16[256,768]{1,0:T(8,128)(2,1)S(1)}, u32[]{:S(2)}, u32[]{:S(2)}) collective-permute-start(bf16[256,768]{1,0:T(8,128)(2,1)S(1)} %get-tuple-element.252), channel_id=1, source_target_pairs={{0,1},{1,0},{2,3},{3,2},{4,5},{5,4},{6,7},{7,6},{8,9},{9,8},{10,11... | collective-permute-start | bytes 1179656 | tf_op jit(solution)/shard_map/ppermute | solution.py:19
  82.2 16.2 %collective-permute-start.27 = (bf16[4,96,768]{2,1,0:T(8,128)(2,1)S(1)}, bf16[4,96,768]{2,1,0:T(8,128)(2,1)S(1)}, u32[]{:S(2)}, u32[]{:S(2)}) collective-permute-start(bf16[4,96,768]{2,1,0:T(8,128)(2,1)S(1)} %get-tuple-element.237), channel_id=1, source_target_pairs={{0,4},{4,0},{8,12},{12,8},{16,20},{20,16},{24,28},{28,24},{1,5},{5... | collective-permute-start | bytes 1769480 | tf_op jit(solution)/shard_map/ppermute | solution.py:19
  87.5 1.8 %collective-permute-start.25 = (bf16[256,768]{1,0:T(8,128)(2,1)S(1)}, bf16[256,768]{1,0:T(8,128)(2,1)S(1)}, u32[]{:S(2)}, u32[]{:S(2)}) collective-permute-start(bf16[256,768]{1,0:T(8,128)(2,1)S(1)} %shard_map.317.total), channel_id=1, source_target_pairs={{0,1},{1,0},{2,3},{3,2},{4,5},{5,4},{6,7},{7,6},{8,9},{9,8},{10,11... | collective-permute-start | bytes 1179656 | tf_op jit(solution)/shard_map/ppermute | solution.py:19
  87.8 11.4 %collective-permute-start.28 = (bf16[256,768]{1,0:T(8,128)(2,1)S(1)}, bf16[256,768]{1,0:T(8,128)(2,1)S(1)}, u32[]{:S(2)}, u32[]{:S(2)}) collective-permute-start(bf16[256,768]{1,0:T(8,128)(2,1)S(1)} %shard_map.320.a), channel_id=1, source_target_pairs={{0,2},{1,3},{2,0},{3,1},{4,6},{5,7},{6,4},{7,5},{8,10},{9,11},{10,... | collective-permute-start | bytes 1179656 | tf_op jit(solution)/shard_map/ppermute | solution.py:19
  89.3 21.4 %collective-permute-start.31 = (bf16[4,96,768]{2,1,0:T(8,128)(2,1)S(1)}, bf16[4,96,768]{2,1,0:T(8,128)(2,1)S(1)}, u32[]{:S(2)}, u32[]{:S(2)}) collective-permute-start(bf16[4,96,768]{2,1,0:T(8,128)(2,1)S(1)} %get-tuple-element.265), channel_id=1, source_target_pairs={{0,4},{4,0},{8,12},{12,8},{16,20},{20,16},{24,28},{28,24},{1,5},{5... | collective-permute-start | bytes 1769480 | tf_op jit(solution)/shard_map/ppermute | solution.py:19
  90.3 33.4 %collective-permute-start.43 = (bf16[2,256,768]{2,1,0:T(8,128)(2,1)S(1)}, bf16[2,256,768]{2,1,0:T(8,128)(2,1)S(1)}, u32[]{:S(2)}, u32[]{:S(2)}) collective-permute-start(bf16[2,256,768]{2,1,0:T(8,128)(2,1)S(1)} %get-tuple-element.306), channel_id=1, source_target_pairs={{0,1},{1,0},{2,3},{3,2},{4,5},{5,4},{6,7},{7,6},{8,9},{9,8},{10,11... | collective-permute-start | bytes 2359304 | tf_op jit(solution)/shard_map/ppermute | solution.py:19
  99.3 2.8 %collective-permute-start.29 = (bf16[256,768]{1,0:T(8,128)(2,1)S(1)}, bf16[256,768]{1,0:T(8,128)(2,1)S(1)}, u32[]{:S(2)}, u32[]{:S(2)}) collective-permute-start(bf16[256,768]{1,0:T(8,128)(2,1)S(1)} %shard_map.321.total), channel_id=1, source_target_pairs={{0,1},{1,0},{2,3},{3,2},{4,5},{5,4},{6,7},{7,6},{8,9},{9,8},{10,11... | collective-permute-start | bytes 1179656 | tf_op jit(solution)/shard_map/ppermute | solution.py:19
  100.1 10.6 %collective-permute-start.30 = (bf16[2,96,768]{2,1,0:T(8,128)(2,1)S(1)}, bf16[2,96,768]{2,1,0:T(8,128)(2,1)S(1)}, u32[]{:S(2)}, u32[]{:S(2)}) collective-permute-start(bf16[2,96,768]{2,1,0:T(8,128)(2,1)S(1)} %get-tuple-element.264), channel_id=1, source_target_pairs={{0,8},{4,12},{8,0},{12,4},{16,24},{20,28},{24,16},{28,20},{1,9},{5... | collective-permute-start | bytes 884744 | tf_op jit(solution)/shard_map/ppermute | solution.py:19
  112.8 12.4 %collective-permute-start.32 = (bf16[256,768]{1,0:T(8,128)(2,1)S(1)}, bf16[256,768]{1,0:T(8,128)(2,1)S(1)}, u32[]{:S(2)}, u32[]{:S(2)}) collective-permute-start(bf16[256,768]{1,0:T(8,128)(2,1)S(1)} %get-tuple-element.271), channel_id=1, source_target_pairs={{0,1},{1,0},{2,3},{3,2},{4,5},{5,4},{6,7},{7,6},{8,9},{9,8},{10,11... | collective-permute-start | bytes 1179656 | tf_op jit(solution)/shard_map/ppermute | solution.py:19
  112.9 13.6 %collective-permute-start.33 = (bf16[256,768]{1,0:T(8,128)(2,1)S(1)}, bf16[256,768]{1,0:T(8,128)(2,1)S(1)}, u32[]{:S(2)}, u32[]{:S(2)}) collective-permute-start(bf16[256,768]{1,0:T(8,128)(2,1)S(1)} %get-tuple-element.272), channel_id=1, source_target_pairs={{0,1},{1,0},{2,3},{3,2},{4,5},{5,4},{6,7},{7,6},{8,9},{9,8},{10,11... | collective-permute-start | bytes 1179656 | tf_op jit(solution)/shard_map/ppermute | solution.py:19
  113.4 1.8 %collective-permute-start.34 = (f32[8,768]{1,0:T(8,128)S(1)}, f32[8,768]{1,0:T(8,128)S(1)}, u32[]{:S(2)}, u32[]{:S(2)}) collective-permute-start(f32[8,768]{1,0:T(8,128)S(1)} %get-tuple-element.275.a), channel_id=1, source_target_pairs={{0,1},{1,0},{2,3},{3,2},{4,5},{5,4},{6,7},{7,6},{8,9},{9,8},{10,11... | collective-permute-start | bytes 73736 | tf_op jit(solution)/shard_map/ppermute | solution.py:19
  115.2 4.5 %collective-permute-start.35 = (f32[8,768]{1,0:T(8,128)S(1)}, f32[8,768]{1,0:T(8,128)S(1)}, u32[]{:S(2)}, u32[]{:S(2)}) collective-permute-start(f32[8,768]{1,0:T(8,128)S(1)} %shard_map.327.a), channel_id=1, source_target_pairs={{0,2},{1,3},{2,0},{3,1},{4,6},{5,7},{6,4},{7,5},{8,10},{9,11},{10,... | collective-permute-start | bytes 73736 | tf_op jit(solution)/shard_map/ppermute | solution.py:19
  117.5 11.3 %collective-permute-start.38 = (bf16[4,96,384]{2,1,0:T(8,128)(2,1)S(1)}, bf16[4,96,384]{2,1,0:T(8,128)(2,1)S(1)}, u32[]{:S(2)}, u32[]{:S(2)}) collective-permute-start(bf16[4,96,384]{2,1,0:T(8,128)(2,1)S(1)} %get-tuple-element.292), channel_id=1, source_target_pairs={{0,4},{4,0},{8,12},{12,8},{16,20},{20,16},{24,28},{28,24},{1,5},{5... | collective-permute-start | bytes 884744 | tf_op jit(solution)/shard_map/ppermute | solution.py:19
  119.7 11.0 %collective-permute-start.39 = (bf16[2,96,768]{2,1,0:T(8,128)(2,1)S(1)}, bf16[2,96,768]{2,1,0:T(8,128)(2,1)S(1)}, u32[]{:S(2)}, u32[]{:S(2)}) collective-permute-start(bf16[2,96,768]{2,1,0:T(8,128)(2,1)S(1)} %get-tuple-element.295), channel_id=1, source_target_pairs={{0,8},{4,12},{8,0},{12,4},{16,24},{20,28},{24,16},{28,20},{1,9},{5... | collective-permute-start | bytes 884744 | tf_op jit(solution)/shard_map/ppermute | solution.py:19
  123.7 13.2 %collective-permute-start.37 = (bf16[4,104,384]{2,1,0:T(8,128)(2,1)S(1)}, bf16[4,104,384]{2,1,0:T(8,128)(2,1)S(1)}, u32[]{:S(2)}, u32[]{:S(2)}) collective-permute-start(bf16[4,104,384]{2,1,0:T(8,128)(2,1)S(1)} %get-tuple-element.287), channel_id=1, source_target_pairs={{0,4},{4,0},{8,12},{12,8},{16,20},{20,16},{24,28},{28,24},{1,5},{5... | collective-permute-start | bytes 958472 | tf_op jit(solution)/shard_map/ppermute | solution.py:19
  125.2 24.0 %collective-permute-start.44 = (bf16[1,256,768]{2,1,0:T(8,128)(2,1)S(1)}, bf16[1,256,768]{2,1,0:T(8,128)(2,1)S(1)}, u32[]{:S(2)}, u32[]{:S(2)}) collective-permute-start(bf16[1,256,768]{2,1,0:T(8,128)(2,1)S(1)} %get-tuple-element.309), channel_id=1, source_target_pairs={{0,2},{1,3},{2,0},{3,1},{4,6},{5,7},{6,4},{7,5},{8,10},{9,11},{10,... | collective-permute-start | bytes 1179656 | tf_op jit(solution)/shard_map/ppermute | solution.py:19
  127.3 23.6 %collective-permute-start.36 = (bf16[256,768]{1,0:T(8,128)(2,1)S(1)}, bf16[256,768]{1,0:T(8,128)(2,1)S(1)}, u32[]{:S(2)}, u32[]{:S(2)}) collective-permute-start(bf16[256,768]{1,0:T(8,128)(2,1)S(1)} %get-tuple-element.276), channel_id=1, source_target_pairs={{0,2},{1,3},{2,0},{3,1},{4,6},{5,7},{6,4},{7,5},{8,10},{9,11},{10,... | collective-permute-start | bytes 1179656 | tf_op jit(solution)/shard_map/ppermute | solution.py:19
  128.8 8.1 %collective-permute-start.41 = (bf16[1,96,768]{2,1,0:T(8,128)(2,1)S(1)}, bf16[1,96,768]{2,1,0:T(8,128)(2,1)S(1)}, u32[]{:S(2)}, u32[]{:S(2)}) collective-permute-start(bf16[1,96,768]{2,1,0:T(8,128)(2,1)S(1)} %get-tuple-element.298), channel_id=1, source_target_pairs={{0,16},{4,20},{8,24},{12,28},{16,0},{20,4},{24,8},{28,12},{1,17},{... | collective-permute-start | bytes 442376 | tf_op jit(solution)/shard_map/ppermute | solution.py:19
  131.3 6.4 %collective-permute-start.40 = (bf16[2,96,384]{2,1,0:T(8,128)(2,1)S(1)}, bf16[2,96,384]{2,1,0:T(8,128)(2,1)S(1)}, u32[]{:S(2)}, u32[]{:S(2)}) collective-permute-start(bf16[2,96,384]{2,1,0:T(8,128)(2,1)S(1)} %get-tuple-element.297), channel_id=1, source_target_pairs={{0,8},{4,12},{8,0},{12,4},{16,24},{20,28},{24,16},{28,20},{1,9},{5... | collective-permute-start | bytes 442376 | tf_op jit(solution)/shard_map/ppermute | solution.py:19
  138.3 6.7 %collective-permute-start.45 = (bf16[2,104,384]{2,1,0:T(8,128)(2,1)S(1)}, bf16[2,104,384]{2,1,0:T(8,128)(2,1)S(1)}, u32[]{:S(2)}, u32[]{:S(2)}) collective-permute-start(bf16[2,104,384]{2,1,0:T(8,128)(2,1)S(1)} %get-tuple-element.313), channel_id=1, source_target_pairs={{0,8},{4,12},{8,0},{12,4},{16,24},{20,28},{24,16},{28,20},{1,9},{5... | collective-permute-start | bytes 479240 | tf_op jit(solution)/shard_map/ppermute | solution.py:19
  139.4 11.5 %collective-permute-start.42 = (bf16[1,96,768]{2,1,0:T(8,128)(2,1)S(1)}, bf16[1,96,768]{2,1,0:T(8,128)(2,1)S(1)}, u32[]{:S(2)}, u32[]{:S(2)}) collective-permute-start(bf16[1,96,768]{2,1,0:T(8,128)(2,1)S(1)} %get-tuple-element.303), channel_id=1, source_target_pairs={{0,16},{4,20},{8,24},{12,28},{16,0},{20,4},{24,8},{28,12},{1,17},{... | collective-permute-start | bytes 442376 | tf_op jit(solution)/shard_map/ppermute | solution.py:19
  145.6 7.6 %collective-permute-start.46 = (bf16[1,104,384]{2,1,0:T(8,128)(2,1)S(1)}, bf16[1,104,384]{2,1,0:T(8,128)(2,1)S(1)}, u32[]{:S(2)}, u32[]{:S(2)}) collective-permute-start(bf16[1,104,384]{2,1,0:T(8,128)(2,1)S(1)} %get-tuple-element.314), channel_id=1, source_target_pairs={{0,16},{4,20},{8,24},{12,28},{16,0},{20,4},{24,8},{28,12},{1,17},{... | collective-permute-start | bytes 239624 | tf_op jit(solution)/shard_map/ppermute | solution.py:19
  146.7 6.5 %collective-permute-start.47 = (bf16[1,96,384]{2,1,0:T(8,128)(2,1)S(1)}, bf16[1,96,384]{2,1,0:T(8,128)(2,1)S(1)}, u32[]{:S(2)}, u32[]{:S(2)}) collective-permute-start(bf16[1,96,384]{2,1,0:T(8,128)(2,1)S(1)} %get-tuple-element.317), channel_id=1, source_target_pairs={{0,16},{4,20},{8,24},{12,28},{16,0},{20,4},{24,8},{28,12},{1,17},{... | collective-permute-start | bytes 221192 | tf_op jit(solution)/shard_map/ppermute | solution.py:19

commit v5 on v4

--- a/solution.py
+++ b/solution.py
@@ -483,6 +483,13 @@
         ref[...] = keep[0] + got[0].astype(F32)
 
 
+def end_kernel(place, keep, got, mlp_got, pre_zero, pre_one, *rest):
+    *rest, result_ref = rest
+    width = result_ref.shape[1]
+    result_ref[...] = result_of(place, keep[:, width:], mlp_got, pre_zero, pre_one, rest[3])
+    output_kernel(place, keep[:, :width], got, *rest)
+
+
 def fold_kernel(bit, place, *refs):
     *parts, keep_ref, send_ref = refs
     half = keep_ref.shape[0]
@@ -509,16 +516,21 @@
     return call(functools.partial(fold_kernel, bit), ((shape, F32), (shape, LOW)), place, *parts)
 
 
-def fold_two_kernel(bit, place, keep, low, high, keep_ref, send_ref):
-    first = place[bit] == 0
+def fold_rows_kernel(bit, place, keep, low, high, mlp_keep, mlp_got, keep_ref, send_ref, mlp_ref):
+    first, cols = place[bit] == 0, low.shape[1]
     low, high = keep[0] + low[...].astype(F32), keep[1] + high[...].astype(F32)
-    keep_ref[...] = jnp.where(first, low, high)
+    keep_ref[:, :cols] = jnp.where(first, low, high)
     send_ref[...] = jnp.where(first, high, low).astype(LOW)
-
-
-def fold_two(bit, place, keep, low, high):
-    kinds = ((low.shape, F32), (low.shape, LOW))
-    return call(functools.partial(fold_two_kernel, bit), kinds, place, keep, low, high)
+    low, high = (mlp_keep[k] + mlp_got[k].astype(F32) for k in range(2))
+    keep_ref[:, cols:] = jnp.where(first, low, high)
+    mlp_ref[...] = jnp.where(first, high, low).astype(LOW)
+
+
+def fold_rows(bit, place, keep, low, high, mlp_keep, mlp_got):
+    shape = (low.shape[0], 2 * low.shape[1])
+    args = (keep, low, high, mlp_keep, mlp_got)
+    kinds = ((shape, F32), (low.shape, LOW), (low.shape, LOW))
+    return call(functools.partial(fold_rows_kernel, bit), kinds, place, *args)
 
 
 def add_kernel(a, b, out):
@@ -1025,8 +1037,7 @@
     other_one = core(total_one)
     b_keep, b_send = fold(5, place, b_keep, after(b_got, total_one))
     b_got = near(b_send)
-    mlp_keep, mlp_send = fold(3, place, mlp_keep, core(after(mlp_send, other_zero)))
-    mlp_got = over(after(mlp_send, total_one))
+    mlp_got = core(after(mlp_send, other_zero))
     res_one, branch_one, gatt_one, delta_one, sums_one = branch_back(
         1, total_one, other_one, residual_one, cots, vecs, w_proj_t, att_one
     )
@@ -1047,7 +1058,7 @@
     keep, send_low, send_high, small, mixed_sums, picked = input_back(
         place, thought_pos, (dq_zero, dq_one), dk, dv, w_in, xhat, grad_residual
     )
-    got_low, got_high = core(send_low), core(send_high)
+    got_low, got_high = core(after(send_low, d_send)), core(after(send_high, d_send))
     small = add_full(small, core(small))
     small = add_full(small, over(small))
     shape = (4, shard_rows + 8, 2 * head_cols)
@@ -1067,8 +1078,9 @@
         scratch=(*scratch, pltpu.VMEM((8, 4 * head_cols), F32)),
     )
     e_got = across(e_send)
-    keep, send = fold_two(3, place, keep, got_low, got_high)
+    keep, send, mlp_send = fold_rows(3, place, keep, got_low, got_high, mlp_keep, mlp_got)
     got = over(after(send, small))
+    mlp_got = over(after(mlp_send, small))
     d_keep, d_send = fold(5, place, d_keep, after(d_got, c_got))
     d_got = near(d_send)
     c_keep, c_send = fold(6, place, c_keep, after(c_got, d_send))
@@ -1082,11 +1094,34 @@
 
     e_keep, e_send = fold(6, place, e_keep, e_got)
     e_got = far(e_send)
-    block_out = result(place, mlp_keep[0], mlp_got[0], residual, vecs)
-    grad_embed, grad_thoughts, grad_up, grad_down = output_side(
-        place, keep, got, spliced, grad_residual, vecs, thought_pos, thoughts, small, picked,
-        b_keep, b_got, c_keep, c_got,
-    )
+    embed_shape = (keep.shape[0], width)
+    grad_embed, grad_thoughts, grad_up, grad_down, block_out = call(
+        end_kernel,
+        (
+            (embed_shape, F32),
+            ((thoughts.shape[0], 1, width // 4), F32),
+            (b_keep.shape[1:], F32),
+            (c_keep.shape[1:], F32),
+            (embed_shape, LOW),
+        ),
+        place,
+        keep,
+        got,
+        mlp_got,
+        *residual,
+        spliced,
+        *grad_residual,
+        vecs,
+        thought_pos,
+        thoughts,
+        small,
+        picked,
+        b_keep,
+        b_got,
+        c_keep,
+        c_got,
+    )
+    grad_thoughts = jnp.moveaxis(grad_thoughts, 1, 0)
     grad_embed, block_out, e_got, d_got = together(grad_embed, block_out, e_got, d_got)
     grad_in, grad_proj, *small = call(
         finish_kernel,

time: 154 us -> 153 us (level)
  Pallas kernels: 64.5 us -> 62.3 us
    pallas_call x52 -> x50, Pallas kernels: 62.6 us -> 60.4 us  [call(): pl.pallas_call(kernel, out_shape=tuple((jax.ShapeDtypeStruct(s, t) for s,...]
  transfers between devices with their start and end apart: 48 -> 48, of which waited for: 19 -> 20; matrix products, arithmetic and copies ran while one was open for 0% -> 0% of each run, Pallas kernels for 40% -> 39%
where the time goes in v5:
time: 153 us
  Pallas kernels  62.3 us (41%)
  starting transfers between devices  53 us (35%)
  waiting for transfers between devices  31.7 us (21%)
  local copies, waits for them, and re-layouts  4.48 us (3%)
    pallas_call x50, Pallas kernels, call(): pl.pallas_call(kernel, out_shape=tuple((jax.ShapeDtypeStruct(s, t) for s,...  60.4 us
    ppermute x48, starting transfers between devices, swapped(): lax.ppermute(array, axis, [(i, i ^ mask) for i in range(lax.axis_size(axi...  53 us
    ppermute x48, waiting for transfers between devices, swapped(): lax.ppermute(array, axis, [(i, i ^ mask) for i in range(lax.axis_size(axi...  31.7 us
    unnamed x20, local copies, waits for them, and re-layouts  3.79 us
  transfers between devices with their start and end apart: 48, of which 20 were waited for; matrix products, arithmetic and copies ran while one was open for 0% of the time, Pallas kernels for 39%

profile of v5, /device:TPU:0, one launch (start us, length us, event | category | flops | bytes accessed | tf_op | source)
XLA Modules:
  0.0 152.6 jit_solution(10260198553273446606)
XLA Ops:
  0.7 1.9 %shard_map.289.refs_0_ = bf16[104,768]{1,0:T(8,128)(2,1)} custom-call(bf16[3,96,192]{2,1,0:T(8,128)(2,1)} %refs_0_.1, bf16[192,96]{1,0:T(8,128)(2,1)} %refs_1_.1, bf16[1,96]{1,0:T(2,128)(2,1)} %bitcast.59, bf16[1,96]{1,0:T(2,128)(2,1)} %bitcast.60, bf16[1,96]{1,0:T(2,128)(2,1)} %bitcast.61, bf16[1,96]{1,0:T(2,128)(2,1)} %bitcast.62, bf16[1,96]{1,0:T(2,128)(2,1)} %bitcast.63, ...), custom_call_target="tpu_custom_call" | custom-call | flops 1000 | tf_op jit(solution)/shard_map/pallas_call | solution.py:765
  2.5 3.0 %collective-permute-start = (bf16[256,768]{1,0:T(8,128)(2,1)}, bf16[256,768]{1,0:T(8,128)(2,1)S(1)}, u32[]{:S(2)}, u32[]{:S(2)}) collective-permute-start(bf16[256,768]{1,0:T(8,128)(2,1)} %bitcast.45), channel_id=1, source_target_pairs={{0,2},{1,3},{2,0},{3,1},{4,6},{5,7},{6,4},{7,5},{8,10},{9,11},{10,... | collective-permute-start | bytes 1179656 | tf_op jit(solution)/shard_map/ppermute | solution.py:19
  5.5 1.5 collective-permute-start.2
  7.1 2.6 %collective-permute-start.1 = (bf16[104,768]{1,0:T(8,128)(2,1)}, bf16[104,768]{1,0:T(8,128)(2,1)S(1)}, u32[]{:S(2)}, u32[]{:S(2)}) collective-permute-start(bf16[104,768]{1,0:T(8,128)(2,1)} %shard_map.289.refs_0_), channel_id=1, source_target_pairs={{0,16},{4,20},{8,24},{12,28},{16,0},{20,4},{24,8},{28,12},{1,17},{... | collective-permute-start | bytes 479240 | tf_op jit(solution)/shard_map/ppermute | solution.py:19
  9.7 0.9 copy-done.4
  10.6 1.0 copy-done.5
  11.6 0.9 copy-done
  12.5 0.9 copy-done.2
  13.5 3.4 %collective-permute-done.1.b = bf16[104,768]{1,0:T(8,128)(2,1)S(1)} collective-permute-done((bf16[104,768]{1,0:T(8,128)(2,1)}, bf16[104,768]{1,0:T(8,128)(2,1)S(1)}, u32[]{:S(2)}, u32[]{:S(2)}) %collective-permute-start.1) | collective-permute-done | bytes 159776 | tf_op jit(solution)/shard_map/ppermute | solution.py:19
  18.3 1.5 collective-permute-start.6
  20.3 3.3 %collective-permute-start.5 = (bf16[96,768]{1,0:T(8,128)(2,1)S(1)}, bf16[96,768]{1,0:T(8,128)(2,1)S(1)}, u32[]{:S(2)}, u32[]{:S(2)}) collective-permute-start(bf16[96,768]{1,0:T(8,128)(2,1)S(1)} %copy-done.1), channel_id=1, source_target_pairs={{0,16},{4,20},{8,24},{12,28},{16,0},{20,4},{24,8},{28,12},{1,17},{... | collective-permute-start | bytes 442376 | tf_op jit(solution)/shard_map/ppermute | solution.py:19
  24.3 3.9 %collective-permute-done.5.b = bf16[96,768]{1,0:T(8,128)(2,1)S(1)} collective-permute-done((bf16[96,768]{1,0:T(8,128)(2,1)S(1)}, bf16[96,768]{1,0:T(8,128)(2,1)S(1)}, u32[]{:S(2)}, u32[]{:S(2)}) %collective-permute-start.5) | collective-permute-done | bytes 147488 | tf_op jit(solution)/shard_map/ppermute | solution.py:19
  28.1 1.9 %collective-permute-done.4 = bf16[104,768]{1,0:T(8,128)(2,1)S(1)} collective-permute-done((bf16[104,768]{1,0:T(8,128)(2,1)S(1)}, bf16[104,768]{1,0:T(8,128)(2,1)S(1)}, u32[]{:S(2)}, u32[]{:S(2)}) %collective-permute-start.4) | collective-permute-done | bytes 159776 | tf_op jit(solution)/shard_map/ppermute | solution.py:19
  31.4 2.2 %collective-permute-start.10 = (bf16[2,96,768]{2,1,0:T(8,128)(2,1)S(1)}, bf16[2,96,768]{2,1,0:T(8,128)(2,1)S(1)}, u32[]{:S(2)}, u32[]{:S(2)}) collective-permute-start(bf16[2,96,768]{2,1,0:T(8,128)(2,1)S(1)} %shard_map.298), channel_id=1, source_target_pairs={{0,8},{4,12},{8,0},{12,4},{16,24},{20,28},{24,16},{28,20},{1,9},{5... | collective-permute-start | bytes 884744 | tf_op jit(solution)/shard_map/ppermute | solution.py:19
  33.5 1.7 %collective-permute-start.11 = (bf16[96,768]{1,0:T(8,128)(2,1)S(1)}, bf16[96,768]{1,0:T(8,128)(2,1)S(1)}, u32[]{:S(2)}, u32[]{:S(2)}) collective-permute-start(bf16[96,768]{1,0:T(8,128)(2,1)S(1)} %bitcast.39), channel_id=1, source_target_pairs={{0,16},{4,20},{8,24},{12,28},{16,0},{20,4},{24,8},{28,12},{1,17},{... | collective-permute-start | bytes 442376 | tf_op jit(solution)/shard_map/ppermute | solution.py:19
  35.3 1.8 %shard_map.294 = (bf16[1024,768]{1,0:T(8,128)(2,1)S(1)}, f32[1024,768]{1,0:T(8,128)S(1)}) custom-call(s32[8]{0:T(128)S(1)} %dynamic-slice_bitcast_fusion.place, bf16[2,256,768]{2,1,0:T(8,128)(2,1)S(1)} %shard_map.293.x_zero, bf16[2,256,768]{2,1,0:T(8,128)(2,1)S(1)} %collective-permute-done.9.x_one, bf16[6,768]{1,0:T(8,128)(2,1)S(1)} %bitcast.52, ...), custom_call_target="tpu_custom_call" | custom-call | flops 1000 | tf_op jit(solution)/shard_map/pallas_call | solution.py:120
  37.0 3.7 %collective-permute-done.8.refs_5_ = bf16[2,104,768]{2,1,0:T(8,128)(2,1)S(1)} collective-permute-done((bf16[2,104,768]{2,1,0:T(8,128)(2,1)S(1)}, bf16[2,104,768]{2,1,0:T(8,128)(2,1)S(1)}, u32[]{:S(2)}, u32[]{:S(2)}) %collective-permute-start.8) | collective-permute-done | bytes 319520 | tf_op jit(solution)/shard_map/ppermute | solution.py:19
  42.1 1.4 shard_map.296
  43.5 3.6 %shard_map.297 = (bf16[512,192]{1,0:T(8,128)(2,1)S(1)}, f32[8,512]{1,0:T(8,128)S(1)}, f32[256,768]{1,0:T(8,128)S(1)}, bf16[256,768]{1,0:T(8,128)(2,1)S(1)}) custom-call(s32[8]{0:T(128)S(1)} %dynamic-slice_bitcast_fusion.place, s32[2]{0:T(128)S(1)} %bitcast.54, bf16[1024,192]{1,0:T(8,128)(2,1)S(1)} %get-tuple-element.200.q_ref, ...), custom_call_target="tpu_custom_call" | custom-call | flops 1000 | tf_op jit(solution)/shard_map/pallas_call | solution.py:120
  47.3 1.6 %collective-permute-start.15 = (bf16[3,96,768]{2,1,0:T(8,128)(2,1)S(1)}, bf16[3,96,768]{2,1,0:T(8,128)(2,1)S(1)}, u32[]{:S(2)}, u32[]{:S(2)}) collective-permute-start(bf16[3,96,768]{2,1,0:T(8,128)(2,1)S(1)} %shard_map.301), channel_id=1, source_target_pairs={{0,4},{4,0},{8,12},{12,8},{16,20},{20,16},{24,28},{28,24},{1,5},{5... | collective-permute-start | bytes 1327112 | tf_op jit(solution)/shard_map/ppermute | solution.py:19
  49.0 1.6 %collective-permute-start.14 = (bf16[256,768]{1,0:T(8,128)(2,1)S(1)}, bf16[256,768]{1,0:T(8,128)(2,1)S(1)}, u32[]{:S(2)}, u32[]{:S(2)}) collective-permute-start(bf16[256,768]{1,0:T(8,128)(2,1)S(1)} %shard_map.299.a), channel_id=1, source_target_pairs={{0,2},{1,3},{2,0},{3,1},{4,6},{5,7},{6,4},{7,5},{8,10},{9,11},{10,... | collective-permute-start | bytes 1179656 | tf_op jit(solution)/shard_map/ppermute | solution.py:19
  50.6 2.2 %collective-permute-start.16 = (bf16[2,96,768]{2,1,0:T(8,128)(2,1)S(1)}, bf16[2,96,768]{2,1,0:T(8,128)(2,1)S(1)}, u32[]{:S(2)}, u32[]{:S(2)}) collective-permute-start(bf16[2,96,768]{2,1,0:T(8,128)(2,1)S(1)} %shard_map.302), channel_id=1, source_target_pairs={{0,8},{4,12},{8,0},{12,4},{16,24},{20,28},{24,16},{28,20},{1,9},{5... | collective-permute-start | bytes 884744 | tf_op jit(solution)/shard_map/ppermute | solution.py:19
  53.5 6.2 %shard_map.300 = (bf16[512,192]{1,0:T(8,128)(2,1)S(1)}, f32[8,512]{1,0:T(8,128)S(1)}, f32[256,768]{1,0:T(8,128)S(1)}, bf16[256,768]{1,0:T(8,128)(2,1)S(1)}) custom-call(s32[8]{0:T(128)S(1)} %dynamic-slice_bitcast_fusion.place, s32[2]{0:T(128)S(1)} %bitcast.55, bf16[1024,192]{1,0:T(8,128)(2,1)S(1)} %get-tuple-element.200.q_ref, ...), custom_call_target="tpu_custom_call" | custom-call | flops 1000 | tf_op jit(solution)/shard_map/pallas_call | solution.py:120
  60.9 1.5 collective-permute-start.20
  62.5 1.6 %collective-permute-start.22 = (bf16[256,768]{1,0:T(8,128)(2,1)S(1)}, bf16[256,768]{1,0:T(8,128)(2,1)S(1)}, u32[]{:S(2)}, u32[]{:S(2)}) collective-permute-start(bf16[256,768]{1,0:T(8,128)(2,1)S(1)} %shard_map.303.a), channel_id=1, source_target_pairs={{0,2},{1,3},{2,0},{3,1},{4,6},{5,7},{6,4},{7,5},{8,10},{9,11},{10,... | collective-permute-start | bytes 1179656 | tf_op jit(solution)/shard_map/ppermute | solution.py:19
  64.7 1.5 %shard_map.305.probs_ref = bf16[3,512,512]{2,1,0:T(8,128)(2,1)S(1)} custom-call(s32[8]{0:T(128)S(1)} %dynamic-slice_bitcast_fusion.place, s32[2]{0:T(128)S(1)} %bitcast.56, bf16[1024,192]{1,0:T(8,128)(2,1)S(1)} %get-tuple-element.200.q_ref, bf16[1024,192]{1,0:T(8,128)(2,1)S(1)} %get-tuple-element.201.k_ref, f32[8,512]{1,0:T(8,128)S(1)} %get-tuple-element.217.log), custom_call_target="tpu_custom_call" | custom-call | flops 1000 | tf_op jit(solution)/shard_map/pallas_call | solution.py:120
  66.3 2.7 %shard_map.304.probs_ref = bf16[3,1024,512]{2,1,0:T(8,128)(2,1)S(1)} custom-call(s32[8]{0:T(128)S(1)} %dynamic-slice_bitcast_fusion.place, s32[2]{0:T(128)S(1)} %bitcast.57, bf16[1024,192]{1,0:T(8,128)(2,1)S(1)} %get-tuple-element.200.q_ref, bf16[1024,192]{1,0:T(8,128)(2,1)S(1)} %get-tuple-element.201.k_ref, f32[8,512]{1,0:T(8,128)S(1)} %get-tuple-element.216.log), custom_call_target="tpu_custom_call" | custom-call | flops 1000 | tf_op jit(solution)/shard_map/pallas_call | solution.py:120
  70.6 2.8 %shard_map.310 = (f32[512,768]{1,0:T(8,128)S(1)}, bf16[512,768]{1,0:T(8,128)(2,1)S(1)}, bf16[512,768]{1,0:T(8,128)(2,1)S(1)}, bf16[512,768]{1,0:T(8,128)(2,1)S(1...) custom-call(bf16[1024,768]{1,0:T(8,128)(2,1)S(1)} %get-tuple-element.235.spliced.rest_0_, ...), custom_call_target="tpu_custom_call" | custom-call | flops 1000 | tf_op jit(solution)/shard_map/pallas_call | solution.py:120
  74.1 1.0 collective-permute-done.21.b
  75.2 1.6 %collective-permute-start.24 = (bf16[256,768]{1,0:T(8,128)(2,1)S(1)}, bf16[256,768]{1,0:T(8,128)(2,1)S(1)}, u32[]{:S(2)}, u32[]{:S(2)}) collective-permute-start(bf16[256,768]{1,0:T(8,128)(2,1)S(1)} %shard_map.311.a), channel_id=1, source_target_pairs={{0,2},{1,3},{2,0},{3,1},{4,6},{5,7},{6,4},{7,5},{8,10},{9,11},{10,... | collective-permute-start | bytes 1179656 | tf_op jit(solution)/shard_map/ppermute | solution.py:19
  76.8 2.8 %shard_map.313 = (f32[512,768]{1,0:T(8,128)S(1)}, bf16[512,768]{1,0:T(8,128)(2,1)S(1)}, bf16[512,768]{1,0:T(8,128)(2,1)S(1)}, bf16[512,768]{1,0:T(8,128)(2,1)S(1...) custom-call(bf16[1024,768]{1,0:T(8,128)(2,1)S(1)} %get-tuple-element.235.spliced.rest_0_, ...), custom_call_target="tpu_custom_call" | custom-call | flops 1000 | tf_op jit(solution)/shard_map/pallas_call | solution.py:120
  79.6 2.1 %shard_map.314 = (f32[4,96,768]{2,1,0:T(8,128)S(1)}, bf16[4,96,768]{2,1,0:T(8,128)(2,1)S(1)}) custom-call(s32[8]{0:T(128)S(1)} %dynamic-slice_bitcast_fusion.place, bf16[512,768]{1,0:T(8,128)(2,1)S(1)} %get-tuple-element.234.refs_0_, bf16[512,768]{1,0:T(8,128)(2,1)S(1)} %get-tuple-element.236.refs_1_, bf16[512,768]{1,0:T(8,128)(2,1)S(1)} %get-tuple-element.237.refs_2_, ...), custom_call_target="tpu_custom_call" | custom-call | flops 1000 | tf_op jit(solution)/shard_map/pallas_call | solution.py:120
  81.8 1.6 %collective-permute-start.27 = (bf16[4,96,768]{2,1,0:T(8,128)(2,1)S(1)}, bf16[4,96,768]{2,1,0:T(8,128)(2,1)S(1)}, u32[]{:S(2)}, u32[]{:S(2)}) collective-permute-start(bf16[4,96,768]{2,1,0:T(8,128)(2,1)S(1)} %get-tuple-element.239), channel_id=1, source_target_pairs={{0,4},{4,0},{8,12},{12,8},{16,20},{20,16},{24,28},{28,24},{1,5},{5... | collective-permute-start | bytes 1769480 | tf_op jit(solution)/shard_map/ppermute | solution.py:19
  83.3 1.4 shard_map.316
  84.8 2.1 %shard_map.315 = (f32[4,96,768]{2,1,0:T(8,128)S(1)}, bf16[4,96,768]{2,1,0:T(8,128)(2,1)S(1)}) custom-call(s32[8]{0:T(128)S(1)} %dynamic-slice_bitcast_fusion.place, bf16[2,256,768]{2,1,0:T(8,128)(2,1)S(1)} %shard_map.307.cot_zero, bf16[2,256,768]{2,1,0:T(8,128)(2,1)S(1)} %collective-permute-done.19.cot_one, ...), custom_call_target="tpu_custom_call" | custom-call | flops 1000 | tf_op jit(solution)/shard_map/pallas_call | solution.py:120
  87.4 0.9 collective-permute-start.28
  88.8 1.1 collective-permute-start.31
  89.8 2.0 %shard_map.318 = (f32[512,768]{1,0:T(8,128)S(1)}, bf16[512,768]{1,0:T(8,128)(2,1)S(1)}, bf16[512,192]{1,0:T(8,128)(2,1)S(1)}, f32[8,512]{1,0:T(8,128)S(1)}, f32[8,768]{1,0:T(8,128)S(1)}) custom-call(bf16[256,768]{1,0:T(8,128)(2,1)S(1)} %shard_map.317.total, bf16[256,768]{1,0:T(8,128)(2,1)S(1)} %collective-permute-done.25.other, ...), custom_call_target="tpu_custom_call" | custom-call | flops 1000 | tf_op jit(solution)/shard_map/pallas_call | solution.py:120
  91.9 3.3 %shard_map.319 = (bf16[512,192]{1,0:T(8,128)(2,1)S(1)}, f32[512,192]{1,0:T(8,128)S(1)}, f32[512,192]{1,0:T(8,128)S(1)}) custom-call(s32[8]{0:T(128)S(1)} %dynamic-slice_bitcast_fusion.place, bf16[1024,192]{1,0:T(8,128)(2,1)S(1)} %get-tuple-element.200.q_ref, bf16[1024,192]{1,0:T(8,128)(2,1)S(1)} %get-tuple-element.201.k_ref, ...), custom_call_target="tpu_custom_call" | custom-call | flops 1000 | tf_op jit(solution)/shard_map/pallas_call | solution.py:120
  95.2 2.7 %collective-permute-done.27.refs_1_ = bf16[4,96,768]{2,1,0:T(8,128)(2,1)S(1)} collective-permute-done((bf16[4,96,768]{2,1,0:T(8,128)(2,1)S(1)}, bf16[4,96,768]{2,1,0:T(8,128)(2,1)S(1)}, u32[]{:S(2)}, u32[]{:S(2)}) %collective-permute-start.27) | collective-permute-done | bytes 589856 | tf_op jit(solution)/shard_map/ppermute | solution.py:19
  99.6 2.2 %collective-permute-start.30 = (bf16[2,96,768]{2,1,0:T(8,128)(2,1)S(1)}, bf16[2,96,768]{2,1,0:T(8,128)(2,1)S(1)}, u32[]{:S(2)}, u32[]{:S(2)}) collective-permute-start(bf16[2,96,768]{2,1,0:T(8,128)(2,1)S(1)} %get-tuple-element.266), channel_id=1, source_target_pairs={{0,8},{4,12},{8,0},{12,4},{16,24},{20,28},{24,16},{28,20},{1,9},{5... | collective-permute-start | bytes 884744 | tf_op jit(solution)/shard_map/ppermute | solution.py:19
  101.7 2.1 %shard_map.322 = (f32[512,768]{1,0:T(8,128)S(1)}, bf16[512,768]{1,0:T(8,128)(2,1)S(1)}, bf16[512,192]{1,0:T(8,128)(2,1)S(1)}, f32[8,512]{1,0:T(8,128)S(1)}, f32[8,768]{1,0:T(8,128)S(1)}) custom-call(bf16[256,768]{1,0:T(8,128)(2,1)S(1)} %shard_map.321.total, bf16[256,768]{1,0:T(8,128)(2,1)S(1)} %collective-permute-done.29.other, ...), custom_call_target="tpu_custom_call" | custom-call | flops 1000 | tf_op jit(solution)/shard_map/pallas_call | solution.py:120
  103.8 5.5 %shard_map.323 = (bf16[512,192]{1,0:T(8,128)(2,1)S(1)}, bf16[1024,192]{1,0:T(8,128)(2,1)S(1)}, bf16[1024,192]{1,0:T(8,128)(2,1)S(1)}) custom-call(s32[8]{0:T(128)S(1)} %dynamic-slice_bitcast_fusion.place, bf16[1024,192]{1,0:T(8,128)(2,1)S(1)} %get-tuple-element.200.q_ref, bf16[1024,192]{1,0:T(8,128)(2,1)S(1)} %get-tuple-element.201.k_ref, ...), custom_call_target="tpu_custom_call" | custom-call | flops 1000 | tf_op jit(solution)/shard_map/pallas_call | solution.py:120
  109.3 1.7 %shard_map.326 = (f32[4,96,384]{2,1,0:T(8,128)S(1)}, bf16[4,96,384]{2,1,0:T(8,128)(2,1)S(1)}) custom-call(s32[8]{0:T(128)S(1)} %dynamic-slice_bitcast_fusion.place, bf16[1024,768]{1,0:T(8,128)(2,1)S(1)} %get-tuple-element.274.normed, bf16[512,192]{1,0:T(8,128)(2,1)S(1)} %get-tuple-element.251.dq_zero, bf16[512,192]{1,0:T(8,128)(2,1)S(1)} %get-tuple-element.262.dq_one, ...), custom_call_target="tpu_custom_call" | custom-call | flops 1000 | tf_op jit(solution)/shard_map/pallas_call | solution.py:120
  111.1 2.2 %shard_map.325 = (f32[2,256,768]{2,1,0:T(8,128)S(1)}, bf16[256,768]{1,0:T(8,128)(2,1)S(1)}, bf16[256,768]{1,0:T(8,128)(2,1)S(1)}, f32[8,768]{1,0:T(8,128)S(1)}, ...) custom-call(s32[8]{0:T(128)S(1)} %dynamic-slice_bitcast_fusion.place, s32[6]{0:T(128)S(1)} %bitcast.58, ...), custom_call_target="tpu_custom_call" | custom-call | flops 1000 | tf_op jit(solution)/shard_map/pallas_call | solution.py:120
  114.0 1.6 %collective-permute-done.35.b = f32[8,768]{1,0:T(8,128)S(1)} collective-permute-done((f32[8,768]{1,0:T(8,128)S(1)}, f32[8,768]{1,0:T(8,128)S(1)}, u32[]{:S(2)}, u32[]{:S(2)}) %collective-permute-start.35) | collective-permute-done | bytes 24608 | tf_op jit(solution)/shard_map/ppermute | solution.py:19
  115.6 1.0 collective-permute-start.36
  116.7 1.5 collective-permute-start.40
  119.5 1.2 collective-permute-start.41
  120.7 1.9 %shard_map.331 = (f32[4,104,384]{2,1,0:T(8,128)S(1)}, bf16[4,104,384]{2,1,0:T(8,128)(2,1)S(1)}) custom-call(s32[8]{0:T(128)S(1)} %dynamic-slice_bitcast_fusion.place, bf16[1024,768]{1,0:T(8,128)(2,1)S(1)} %get-tuple-element.274.normed, bf16[1024,192]{1,0:T(8,128)(2,1)S(1)} %get-tuple-element.268.dk, bf16[1024,192]{1,0:T(8,128)(2,1)S(1)} %get-tuple-element.269.dv, ...), custom_call_target="tpu_custom_call" | custom-call | flops 1000 | tf_op jit(solution)/shard_map/pallas_call | solution.py:120
  122.5 1.6 %collective-permute-start.39 = (bf16[4,104,384]{2,1,0:T(8,128)(2,1)S(1)}, bf16[4,104,384]{2,1,0:T(8,128)(2,1)S(1)}, u32[]{:S(2)}, u32[]{:S(2)}) collective-permute-start(bf16[4,104,384]{2,1,0:T(8,128)(2,1)S(1)} %get-tuple-element.298), channel_id=1, source_target_pairs={{0,4},{4,0},{8,12},{12,8},{16,20},{20,16},{24,28},{28,24},{1,5},{5... | collective-permute-start | bytes 958472 | tf_op jit(solution)/shard_map/ppermute | solution.py:19
  124.1 1.0 shard_map.327
  126.0 1.2 collective-permute-start.37
  127.8 1.8 %collective-permute-start.43 = (bf16[1,96,768]{2,1,0:T(8,128)(2,1)S(1)}, bf16[1,96,768]{2,1,0:T(8,128)(2,1)S(1)}, u32[]{:S(2)}, u32[]{:S(2)}) collective-permute-start(bf16[1,96,768]{2,1,0:T(8,128)(2,1)S(1)} %get-tuple-element.306), channel_id=1, source_target_pairs={{0,16},{4,20},{8,24},{12,28},{16,0},{20,4},{24,8},{28,12},{1,17},{... | collective-permute-start | bytes 442376 | tf_op jit(solution)/shard_map/ppermute | solution.py:19
  130.2 1.6 %collective-permute-start.42 = (bf16[2,96,384]{2,1,0:T(8,128)(2,1)S(1)}, bf16[2,96,384]{2,1,0:T(8,128)(2,1)S(1)}, u32[]{:S(2)}, u32[]{:S(2)}) collective-permute-start(bf16[2,96,384]{2,1,0:T(8,128)(2,1)S(1)} %get-tuple-element.305), channel_id=1, source_target_pairs={{0,8},{4,12},{8,0},{12,4},{16,24},{20,28},{24,16},{28,20},{1,9},{5... | collective-permute-start | bytes 442376 | tf_op jit(solution)/shard_map/ppermute | solution.py:19
  131.8 4.0 %collective-permute-done.43.rest_9_ = bf16[1,96,768]{2,1,0:T(8,128)(2,1)S(1)} collective-permute-done((bf16[1,96,768]{2,1,0:T(8,128)(2,1)S(1)}, bf16[1,96,768]{2,1,0:T(8,128)(2,1)S(1)}, u32[]{:S(2)}, u32[]{:S(2)}) %collective-permute-start.43) | collective-permute-done | bytes 147488 | tf_op jit(solution)/shard_map/ppermute | solution.py:19
  135.7 1.0 collective-permute-done.42.refs_1_
  138.2 1.9 %collective-permute-start.44 = (bf16[1,96,768]{2,1,0:T(8,128)(2,1)S(1)}, bf16[1,96,768]{2,1,0:T(8,128)(2,1)S(1)}, u32[]{:S(2)}, u32[]{:S(2)}) collective-permute-start(bf16[1,96,768]{2,1,0:T(8,128)(2,1)S(1)} %get-tuple-element.311), channel_id=1, source_target_pairs={{0,16},{4,20},{8,24},{12,28},{16,0},{20,4},{24,8},{28,12},{1,17},{... | collective-permute-start | bytes 442376 | tf_op jit(solution)/shard_map/ppermute | solution.py:19
  140.1 2.7 %collective-permute-done.45.refs_1_ = bf16[2,104,384]{2,1,0:T(8,128)(2,1)S(1)} collective-permute-done((bf16[2,104,384]{2,1,0:T(8,128)(2,1)S(1)}, bf16[2,104,384]{2,1,0:T(8,128)(2,1)S(1)}, u32[]{:S(2)}, u32[]{:S(2)}) %collective-permute-start.45) | collective-permute-done | bytes 159776 | tf_op jit(solution)/shard_map/ppermute | solution.py:19
  143.4 1.7 %collective-permute-start.46 = (bf16[1,104,384]{2,1,0:T(8,128)(2,1)S(1)}, bf16[1,104,384]{2,1,0:T(8,128)(2,1)S(1)}, u32[]{:S(2)}, u32[]{:S(2)}) collective-permute-start(bf16[1,104,384]{2,1,0:T(8,128)(2,1)S(1)} %get-tuple-element.318), channel_id=1, source_target_pairs={{0,16},{4,20},{8,24},{12,28},{16,0},{20,4},{24,8},{28,12},{1,17},{... | collective-permute-start | bytes 239624 | tf_op jit(solution)/shard_map/ppermute | solution.py:19
  145.7 1.4 collective-permute-start.47
  147.1 1.5 collective-permute-done.44.rest_11_
  148.6 2.4 %shard_map.335 = (f32[256,768]{1,0:T(8,128)}, f32[6,1,192]{2,1,0:T(1,128)}, f32[96,768]{1,0:T(8,128)}, f32[96,768]{1,0:T(8,128)}, bf16[256,768]{1,0:T(8,128)(2,1)}) custom-call(s32[8]{0:T(128)S(1)} %dynamic-slice_bitcast_fusion.place, f32[256,1536]{1,0:T(8,128)S(1)} %get-tuple-element.283.keep, bf16[256,768]{1,0:T(8,128)(2,1)S(1)} %collective-permute-done.37.got, ...), custom_call_target="tpu_custom_call" | custom-call | flops 1000 | tf_op jit(solution)/shard_map/pallas_call | solution.py:120
  151.7 0.9 shard_map.339
  (104 shorter events, 20.8 us)
Async XLA Ops:
  0.6 19.7 %copy-start.1 = (bf16[96,768]{1,0:T(8,128)(2,1)S(1)}, bf16[96,768]{1,0:T(8,128)(2,1)}, u32[]{:S(2)}) copy-start(bf16[96,768]{1,0:T(8,128)(2,1)} %a.2) | copy-start | bytes 442372
  2.5 14.4 %collective-permute-start = (bf16[256,768]{1,0:T(8,128)(2,1)}, bf16[256,768]{1,0:T(8,128)(2,1)S(1)}, u32[]{:S(2)}, u32[]{:S(2)}) collective-permute-start(bf16[256,768]{1,0:T(8,128)(2,1)} %bitcast.45), channel_id=1, source_target_pairs={{0,2},{1,3},{2,0},{3,1},{4,6},{5,7},{6,4},{7,5},{8,10},{9,11},{10,... | collective-permute-start | bytes 1179656 | tf_op jit(solution)/shard_map/ppermute | solution.py:19
  5.5 8.0 %collective-permute-start.2 = (bf16[104,768]{1,0:T(8,128)(2,1)}, bf16[104,768]{1,0:T(8,128)(2,1)S(1)}, u32[]{:S(2)}, u32[]{:S(2)}) collective-permute-start(bf16[104,768]{1,0:T(8,128)(2,1)} %shard_map.289.refs_0_), channel_id=1, source_target_pairs={{0,4},{4,0},{8,12},{12,8},{16,20},{20,16},{24,28},{28,24},{1,5},{5... | collective-permute-start | bytes 479240 | tf_op jit(solution)/shard_map/ppermute | solution.py:19
  7.1 9.8 %collective-permute-start.1 = (bf16[104,768]{1,0:T(8,128)(2,1)}, bf16[104,768]{1,0:T(8,128)(2,1)S(1)}, u32[]{:S(2)}, u32[]{:S(2)}) collective-permute-start(bf16[104,768]{1,0:T(8,128)(2,1)} %shard_map.289.refs_0_), channel_id=1, source_target_pairs={{0,16},{4,20},{8,24},{12,28},{16,0},{20,4},{24,8},{28,12},{1,17},{... | collective-permute-start | bytes 479240 | tf_op jit(solution)/shard_map/ppermute | solution.py:19
  9.6 0.9 copy-start.4
  10.6 1.0 copy-start.5
  11.6 0.9 copy-start
  12.5 0.9 copy-start.2
  13.5 20.1 %copy-start.3 = (bf16[768,96]{0,1:T(8,128)(2,1)S(1)}, bf16[768,96]{0,1:T(8,128)(2,1)}, u32[]{:S(2)}) copy-start(bf16[768,96]{0,1:T(8,128)(2,1)} %param.32) | copy-start | bytes 442372
  13.5 21.8 %copy-start.7 = (bf16[1,6,768]{2,1,0:T(8,128)(2,1)S(1)}, bf16[1,6,768]{2,1,0:T(8,128)(2,1)}, u32[]{:S(2)}) copy-start(bf16[1,6,768]{2,1,0:T(8,128)(2,1)} %param.19) | copy-start | bytes 27652
  13.5 21.8 %copy-start.9 = (s32[1,6]{1,0:T(1,128)S(1)}, s32[1,6]{1,0:T(1,128)}, u32[]{:S(2)}) copy-start(s32[1,6]{1,0:T(1,128)} %rest_4_.1) | copy-start | bytes 76
  16.9 13.2 %collective-permute-start.7 = (bf16[256,768]{1,0:T(8,128)(2,1)}, bf16[256,768]{1,0:T(8,128)(2,1)S(1)}, u32[]{:S(2)}, u32[]{:S(2)}) collective-permute-start(bf16[256,768]{1,0:T(8,128)(2,1)} %bitcast.47), channel_id=1, source_target_pairs={{0,2},{1,3},{2,0},{3,1},{4,6},{5,7},{6,4},{7,5},{8,10},{9,11},{10,... | collective-permute-start | bytes 1179656 | tf_op jit(solution)/shard_map/ppermute | solution.py:19
  17.5 12.6 %collective-permute-start.3 = (bf16[2,104,768]{2,1,0:T(8,128)(2,1)S(1)}, bf16[2,104,768]{2,1,0:T(8,128)(2,1)S(1)}, u32[]{:S(2)}, u32[]{:S(2)}) collective-permute-start(bf16[2,104,768]{2,1,0:T(8,128)(2,1)S(1)} %shard_map.292), channel_id=1, source_target_pairs={{0,8},{4,12},{8,0},{12,4},{16,24},{20,28},{24,16},{28,20},{1,9},{5... | collective-permute-start | bytes 958472 | tf_op jit(solution)/shard_map/ppermute | solution.py:19
  18.3 11.8 %collective-permute-start.6 = (bf16[2,96,768]{2,1,0:T(8,128)(2,1)S(1)}, bf16[2,96,768]{2,1,0:T(8,128)(2,1)S(1)}, u32[]{:S(2)}, u32[]{:S(2)}) collective-permute-start(bf16[2,96,768]{2,1,0:T(8,128)(2,1)S(1)} %shard_map.291), channel_id=1, source_target_pairs={{0,4},{4,0},{8,12},{12,8},{16,20},{20,16},{24,28},{28,24},{1,5},{5... | collective-permute-start | bytes 884744 | tf_op jit(solution)/shard_map/ppermute | solution.py:19
  19.8 10.3 %collective-permute-start.4 = (bf16[104,768]{1,0:T(8,128)(2,1)S(1)}, bf16[104,768]{1,0:T(8,128)(2,1)S(1)}, u32[]{:S(2)}, u32[]{:S(2)}) collective-permute-start(bf16[104,768]{1,0:T(8,128)(2,1)S(1)} %collective-permute-done.1.b), channel_id=1, source_target_pairs={{0,4},{4,0},{8,12},{12,8},{16,20},{20,16},{24,28},{28,24},{1,5},{5... | collective-permute-start | bytes 479240 | tf_op jit(solution)/shard_map/ppermute | solution.py:19
  20.3 7.8 %collective-permute-start.5 = (bf16[96,768]{1,0:T(8,128)(2,1)S(1)}, bf16[96,768]{1,0:T(8,128)(2,1)S(1)}, u32[]{:S(2)}, u32[]{:S(2)}) collective-permute-start(bf16[96,768]{1,0:T(8,128)(2,1)S(1)} %copy-done.1), channel_id=1, source_target_pairs={{0,16},{4,20},{8,24},{12,28},{16,0},{20,4},{24,8},{28,12},{1,17},{... | collective-permute-start | bytes 442376 | tf_op jit(solution)/shard_map/ppermute | solution.py:19
  30.7 4.6 %collective-permute-start.9 = (bf16[2,256,768]{2,1,0:T(8,128)(2,1)S(1)}, bf16[2,256,768]{2,1,0:T(8,128)(2,1)S(1)}, u32[]{:S(2)}, u32[]{:S(2)}) collective-permute-start(bf16[2,256,768]{2,1,0:T(8,128)(2,1)S(1)} %shard_map.293.x_zero), channel_id=1, source_target_pairs={{0,1},{1,0},{2,3},{3,2},{4,5},{5,4},{6,7},{7,6},{8,9},{9,8},{10,11... | collective-permute-start | bytes 2359304 | tf_op jit(solution)/shard_map/ppermute | solution.py:19
  30.8 10.0 %collective-permute-start.8 = (bf16[2,104,768]{2,1,0:T(8,128)(2,1)S(1)}, bf16[2,104,768]{2,1,0:T(8,128)(2,1)S(1)}, u32[]{:S(2)}, u32[]{:S(2)}) collective-permute-start(bf16[2,104,768]{2,1,0:T(8,128)(2,1)S(1)} %collective-permute-done.3.refs_3_), channel_id=1, source_target_pairs={{0,4},{4,0},{8,12},{12,8},{16,20},{20,16},{24,28},{28,24},{1,5},{5... | collective-permute-start | bytes 958472 | tf_op jit(solution)/shard_map/ppermute | solution.py:19
  31.4 15.8 %collective-permute-start.10 = (bf16[2,96,768]{2,1,0:T(8,128)(2,1)S(1)}, bf16[2,96,768]{2,1,0:T(8,128)(2,1)S(1)}, u32[]{:S(2)}, u32[]{:S(2)}) collective-permute-start(bf16[2,96,768]{2,1,0:T(8,128)(2,1)S(1)} %shard_map.298), channel_id=1, source_target_pairs={{0,8},{4,12},{8,0},{12,4},{16,24},{20,28},{24,16},{28,20},{1,9},{5... | collective-permute-start | bytes 884744 | tf_op jit(solution)/shard_map/ppermute | solution.py:19
  33.5 13.6 %collective-permute-start.11 = (bf16[96,768]{1,0:T(8,128)(2,1)S(1)}, bf16[96,768]{1,0:T(8,128)(2,1)S(1)}, u32[]{:S(2)}, u32[]{:S(2)}) collective-permute-start(bf16[96,768]{1,0:T(8,128)(2,1)S(1)} %bitcast.39), channel_id=1, source_target_pairs={{0,16},{4,20},{8,24},{12,28},{16,0},{20,4},{24,8},{28,12},{1,17},{... | collective-permute-start | bytes 442376 | tf_op jit(solution)/shard_map/ppermute | solution.py:19
  40.7 6.4 %collective-permute-start.12 = (bf16[96,768]{1,0:T(8,128)(2,1)S(1)}, bf16[96,768]{1,0:T(8,128)(2,1)S(1)}, u32[]{:S(2)}, u32[]{:S(2)}) collective-permute-start(bf16[96,768]{1,0:T(8,128)(2,1)S(1)} %collective-permute-done.5.b), channel_id=1, source_target_pairs={{0,4},{4,0},{8,12},{12,8},{16,20},{20,16},{24,28},{28,24},{1,5},{5... | collective-permute-start | bytes 442376 | tf_op jit(solution)/shard_map/ppermute | solution.py:19
  42.1 1.4 copy-start.8
  47.1 5.7 %copy-start.6 = (bf16[1,256,768]{2,1,0:T(8,128)(2,1)S(1)}, bf16[1,256,768]{2,1,0:T(8,128)(2,1)}, u32[]{:S(2)}) copy-start(bf16[1,256,768]{2,1,0:T(8,128)(2,1)} %param.34) | copy-start | bytes 1179652
  47.2 1.8 %collective-permute-start.13 = (bf16[256,768]{1,0:T(8,128)(2,1)S(1)}, bf16[256,768]{1,0:T(8,128)(2,1)S(1)}, u32[]{:S(2)}, u32[]{:S(2)}) collective-permute-start(bf16[256,768]{1,0:T(8,128)(2,1)S(1)} %get-tuple-element.208), channel_id=1, source_target_pairs={{0,1},{1,0},{2,3},{3,2},{4,5},{5,4},{6,7},{7,6},{8,9},{9,8},{10,11... | collective-permute-start | bytes 1179656 | tf_op jit(solution)/shard_map/ppermute | solution.py:19
  47.3 12.6 %collective-permute-start.15 = (bf16[3,96,768]{2,1,0:T(8,128)(2,1)S(1)}, bf16[3,96,768]{2,1,0:T(8,128)(2,1)S(1)}, u32[]{:S(2)}, u32[]{:S(2)}) collective-permute-start(bf16[3,96,768]{2,1,0:T(8,128)(2,1)S(1)} %shard_map.301), channel_id=1, source_target_pairs={{0,4},{4,0},{8,12},{12,8},{16,20},{20,16},{24,28},{28,24},{1,5},{5... | collective-permute-start | bytes 1327112 | tf_op jit(solution)/shard_map/ppermute | solution.py:19
  49.0 11.2 %collective-permute-start.14 = (bf16[256,768]{1,0:T(8,128)(2,1)S(1)}, bf16[256,768]{1,0:T(8,128)(2,1)S(1)}, u32[]{:S(2)}, u32[]{:S(2)}) collective-permute-start(bf16[256,768]{1,0:T(8,128)(2,1)S(1)} %shard_map.299.a), channel_id=1, source_target_pairs={{0,2},{1,3},{2,0},{3,1},{4,6},{5,7},{6,4},{7,5},{8,10},{9,11},{10,... | collective-permute-start | bytes 1179656 | tf_op jit(solution)/shard_map/ppermute | solution.py:19
  50.6 9.2 %collective-permute-start.16 = (bf16[2,96,768]{2,1,0:T(8,128)(2,1)S(1)}, bf16[2,96,768]{2,1,0:T(8,128)(2,1)S(1)}, u32[]{:S(2)}, u32[]{:S(2)}) collective-permute-start(bf16[2,96,768]{2,1,0:T(8,128)(2,1)S(1)} %shard_map.302), channel_id=1, source_target_pairs={{0,8},{4,12},{8,0},{12,4},{16,24},{20,28},{24,16},{28,20},{1,9},{5... | collective-permute-start | bytes 884744 | tf_op jit(solution)/shard_map/ppermute | solution.py:19
  53.4 15.6 %collective-permute-start.19 = (bf16[2,256,768]{2,1,0:T(8,128)(2,1)S(1)}, bf16[2,256,768]{2,1,0:T(8,128)(2,1)S(1)}, u32[]{:S(2)}, u32[]{:S(2)}) collective-permute-start(bf16[2,256,768]{2,1,0:T(8,128)(2,1)S(1)} %shard_map.307.cot_zero), channel_id=1, source_target_pairs={{0,1},{1,0},{2,3},{3,2},{4,5},{5,4},{6,7},{7,6},{8,9},{9,8},{10,11... | collective-permute-start | bytes 2359304 | tf_op jit(solution)/shard_map/ppermute | solution.py:19
  60.3 2.2 %collective-permute-start.17 = (bf16[256,768]{1,0:T(8,128)(2,1)S(1)}, bf16[256,768]{1,0:T(8,128)(2,1)S(1)}, u32[]{:S(2)}, u32[]{:S(2)}) collective-permute-start(bf16[256,768]{1,0:T(8,128)(2,1)S(1)} %get-tuple-element.214), channel_id=1, source_target_pairs={{0,1},{1,0},{2,3},{3,2},{4,5},{5,4},{6,7},{7,6},{8,9},{9,8},{10,11... | collective-permute-start | bytes 1179656 | tf_op jit(solution)/shard_map/ppermute | solution.py:19
  60.4 9.6 %collective-permute-start.18 = (bf16[256,768]{1,0:T(8,128)(2,1)S(1)}, bf16[256,768]{1,0:T(8,128)(2,1)S(1)}, u32[]{:S(2)}, u32[]{:S(2)}) collective-permute-start(bf16[256,768]{1,0:T(8,128)(2,1)S(1)} %shard_map.306.total), channel_id=1, source_target_pairs={{0,1},{1,0},{2,3},{3,2},{4,5},{5,4},{6,7},{7,6},{8,9},{9,8},{10,11... | collective-permute-start | bytes 1179656 | tf_op jit(solution)/shard_map/ppermute | solution.py:19
  60.9 9.0 %collective-permute-start.20 = (bf16[2,96,768]{2,1,0:T(8,128)(2,1)S(1)}, bf16[2,96,768]{2,1,0:T(8,128)(2,1)S(1)}, u32[]{:S(2)}, u32[]{:S(2)}) collective-permute-start(bf16[2,96,768]{2,1,0:T(8,128)(2,1)S(1)} %collective-permute-done.16.refs_3_), channel_id=1, source_target_pairs={{0,4},{4,0},{8,12},{12,8},{16,20},{20,16},{24,28},{28,24},{1,5},{5... | collective-permute-start | bytes 884744 | tf_op jit(solution)/shard_map/ppermute | solution.py:19
  62.5 10.9 %collective-permute-start.22 = (bf16[256,768]{1,0:T(8,128)(2,1)S(1)}, bf16[256,768]{1,0:T(8,128)(2,1)S(1)}, u32[]{:S(2)}, u32[]{:S(2)}) collective-permute-start(bf16[256,768]{1,0:T(8,128)(2,1)S(1)} %shard_map.303.a), channel_id=1, source_target_pairs={{0,2},{1,3},{2,0},{3,1},{4,6},{5,7},{6,4},{7,5},{8,10},{9,11},{10,... | collective-permute-start | bytes 1179656 | tf_op jit(solution)/shard_map/ppermute | solution.py:19
  73.3 1.8 %collective-permute-start.21 = (bf16[256,768]{1,0:T(8,128)(2,1)S(1)}, bf16[256,768]{1,0:T(8,128)(2,1)S(1)}, u32[]{:S(2)}, u32[]{:S(2)}) collective-permute-start(bf16[256,768]{1,0:T(8,128)(2,1)S(1)} %get-tuple-element.233), channel_id=1, source_target_pairs={{0,1},{1,0},{2,3},{3,2},{4,5},{5,4},{6,7},{7,6},{8,9},{9,8},{10,11... | collective-permute-start | bytes 1179656 | tf_op jit(solution)/shard_map/ppermute | solution.py:19
  73.5 3.2 %collective-permute-start.23 = (bf16[256,768]{1,0:T(8,128)(2,1)S(1)}, bf16[256,768]{1,0:T(8,128)(2,1)S(1)}, u32[]{:S(2)}, u32[]{:S(2)}) collective-permute-start(bf16[256,768]{1,0:T(8,128)(2,1)S(1)} %shard_map.312.total), channel_id=1, source_target_pairs={{0,1},{1,0},{2,3},{3,2},{4,5},{5,4},{6,7},{7,6},{8,9},{9,8},{10,11... | collective-permute-start | bytes 1179656 | tf_op jit(solution)/shard_map/ppermute | solution.py:19
  75.2 11.7 %collective-permute-start.24 = (bf16[256,768]{1,0:T(8,128)(2,1)S(1)}, bf16[256,768]{1,0:T(8,128)(2,1)S(1)}, u32[]{:S(2)}, u32[]{:S(2)}) collective-permute-start(bf16[256,768]{1,0:T(8,128)(2,1)S(1)} %shard_map.311.a), channel_id=1, source_target_pairs={{0,2},{1,3},{2,0},{3,1},{4,6},{5,7},{6,4},{7,5},{8,10},{9,11},{10,... | collective-permute-start | bytes 1179656 | tf_op jit(solution)/shard_map/ppermute | solution.py:19
  79.6 7.7 %collective-permute-start.26 = (bf16[256,768]{1,0:T(8,128)(2,1)S(1)}, bf16[256,768]{1,0:T(8,128)(2,1)S(1)}, u32[]{:S(2)}, u32[]{:S(2)}) collective-permute-start(bf16[256,768]{1,0:T(8,128)(2,1)S(1)} %get-tuple-element.254), channel_id=1, source_target_pairs={{0,1},{1,0},{2,3},{3,2},{4,5},{5,4},{6,7},{7,6},{8,9},{9,8},{10,11... | collective-permute-start | bytes 1179656 | tf_op jit(solution)/shard_map/ppermute | solution.py:19
  81.8 16.2 %collective-permute-start.27 = (bf16[4,96,768]{2,1,0:T(8,128)(2,1)S(1)}, bf16[4,96,768]{2,1,0:T(8,128)(2,1)S(1)}, u32[]{:S(2)}, u32[]{:S(2)}) collective-permute-start(bf16[4,96,768]{2,1,0:T(8,128)(2,1)S(1)} %get-tuple-element.239), channel_id=1, source_target_pairs={{0,4},{4,0},{8,12},{12,8},{16,20},{20,16},{24,28},{28,24},{1,5},{5... | collective-permute-start | bytes 1769480 | tf_op jit(solution)/shard_map/ppermute | solution.py:19
  87.0 1.8 %collective-permute-start.25 = (bf16[256,768]{1,0:T(8,128)(2,1)S(1)}, bf16[256,768]{1,0:T(8,128)(2,1)S(1)}, u32[]{:S(2)}, u32[]{:S(2)}) collective-permute-start(bf16[256,768]{1,0:T(8,128)(2,1)S(1)} %shard_map.317.total), channel_id=1, source_target_pairs={{0,1},{1,0},{2,3},{3,2},{4,5},{5,4},{6,7},{7,6},{8,9},{9,8},{10,11... | collective-permute-start | bytes 1179656 | tf_op jit(solution)/shard_map/ppermute | solution.py:19
  87.4 11.4 %collective-permute-start.28 = (bf16[256,768]{1,0:T(8,128)(2,1)S(1)}, bf16[256,768]{1,0:T(8,128)(2,1)S(1)}, u32[]{:S(2)}, u32[]{:S(2)}) collective-permute-start(bf16[256,768]{1,0:T(8,128)(2,1)S(1)} %shard_map.320.a), channel_id=1, source_target_pairs={{0,2},{1,3},{2,0},{3,1},{4,6},{5,7},{6,4},{7,5},{8,10},{9,11},{10,... | collective-permute-start | bytes 1179656 | tf_op jit(solution)/shard_map/ppermute | solution.py:19
  88.8 22.3 %collective-permute-start.31 = (bf16[4,96,768]{2,1,0:T(8,128)(2,1)S(1)}, bf16[4,96,768]{2,1,0:T(8,128)(2,1)S(1)}, u32[]{:S(2)}, u32[]{:S(2)}) collective-permute-start(bf16[4,96,768]{2,1,0:T(8,128)(2,1)S(1)} %get-tuple-element.267), channel_id=1, source_target_pairs={{0,4},{4,0},{8,12},{12,8},{16,20},{20,16},{24,28},{28,24},{1,5},{5... | collective-permute-start | bytes 1769480 | tf_op jit(solution)/shard_map/ppermute | solution.py:19
  89.8 32.7 %collective-permute-start.34 = (bf16[2,256,768]{2,1,0:T(8,128)(2,1)S(1)}, bf16[2,256,768]{2,1,0:T(8,128)(2,1)S(1)}, u32[]{:S(2)}, u32[]{:S(2)}) collective-permute-start(bf16[2,256,768]{2,1,0:T(8,128)(2,1)S(1)} %get-tuple-element.282), channel_id=1, source_target_pairs={{0,1},{1,0},{2,3},{3,2},{4,5},{5,4},{6,7},{7,6},{8,9},{9,8},{10,11... | collective-permute-start | bytes 2359304 | tf_op jit(solution)/shard_map/ppermute | solution.py:19
  98.8 2.9 %collective-permute-start.29 = (bf16[256,768]{1,0:T(8,128)(2,1)S(1)}, bf16[256,768]{1,0:T(8,128)(2,1)S(1)}, u32[]{:S(2)}, u32[]{:S(2)}) collective-permute-start(bf16[256,768]{1,0:T(8,128)(2,1)S(1)} %shard_map.321.total), channel_id=1, source_target_pairs={{0,1},{1,0},{2,3},{3,2},{4,5},{5,4},{6,7},{7,6},{8,9},{9,8},{10,11... | collective-permute-start | bytes 1179656 | tf_op jit(solution)/shard_map/ppermute | solution.py:19
  99.6 11.5 %collective-permute-start.30 = (bf16[2,96,768]{2,1,0:T(8,128)(2,1)S(1)}, bf16[2,96,768]{2,1,0:T(8,128)(2,1)S(1)}, u32[]{:S(2)}, u32[]{:S(2)}) collective-permute-start(bf16[2,96,768]{2,1,0:T(8,128)(2,1)S(1)} %get-tuple-element.266), channel_id=1, source_target_pairs={{0,8},{4,12},{8,0},{12,4},{16,24},{20,28},{24,16},{28,20},{1,9},{5... | collective-permute-start | bytes 884744 | tf_op jit(solution)/shard_map/ppermute | solution.py:19
  113.2 10.9 %collective-permute-start.33 = (bf16[256,768]{1,0:T(8,128)(2,1)S(1)}, bf16[256,768]{1,0:T(8,128)(2,1)S(1)}, u32[]{:S(2)}, u32[]{:S(2)}) collective-permute-start(bf16[256,768]{1,0:T(8,128)(2,1)S(1)} %get-tuple-element.280), channel_id=1, source_target_pairs={{0,1},{1,0},{2,3},{3,2},{4,5},{5,4},{6,7},{7,6},{8,9},{9,8},{10,11... | collective-permute-start | bytes 1179656 | tf_op jit(solution)/shard_map/ppermute | solution.py:19
  113.5 10.6 %collective-permute-start.32 = (bf16[256,768]{1,0:T(8,128)(2,1)S(1)}, bf16[256,768]{1,0:T(8,128)(2,1)S(1)}, u32[]{:S(2)}, u32[]{:S(2)}) collective-permute-start(bf16[256,768]{1,0:T(8,128)(2,1)S(1)} %get-tuple-element.278), channel_id=1, source_target_pairs={{0,1},{1,0},{2,3},{3,2},{4,5},{5,4},{6,7},{7,6},{8,9},{9,8},{10,11... | collective-permute-start | bytes 1179656 | tf_op jit(solution)/shard_map/ppermute | solution.py:19
  113.8 1.8 %collective-permute-start.35 = (f32[8,768]{1,0:T(8,128)S(1)}, f32[8,768]{1,0:T(8,128)S(1)}, u32[]{:S(2)}, u32[]{:S(2)}) collective-permute-start(f32[8,768]{1,0:T(8,128)S(1)} %get-tuple-element.285.a), channel_id=1, source_target_pairs={{0,1},{1,0},{2,3},{3,2},{4,5},{5,4},{6,7},{7,6},{8,9},{9,8},{10,11... | collective-permute-start | bytes 73736 | tf_op jit(solution)/shard_map/ppermute | solution.py:19
  115.6 3.8 %collective-permute-start.36 = (f32[8,768]{1,0:T(8,128)S(1)}, f32[8,768]{1,0:T(8,128)S(1)}, u32[]{:S(2)}, u32[]{:S(2)}) collective-permute-start(f32[8,768]{1,0:T(8,128)S(1)} %shard_map.328.a), channel_id=1, source_target_pairs={{0,2},{1,3},{2,0},{3,1},{4,6},{5,7},{6,4},{7,5},{8,10},{9,11},{10,... | collective-permute-start | bytes 73736 | tf_op jit(solution)/shard_map/ppermute | solution.py:19
  116.7 11.2 %collective-permute-start.40 = (bf16[4,96,384]{2,1,0:T(8,128)(2,1)S(1)}, bf16[4,96,384]{2,1,0:T(8,128)(2,1)S(1)}, u32[]{:S(2)}, u32[]{:S(2)}) collective-permute-start(bf16[4,96,384]{2,1,0:T(8,128)(2,1)S(1)} %get-tuple-element.300), channel_id=1, source_target_pairs={{0,4},{4,0},{8,12},{12,8},{16,20},{20,16},{24,28},{28,24},{1,5},{5... | collective-permute-start | bytes 884744 | tf_op jit(solution)/shard_map/ppermute | solution.py:19
  119.5 10.2 %collective-permute-start.41 = (bf16[2,96,768]{2,1,0:T(8,128)(2,1)S(1)}, bf16[2,96,768]{2,1,0:T(8,128)(2,1)S(1)}, u32[]{:S(2)}, u32[]{:S(2)}) collective-permute-start(bf16[2,96,768]{2,1,0:T(8,128)(2,1)S(1)} %get-tuple-element.303), channel_id=1, source_target_pairs={{0,8},{4,12},{8,0},{12,4},{16,24},{20,28},{24,16},{28,20},{1,9},{5... | collective-permute-start | bytes 884744 | tf_op jit(solution)/shard_map/ppermute | solution.py:19
  122.5 13.2 %collective-permute-start.39 = (bf16[4,104,384]{2,1,0:T(8,128)(2,1)S(1)}, bf16[4,104,384]{2,1,0:T(8,128)(2,1)S(1)}, u32[]{:S(2)}, u32[]{:S(2)}) collective-permute-start(bf16[4,104,384]{2,1,0:T(8,128)(2,1)S(1)} %get-tuple-element.298), channel_id=1, source_target_pairs={{0,4},{4,0},{8,12},{12,8},{16,20},{20,16},{24,28},{28,24},{1,5},{5... | collective-permute-start | bytes 958472 | tf_op jit(solution)/shard_map/ppermute | solution.py:19
  125.1 23.5 %collective-permute-start.38 = (bf16[256,768]{1,0:T(8,128)(2,1)S(1)}, bf16[256,768]{1,0:T(8,128)(2,1)S(1)}, u32[]{:S(2)}, u32[]{:S(2)}) collective-permute-start(bf16[256,768]{1,0:T(8,128)(2,1)S(1)} %get-tuple-element.288), channel_id=1, source_target_pairs={{0,2},{1,3},{2,0},{3,1},{4,6},{5,7},{6,4},{7,5},{8,10},{9,11},{10,... | collective-permute-start | bytes 1179656 | tf_op jit(solution)/shard_map/ppermute | solution.py:19
  126.0 22.6 %collective-permute-start.37 = (bf16[256,768]{1,0:T(8,128)(2,1)S(1)}, bf16[256,768]{1,0:T(8,128)(2,1)S(1)}, u32[]{:S(2)}, u32[]{:S(2)}) collective-permute-start(bf16[256,768]{1,0:T(8,128)(2,1)S(1)} %get-tuple-element.286), channel_id=1, source_target_pairs={{0,2},{1,3},{2,0},{3,1},{4,6},{5,7},{6,4},{7,5},{8,10},{9,11},{10,... | collective-permute-start | bytes 1179656 | tf_op jit(solution)/shard_map/ppermute | solution.py:19
  127.8 7.9 %collective-permute-start.43 = (bf16[1,96,768]{2,1,0:T(8,128)(2,1)S(1)}, bf16[1,96,768]{2,1,0:T(8,128)(2,1)S(1)}, u32[]{:S(2)}, u32[]{:S(2)}) collective-permute-start(bf16[1,96,768]{2,1,0:T(8,128)(2,1)S(1)} %get-tuple-element.306), channel_id=1, source_target_pairs={{0,16},{4,20},{8,24},{12,28},{16,0},{20,4},{24,8},{28,12},{1,17},{... | collective-permute-start | bytes 442376 | tf_op jit(solution)/shard_map/ppermute | solution.py:19
  130.2 6.5 %collective-permute-start.42 = (bf16[2,96,384]{2,1,0:T(8,128)(2,1)S(1)}, bf16[2,96,384]{2,1,0:T(8,128)(2,1)S(1)}, u32[]{:S(2)}, u32[]{:S(2)}) collective-permute-start(bf16[2,96,384]{2,1,0:T(8,128)(2,1)S(1)} %get-tuple-element.305), channel_id=1, source_target_pairs={{0,8},{4,12},{8,0},{12,4},{16,24},{20,28},{24,16},{28,20},{1,9},{5... | collective-permute-start | bytes 442376 | tf_op jit(solution)/shard_map/ppermute | solution.py:19
  137.3 5.5 %collective-permute-start.45 = (bf16[2,104,384]{2,1,0:T(8,128)(2,1)S(1)}, bf16[2,104,384]{2,1,0:T(8,128)(2,1)S(1)}, u32[]{:S(2)}, u32[]{:S(2)}) collective-permute-start(bf16[2,104,384]{2,1,0:T(8,128)(2,1)S(1)} %get-tuple-element.317), channel_id=1, source_target_pairs={{0,8},{4,12},{8,0},{12,4},{16,24},{20,28},{24,16},{28,20},{1,9},{5... | collective-permute-start | bytes 479240 | tf_op jit(solution)/shard_map/ppermute | solution.py:19
  138.2 10.4 %collective-permute-start.44 = (bf16[1,96,768]{2,1,0:T(8,128)(2,1)S(1)}, bf16[1,96,768]{2,1,0:T(8,128)(2,1)S(1)}, u32[]{:S(2)}, u32[]{:S(2)}) collective-permute-start(bf16[1,96,768]{2,1,0:T(8,128)(2,1)S(1)} %get-tuple-element.311), channel_id=1, source_target_pairs={{0,16},{4,20},{8,24},{12,28},{16,0},{20,4},{24,8},{28,12},{1,17},{... | collective-permute-start | bytes 442376 | tf_op jit(solution)/shard_map/ppermute | solution.py:19
  143.4 8.3 %collective-permute-start.46 = (bf16[1,104,384]{2,1,0:T(8,128)(2,1)S(1)}, bf16[1,104,384]{2,1,0:T(8,128)(2,1)S(1)}, u32[]{:S(2)}, u32[]{:S(2)}) collective-permute-start(bf16[1,104,384]{2,1,0:T(8,128)(2,1)S(1)} %get-tuple-element.318), channel_id=1, source_target_pairs={{0,16},{4,20},{8,24},{12,28},{16,0},{20,4},{24,8},{28,12},{1,17},{... | collective-permute-start | bytes 239624 | tf_op jit(solution)/shard_map/ppermute | solution.py:19
  145.7 6.0 %collective-permute-start.47 = (bf16[1,96,384]{2,1,0:T(8,128)(2,1)S(1)}, bf16[1,96,384]{2,1,0:T(8,128)(2,1)S(1)}, u32[]{:S(2)}, u32[]{:S(2)}) collective-permute-start(bf16[1,96,384]{2,1,0:T(8,128)(2,1)S(1)} %get-tuple-element.321), channel_id=1, source_target_pairs={{0,16},{4,20},{8,24},{12,28},{16,0},{20,4},{24,8},{28,12},{1,17},{... | collective-permute-start | bytes 221192 | tf_op jit(solution)/shard_map/ppermute | solution.py:19

commit v6 on v5

--- a/solution.py
+++ b/solution.py
@@ -957,7 +957,7 @@
     pack_near, pack_far_across = near(stacked(pack_here, pack_far)), across(pack_far)
     up_far = far(after(w_up, pack_far))
     both_across = across(both)
-    cot_far = over(after(cot_own, x_far))
+    cot_far = over(after(cot_own, pack_far))
     pack_near, pack_far_across, up_far, both_across, cot_far = together(
         pack_near, pack_far_across, up_far, both_across, cot_far
     )
@@ -1024,7 +1024,7 @@
         cot_grad_kernel, after(place, b_send), (hidden_cols,), *cots, hidden_zero, hidden_one
     )
     mlp_keep, mlp_send = down_part((hidden_zero, after(hidden_one, b_send)), w_down_t)
-    total_zero = add_low(after(mine_zero, c_send, mlp_send), far_zero, cost=0)
+    total_zero = add_low(after(mine_zero, b_send), far_zero, cost=0)
     other_zero = core(total_zero)
     residual = (residual_zero, residual_one)
 
@@ -1053,7 +1053,7 @@
     d_got = across(after(d_send, dk))
     c_keep, c_send = fold(5, place, c_keep, c_got)
     c_got = near(c_send)
-    b_keep, b_send = fold(6, place, b_keep, b_got)
+    b_keep, b_send = fold(6, place, b_keep, after(b_got, c_send))
     b_got = far(b_send)
     keep, send_low, send_high, small, mixed_sums, picked = input_back(
         place, thought_pos, (dq_zero, dq_one), dk, dv, w_in, xhat, grad_residual

time: 153 us -> 153 us (level)
  transfers between devices with their start and end apart: 48 -> 48, of which waited for: 20 -> 18; matrix products, arithmetic and copies ran while one was open for 0% -> 0% of each run, Pallas kernels for 39% -> 39%
where the time goes in v6:
time: 153 us
  Pallas kernels  62.2 us (41%)
  starting transfers between devices  53.2 us (35%)
  waiting for transfers between devices  31.4 us (21%)
  local copies, waits for them, and re-layouts  4.48 us (3%)
    pallas_call x50, Pallas kernels, call(): pl.pallas_call(kernel, out_shape=tuple((jax.ShapeDtypeStruct(s, t) for s,...  60.4 us
    ppermute x48, starting transfers between devices, swapped(): lax.ppermute(array, axis, [(i, i ^ mask) for i in range(lax.axis_size(axi...  53.2 us
    ppermute x48, waiting for transfers between devices, swapped(): lax.ppermute(array, axis, [(i, i ^ mask) for i in range(lax.axis_size(axi...  31.4 us
    unnamed x20, local copies, waits for them, and re-layouts  3.79 us
  transfers between devices with their start and end apart: 48, of which 18 were waited for; matrix products, arithmetic and copies ran while one was open for 0% of the time, Pallas kernels for 39%

profile of v6, /device:TPU:0, one launch (start us, length us, event | category | flops | bytes accessed | tf_op | source)
XLA Modules:
  0.0 152.6 jit_solution(16986133397755897047)
XLA Ops:
  0.7 1.9 %shard_map.289.refs_0_ = bf16[104,768]{1,0:T(8,128)(2,1)} custom-call(bf16[3,96,192]{2,1,0:T(8,128)(2,1)} %refs_0_.1, bf16[192,96]{1,0:T(8,128)(2,1)} %refs_1_.1, bf16[1,96]{1,0:T(2,128)(2,1)} %bitcast.59, bf16[1,96]{1,0:T(2,128)(2,1)} %bitcast.60, bf16[1,96]{1,0:T(2,128)(2,1)} %bitcast.61, bf16[1,96]{1,0:T(2,128)(2,1)} %bitcast.62, bf16[1,96]{1,0:T(2,128)(2,1)} %bitcast.63, ...), custom_call_target="tpu_custom_call" | custom-call | flops 1000 | tf_op jit(solution)/shard_map/pallas_call | solution.py:765
  2.5 3.0 %collective-permute-start = (bf16[256,768]{1,0:T(8,128)(2,1)}, bf16[256,768]{1,0:T(8,128)(2,1)S(1)}, u32[]{:S(2)}, u32[]{:S(2)}) collective-permute-start(bf16[256,768]{1,0:T(8,128)(2,1)} %bitcast.45), channel_id=1, source_target_pairs={{0,2},{1,3},{2,0},{3,1},{4,6},{5,7},{6,4},{7,5},{8,10},{9,11},{10,... | collective-permute-start | bytes 1179656 | tf_op jit(solution)/shard_map/ppermute | solution.py:19
  5.5 1.5 collective-permute-start.2
  7.1 2.6 %collective-permute-start.1 = (bf16[104,768]{1,0:T(8,128)(2,1)}, bf16[104,768]{1,0:T(8,128)(2,1)S(1)}, u32[]{:S(2)}, u32[]{:S(2)}) collective-permute-start(bf16[104,768]{1,0:T(8,128)(2,1)} %shard_map.289.refs_0_), channel_id=1, source_target_pairs={{0,16},{4,20},{8,24},{12,28},{16,0},{20,4},{24,8},{28,12},{1,17},{... | collective-permute-start | bytes 479240 | tf_op jit(solution)/shard_map/ppermute | solution.py:19
  9.7 0.9 copy-done.4
  10.6 1.0 copy-done.5
  11.6 0.9 copy-done
  12.5 0.9 copy-done.2
  13.5 3.4 %collective-permute-done.1.b = bf16[104,768]{1,0:T(8,128)(2,1)S(1)} collective-permute-done((bf16[104,768]{1,0:T(8,128)(2,1)}, bf16[104,768]{1,0:T(8,128)(2,1)S(1)}, u32[]{:S(2)}, u32[]{:S(2)}) %collective-permute-start.1) | collective-permute-done | bytes 159776 | tf_op jit(solution)/shard_map/ppermute | solution.py:19
  18.3 1.5 collective-permute-start.6
  20.3 3.3 %collective-permute-start.5 = (bf16[96,768]{1,0:T(8,128)(2,1)S(1)}, bf16[96,768]{1,0:T(8,128)(2,1)S(1)}, u32[]{:S(2)}, u32[]{:S(2)}) collective-permute-start(bf16[96,768]{1,0:T(8,128)(2,1)S(1)} %copy-done.1), channel_id=1, source_target_pairs={{0,16},{4,20},{8,24},{12,28},{16,0},{20,4},{24,8},{28,12},{1,17},{... | collective-permute-start | bytes 442376 | tf_op jit(solution)/shard_map/ppermute | solution.py:19
  24.3 3.9 %collective-permute-done.5.b = bf16[96,768]{1,0:T(8,128)(2,1)S(1)} collective-permute-done((bf16[96,768]{1,0:T(8,128)(2,1)S(1)}, bf16[96,768]{1,0:T(8,128)(2,1)S(1)}, u32[]{:S(2)}, u32[]{:S(2)}) %collective-permute-start.5) | collective-permute-done | bytes 147488 | tf_op jit(solution)/shard_map/ppermute | solution.py:19
  28.1 1.9 %collective-permute-done.4 = bf16[104,768]{1,0:T(8,128)(2,1)S(1)} collective-permute-done((bf16[104,768]{1,0:T(8,128)(2,1)S(1)}, bf16[104,768]{1,0:T(8,128)(2,1)S(1)}, u32[]{:S(2)}, u32[]{:S(2)}) %collective-permute-start.4) | collective-permute-done | bytes 159776 | tf_op jit(solution)/shard_map/ppermute | solution.py:19
  31.4 2.2 %collective-permute-start.10 = (bf16[2,96,768]{2,1,0:T(8,128)(2,1)S(1)}, bf16[2,96,768]{2,1,0:T(8,128)(2,1)S(1)}, u32[]{:S(2)}, u32[]{:S(2)}) collective-permute-start(bf16[2,96,768]{2,1,0:T(8,128)(2,1)S(1)} %shard_map.298), channel_id=1, source_target_pairs={{0,8},{4,12},{8,0},{12,4},{16,24},{20,28},{24,16},{28,20},{1,9},{5... | collective-permute-start | bytes 884744 | tf_op jit(solution)/shard_map/ppermute | solution.py:19
  33.5 1.7 %collective-permute-start.11 = (bf16[96,768]{1,0:T(8,128)(2,1)S(1)}, bf16[96,768]{1,0:T(8,128)(2,1)S(1)}, u32[]{:S(2)}, u32[]{:S(2)}) collective-permute-start(bf16[96,768]{1,0:T(8,128)(2,1)S(1)} %bitcast.39), channel_id=1, source_target_pairs={{0,16},{4,20},{8,24},{12,28},{16,0},{20,4},{24,8},{28,12},{1,17},{... | collective-permute-start | bytes 442376 | tf_op jit(solution)/shard_map/ppermute | solution.py:19
  35.3 1.8 %shard_map.294 = (bf16[1024,768]{1,0:T(8,128)(2,1)S(1)}, f32[1024,768]{1,0:T(8,128)S(1)}) custom-call(s32[8]{0:T(128)S(1)} %dynamic-slice_bitcast_fusion.place, bf16[2,256,768]{2,1,0:T(8,128)(2,1)S(1)} %shard_map.293.x_zero, bf16[2,256,768]{2,1,0:T(8,128)(2,1)S(1)} %collective-permute-done.9.x_one, bf16[6,768]{1,0:T(8,128)(2,1)S(1)} %bitcast.52, ...), custom_call_target="tpu_custom_call" | custom-call | flops 1000 | tf_op jit(solution)/shard_map/pallas_call | solution.py:120
  37.0 3.7 %collective-permute-done.8.refs_5_ = bf16[2,104,768]{2,1,0:T(8,128)(2,1)S(1)} collective-permute-done((bf16[2,104,768]{2,1,0:T(8,128)(2,1)S(1)}, bf16[2,104,768]{2,1,0:T(8,128)(2,1)S(1)}, u32[]{:S(2)}, u32[]{:S(2)}) %collective-permute-start.8) | collective-permute-done | bytes 319520 | tf_op jit(solution)/shard_map/ppermute | solution.py:19
  42.1 1.4 shard_map.296
  43.5 3.6 %shard_map.297 = (bf16[512,192]{1,0:T(8,128)(2,1)S(1)}, f32[8,512]{1,0:T(8,128)S(1)}, f32[256,768]{1,0:T(8,128)S(1)}, bf16[256,768]{1,0:T(8,128)(2,1)S(1)}) custom-call(s32[8]{0:T(128)S(1)} %dynamic-slice_bitcast_fusion.place, s32[2]{0:T(128)S(1)} %bitcast.54, bf16[1024,192]{1,0:T(8,128)(2,1)S(1)} %get-tuple-element.201.q_ref, ...), custom_call_target="tpu_custom_call" | custom-call | flops 1000 | tf_op jit(solution)/shard_map/pallas_call | solution.py:120
  47.3 1.6 %collective-permute-start.15 = (bf16[3,96,768]{2,1,0:T(8,128)(2,1)S(1)}, bf16[3,96,768]{2,1,0:T(8,128)(2,1)S(1)}, u32[]{:S(2)}, u32[]{:S(2)}) collective-permute-start(bf16[3,96,768]{2,1,0:T(8,128)(2,1)S(1)} %shard_map.301), channel_id=1, source_target_pairs={{0,4},{4,0},{8,12},{12,8},{16,20},{20,16},{24,28},{28,24},{1,5},{5... | collective-permute-start | bytes 1327112 | tf_op jit(solution)/shard_map/ppermute | solution.py:19
  49.0 1.6 %collective-permute-start.14 = (bf16[256,768]{1,0:T(8,128)(2,1)S(1)}, bf16[256,768]{1,0:T(8,128)(2,1)S(1)}, u32[]{:S(2)}, u32[]{:S(2)}) collective-permute-start(bf16[256,768]{1,0:T(8,128)(2,1)S(1)} %shard_map.299.a), channel_id=1, source_target_pairs={{0,2},{1,3},{2,0},{3,1},{4,6},{5,7},{6,4},{7,5},{8,10},{9,11},{10,... | collective-permute-start | bytes 1179656 | tf_op jit(solution)/shard_map/ppermute | solution.py:19
  50.6 2.2 %collective-permute-start.16 = (bf16[2,96,768]{2,1,0:T(8,128)(2,1)S(1)}, bf16[2,96,768]{2,1,0:T(8,128)(2,1)S(1)}, u32[]{:S(2)}, u32[]{:S(2)}) collective-permute-start(bf16[2,96,768]{2,1,0:T(8,128)(2,1)S(1)} %shard_map.302), channel_id=1, source_target_pairs={{0,8},{4,12},{8,0},{12,4},{16,24},{20,28},{24,16},{28,20},{1,9},{5... | collective-permute-start | bytes 884744 | tf_op jit(solution)/shard_map/ppermute | solution.py:19
  53.5 6.2 %shard_map.300 = (bf16[512,192]{1,0:T(8,128)(2,1)S(1)}, f32[8,512]{1,0:T(8,128)S(1)}, f32[256,768]{1,0:T(8,128)S(1)}, bf16[256,768]{1,0:T(8,128)(2,1)S(1)}) custom-call(s32[8]{0:T(128)S(1)} %dynamic-slice_bitcast_fusion.place, s32[2]{0:T(128)S(1)} %bitcast.55, bf16[1024,192]{1,0:T(8,128)(2,1)S(1)} %get-tuple-element.201.q_ref, ...), custom_call_target="tpu_custom_call" | custom-call | flops 1000 | tf_op jit(solution)/shard_map/pallas_call | solution.py:120
  60.9 1.5 collective-permute-start.20
  62.5 1.6 %collective-permute-start.22 = (bf16[256,768]{1,0:T(8,128)(2,1)S(1)}, bf16[256,768]{1,0:T(8,128)(2,1)S(1)}, u32[]{:S(2)}, u32[]{:S(2)}) collective-permute-start(bf16[256,768]{1,0:T(8,128)(2,1)S(1)} %shard_map.303.a), channel_id=1, source_target_pairs={{0,2},{1,3},{2,0},{3,1},{4,6},{5,7},{6,4},{7,5},{8,10},{9,11},{10,... | collective-permute-start | bytes 1179656 | tf_op jit(solution)/shard_map/ppermute | solution.py:19
  64.7 1.5 %shard_map.305.probs_ref = bf16[3,512,512]{2,1,0:T(8,128)(2,1)S(1)} custom-call(s32[8]{0:T(128)S(1)} %dynamic-slice_bitcast_fusion.place, s32[2]{0:T(128)S(1)} %bitcast.56, bf16[1024,192]{1,0:T(8,128)(2,1)S(1)} %get-tuple-element.201.q_ref, bf16[1024,192]{1,0:T(8,128)(2,1)S(1)} %get-tuple-element.202.k_ref, f32[8,512]{1,0:T(8,128)S(1)} %get-tuple-element.218.log), custom_call_target="tpu_custom_call" | custom-call | flops 1000 | tf_op jit(solution)/shard_map/pallas_call | solution.py:120
  66.3 2.7 %shard_map.304.probs_ref = bf16[3,1024,512]{2,1,0:T(8,128)(2,1)S(1)} custom-call(s32[8]{0:T(128)S(1)} %dynamic-slice_bitcast_fusion.place, s32[2]{0:T(128)S(1)} %bitcast.57, bf16[1024,192]{1,0:T(8,128)(2,1)S(1)} %get-tuple-element.201.q_ref, bf16[1024,192]{1,0:T(8,128)(2,1)S(1)} %get-tuple-element.202.k_ref, f32[8,512]{1,0:T(8,128)S(1)} %get-tuple-element.217.log), custom_call_target="tpu_custom_call" | custom-call | flops 1000 | tf_op jit(solution)/shard_map/pallas_call | solution.py:120
  69.0 0.9 collective-permute-done.20.refs_5_
  70.6 2.8 %shard_map.310 = (f32[512,768]{1,0:T(8,128)S(1)}, bf16[512,768]{1,0:T(8,128)(2,1)S(1)}, bf16[512,768]{1,0:T(8,128)(2,1)S(1)}, bf16[512,768]{1,0:T(8,128)(2,1)S(1...) custom-call(bf16[1024,768]{1,0:T(8,128)(2,1)S(1)} %get-tuple-element.236.spliced.rest_0_, ...), custom_call_target="tpu_custom_call" | custom-call | flops 1000 | tf_op jit(solution)/shard_map/pallas_call | solution.py:120
  74.1 1.0 collective-permute-done.21.b
  75.2 1.6 %collective-permute-start.24 = (bf16[256,768]{1,0:T(8,128)(2,1)S(1)}, bf16[256,768]{1,0:T(8,128)(2,1)S(1)}, u32[]{:S(2)}, u32[]{:S(2)}) collective-permute-start(bf16[256,768]{1,0:T(8,128)(2,1)S(1)} %shard_map.311.a), channel_id=1, source_target_pairs={{0,2},{1,3},{2,0},{3,1},{4,6},{5,7},{6,4},{7,5},{8,10},{9,11},{10,... | collective-permute-start | bytes 1179656 | tf_op jit(solution)/shard_map/ppermute | solution.py:19
  76.8 2.8 %shard_map.313 = (f32[512,768]{1,0:T(8,128)S(1)}, bf16[512,768]{1,0:T(8,128)(2,1)S(1)}, bf16[512,768]{1,0:T(8,128)(2,1)S(1)}, bf16[512,768]{1,0:T(8,128)(2,1)S(1...) custom-call(bf16[1024,768]{1,0:T(8,128)(2,1)S(1)} %get-tuple-element.236.spliced.rest_0_, ...), custom_call_target="tpu_custom_call" | custom-call | flops 1000 | tf_op jit(solution)/shard_map/pallas_call | solution.py:120
  79.6 2.1 %shard_map.314 = (f32[4,96,768]{2,1,0:T(8,128)S(1)}, bf16[4,96,768]{2,1,0:T(8,128)(2,1)S(1)}) custom-call(s32[8]{0:T(128)S(1)} %dynamic-slice_bitcast_fusion.place, bf16[512,768]{1,0:T(8,128)(2,1)S(1)} %get-tuple-element.235.refs_0_, bf16[512,768]{1,0:T(8,128)(2,1)S(1)} %get-tuple-element.237.refs_1_, bf16[512,768]{1,0:T(8,128)(2,1)S(1)} %get-tuple-element.238.refs_2_, ...), custom_call_target="tpu_custom_call" | custom-call | flops 1000 | tf_op jit(solution)/shard_map/pallas_call | solution.py:120
  81.7 1.6 %collective-permute-start.27 = (bf16[4,96,768]{2,1,0:T(8,128)(2,1)S(1)}, bf16[4,96,768]{2,1,0:T(8,128)(2,1)S(1)}, u32[]{:S(2)}, u32[]{:S(2)}) collective-permute-start(bf16[4,96,768]{2,1,0:T(8,128)(2,1)S(1)} %get-tuple-element.240), channel_id=1, source_target_pairs={{0,4},{4,0},{8,12},{12,8},{16,20},{20,16},{24,28},{28,24},{1,5},{5... | collective-permute-start | bytes 1769480 | tf_op jit(solution)/shard_map/ppermute | solution.py:19
  83.3 3.1 %collective-permute-done.24.b = bf16[256,768]{1,0:T(8,128)(2,1)S(1)} collective-permute-done((bf16[256,768]{1,0:T(8,128)(2,1)S(1)}, bf16[256,768]{1,0:T(8,128)(2,1)S(1)}, u32[]{:S(2)}, u32[]{:S(2)}) %collective-permute-start.24) | collective-permute-done | bytes 393248 | tf_op jit(solution)/shard_map/ppermute | solution.py:19
  86.7 1.6 %collective-permute-start.28 = (bf16[256,768]{1,0:T(8,128)(2,1)S(1)}, bf16[256,768]{1,0:T(8,128)(2,1)S(1)}, u32[]{:S(2)}, u32[]{:S(2)}) collective-permute-start(bf16[256,768]{1,0:T(8,128)(2,1)S(1)} %shard_map.318.a), channel_id=1, source_target_pairs={{0,2},{1,3},{2,0},{3,1},{4,6},{5,7},{6,4},{7,5},{8,10},{9,11},{10,... | collective-permute-start | bytes 1179656 | tf_op jit(solution)/shard_map/ppermute | solution.py:19
  88.2 2.1 %shard_map.323 = (f32[4,96,768]{2,1,0:T(8,128)S(1)}, bf16[4,96,768]{2,1,0:T(8,128)(2,1)S(1)}) custom-call(s32[8]{0:T(128)S(1)} %dynamic-slice_bitcast_fusion.place, bf16[2,256,768]{2,1,0:T(8,128)(2,1)S(1)} %shard_map.307.cot_zero, bf16[2,256,768]{2,1,0:T(8,128)(2,1)S(1)} %collective-permute-done.19.cot_one, ...), custom_call_target="tpu_custom_call" | custom-call | flops 1000 | tf_op jit(solution)/shard_map/pallas_call | solution.py:120
  90.4 1.6 %collective-permute-start.31 = (bf16[4,96,768]{2,1,0:T(8,128)(2,1)S(1)}, bf16[4,96,768]{2,1,0:T(8,128)(2,1)S(1)}, u32[]{:S(2)}, u32[]{:S(2)}) collective-permute-start(bf16[4,96,768]{2,1,0:T(8,128)(2,1)S(1)} %get-tuple-element.266), channel_id=1, source_target_pairs={{0,4},{4,0},{8,12},{12,8},{16,20},{20,16},{24,28},{28,24},{1,5},{5... | collective-permute-start | bytes 1769480 | tf_op jit(solution)/shard_map/ppermute | solution.py:19
  91.9 1.4 shard_map.326
  93.4 2.0 %shard_map.316 = (f32[512,768]{1,0:T(8,128)S(1)}, bf16[512,768]{1,0:T(8,128)(2,1)S(1)}, bf16[512,192]{1,0:T(8,128)(2,1)S(1)}, f32[8,512]{1,0:T(8,128)S(1)}, f32[8,768]{1,0:T(8,128)S(1)}) custom-call(bf16[256,768]{1,0:T(8,128)(2,1)S(1)} %shard_map.315.total, bf16[256,768]{1,0:T(8,128)(2,1)S(1)} %collective-permute-done.25.other, ...), custom_call_target="tpu_custom_call" | custom-call | flops 1000 | tf_op jit(solution)/shard_map/pallas_call | solution.py:120
  95.5 3.3 %shard_map.317 = (bf16[512,192]{1,0:T(8,128)(2,1)S(1)}, f32[512,192]{1,0:T(8,128)S(1)}, f32[512,192]{1,0:T(8,128)S(1)}) custom-call(s32[8]{0:T(128)S(1)} %dynamic-slice_bitcast_fusion.place, bf16[1024,192]{1,0:T(8,128)(2,1)S(1)} %get-tuple-element.201.q_ref, bf16[1024,192]{1,0:T(8,128)(2,1)S(1)} %get-tuple-element.202.k_ref, ...), custom_call_target="tpu_custom_call" | custom-call | flops 1000 | tf_op jit(solution)/shard_map/pallas_call | solution.py:120
  100.2 2.2 %collective-permute-start.30 = (bf16[2,96,768]{2,1,0:T(8,128)(2,1)S(1)}, bf16[2,96,768]{2,1,0:T(8,128)(2,1)S(1)}, u32[]{:S(2)}, u32[]{:S(2)}) collective-permute-start(bf16[2,96,768]{2,1,0:T(8,128)(2,1)S(1)} %get-tuple-element.261), channel_id=1, source_target_pairs={{0,8},{4,12},{8,0},{12,4},{16,24},{20,28},{24,16},{28,20},{1,9},{5... | collective-permute-start | bytes 884744 | tf_op jit(solution)/shard_map/ppermute | solution.py:19
  102.3 2.1 %shard_map.320 = (f32[512,768]{1,0:T(8,128)S(1)}, bf16[512,768]{1,0:T(8,128)(2,1)S(1)}, bf16[512,192]{1,0:T(8,128)(2,1)S(1)}, f32[8,512]{1,0:T(8,128)S(1)}, f32[8,768]{1,0:T(8,128)S(1)}) custom-call(bf16[256,768]{1,0:T(8,128)(2,1)S(1)} %shard_map.319.total, bf16[256,768]{1,0:T(8,128)(2,1)S(1)} %collective-permute-done.29.other, ...), custom_call_target="tpu_custom_call" | custom-call | flops 1000 | tf_op jit(solution)/shard_map/pallas_call | solution.py:120
  104.4 5.5 %shard_map.321 = (bf16[512,192]{1,0:T(8,128)(2,1)S(1)}, bf16[1024,192]{1,0:T(8,128)(2,1)S(1)}, bf16[1024,192]{1,0:T(8,128)(2,1)S(1)}) custom-call(s32[8]{0:T(128)S(1)} %dynamic-slice_bitcast_fusion.place, bf16[1024,192]{1,0:T(8,128)(2,1)S(1)} %get-tuple-element.201.q_ref, bf16[1024,192]{1,0:T(8,128)(2,1)S(1)} %get-tuple-element.202.k_ref, ...), custom_call_target="tpu_custom_call" | custom-call | flops 1000 | tf_op jit(solution)/shard_map/pallas_call | solution.py:120
  109.9 1.7 %shard_map.325 = (f32[4,96,384]{2,1,0:T(8,128)S(1)}, bf16[4,96,384]{2,1,0:T(8,128)(2,1)S(1)}) custom-call(s32[8]{0:T(128)S(1)} %dynamic-slice_bitcast_fusion.place, bf16[1024,768]{1,0:T(8,128)(2,1)S(1)} %get-tuple-element.273.normed, bf16[512,192]{1,0:T(8,128)(2,1)S(1)} %get-tuple-element.246.dq_zero, bf16[512,192]{1,0:T(8,128)(2,1)S(1)} %get-tuple-element.257.dq_one, ...), custom_call_target="tpu_custom_call" | custom-call | flops 1000 | tf_op jit(solution)/shard_map/pallas_call | solution.py:120
  111.7 2.2 %shard_map.324 = (f32[2,256,768]{2,1,0:T(8,128)S(1)}, bf16[256,768]{1,0:T(8,128)(2,1)S(1)}, bf16[256,768]{1,0:T(8,128)(2,1)S(1)}, f32[8,768]{1,0:T(8,128)S(1)}, ...) custom-call(s32[8]{0:T(128)S(1)} %dynamic-slice_bitcast_fusion.place, s32[6]{0:T(128)S(1)} %bitcast.58, ...), custom_call_target="tpu_custom_call" | custom-call | flops 1000 | tf_op jit(solution)/shard_map/pallas_call | solution.py:120
  114.5 1.7 %collective-permute-done.35.b = f32[8,768]{1,0:T(8,128)S(1)} collective-permute-done((f32[8,768]{1,0:T(8,128)S(1)}, f32[8,768]{1,0:T(8,128)S(1)}, u32[]{:S(2)}, u32[]{:S(2)}) %collective-permute-start.35) | collective-permute-done | bytes 24608 | tf_op jit(solution)/shard_map/ppermute | solution.py:19
  116.8 1.4 collective-permute-start.40
  118.8 1.2 collective-permute-done.36.b
  120.7 1.9 %shard_map.332 = (f32[4,104,384]{2,1,0:T(8,128)S(1)}, bf16[4,104,384]{2,1,0:T(8,128)(2,1)S(1)}) custom-call(s32[8]{0:T(128)S(1)} %dynamic-slice_bitcast_fusion.place, bf16[1024,768]{1,0:T(8,128)(2,1)S(1)} %get-tuple-element.273.normed, bf16[1024,192]{1,0:T(8,128)(2,1)S(1)} %get-tuple-element.267.dk, bf16[1024,192]{1,0:T(8,128)(2,1)S(1)} %get-tuple-element.268.dv, ...), custom_call_target="tpu_custom_call" | custom-call | flops 1000 | tf_op jit(solution)/shard_map/pallas_call | solution.py:120
  122.5 1.6 %collective-permute-start.39 = (bf16[4,104,384]{2,1,0:T(8,128)(2,1)S(1)}, bf16[4,104,384]{2,1,0:T(8,128)(2,1)S(1)}, u32[]{:S(2)}, u32[]{:S(2)}) collective-permute-start(bf16[4,104,384]{2,1,0:T(8,128)(2,1)S(1)} %get-tuple-element.303), channel_id=1, source_target_pairs={{0,4},{4,0},{8,12},{12,8},{16,20},{20,16},{24,28},{28,24},{1,5},{5... | collective-permute-start | bytes 958472 | tf_op jit(solution)/shard_map/ppermute | solution.py:19
  124.1 1.0 shard_map.327
  125.9 1.2 collective-permute-start.37
  127.8 1.8 %collective-permute-start.43 = (bf16[1,96,768]{2,1,0:T(8,128)(2,1)S(1)}, bf16[1,96,768]{2,1,0:T(8,128)(2,1)S(1)}, u32[]{:S(2)}, u32[]{:S(2)}) collective-permute-start(bf16[1,96,768]{2,1,0:T(8,128)(2,1)S(1)} %get-tuple-element.308), channel_id=1, source_target_pairs={{0,16},{4,20},{8,24},{12,28},{16,0},{20,4},{24,8},{28,12},{1,17},{... | collective-permute-start | bytes 442376 | tf_op jit(solution)/shard_map/ppermute | solution.py:19
  130.2 1.6 %collective-permute-start.42 = (bf16[2,96,384]{2,1,0:T(8,128)(2,1)S(1)}, bf16[2,96,384]{2,1,0:T(8,128)(2,1)S(1)}, u32[]{:S(2)}, u32[]{:S(2)}) collective-permute-start(bf16[2,96,384]{2,1,0:T(8,128)(2,1)S(1)} %get-tuple-element.307), channel_id=1, source_target_pairs={{0,8},{4,12},{8,0},{12,4},{16,24},{20,28},{24,16},{28,20},{1,9},{5... | collective-permute-start | bytes 442376 | tf_op jit(solution)/shard_map/ppermute | solution.py:19
  131.8 4.0 %collective-permute-done.43.rest_9_ = bf16[1,96,768]{2,1,0:T(8,128)(2,1)S(1)} collective-permute-done((bf16[1,96,768]{2,1,0:T(8,128)(2,1)S(1)}, bf16[1,96,768]{2,1,0:T(8,128)(2,1)S(1)}, u32[]{:S(2)}, u32[]{:S(2)}) %collective-permute-start.43) | collective-permute-done | bytes 147488 | tf_op jit(solution)/shard_map/ppermute | solution.py:19
  135.7 0.9 collective-permute-done.42.refs_1_
  138.2 2.0 %collective-permute-start.44 = (bf16[1,96,768]{2,1,0:T(8,128)(2,1)S(1)}, bf16[1,96,768]{2,1,0:T(8,128)(2,1)S(1)}, u32[]{:S(2)}, u32[]{:S(2)}) collective-permute-start(bf16[1,96,768]{2,1,0:T(8,128)(2,1)S(1)} %get-tuple-element.313), channel_id=1, source_target_pairs={{0,16},{4,20},{8,24},{12,28},{16,0},{20,4},{24,8},{28,12},{1,17},{... | collective-permute-start | bytes 442376 | tf_op jit(solution)/shard_map/ppermute | solution.py:19
  140.1 2.9 %collective-permute-done.45.refs_1_ = bf16[2,104,384]{2,1,0:T(8,128)(2,1)S(1)} collective-permute-done((bf16[2,104,384]{2,1,0:T(8,128)(2,1)S(1)}, bf16[2,104,384]{2,1,0:T(8,128)(2,1)S(1)}, u32[]{:S(2)}, u32[]{:S(2)}) %collective-permute-start.45) | collective-permute-done | bytes 159776 | tf_op jit(solution)/shard_map/ppermute | solution.py:19
  143.6 1.4 collective-permute-start.46
  145.6 1.7 %collective-permute-start.47 = (bf16[1,96,384]{2,1,0:T(8,128)(2,1)S(1)}, bf16[1,96,384]{2,1,0:T(8,128)(2,1)S(1)}, u32[]{:S(2)}, u32[]{:S(2)}) collective-permute-start(bf16[1,96,384]{2,1,0:T(8,128)(2,1)S(1)} %get-tuple-element.323), channel_id=1, source_target_pairs={{0,16},{4,20},{8,24},{12,28},{16,0},{20,4},{24,8},{28,12},{1,17},{... | collective-permute-start | bytes 221192 | tf_op jit(solution)/shard_map/ppermute | solution.py:19
  147.3 1.3 collective-permute-done.44.rest_11_
  148.6 2.4 %shard_map.335 = (f32[256,768]{1,0:T(8,128)}, f32[6,1,192]{2,1,0:T(1,128)}, f32[96,768]{1,0:T(8,128)}, f32[96,768]{1,0:T(8,128)}, bf16[256,768]{1,0:T(8,128)(2,1)}) custom-call(s32[8]{0:T(128)S(1)} %dynamic-slice_bitcast_fusion.place, f32[256,1536]{1,0:T(8,128)S(1)} %get-tuple-element.284.keep, bf16[256,768]{1,0:T(8,128)(2,1)S(1)} %collective-permute-done.37.got, ...), custom_call_target="tpu_custom_call" | custom-call | flops 1000 | tf_op jit(solution)/shard_map/pallas_call | solution.py:120
  151.7 0.9 shard_map.339
  (104 shorter events, 19.3 us)
Async XLA Ops:
  0.6 19.7 %copy-start.1 = (bf16[96,768]{1,0:T(8,128)(2,1)S(1)}, bf16[96,768]{1,0:T(8,128)(2,1)}, u32[]{:S(2)}) copy-start(bf16[96,768]{1,0:T(8,128)(2,1)} %a.2) | copy-start | bytes 442372
  2.5 14.4 %collective-permute-start = (bf16[256,768]{1,0:T(8,128)(2,1)}, bf16[256,768]{1,0:T(8,128)(2,1)S(1)}, u32[]{:S(2)}, u32[]{:S(2)}) collective-permute-start(bf16[256,768]{1,0:T(8,128)(2,1)} %bitcast.45), channel_id=1, source_target_pairs={{0,2},{1,3},{2,0},{3,1},{4,6},{5,7},{6,4},{7,5},{8,10},{9,11},{10,... | collective-permute-start | bytes 1179656 | tf_op jit(solution)/shard_map/ppermute | solution.py:19
  5.5 8.0 %collective-permute-start.2 = (bf16[104,768]{1,0:T(8,128)(2,1)}, bf16[104,768]{1,0:T(8,128)(2,1)S(1)}, u32[]{:S(2)}, u32[]{:S(2)}) collective-permute-start(bf16[104,768]{1,0:T(8,128)(2,1)} %shard_map.289.refs_0_), channel_id=1, source_target_pairs={{0,4},{4,0},{8,12},{12,8},{16,20},{20,16},{24,28},{28,24},{1,5},{5... | collective-permute-start | bytes 479240 | tf_op jit(solution)/shard_map/ppermute | solution.py:19
  7.1 9.8 %collective-permute-start.1 = (bf16[104,768]{1,0:T(8,128)(2,1)}, bf16[104,768]{1,0:T(8,128)(2,1)S(1)}, u32[]{:S(2)}, u32[]{:S(2)}) collective-permute-start(bf16[104,768]{1,0:T(8,128)(2,1)} %shard_map.289.refs_0_), channel_id=1, source_target_pairs={{0,16},{4,20},{8,24},{12,28},{16,0},{20,4},{24,8},{28,12},{1,17},{... | collective-permute-start | bytes 479240 | tf_op jit(solution)/shard_map/ppermute | solution.py:19
  9.6 0.9 copy-start.4
  10.6 1.0 copy-start.5
  11.6 0.9 copy-start
  12.5 0.9 copy-start.2
  13.5 20.1 %copy-start.3 = (bf16[768,96]{0,1:T(8,128)(2,1)S(1)}, bf16[768,96]{0,1:T(8,128)(2,1)}, u32[]{:S(2)}) copy-start(bf16[768,96]{0,1:T(8,128)(2,1)} %param.32) | copy-start | bytes 442372
  13.5 21.8 %copy-start.7 = (bf16[1,6,768]{2,1,0:T(8,128)(2,1)S(1)}, bf16[1,6,768]{2,1,0:T(8,128)(2,1)}, u32[]{:S(2)}) copy-start(bf16[1,6,768]{2,1,0:T(8,128)(2,1)} %param.19) | copy-start | bytes 27652
  13.5 21.8 %copy-start.9 = (s32[1,6]{1,0:T(1,128)S(1)}, s32[1,6]{1,0:T(1,128)}, u32[]{:S(2)}) copy-start(s32[1,6]{1,0:T(1,128)} %rest_4_.1) | copy-start | bytes 76
  16.9 13.2 %collective-permute-start.7 = (bf16[256,768]{1,0:T(8,128)(2,1)}, bf16[256,768]{1,0:T(8,128)(2,1)S(1)}, u32[]{:S(2)}, u32[]{:S(2)}) collective-permute-start(bf16[256,768]{1,0:T(8,128)(2,1)} %bitcast.47), channel_id=1, source_target_pairs={{0,2},{1,3},{2,0},{3,1},{4,6},{5,7},{6,4},{7,5},{8,10},{9,11},{10,... | collective-permute-start | bytes 1179656 | tf_op jit(solution)/shard_map/ppermute | solution.py:19
  17.5 12.6 %collective-permute-start.3 = (bf16[2,104,768]{2,1,0:T(8,128)(2,1)S(1)}, bf16[2,104,768]{2,1,0:T(8,128)(2,1)S(1)}, u32[]{:S(2)}, u32[]{:S(2)}) collective-permute-start(bf16[2,104,768]{2,1,0:T(8,128)(2,1)S(1)} %shard_map.292), channel_id=1, source_target_pairs={{0,8},{4,12},{8,0},{12,4},{16,24},{20,28},{24,16},{28,20},{1,9},{5... | collective-permute-start | bytes 958472 | tf_op jit(solution)/shard_map/ppermute | solution.py:19
  18.3 11.8 %collective-permute-start.6 = (bf16[2,96,768]{2,1,0:T(8,128)(2,1)S(1)}, bf16[2,96,768]{2,1,0:T(8,128)(2,1)S(1)}, u32[]{:S(2)}, u32[]{:S(2)}) collective-permute-start(bf16[2,96,768]{2,1,0:T(8,128)(2,1)S(1)} %shard_map.291), channel_id=1, source_target_pairs={{0,4},{4,0},{8,12},{12,8},{16,20},{20,16},{24,28},{28,24},{1,5},{5... | collective-permute-start | bytes 884744 | tf_op jit(solution)/shard_map/ppermute | solution.py:19
  19.8 10.3 %collective-permute-start.4 = (bf16[104,768]{1,0:T(8,128)(2,1)S(1)}, bf16[104,768]{1,0:T(8,128)(2,1)S(1)}, u32[]{:S(2)}, u32[]{:S(2)}) collective-permute-start(bf16[104,768]{1,0:T(8,128)(2,1)S(1)} %collective-permute-done.1.b), channel_id=1, source_target_pairs={{0,4},{4,0},{8,12},{12,8},{16,20},{20,16},{24,28},{28,24},{1,5},{5... | collective-permute-start | bytes 479240 | tf_op jit(solution)/shard_map/ppermute | solution.py:19
  20.3 7.8 %collective-permute-start.5 = (bf16[96,768]{1,0:T(8,128)(2,1)S(1)}, bf16[96,768]{1,0:T(8,128)(2,1)S(1)}, u32[]{:S(2)}, u32[]{:S(2)}) collective-permute-start(bf16[96,768]{1,0:T(8,128)(2,1)S(1)} %copy-done.1), channel_id=1, source_target_pairs={{0,16},{4,20},{8,24},{12,28},{16,0},{20,4},{24,8},{28,12},{1,17},{... | collective-permute-start | bytes 442376 | tf_op jit(solution)/shard_map/ppermute | solution.py:19
  30.7 4.6 %collective-permute-start.9 = (bf16[2,256,768]{2,1,0:T(8,128)(2,1)S(1)}, bf16[2,256,768]{2,1,0:T(8,128)(2,1)S(1)}, u32[]{:S(2)}, u32[]{:S(2)}) collective-permute-start(bf16[2,256,768]{2,1,0:T(8,128)(2,1)S(1)} %shard_map.293.x_zero), channel_id=1, source_target_pairs={{0,1},{1,0},{2,3},{3,2},{4,5},{5,4},{6,7},{7,6},{8,9},{9,8},{10,11... | collective-permute-start | bytes 2359304 | tf_op jit(solution)/shard_map/ppermute | solution.py:19
  30.8 10.0 %collective-permute-start.8 = (bf16[2,104,768]{2,1,0:T(8,128)(2,1)S(1)}, bf16[2,104,768]{2,1,0:T(8,128)(2,1)S(1)}, u32[]{:S(2)}, u32[]{:S(2)}) collective-permute-start(bf16[2,104,768]{2,1,0:T(8,128)(2,1)S(1)} %collective-permute-done.3.refs_3_), channel_id=1, source_target_pairs={{0,4},{4,0},{8,12},{12,8},{16,20},{20,16},{24,28},{28,24},{1,5},{5... | collective-permute-start | bytes 958472 | tf_op jit(solution)/shard_map/ppermute | solution.py:19
  31.4 15.8 %collective-permute-start.10 = (bf16[2,96,768]{2,1,0:T(8,128)(2,1)S(1)}, bf16[2,96,768]{2,1,0:T(8,128)(2,1)S(1)}, u32[]{:S(2)}, u32[]{:S(2)}) collective-permute-start(bf16[2,96,768]{2,1,0:T(8,128)(2,1)S(1)} %shard_map.298), channel_id=1, source_target_pairs={{0,8},{4,12},{8,0},{12,4},{16,24},{20,28},{24,16},{28,20},{1,9},{5... | collective-permute-start | bytes 884744 | tf_op jit(solution)/shard_map/ppermute | solution.py:19
  33.5 13.6 %collective-permute-start.11 = (bf16[96,768]{1,0:T(8,128)(2,1)S(1)}, bf16[96,768]{1,0:T(8,128)(2,1)S(1)}, u32[]{:S(2)}, u32[]{:S(2)}) collective-permute-start(bf16[96,768]{1,0:T(8,128)(2,1)S(1)} %bitcast.39), channel_id=1, source_target_pairs={{0,16},{4,20},{8,24},{12,28},{16,0},{20,4},{24,8},{28,12},{1,17},{... | collective-permute-start | bytes 442376 | tf_op jit(solution)/shard_map/ppermute | solution.py:19
  40.7 6.4 %collective-permute-start.12 = (bf16[96,768]{1,0:T(8,128)(2,1)S(1)}, bf16[96,768]{1,0:T(8,128)(2,1)S(1)}, u32[]{:S(2)}, u32[]{:S(2)}) collective-permute-start(bf16[96,768]{1,0:T(8,128)(2,1)S(1)} %collective-permute-done.5.b), channel_id=1, source_target_pairs={{0,4},{4,0},{8,12},{12,8},{16,20},{20,16},{24,28},{28,24},{1,5},{5... | collective-permute-start | bytes 442376 | tf_op jit(solution)/shard_map/ppermute | solution.py:19
  42.1 1.4 copy-start.8
  47.1 5.7 %copy-start.6 = (bf16[1,256,768]{2,1,0:T(8,128)(2,1)S(1)}, bf16[1,256,768]{2,1,0:T(8,128)(2,1)}, u32[]{:S(2)}) copy-start(bf16[1,256,768]{2,1,0:T(8,128)(2,1)} %param.34) | copy-start | bytes 1179652
  47.2 1.8 %collective-permute-start.13 = (bf16[256,768]{1,0:T(8,128)(2,1)S(1)}, bf16[256,768]{1,0:T(8,128)(2,1)S(1)}, u32[]{:S(2)}, u32[]{:S(2)}) collective-permute-start(bf16[256,768]{1,0:T(8,128)(2,1)S(1)} %get-tuple-element.209), channel_id=1, source_target_pairs={{0,1},{1,0},{2,3},{3,2},{4,5},{5,4},{6,7},{7,6},{8,9},{9,8},{10,11... | collective-permute-start | bytes 1179656 | tf_op jit(solution)/shard_map/ppermute | solution.py:19
  47.3 12.6 %collective-permute-start.15 = (bf16[3,96,768]{2,1,0:T(8,128)(2,1)S(1)}, bf16[3,96,768]{2,1,0:T(8,128)(2,1)S(1)}, u32[]{:S(2)}, u32[]{:S(2)}) collective-permute-start(bf16[3,96,768]{2,1,0:T(8,128)(2,1)S(1)} %shard_map.301), channel_id=1, source_target_pairs={{0,4},{4,0},{8,12},{12,8},{16,20},{20,16},{24,28},{28,24},{1,5},{5... | collective-permute-start | bytes 1327112 | tf_op jit(solution)/shard_map/ppermute | solution.py:19
  49.0 11.2 %collective-permute-start.14 = (bf16[256,768]{1,0:T(8,128)(2,1)S(1)}, bf16[256,768]{1,0:T(8,128)(2,1)S(1)}, u32[]{:S(2)}, u32[]{:S(2)}) collective-permute-start(bf16[256,768]{1,0:T(8,128)(2,1)S(1)} %shard_map.299.a), channel_id=1, source_target_pairs={{0,2},{1,3},{2,0},{3,1},{4,6},{5,7},{6,4},{7,5},{8,10},{9,11},{10,... | collective-permute-start | bytes 1179656 | tf_op jit(solution)/shard_map/ppermute | solution.py:19
  50.6 9.2 %collective-permute-start.16 = (bf16[2,96,768]{2,1,0:T(8,128)(2,1)S(1)}, bf16[2,96,768]{2,1,0:T(8,128)(2,1)S(1)}, u32[]{:S(2)}, u32[]{:S(2)}) collective-permute-start(bf16[2,96,768]{2,1,0:T(8,128)(2,1)S(1)} %shard_map.302), channel_id=1, source_target_pairs={{0,8},{4,12},{8,0},{12,4},{16,24},{20,28},{24,16},{28,20},{1,9},{5... | collective-permute-start | bytes 884744 | tf_op jit(solution)/shard_map/ppermute | solution.py:19
  53.4 15.6 %collective-permute-start.19 = (bf16[2,256,768]{2,1,0:T(8,128)(2,1)S(1)}, bf16[2,256,768]{2,1,0:T(8,128)(2,1)S(1)}, u32[]{:S(2)}, u32[]{:S(2)}) collective-permute-start(bf16[2,256,768]{2,1,0:T(8,128)(2,1)S(1)} %shard_map.307.cot_zero), channel_id=1, source_target_pairs={{0,1},{1,0},{2,3},{3,2},{4,5},{5,4},{6,7},{7,6},{8,9},{9,8},{10,11... | collective-permute-start | bytes 2359304 | tf_op jit(solution)/shard_map/ppermute | solution.py:19
  60.3 2.2 %collective-permute-start.17 = (bf16[256,768]{1,0:T(8,128)(2,1)S(1)}, bf16[256,768]{1,0:T(8,128)(2,1)S(1)}, u32[]{:S(2)}, u32[]{:S(2)}) collective-permute-start(bf16[256,768]{1,0:T(8,128)(2,1)S(1)} %get-tuple-element.215), channel_id=1, source_target_pairs={{0,1},{1,0},{2,3},{3,2},{4,5},{5,4},{6,7},{7,6},{8,9},{9,8},{10,11... | collective-permute-start | bytes 1179656 | tf_op jit(solution)/shard_map/ppermute | solution.py:19
  60.4 9.6 %collective-permute-start.18 = (bf16[256,768]{1,0:T(8,128)(2,1)S(1)}, bf16[256,768]{1,0:T(8,128)(2,1)S(1)}, u32[]{:S(2)}, u32[]{:S(2)}) collective-permute-start(bf16[256,768]{1,0:T(8,128)(2,1)S(1)} %shard_map.306.total), channel_id=1, source_target_pairs={{0,1},{1,0},{2,3},{3,2},{4,5},{5,4},{6,7},{7,6},{8,9},{9,8},{10,11... | collective-permute-start | bytes 1179656 | tf_op jit(solution)/shard_map/ppermute | solution.py:19
  60.9 9.0 %collective-permute-start.20 = (bf16[2,96,768]{2,1,0:T(8,128)(2,1)S(1)}, bf16[2,96,768]{2,1,0:T(8,128)(2,1)S(1)}, u32[]{:S(2)}, u32[]{:S(2)}) collective-permute-start(bf16[2,96,768]{2,1,0:T(8,128)(2,1)S(1)} %collective-permute-done.16.refs_3_), channel_id=1, source_target_pairs={{0,4},{4,0},{8,12},{12,8},{16,20},{20,16},{24,28},{28,24},{1,5},{5... | collective-permute-start | bytes 884744 | tf_op jit(solution)/shard_map/ppermute | solution.py:19
  62.5 10.9 %collective-permute-start.22 = (bf16[256,768]{1,0:T(8,128)(2,1)S(1)}, bf16[256,768]{1,0:T(8,128)(2,1)S(1)}, u32[]{:S(2)}, u32[]{:S(2)}) collective-permute-start(bf16[256,768]{1,0:T(8,128)(2,1)S(1)} %shard_map.303.a), channel_id=1, source_target_pairs={{0,2},{1,3},{2,0},{3,1},{4,6},{5,7},{6,4},{7,5},{8,10},{9,11},{10,... | collective-permute-start | bytes 1179656 | tf_op jit(solution)/shard_map/ppermute | solution.py:19
  73.3 1.8 %collective-permute-start.21 = (bf16[256,768]{1,0:T(8,128)(2,1)S(1)}, bf16[256,768]{1,0:T(8,128)(2,1)S(1)}, u32[]{:S(2)}, u32[]{:S(2)}) collective-permute-start(bf16[256,768]{1,0:T(8,128)(2,1)S(1)} %get-tuple-element.234), channel_id=1, source_target_pairs={{0,1},{1,0},{2,3},{3,2},{4,5},{5,4},{6,7},{7,6},{8,9},{9,8},{10,11... | collective-permute-start | bytes 1179656 | tf_op jit(solution)/shard_map/ppermute | solution.py:19
  73.5 3.2 %collective-permute-start.23 = (bf16[256,768]{1,0:T(8,128)(2,1)S(1)}, bf16[256,768]{1,0:T(8,128)(2,1)S(1)}, u32[]{:S(2)}, u32[]{:S(2)}) collective-permute-start(bf16[256,768]{1,0:T(8,128)(2,1)S(1)} %shard_map.312.total), channel_id=1, source_target_pairs={{0,1},{1,0},{2,3},{3,2},{4,5},{5,4},{6,7},{7,6},{8,9},{9,8},{10,11... | collective-permute-start | bytes 1179656 | tf_op jit(solution)/shard_map/ppermute | solution.py:19
  75.2 11.2 %collective-permute-start.24 = (bf16[256,768]{1,0:T(8,128)(2,1)S(1)}, bf16[256,768]{1,0:T(8,128)(2,1)S(1)}, u32[]{:S(2)}, u32[]{:S(2)}) collective-permute-start(bf16[256,768]{1,0:T(8,128)(2,1)S(1)} %shard_map.311.a), channel_id=1, source_target_pairs={{0,2},{1,3},{2,0},{3,1},{4,6},{5,7},{6,4},{7,5},{8,10},{9,11},{10,... | collective-permute-start | bytes 1179656 | tf_op jit(solution)/shard_map/ppermute | solution.py:19
  79.6 7.0 %collective-permute-start.26 = (bf16[256,768]{1,0:T(8,128)(2,1)S(1)}, bf16[256,768]{1,0:T(8,128)(2,1)S(1)}, u32[]{:S(2)}, u32[]{:S(2)}) collective-permute-start(bf16[256,768]{1,0:T(8,128)(2,1)S(1)} %get-tuple-element.249), channel_id=1, source_target_pairs={{0,1},{1,0},{2,3},{3,2},{4,5},{5,4},{6,7},{7,6},{8,9},{9,8},{10,11... | collective-permute-start | bytes 1179656 | tf_op jit(solution)/shard_map/ppermute | solution.py:19
  81.7 17.1 %collective-permute-start.27 = (bf16[4,96,768]{2,1,0:T(8,128)(2,1)S(1)}, bf16[4,96,768]{2,1,0:T(8,128)(2,1)S(1)}, u32[]{:S(2)}, u32[]{:S(2)}) collective-permute-start(bf16[4,96,768]{2,1,0:T(8,128)(2,1)S(1)} %get-tuple-element.240), channel_id=1, source_target_pairs={{0,4},{4,0},{8,12},{12,8},{16,20},{20,16},{24,28},{28,24},{1,5},{5... | collective-permute-start | bytes 1769480 | tf_op jit(solution)/shard_map/ppermute | solution.py:19
  86.5 3.8 %collective-permute-start.25 = (bf16[256,768]{1,0:T(8,128)(2,1)S(1)}, bf16[256,768]{1,0:T(8,128)(2,1)S(1)}, u32[]{:S(2)}, u32[]{:S(2)}) collective-permute-start(bf16[256,768]{1,0:T(8,128)(2,1)S(1)} %shard_map.315.total), channel_id=1, source_target_pairs={{0,1},{1,0},{2,3},{3,2},{4,5},{5,4},{6,7},{7,6},{8,9},{9,8},{10,11... | collective-permute-start | bytes 1179656 | tf_op jit(solution)/shard_map/ppermute | solution.py:19
  86.7 12.1 %collective-permute-start.28 = (bf16[256,768]{1,0:T(8,128)(2,1)S(1)}, bf16[256,768]{1,0:T(8,128)(2,1)S(1)}, u32[]{:S(2)}, u32[]{:S(2)}) collective-permute-start(bf16[256,768]{1,0:T(8,128)(2,1)S(1)} %shard_map.318.a), channel_id=1, source_target_pairs={{0,2},{1,3},{2,0},{3,1},{4,6},{5,7},{6,4},{7,5},{8,10},{9,11},{10,... | collective-permute-start | bytes 1179656 | tf_op jit(solution)/shard_map/ppermute | solution.py:19
  90.4 21.3 %collective-permute-start.31 = (bf16[4,96,768]{2,1,0:T(8,128)(2,1)S(1)}, bf16[4,96,768]{2,1,0:T(8,128)(2,1)S(1)}, u32[]{:S(2)}, u32[]{:S(2)}) collective-permute-start(bf16[4,96,768]{2,1,0:T(8,128)(2,1)S(1)} %get-tuple-element.266), channel_id=1, source_target_pairs={{0,4},{4,0},{8,12},{12,8},{16,20},{20,16},{24,28},{28,24},{1,5},{5... | collective-permute-start | bytes 1769480 | tf_op jit(solution)/shard_map/ppermute | solution.py:19
  93.4 29.2 %collective-permute-start.34 = (bf16[2,256,768]{2,1,0:T(8,128)(2,1)S(1)}, bf16[2,256,768]{2,1,0:T(8,128)(2,1)S(1)}, u32[]{:S(2)}, u32[]{:S(2)}) collective-permute-start(bf16[2,256,768]{2,1,0:T(8,128)(2,1)S(1)} %get-tuple-element.283), channel_id=1, source_target_pairs={{0,1},{1,0},{2,3},{3,2},{4,5},{5,4},{6,7},{7,6},{8,9},{9,8},{10,11... | collective-permute-start | bytes 2359304 | tf_op jit(solution)/shard_map/ppermute | solution.py:19
  98.9 3.4 %collective-permute-start.29 = (bf16[256,768]{1,0:T(8,128)(2,1)S(1)}, bf16[256,768]{1,0:T(8,128)(2,1)S(1)}, u32[]{:S(2)}, u32[]{:S(2)}) collective-permute-start(bf16[256,768]{1,0:T(8,128)(2,1)S(1)} %shard_map.319.total), channel_id=1, source_target_pairs={{0,1},{1,0},{2,3},{3,2},{4,5},{5,4},{6,7},{7,6},{8,9},{9,8},{10,11... | collective-permute-start | bytes 1179656 | tf_op jit(solution)/shard_map/ppermute | solution.py:19
  100.2 11.5 %collective-permute-start.30 = (bf16[2,96,768]{2,1,0:T(8,128)(2,1)S(1)}, bf16[2,96,768]{2,1,0:T(8,128)(2,1)S(1)}, u32[]{:S(2)}, u32[]{:S(2)}) collective-permute-start(bf16[2,96,768]{2,1,0:T(8,128)(2,1)S(1)} %get-tuple-element.261), channel_id=1, source_target_pairs={{0,8},{4,12},{8,0},{12,4},{16,24},{20,28},{24,16},{28,20},{1,9},{5... | collective-permute-start | bytes 884744 | tf_op jit(solution)/shard_map/ppermute | solution.py:19
  113.8 10.3 %collective-permute-start.33 = (bf16[256,768]{1,0:T(8,128)(2,1)S(1)}, bf16[256,768]{1,0:T(8,128)(2,1)S(1)}, u32[]{:S(2)}, u32[]{:S(2)}) collective-permute-start(bf16[256,768]{1,0:T(8,128)(2,1)S(1)} %get-tuple-element.279), channel_id=1, source_target_pairs={{0,1},{1,0},{2,3},{3,2},{4,5},{5,4},{6,7},{7,6},{8,9},{9,8},{10,11... | collective-permute-start | bytes 1179656 | tf_op jit(solution)/shard_map/ppermute | solution.py:19
  113.9 10.2 %collective-permute-start.32 = (bf16[256,768]{1,0:T(8,128)(2,1)S(1)}, bf16[256,768]{1,0:T(8,128)(2,1)S(1)}, u32[]{:S(2)}, u32[]{:S(2)}) collective-permute-start(bf16[256,768]{1,0:T(8,128)(2,1)S(1)} %get-tuple-element.277), channel_id=1, source_target_pairs={{0,1},{1,0},{2,3},{3,2},{4,5},{5,4},{6,7},{7,6},{8,9},{9,8},{10,11... | collective-permute-start | bytes 1179656 | tf_op jit(solution)/shard_map/ppermute | solution.py:19
  114.4 1.8 %collective-permute-start.35 = (f32[8,768]{1,0:T(8,128)S(1)}, f32[8,768]{1,0:T(8,128)S(1)}, u32[]{:S(2)}, u32[]{:S(2)}) collective-permute-start(f32[8,768]{1,0:T(8,128)S(1)} %get-tuple-element.286.a), channel_id=1, source_target_pairs={{0,1},{1,0},{2,3},{3,2},{4,5},{5,4},{6,7},{7,6},{8,9},{9,8},{10,11... | collective-permute-start | bytes 73736 | tf_op jit(solution)/shard_map/ppermute | solution.py:19
  116.2 3.8 %collective-permute-start.36 = (f32[8,768]{1,0:T(8,128)S(1)}, f32[8,768]{1,0:T(8,128)S(1)}, u32[]{:S(2)}, u32[]{:S(2)}) collective-permute-start(f32[8,768]{1,0:T(8,128)S(1)} %shard_map.328.a), channel_id=1, source_target_pairs={{0,2},{1,3},{2,0},{3,1},{4,6},{5,7},{6,4},{7,5},{8,10},{9,11},{10,... | collective-permute-start | bytes 73736 | tf_op jit(solution)/shard_map/ppermute | solution.py:19
  116.8 11.0 %collective-permute-start.40 = (bf16[4,96,384]{2,1,0:T(8,128)(2,1)S(1)}, bf16[4,96,384]{2,1,0:T(8,128)(2,1)S(1)}, u32[]{:S(2)}, u32[]{:S(2)}) collective-permute-start(bf16[4,96,384]{2,1,0:T(8,128)(2,1)S(1)} %get-tuple-element.305), channel_id=1, source_target_pairs={{0,4},{4,0},{8,12},{12,8},{16,20},{20,16},{24,28},{28,24},{1,5},{5... | collective-permute-start | bytes 884744 | tf_op jit(solution)/shard_map/ppermute | solution.py:19
  120.0 9.6 %collective-permute-start.41 = (bf16[2,96,768]{2,1,0:T(8,128)(2,1)S(1)}, bf16[2,96,768]{2,1,0:T(8,128)(2,1)S(1)}, u32[]{:S(2)}, u32[]{:S(2)}) collective-permute-start(bf16[2,96,768]{2,1,0:T(8,128)(2,1)S(1)} %get-tuple-element.295), channel_id=1, source_target_pairs={{0,8},{4,12},{8,0},{12,4},{16,24},{20,28},{24,16},{28,20},{1,9},{5... | collective-permute-start | bytes 884744 | tf_op jit(solution)/shard_map/ppermute | solution.py:19
  122.5 13.2 %collective-permute-start.39 = (bf16[4,104,384]{2,1,0:T(8,128)(2,1)S(1)}, bf16[4,104,384]{2,1,0:T(8,128)(2,1)S(1)}, u32[]{:S(2)}, u32[]{:S(2)}) collective-permute-start(bf16[4,104,384]{2,1,0:T(8,128)(2,1)S(1)} %get-tuple-element.303), channel_id=1, source_target_pairs={{0,4},{4,0},{8,12},{12,8},{16,20},{20,16},{24,28},{28,24},{1,5},{5... | collective-permute-start | bytes 958472 | tf_op jit(solution)/shard_map/ppermute | solution.py:19
  125.1 23.5 %collective-permute-start.38 = (bf16[256,768]{1,0:T(8,128)(2,1)S(1)}, bf16[256,768]{1,0:T(8,128)(2,1)S(1)}, u32[]{:S(2)}, u32[]{:S(2)}) collective-permute-start(bf16[256,768]{1,0:T(8,128)(2,1)S(1)} %get-tuple-element.289), channel_id=1, source_target_pairs={{0,2},{1,3},{2,0},{3,1},{4,6},{5,7},{6,4},{7,5},{8,10},{9,11},{10,... | collective-permute-start | bytes 1179656 | tf_op jit(solution)/shard_map/ppermute | solution.py:19
  125.9 22.6 %collective-permute-start.37 = (bf16[256,768]{1,0:T(8,128)(2,1)S(1)}, bf16[256,768]{1,0:T(8,128)(2,1)S(1)}, u32[]{:S(2)}, u32[]{:S(2)}) collective-permute-start(bf16[256,768]{1,0:T(8,128)(2,1)S(1)} %get-tuple-element.287), channel_id=1, source_target_pairs={{0,2},{1,3},{2,0},{3,1},{4,6},{5,7},{6,4},{7,5},{8,10},{9,11},{10,... | collective-permute-start | bytes 1179656 | tf_op jit(solution)/shard_map/ppermute | solution.py:19
  127.8 7.9 %collective-permute-start.43 = (bf16[1,96,768]{2,1,0:T(8,128)(2,1)S(1)}, bf16[1,96,768]{2,1,0:T(8,128)(2,1)S(1)}, u32[]{:S(2)}, u32[]{:S(2)}) collective-permute-start(bf16[1,96,768]{2,1,0:T(8,128)(2,1)S(1)} %get-tuple-element.308), channel_id=1, source_target_pairs={{0,16},{4,20},{8,24},{12,28},{16,0},{20,4},{24,8},{28,12},{1,17},{... | collective-permute-start | bytes 442376 | tf_op jit(solution)/shard_map/ppermute | solution.py:19
  130.2 6.5 %collective-permute-start.42 = (bf16[2,96,384]{2,1,0:T(8,128)(2,1)S(1)}, bf16[2,96,384]{2,1,0:T(8,128)(2,1)S(1)}, u32[]{:S(2)}, u32[]{:S(2)}) collective-permute-start(bf16[2,96,384]{2,1,0:T(8,128)(2,1)S(1)} %get-tuple-element.307), channel_id=1, source_target_pairs={{0,8},{4,12},{8,0},{12,4},{16,24},{20,28},{24,16},{28,20},{1,9},{5... | collective-permute-start | bytes 442376 | tf_op jit(solution)/shard_map/ppermute | solution.py:19
  137.3 5.8 %collective-permute-start.45 = (bf16[2,104,384]{2,1,0:T(8,128)(2,1)S(1)}, bf16[2,104,384]{2,1,0:T(8,128)(2,1)S(1)}, u32[]{:S(2)}, u32[]{:S(2)}) collective-permute-start(bf16[2,104,384]{2,1,0:T(8,128)(2,1)S(1)} %get-tuple-element.319), channel_id=1, source_target_pairs={{0,8},{4,12},{8,0},{12,4},{16,24},{20,28},{24,16},{28,20},{1,9},{5... | collective-permute-start | bytes 479240 | tf_op jit(solution)/shard_map/ppermute | solution.py:19
  138.2 10.4 %collective-permute-start.44 = (bf16[1,96,768]{2,1,0:T(8,128)(2,1)S(1)}, bf16[1,96,768]{2,1,0:T(8,128)(2,1)S(1)}, u32[]{:S(2)}, u32[]{:S(2)}) collective-permute-start(bf16[1,96,768]{2,1,0:T(8,128)(2,1)S(1)} %get-tuple-element.313), channel_id=1, source_target_pairs={{0,16},{4,20},{8,24},{12,28},{16,0},{20,4},{24,8},{28,12},{1,17},{... | collective-permute-start | bytes 442376 | tf_op jit(solution)/shard_map/ppermute | solution.py:19
  143.6 8.0 %collective-permute-start.46 = (bf16[1,104,384]{2,1,0:T(8,128)(2,1)S(1)}, bf16[1,104,384]{2,1,0:T(8,128)(2,1)S(1)}, u32[]{:S(2)}, u32[]{:S(2)}) collective-permute-start(bf16[1,104,384]{2,1,0:T(8,128)(2,1)S(1)} %get-tuple-element.320), channel_id=1, source_target_pairs={{0,16},{4,20},{8,24},{12,28},{16,0},{20,4},{24,8},{28,12},{1,17},{... | collective-permute-start | bytes 239624 | tf_op jit(solution)/shard_map/ppermute | solution.py:19
  145.6 6.1 %collective-permute-start.47 = (bf16[1,96,384]{2,1,0:T(8,128)(2,1)S(1)}, bf16[1,96,384]{2,1,0:T(8,128)(2,1)S(1)}, u32[]{:S(2)}, u32[]{:S(2)}) collective-permute-start(bf16[1,96,384]{2,1,0:T(8,128)(2,1)S(1)} %get-tuple-element.323), channel_id=1, source_target_pairs={{0,16},{4,20},{8,24},{12,28},{16,0},{20,4},{24,8},{28,12},{1,17},{... | collective-permute-start | bytes 221192 | tf_op jit(solution)/shard_map/ppermute | solution.py:19
